TPU v7x, 256 devices: a whole 4x4x8 slice. The times are simulated.
256 devices in a mesh: dp: 8 (over x, z_hi), context: 32 (over y, z_lo, core).
Axes of the slice: x: 4, y: 4, z: 8 (z_hi: 2, z_lo: 4; z = z_hi * 4 + z_lo), core: 2. Of those that a mesh axis runs over, the one named last changes fastest.
Arguments:
- grad_out: bfloat16 [8, 4096, 4096], P('dp', 'context'), may hold values from -6 to 6
- attn: bfloat16 [8, 4096, 4096], P('dp', 'context'), may hold values from -0.032958984 to 0.032958984
- w_out: bfloat16 [4096, 4096], P('context'), may hold values from -0.09375 to 0.09375
Outputs:
- grad_attn: bfloat16 [8, 4096, 4096], P('dp', None, 'context')
- grad_w: bfloat16 [4096, 4096], P('context')
All inputs are finite; a program needn't handle non-finite values.
Results may differ from a plain program's by a relative error of at most 0.013.
Values may be sent and summed in bfloat16 or wider, within the bound.
No kernel may reach another device: no remote copies, remote signals or barrier semaphores. Data moves between devices by JAX's collectives and lax.ppermute only.
A program may use at most 128 MiB of HBM per device.

v0:
```python
import jax
import jax.numpy as jnp
from jax import lax
from jax.sharding import Mesh, PartitionSpec as P

CHUNKS = (2048, 2048)
RING8 = ("h", "l")


def shift(v, axis, by):
    n = lax.axis_size(axis)
    return lax.ppermute(v, axis, [(i, (i + by) % n) for i in range(n)])


def pick(v, index, axis):
    return lax.dynamic_index_in_dim(v, index, axis, keepdims=False)


def around(own, axis):
    half = own.shape[0] // 2
    above = shift(own, axis, -1)
    below = shift(own, axis, 1)
    far_a = shift(above[:half], axis, -1)
    far_b = shift(below[half:], axis, 1)
    return [own, above, far_a, far_b, below]


def rolled(pieces, by):
    n = len(pieces)
    twice = jnp.stack(pieces + pieces)
    return lax.dynamic_slice_in_dim(twice, (n - by) & (n - 1), n, 0)


def local(grad_out, attn, w_out):
    f32, bf16 = jnp.float32, jnp.bfloat16
    g = grad_out[0]
    a = attn[0]
    toks, feats = g.shape
    heads = w_out.shape[0]
    quarter = heads // 4
    x, l = lax.axis_index("x"), lax.axis_index("l")

    cuts, at = [], 0
    for size in CHUNKS:
        size = size * feats // sum(CHUNKS)
        cuts.append((at, at + size))
        at += size
    g_cols = [lax.all_gather(g[:, lo:hi], ("y", "c"), axis=0, tiled=True) for lo, hi in cuts]

    w = jnp.concatenate(around(w_out, RING8), 0)

    a = a.reshape(toks, 4, 4, 2, heads).transpose(1, 3, 0, 2, 4).reshape(8, toks, 4 * heads)
    acts = lax.all_to_all(a, ("y", "c"), split_axis=0, concat_axis=0, tiled=True).reshape(8 * toks, 4 * heads)

    sums = []
    for j, gj in enumerate(g_cols):
        part = lax.dot_general(acts, gj, (((0,), (0,)), ((), ())), preferred_element_type=f32).astype(bf16)
        part = part.reshape(4, 4, quarter, -1)
        tot = pick(part, x, 1).astype(f32)
        for d in (1, 2, 3):
            tot = tot + shift(pick(part, (x + d) & 3, 1), "x", d).astype(f32)
        tot = tot.astype(bf16)
        acc = pick(tot, l, 0).astype(f32)
        acc = acc + shift(pick(tot, (l + 1) & 3, 0), RING8, 1).astype(f32)
        acc = acc + shift(pick(tot, (l + 3) & 3, 0), RING8, -1).astype(f32)
        acc = acc + shift(pick(tot, (l + 2) & 3, 0), RING8, 2 if j % 2 else -2).astype(f32)
        acc = acc.astype(bf16)
        sums.append((acc.astype(f32) + shift(acc, "h", 1).astype(f32)).astype(bf16))
    done = jnp.concatenate(sums, 1)
    grad_w = rolled([done] + [shift(done, "x", -d) for d in (1, 2, 3)], x).reshape(heads, feats)

    gall = jnp.concatenate(g_cols, 1)
    res = lax.dot_general(gall, w, (((1,), (1,)), ((), ())), preferred_element_type=f32).astype(bf16)
    res = res.reshape(4, 2, toks, 4, heads)
    outs = [res[:, :, :, 0]] + [shift(res[:, :, :, 4 - d], "l", -d) for d in (1, 2, 3)]
    out = rolled(outs, l)
    out = out.transpose(1, 0, 2, 3, 4).reshape(1, 4 * 4 * 2 * toks, heads)
    return out, grad_w


def solution(mesh):
    fine = Mesh(mesh.devices.reshape(4, 2, 4, 4, 2), ("x", "h", "y", "l", "c"))
    dp, context = ("x", "h"), ("y", "l", "c")
    in_specs = (P(dp, context, None), P(dp, context, None), P(context, None))
    out_specs = (P(dp, None, context), P(context, None))
    return jax.shard_map(local, mesh=fine, in_specs=in_specs, out_specs=out_specs, check_vma=False)
```

profile of v0, /device:TPU:8, one launch (start us, length us, event | category | flops | bytes accessed | tf_op | source)
XLA Modules:
  0.0 210.7 jit_solution(10375536322798868595)
XLA Ops:
  7.2 2.3 %fusion.23 = (bf16[128,2048]{1,0:T(8,128)(2,1)}, bf16[128,2048]{1,0:T(8,128)(2,1)}) fusion(bf16[128,4096]{1,0:T(8,128)(2,1)} %bitcast.97), kind=kLoop, calls=%fused_computation.67 | loop fusion | bytes 2097152 | tf_op jit(solution)/shard_map/slice | solution.py:48
  10.3 5.9 %collective-permute-start = (bf16[128,4096]{1,0:T(8,128)(2,1)}, bf16[128,4096]{1,0:T(8,128)(2,1)S(1)}, u32[]{:S(2)}, u32[]{:S(2)}) collective-permute-start(bf16[128,4096]{1,0:T(8,128)(2,1)} %param.5), channel_id=1, source_target_pairs={{0,38},{2,0},{4,2},{6,4},{32,6},{34,32},{36,34},{38,36},{1,39},{3,... | collective-permute-start | bytes 3145736 | tf_op jit(solution)/shard_map/ppermute | solution.py:12
  18.9 4.9 %all-to-all-start = ((bf16[8,128,512]{1,2,0:T(8,128)(2,1)}), bf16[8,128,512]{1,2,0:T(8,128)(2,1)S(1)}, u32[]{:S(2)}, u32[]{:S(2)}) async-start(bf16[8,128,512]{1,2,0:T(8,128)(2,1)} %bitcast.12), calls=%async_computation | async-start | bytes 2097152 | tf_op jit(solution)/shard_map/all_to_all | solution.py:53
  23.8 15.2 %collective-permute-done = bf16[128,4096]{1,0:T(8,128)(2,1)S(1)} collective-permute-done((bf16[128,4096]{1,0:T(8,128)(2,1)}, bf16[128,4096]{1,0:T(8,128)(2,1)S(1)}, u32[]{:S(2)}, u32[]{:S(2)}) %collective-permute-start) | collective-permute-done | bytes 1048608 | tf_op jit(solution)/shard_map/ppermute | solution.py:12
  39.8 3.6 %collective-permute-start.1 = (bf16[64,4096]{1,0:T(8,128)(2,1)}, bf16[64,4096]{1,0:T(8,128)(2,1)}, u32[]{:S(2)}, u32[]{:S(2)}) collective-permute-start(bf16[64,4096]{1,0:T(8,128)(2,1)} %slice.34), channel_id=1, source_target_pairs={{0,38},{2,0},{4,2},{6,4},{32,6},{34,32},{36,34},{38,36},{1,39},{3,... | collective-permute-start | bytes 1572872 | tf_op jit(solution)/shard_map/ppermute | solution.py:12
  43.3 2.3 %constant_dynamic-update-slice_fusion.4 = bf16[512,4096]{1,0:T(8,128)(2,1)} fusion(bf16[128,4096]{1,0:T(8,128)(2,1)} %param.5), kind=kLoop, calls=%fused_computation.63 | loop fusion | bytes 2097152
  45.7 2.8 %all-to-all-done = bf16[8,128,512]{1,2,0:T(8,128)(2,1)S(1)} async-done(((bf16[8,128,512]{1,2,0:T(8,128)(2,1)}), bf16[8,128,512]{1,2,0:T(8,128)(2,1)S(1)}, u32[]{:S(2)}, u32[]{:S(2)}) %all-to-all-start) | async-done | bytes 1048608 | tf_op jit(solution)/shard_map/all_to_all | solution.py:53
  50.9 3.0 %collective-permute-done.1 = bf16[64,4096]{1,0:T(8,128)(2,1)} collective-permute-done((bf16[64,4096]{1,0:T(8,128)(2,1)}, bf16[64,4096]{1,0:T(8,128)(2,1)}, u32[]{:S(2)}, u32[]{:S(2)}) %collective-permute-start.1) | collective-permute-done | bytes 524320 | tf_op jit(solution)/shard_map/ppermute | solution.py:12
  55.8 8.0 %collective-permute-done.3 = bf16[64,4096]{1,0:T(8,128)(2,1)S(1)} collective-permute-done((bf16[64,4096]{1,0:T(8,128)(2,1)S(1)}, bf16[64,4096]{1,0:T(8,128)(2,1)S(1)}, u32[]{:S(2)}, u32[]{:S(2)}) %collective-permute-start.3) | collective-permute-done | bytes 524320 | tf_op jit(solution)/shard_map/ppermute | solution.py:12
  65.8 24.5 %all-gather.3.cloned.1.call-done = bf16[1024,2048]{1,0:T(8,128)(2,1)} async-done(((bf16[128,2048]{1,0:T(8,128)(2,1)}), bf16[1024,2048]{1,0:T(8,128)(2,1)}) %all-gather.3.cloned.1.call-update) | async-done | bytes 4194320 | tf_op jit(solution)/shard_map/all_gather | solution.py:48
  90.3 9.2 %fusion.4 = bf16[1024,512]{1,0:T(8,128)(2,1)S(1)} fusion(bf16[512,4096]{1,0:T(8,128)(2,1)} %constant_dynamic-update-slice_fusion, bf16[1024,2048]{1,0:T(8,128)(2,1)} %all-gather.5.cloned.1.call-done, bf16[1024,2048]{1,0:T(8,128)(2,1)} %all-gather.3.cloned.1.call-done), kind=kOutput, calls=%fused_computation.6 | convolution fusion | flops 4312268800 | bytes 13631488 | tf_op jit(solution)/shard_map/dot_general | solution.py:73
  99.8 2.0 fusion.22
  101.8 3.6 %collective-permute-start.4 = (bf16[4,2,128,128]{3,2,1,0:T(8,128)(2,1)S(1)}, bf16[4,2,128,128]{3,2,1,0:T(8,128)(2,1)S(1)}, u32[]{:S(2)}, u32[]{:S(2)}) collective-permute-start(bf16[4,2,128,128]{3,2,1,0:T(8,128)(2,1)S(1)} %bitcast.103), channel_id=1, source_target_pairs={{0,6},{2,0},{4,2},{6,4},{1,7},{3,1},{5,3},{7,5},{8,14},{10,8},{12,... | collective-permute-start | bytes 786440 | tf_op jit(solution)/shard_map/ppermute | solution.py:12
  106.9 2.4 %convolution_convert_fusion = bf16[512,2048]{1,0:T(8,128)(2,1)S(1)} fusion(bf16[1024,512]{1,0:T(8,128)(2,1)S(1)} %bitcast.99, bf16[1024,2048]{1,0:T(8,128)(2,1)S(1)} %copy-done.2), kind=kOutput, calls=%fused_computation.4 | convolution fusion | flops 2148532224 | bytes 7340032 | tf_op jit(solution)/shard_map/dot_general | solution.py:57
  109.6 2.8 %collective-permute-start.16 = (bf16[4,32,2048]{2,1,0:T(8,128)(2,1)S(1)}, bf16[4,32,2048]{2,1,0:T(8,128)(2,1)S(1)}, u32[]{:S(2)}, u32[]{:S(2)}) collective-permute-start(bf16[4,32,2048]{2,1,0:T(8,128)(2,1)S(1)} %get-tuple-element.6), channel_id=1, source_target_pairs={{0,192},{64,0},{128,64},{192,128},{1,193},{65,1},{129,65},{193,129... | collective-permute-start | bytes 1572872 | tf_op jit(solution)/shard_map/ppermute | solution.py:12
  113.2 2.4 %convolution_convert_fusion.1 = bf16[512,2048]{1,0:T(8,128)(2,1)S(1)} fusion(bf16[1024,512]{1,0:T(8,128)(2,1)S(1)} %bitcast.100, bf16[1024,2048]{1,0:T(8,128)(2,1)S(1)} %copy-done.1), kind=kOutput, calls=%fused_computation.5 | convolution fusion | flops 2148532224 | bytes 7340032 | tf_op jit(solution)/shard_map/dot_general | solution.py:57
  116.8 11.4 %collective-permute-done.5 = bf16[4,2,128,128]{3,2,1,0:T(8,128)(2,1)S(1)} collective-permute-done((bf16[4,2,128,128]{3,2,1,0:T(8,128)(2,1)S(1)}, bf16[4,2,128,128]{3,2,1,0:T(8,128)(2,1)S(1)}, u32[]{:S(2)}, u32[]{:S(2)}) %collective-permute-start.5) | collective-permute-done | bytes 262176 | tf_op jit(solution)/shard_map/ppermute | solution.py:12
  128.2 2.7 %collective-permute-start.9 = (bf16[4,32,2048]{2,1,0:T(8,128)(2,1)S(1)}, bf16[4,32,2048]{2,1,0:T(8,128)(2,1)S(1)}, u32[]{:S(2)}, u32[]{:S(2)}) collective-permute-start(bf16[4,32,2048]{2,1,0:T(8,128)(2,1)S(1)} %get-tuple-element.3), channel_id=1, source_target_pairs={{0,192},{64,0},{128,64},{192,128},{1,193},{65,1},{129,65},{193,129... | collective-permute-start | bytes 1572872 | tf_op jit(solution)/shard_map/ppermute | solution.py:12
  133.3 1.9 collective-permute-done.16
  135.2 4.8 %collective-permute-done.14 = bf16[4,32,2048]{2,1,0:T(8,128)(2,1)S(1)} collective-permute-done((bf16[4,32,2048]{2,1,0:T(8,128)(2,1)S(1)}, bf16[4,32,2048]{2,1,0:T(8,128)(2,1)S(1)}, u32[]{:S(2)}, u32[]{:S(2)}) %collective-permute-start.14) | collective-permute-done | bytes 524320 | tf_op jit(solution)/shard_map/ppermute | solution.py:12
  140.4 2.0 collective-permute-start.19
  142.4 3.2 %collective-permute-start.18 = (bf16[32,2048]{1,0:T(8,128)(2,1)S(1)}, bf16[32,2048]{1,0:T(8,128)(2,1)S(1)}, u32[]{:S(2)}, u32[]{:S(2)}) collective-permute-start(bf16[32,2048]{1,0:T(8,128)(2,1)S(1)} %get-tuple-element.19), channel_id=1, source_target_pairs={{0,38},{2,0},{4,2},{6,4},{32,6},{34,32},{36,34},{38,36},{1,39},{3,... | collective-permute-start | bytes 393224 | tf_op jit(solution)/shard_map/ppermute | solution.py:12
  145.6 11.2 %collective-permute-done.9 = bf16[4,32,2048]{2,1,0:T(8,128)(2,1)S(1)} collective-permute-done((bf16[4,32,2048]{2,1,0:T(8,128)(2,1)S(1)}, bf16[4,32,2048]{2,1,0:T(8,128)(2,1)S(1)}, u32[]{:S(2)}, u32[]{:S(2)}) %collective-permute-start.9) | collective-permute-done | bytes 524320 | tf_op jit(solution)/shard_map/ppermute | solution.py:12
  156.8 2.5 %collective-permute-start.17 = (bf16[32,2048]{1,0:T(8,128)(2,1)S(1)}, bf16[32,2048]{1,0:T(8,128)(2,1)S(1)}, u32[]{:S(2)}, u32[]{:S(2)}) collective-permute-start(bf16[32,2048]{1,0:T(8,128)(2,1)S(1)} %get-tuple-element.17), channel_id=1, source_target_pairs={{0,2},{2,4},{4,6},{6,32},{32,34},{34,36},{36,38},{38,0},{1,3},{3,5... | collective-permute-start | bytes 393224 | tf_op jit(solution)/shard_map/ppermute | solution.py:12
  160.9 4.1 %collective-permute-start.12 = (bf16[32,2048]{1,0:T(8,128)(2,1)S(1)}, bf16[32,2048]{1,0:T(8,128)(2,1)S(1)}, u32[]{:S(2)}, u32[]{:S(2)}) collective-permute-start(bf16[32,2048]{1,0:T(8,128)(2,1)S(1)} %get-tuple-element.15), channel_id=1, source_target_pairs={{0,36},{2,38},{4,0},{6,2},{32,4},{34,6},{36,32},{38,34},{1,37},{3,... | collective-permute-start | bytes 393224 | tf_op jit(solution)/shard_map/ppermute | solution.py:12
  167.0 2.1 %collective-permute-start.20 = (bf16[32,2048]{1,0:T(8,128)(2,1)S(1)}, bf16[32,2048]{1,0:T(8,128)(2,1)S(1)}, u32[]{:S(2)}, u32[]{:S(2)}) collective-permute-start(bf16[32,2048]{1,0:T(8,128)(2,1)S(1)} %fusion.15), channel_id=1, source_target_pairs={{0,32},{32,0},{1,33},{33,1},{2,34},{34,2},{3,35},{35,3},{4,36},{36... | collective-permute-start | bytes 393224 | tf_op jit(solution)/shard_map/ppermute | solution.py:12
  169.1 2.3 %collective-permute-done.12 = bf16[32,2048]{1,0:T(8,128)(2,1)S(1)} collective-permute-done((bf16[32,2048]{1,0:T(8,128)(2,1)S(1)}, bf16[32,2048]{1,0:T(8,128)(2,1)S(1)}, u32[]{:S(2)}, u32[]{:S(2)}) %collective-permute-start.12) | collective-permute-done | bytes 131104 | tf_op jit(solution)/shard_map/ppermute | solution.py:12
  171.5 11.2 %collective-permute-done.11 = bf16[32,2048]{1,0:T(8,128)(2,1)S(1)} collective-permute-done((bf16[32,2048]{1,0:T(8,128)(2,1)S(1)}, bf16[32,2048]{1,0:T(8,128)(2,1)S(1)}, u32[]{:S(2)}, u32[]{:S(2)}) %collective-permute-start.11) | collective-permute-done | bytes 131104 | tf_op jit(solution)/shard_map/ppermute | solution.py:12
  182.9 8.8 %collective-permute-done.13 = bf16[32,2048]{1,0:T(8,128)(2,1)S(1)} collective-permute-done((bf16[32,2048]{1,0:T(8,128)(2,1)S(1)}, bf16[32,2048]{1,0:T(8,128)(2,1)S(1)}, u32[]{:S(2)}, u32[]{:S(2)}) %collective-permute-start.13) | collective-permute-done | bytes 131104 | tf_op jit(solution)/shard_map/ppermute | solution.py:12
  192.0 1.9 collective-permute-start.23
  193.9 4.3 %collective-permute-done.21 = bf16[32,4096]{1,0:T(8,128)(2,1)S(1)} collective-permute-done((bf16[32,4096]{1,0:T(8,128)(2,1)S(1)}, bf16[32,4096]{1,0:T(8,128)(2,1)S(1)}, u32[]{:S(2)}, u32[]{:S(2)}) %collective-permute-start.21) | collective-permute-done | bytes 262176 | tf_op jit(solution)/shard_map/ppermute | solution.py:12
  200.0 2.7 %collective-permute-done.23 = bf16[32,4096]{1,0:T(8,128)(2,1)S(1)} collective-permute-done((bf16[32,4096]{1,0:T(8,128)(2,1)S(1)}, bf16[32,4096]{1,0:T(8,128)(2,1)S(1)}, u32[]{:S(2)}, u32[]{:S(2)}) %collective-permute-start.23) | collective-permute-done | bytes 262176 | tf_op jit(solution)/shard_map/ppermute | solution.py:12
  (79 shorter events, 24.2 us)
Async XLA Ops:
  7.2 58.6 %all-gather.5.cloned.1.call-start = ((), (), s32[]{:S(2)}) async-start(), calls=%async_computation.2 | async-start | bytes 4718592 | tf_op jit(solution)/shard_map/all_gather | solution.py:48
  9.5 80.8 %all-gather.3.cloned.1.call-start = ((), (), s32[]{:S(2)}) async-start(), calls=%async_computation.1 | async-start | bytes 4718592 | tf_op jit(solution)/shard_map/all_gather | solution.py:48
  10.3 28.7 %collective-permute-start = (bf16[128,4096]{1,0:T(8,128)(2,1)}, bf16[128,4096]{1,0:T(8,128)(2,1)S(1)}, u32[]{:S(2)}, u32[]{:S(2)}) collective-permute-start(bf16[128,4096]{1,0:T(8,128)(2,1)} %param.5), channel_id=1, source_target_pairs={{0,38},{2,0},{4,2},{6,4},{32,6},{34,32},{36,34},{38,36},{1,39},{3,... | collective-permute-start | bytes 3145736 | tf_op jit(solution)/shard_map/ppermute | solution.py:12
  16.2 33.5 %collective-permute-start.2 = (bf16[128,4096]{1,0:T(8,128)(2,1)}, bf16[128,4096]{1,0:T(8,128)(2,1)S(1)}, u32[]{:S(2)}, u32[]{:S(2)}) collective-permute-start(bf16[128,4096]{1,0:T(8,128)(2,1)} %param.5), channel_id=1, source_target_pairs={{0,2},{2,4},{4,6},{6,32},{32,34},{34,36},{36,38},{38,0},{1,3},{3,5... | collective-permute-start | bytes 3145736 | tf_op jit(solution)/shard_map/ppermute | solution.py:12
  18.9 29.6 %all-to-all-start = ((bf16[8,128,512]{1,2,0:T(8,128)(2,1)}), bf16[8,128,512]{1,2,0:T(8,128)(2,1)S(1)}, u32[]{:S(2)}, u32[]{:S(2)}) async-start(bf16[8,128,512]{1,2,0:T(8,128)(2,1)} %bitcast.12), calls=%async_computation | async-start | bytes 2097152 | tf_op jit(solution)/shard_map/all_to_all | solution.py:53
  39.8 14.2 %collective-permute-start.1 = (bf16[64,4096]{1,0:T(8,128)(2,1)}, bf16[64,4096]{1,0:T(8,128)(2,1)}, u32[]{:S(2)}, u32[]{:S(2)}) collective-permute-start(bf16[64,4096]{1,0:T(8,128)(2,1)} %slice.34), channel_id=1, source_target_pairs={{0,38},{2,0},{4,2},{6,4},{32,6},{34,32},{36,34},{38,36},{1,39},{3,... | collective-permute-start | bytes 1572872 | tf_op jit(solution)/shard_map/ppermute | solution.py:12
  49.8 14.1 %collective-permute-start.3 = (bf16[64,4096]{1,0:T(8,128)(2,1)S(1)}, bf16[64,4096]{1,0:T(8,128)(2,1)S(1)}, u32[]{:S(2)}, u32[]{:S(2)}) collective-permute-start(bf16[64,4096]{1,0:T(8,128)(2,1)S(1)} %slice.35), channel_id=1, source_target_pairs={{0,2},{2,4},{4,6},{6,32},{32,34},{34,36},{36,38},{38,0},{1,3},{3,5... | collective-permute-start | bytes 1572872 | tf_op jit(solution)/shard_map/ppermute | solution.py:12
  99.8 7.1 %copy-start.2 = (bf16[1024,2048]{1,0:T(8,128)(2,1)S(1)}, bf16[1024,2048]{1,0:T(8,128)(2,1)}, u32[]{:S(2)}) copy-start(bf16[1024,2048]{1,0:T(8,128)(2,1)} %all-gather.5.cloned.1.call-done) | copy-start | bytes 12582916
  101.8 5.1 %copy-start = (bf16[8,128,512]{2,1,0:T(8,128)(2,1)S(1)}, bf16[8,128,512]{2,1,0:T(8,128)(2,1)}, u32[]{:S(2)}) copy-start(bf16[8,128,512]{2,1,0:T(8,128)(2,1)} %copy.22) | copy-start | bytes 3145732
  101.8 13.9 %collective-permute-start.4 = (bf16[4,2,128,128]{3,2,1,0:T(8,128)(2,1)S(1)}, bf16[4,2,128,128]{3,2,1,0:T(8,128)(2,1)S(1)}, u32[]{:S(2)}, u32[]{:S(2)}) collective-permute-start(bf16[4,2,128,128]{3,2,1,0:T(8,128)(2,1)S(1)} %bitcast.103), channel_id=1, source_target_pairs={{0,6},{2,0},{4,2},{6,4},{1,7},{3,1},{5,3},{7,5},{8,14},{10,8},{12,... | collective-permute-start | bytes 786440 | tf_op jit(solution)/shard_map/ppermute | solution.py:12
  105.5 22.7 %collective-permute-start.5 = (bf16[4,2,128,128]{3,2,1,0:T(8,128)(2,1)S(1)}, bf16[4,2,128,128]{3,2,1,0:T(8,128)(2,1)S(1)}, u32[]{:S(2)}, u32[]{:S(2)}) collective-permute-start(bf16[4,2,128,128]{3,2,1,0:T(8,128)(2,1)S(1)} %bitcast.102), channel_id=1, source_target_pairs={{0,4},{2,6},{4,0},{6,2},{1,5},{3,7},{5,1},{7,3},{8,12},{10,14},{12... | collective-permute-start | bytes 786440 | tf_op jit(solution)/shard_map/ppermute | solution.py:12
  105.6 25.3 %collective-permute-start.6 = (bf16[4,2,128,128]{3,2,1,0:T(8,128)(2,1)S(1)}, bf16[4,2,128,128]{3,2,1,0:T(8,128)(2,1)S(1)}, u32[]{:S(2)}, u32[]{:S(2)}) collective-permute-start(bf16[4,2,128,128]{3,2,1,0:T(8,128)(2,1)S(1)} %bitcast.101), channel_id=1, source_target_pairs={{0,2},{2,4},{4,6},{6,0},{1,3},{3,5},{5,7},{7,1},{8,10},{10,12},{12... | collective-permute-start | bytes 786440 | tf_op jit(solution)/shard_map/ppermute | solution.py:12
  106.9 6.2 %copy-start.1 = (bf16[1024,2048]{1,0:T(8,128)(2,1)S(1)}, bf16[1024,2048]{1,0:T(8,128)(2,1)}, u32[]{:S(2)}) copy-start(bf16[1024,2048]{1,0:T(8,128)(2,1)} %all-gather.3.cloned.1.call-done) | copy-start | bytes 12582916
  109.6 25.7 %collective-permute-start.16 = (bf16[4,32,2048]{2,1,0:T(8,128)(2,1)S(1)}, bf16[4,32,2048]{2,1,0:T(8,128)(2,1)S(1)}, u32[]{:S(2)}, u32[]{:S(2)}) collective-permute-start(bf16[4,32,2048]{2,1,0:T(8,128)(2,1)S(1)} %get-tuple-element.6), channel_id=1, source_target_pairs={{0,192},{64,0},{128,64},{192,128},{1,193},{65,1},{129,65},{193,129... | collective-permute-start | bytes 1572872 | tf_op jit(solution)/shard_map/ppermute | solution.py:12
  112.3 22.9 %collective-permute-start.15 = (bf16[4,32,2048]{2,1,0:T(8,128)(2,1)S(1)}, bf16[4,32,2048]{2,1,0:T(8,128)(2,1)S(1)}, u32[]{:S(2)}, u32[]{:S(2)}) collective-permute-start(bf16[4,32,2048]{2,1,0:T(8,128)(2,1)S(1)} %get-tuple-element.7), channel_id=1, source_target_pairs={{0,128},{64,192},{128,0},{192,64},{1,129},{65,193},{129,1},{193,65... | collective-permute-start | bytes 1572872 | tf_op jit(solution)/shard_map/ppermute | solution.py:12
  115.8 24.2 %collective-permute-start.14 = (bf16[4,32,2048]{2,1,0:T(8,128)(2,1)S(1)}, bf16[4,32,2048]{2,1,0:T(8,128)(2,1)S(1)}, u32[]{:S(2)}, u32[]{:S(2)}) collective-permute-start(bf16[4,32,2048]{2,1,0:T(8,128)(2,1)S(1)} %get-tuple-element.5), channel_id=1, source_target_pairs={{0,64},{64,128},{128,192},{192,0},{1,65},{65,129},{129,193},{193,1... | collective-permute-start | bytes 1572872 | tf_op jit(solution)/shard_map/ppermute | solution.py:12
  128.2 28.6 %collective-permute-start.9 = (bf16[4,32,2048]{2,1,0:T(8,128)(2,1)S(1)}, bf16[4,32,2048]{2,1,0:T(8,128)(2,1)S(1)}, u32[]{:S(2)}, u32[]{:S(2)}) collective-permute-start(bf16[4,32,2048]{2,1,0:T(8,128)(2,1)S(1)} %get-tuple-element.3), channel_id=1, source_target_pairs={{0,192},{64,0},{128,64},{192,128},{1,193},{65,1},{129,65},{193,129... | collective-permute-start | bytes 1572872 | tf_op jit(solution)/shard_map/ppermute | solution.py:12
  131.0 28.3 %collective-permute-start.8 = (bf16[4,32,2048]{2,1,0:T(8,128)(2,1)S(1)}, bf16[4,32,2048]{2,1,0:T(8,128)(2,1)S(1)}, u32[]{:S(2)}, u32[]{:S(2)}) collective-permute-start(bf16[4,32,2048]{2,1,0:T(8,128)(2,1)S(1)} %get-tuple-element.4), channel_id=1, source_target_pairs={{0,128},{64,192},{128,0},{192,64},{1,129},{65,193},{129,1},{193,65... | collective-permute-start | bytes 1572872 | tf_op jit(solution)/shard_map/ppermute | solution.py:12
  135.2 25.3 %collective-permute-start.7 = (bf16[4,32,2048]{2,1,0:T(8,128)(2,1)S(1)}, bf16[4,32,2048]{2,1,0:T(8,128)(2,1)S(1)}, u32[]{:S(2)}, u32[]{:S(2)}) collective-permute-start(bf16[4,32,2048]{2,1,0:T(8,128)(2,1)S(1)} %get-tuple-element.2), channel_id=1, source_target_pairs={{0,64},{64,128},{128,192},{192,0},{1,65},{65,129},{129,193},{193,1... | collective-permute-start | bytes 1572872 | tf_op jit(solution)/shard_map/ppermute | solution.py:12
  140.4 25.3 %collective-permute-start.19 = (bf16[32,2048]{1,0:T(8,128)(2,1)S(1)}, bf16[32,2048]{1,0:T(8,128)(2,1)S(1)}, u32[]{:S(2)}, u32[]{:S(2)}) collective-permute-start(bf16[32,2048]{1,0:T(8,128)(2,1)S(1)} %get-tuple-element.18), channel_id=1, source_target_pairs={{0,4},{2,6},{4,32},{6,34},{32,36},{34,38},{36,0},{38,2},{1,5},{3,7... | collective-permute-start | bytes 393224 | tf_op jit(solution)/shard_map/ppermute | solution.py:12
  142.4 24.5 %collective-permute-start.18 = (bf16[32,2048]{1,0:T(8,128)(2,1)S(1)}, bf16[32,2048]{1,0:T(8,128)(2,1)S(1)}, u32[]{:S(2)}, u32[]{:S(2)}) collective-permute-start(bf16[32,2048]{1,0:T(8,128)(2,1)S(1)} %get-tuple-element.19), channel_id=1, source_target_pairs={{0,38},{2,0},{4,2},{6,4},{32,6},{34,32},{36,34},{38,36},{1,39},{3,... | collective-permute-start | bytes 393224 | tf_op jit(solution)/shard_map/ppermute | solution.py:12
  156.8 10.1 %collective-permute-start.17 = (bf16[32,2048]{1,0:T(8,128)(2,1)S(1)}, bf16[32,2048]{1,0:T(8,128)(2,1)S(1)}, u32[]{:S(2)}, u32[]{:S(2)}) collective-permute-start(bf16[32,2048]{1,0:T(8,128)(2,1)S(1)} %get-tuple-element.17), channel_id=1, source_target_pairs={{0,2},{2,4},{4,6},{6,32},{32,34},{34,36},{36,38},{38,0},{1,3},{3,5... | collective-permute-start | bytes 393224 | tf_op jit(solution)/shard_map/ppermute | solution.py:12
  160.9 10.6 %collective-permute-start.12 = (bf16[32,2048]{1,0:T(8,128)(2,1)S(1)}, bf16[32,2048]{1,0:T(8,128)(2,1)S(1)}, u32[]{:S(2)}, u32[]{:S(2)}) collective-permute-start(bf16[32,2048]{1,0:T(8,128)(2,1)S(1)} %get-tuple-element.15), channel_id=1, source_target_pairs={{0,36},{2,38},{4,0},{6,2},{32,4},{34,6},{36,32},{38,34},{1,37},{3,... | collective-permute-start | bytes 393224 | tf_op jit(solution)/shard_map/ppermute | solution.py:12
  164.9 17.8 %collective-permute-start.11 = (bf16[32,2048]{1,0:T(8,128)(2,1)S(1)}, bf16[32,2048]{1,0:T(8,128)(2,1)S(1)}, u32[]{:S(2)}, u32[]{:S(2)}) collective-permute-start(bf16[32,2048]{1,0:T(8,128)(2,1)S(1)} %get-tuple-element.16), channel_id=1, source_target_pairs={{0,38},{2,0},{4,2},{6,4},{32,6},{34,32},{36,34},{38,36},{1,39},{3,... | collective-permute-start | bytes 393224 | tf_op jit(solution)/shard_map/ppermute | solution.py:12
  165.8 16.9 %collective-permute-start.10 = (bf16[32,2048]{1,0:T(8,128)(2,1)S(1)}, bf16[32,2048]{1,0:T(8,128)(2,1)S(1)}, u32[]{:S(2)}, u32[]{:S(2)}) collective-permute-start(bf16[32,2048]{1,0:T(8,128)(2,1)S(1)} %get-tuple-element.14), channel_id=1, source_target_pairs={{0,2},{2,4},{4,6},{6,32},{32,34},{34,36},{36,38},{38,0},{1,3},{3,5... | collective-permute-start | bytes 393224 | tf_op jit(solution)/shard_map/ppermute | solution.py:12
  167.0 15.8 %collective-permute-start.20 = (bf16[32,2048]{1,0:T(8,128)(2,1)S(1)}, bf16[32,2048]{1,0:T(8,128)(2,1)S(1)}, u32[]{:S(2)}, u32[]{:S(2)}) collective-permute-start(bf16[32,2048]{1,0:T(8,128)(2,1)S(1)} %fusion.15), channel_id=1, source_target_pairs={{0,32},{32,0},{1,33},{33,1},{2,34},{34,2},{3,35},{35,3},{4,36},{36... | collective-permute-start | bytes 393224 | tf_op jit(solution)/shard_map/ppermute | solution.py:12
  182.8 9.0 %collective-permute-start.13 = (bf16[32,2048]{1,0:T(8,128)(2,1)S(1)}, bf16[32,2048]{1,0:T(8,128)(2,1)S(1)}, u32[]{:S(2)}, u32[]{:S(2)}) collective-permute-start(bf16[32,2048]{1,0:T(8,128)(2,1)S(1)} %fusion.18), channel_id=1, source_target_pairs={{0,32},{32,0},{1,33},{33,1},{2,34},{34,2},{3,35},{35,3},{4,36},{36... | collective-permute-start | bytes 393224 | tf_op jit(solution)/shard_map/ppermute | solution.py:12
  191.8 6.4 %collective-permute-start.21 = (bf16[32,4096]{1,0:T(8,128)(2,1)S(1)}, bf16[32,4096]{1,0:T(8,128)(2,1)S(1)}, u32[]{:S(2)}, u32[]{:S(2)}) collective-permute-start(bf16[32,4096]{1,0:T(8,128)(2,1)S(1)} %pad_maximum_fusion), channel_id=1, source_target_pairs={{0,192},{64,0},{128,64},{192,128},{1,193},{65,1},{129,65},{193,129... | collective-permute-start | bytes 786440 | tf_op jit(solution)/shard_map/ppermute | solution.py:12
  191.9 8.1 %collective-permute-start.22 = (bf16[32,4096]{1,0:T(8,128)(2,1)S(1)}, bf16[32,4096]{1,0:T(8,128)(2,1)S(1)}, u32[]{:S(2)}, u32[]{:S(2)}) collective-permute-start(bf16[32,4096]{1,0:T(8,128)(2,1)S(1)} %pad_maximum_fusion), channel_id=1, source_target_pairs={{0,128},{64,192},{128,0},{192,64},{1,129},{65,193},{129,1},{193,65... | collective-permute-start | bytes 786440 | tf_op jit(solution)/shard_map/ppermute | solution.py:12
  192.0 10.7 %collective-permute-start.23 = (bf16[32,4096]{1,0:T(8,128)(2,1)S(1)}, bf16[32,4096]{1,0:T(8,128)(2,1)S(1)}, u32[]{:S(2)}, u32[]{:S(2)}) collective-permute-start(bf16[32,4096]{1,0:T(8,128)(2,1)S(1)} %pad_maximum_fusion), channel_id=1, source_target_pairs={{0,64},{64,128},{128,192},{192,0},{1,65},{65,129},{129,193},{193,1... | collective-permute-start | bytes 786440 | tf_op jit(solution)/shard_map/ppermute | solution.py:12
Sparse Core Ops, SparseCore 0:
  9.9 46.2 all-gather.4
  58.0 32.2 all-gather.2
where the time goes:
time: 211 us
  waiting for transfers between devices  116 us (55%)
  starting transfers between devices  45.8 us (22%)
  local copies, waits for them, and re-layouts  19.7 us (9%)
  between operations  14.4 us (7%)
  matrix products  14 us (7%)
    ppermute x24, waiting for transfers between devices, shift(): return lax.ppermute(v, axis, [(i, (i + by) % n) for i in range(n)])  87.8 us
    ppermute x24, starting transfers between devices, shift(): return lax.ppermute(v, axis, [(i, (i + by) % n) for i in range(n)])  40.8 us
    all_gather x2, waiting for transfers between devices, local(): lax.all_gather(g[:, lo:hi], ('y', 'c'), axis=0, tiled=True)  24.5 us
    dot_general x1, matrix products, local(): lax.dot_general(gall, w, (((1,), (1,)), ((), ())), preferred_element_type...  9.17 us
    unnamed x26, local copies, waits for them, and re-layouts  8.18 us
    all_to_all x1, starting transfers between devices, local(): lax.all_to_all(a, ('y', 'c'), split_axis=0, concat_axis=0, tiled=True)  4.92 us
    dot_general x2, matrix products, local(): lax.dot_general(acts, gj, (((0,), (0,)), ((), ())), preferred_element_typ...  4.88 us
  transfers between devices with their start and end apart: 27, of which 16 were waited for; matrix products, arithmetic and copies ran while one was open for 9% of the time, Pallas kernels for 0%

commit v1 on v0

v1 whole, which is shorter than its diff:
```python
import jax
import jax.numpy as jnp
from jax import lax
from jax.sharding import Mesh, PartitionSpec as P

CHUNKS = (2048, 2048)
RING8 = ("h", "l")


def shift(v, axis, by):
    n = lax.axis_size(axis)
    return lax.ppermute(v, axis, [(i, (i + by) % n) for i in range(n)])


def exchange(v, axis):
    return lax.all_to_all(v, axis, split_axis=0, concat_axis=0, tiled=True)


def after(v, *others):
    return lax.optimization_barrier((v, *others))[0]


def around(own, axis):
    half = own.shape[0] // 2
    above = shift(own, axis, -1)
    below = shift(own, axis, 1)
    far_a = shift(above[:half], axis, -1)
    far_b = shift(below[half:], axis, 1)
    return [own, above, far_a, far_b, below]


def local(grad_out, attn, w_out):
    f32, bf16 = jnp.float32, jnp.bfloat16
    g = grad_out[0]
    a = attn[0]
    toks, feats = g.shape
    heads = w_out.shape[0]
    quarter = heads // 4
    l = lax.axis_index("l")

    cuts, at = [], 0
    for size in CHUNKS:
        size = size * feats // sum(CHUNKS)
        cuts.append((at, at + size))
        at += size
    g_cols = [lax.all_gather(g[:, lo:hi], ("y", "c"), axis=0, tiled=True) for lo, hi in cuts]

    a = a.reshape(toks, 4, 4, 2, heads).transpose(1, 3, 0, 2, 4).reshape(8, toks, 4 * heads)
    acts = exchange(a, ("y", "c")).reshape(8 * toks, 4 * heads)

    w_parts = around(w_out, RING8)

    sums, part = [], None
    for gj in g_cols:
        if part is not None:
            gj = after(gj, part)
        part = lax.dot_general(acts, gj, (((0,), (0,)), ((), ())), preferred_element_type=f32).astype(bf16)
        part = part.reshape(4, 4, quarter, -1)
        tot = exchange(part.transpose(1, 0, 2, 3), "x").astype(f32).sum(0).astype(bf16)
        tot = exchange(tot, "l").astype(f32).sum(0).astype(bf16)
        tot = (tot.astype(f32) + shift(tot, "h", 1).astype(f32)).astype(bf16)
        sums.append(exchange(jnp.broadcast_to(tot[None], (4,) + tot.shape), "x").reshape(heads, -1))
    grad_w = jnp.concatenate(sums, 1)

    w = jnp.concatenate(w_parts, 0)
    w = lax.dynamic_slice_in_dim(jnp.concatenate([w, w], 0), ((4 - l) & 3) * heads, 4 * heads, 0)
    gall = after(jnp.concatenate(g_cols, 1), part)
    res = lax.dot_general(gall, w, (((1,), (1,)), ((), ())), preferred_element_type=f32).astype(bf16)
    res = res.reshape(8 * toks, 4, heads).transpose(1, 0, 2)
    out = exchange(res, "l")
    out = out.reshape(4, 4, 2 * toks, heads).transpose(1, 0, 2, 3).reshape(1, 4 * 8 * toks, heads)
    return out, grad_w


def solution(mesh):
    fine = Mesh(mesh.devices.reshape(4, 2, 4, 4, 2), ("x", "h", "y", "l", "c"))
    dp, context = ("x", "h"), ("y", "l", "c")
    in_specs = (P(dp, context, None), P(dp, context, None), P(context, None))
    out_specs = (P(dp, None, context), P(context, None))
    return jax.shard_map(local, mesh=fine, in_specs=in_specs, out_specs=out_specs, check_vma=False)
```

time: 211 us -> 267 us (1.27)
  the two profiles are of different devices: /device:TPU:8 before, /device:TPU:64 now
where the time goes in v1:
time: 267 us; the launch traced here: 263 us
  waiting for transfers between devices  129 us (48%)
  starting transfers between devices  49.3 us (18%)
  local copies, waits for them, and re-layouts  36.6 us (14%)
  matrix products  20.5 us (8%)
  between operations  14.2 us (5%)
  other arithmetic  13.3 us (5%)
    all_to_all x8, waiting for transfers between devices, exchange(): return lax.all_to_all(v, axis, split_axis=0, concat_axis=0, tiled=True)  82.5 us
    all_to_all x8, starting transfers between devices, exchange(): return lax.all_to_all(v, axis, split_axis=0, concat_axis=0, tiled=True)  36.1 us
    all_gather x2, waiting for transfers between devices, local(): lax.all_gather(g[:, lo:hi], ('y', 'c'), axis=0, tiled=True)  31.9 us
    unnamed x14, local copies, waits for them, and re-layouts  18.8 us
    ppermute x6, waiting for transfers between devices, shift(): return lax.ppermute(v, axis, [(i, (i + by) % n) for i in range(n)])  14.2 us
    ppermute x6, starting transfers between devices, shift(): return lax.ppermute(v, axis, [(i, (i + by) % n) for i in range(n)])  13.1 us
    dot_general x2, matrix products, local(): lax.dot_general(acts, gj, (((0,), (0,)), ((), ())), preferred_element_typ...  10.5 us
    dot_general x1, matrix products, local(): lax.dot_general(gall, w, (((1,), (1,)), ((), ())), preferred_element_type...  10.1 us
  transfers between devices with their start and end apart: 16, of which 9 were waited for; matrix products, arithmetic and copies ran while one was open for 25% of the time, Pallas kernels for 0%

profile of v1, /device:TPU:64, one launch (start us, length us, event | category | flops | bytes accessed | tf_op | source)
XLA Modules:
  0.0 263.2 jit_solution(8318306603552850730)
XLA Ops:
  7.2 2.4 fusion.6
  10.5 1.9 collective-permute-start.2
  12.5 2.3 copy.17
  14.7 2.3 copy.18
  17.0 4.5 %all-to-all-start = ((bf16[8,128,512]{1,2,0:T(8,128)(2,1)}), bf16[8,128,512]{1,2,0:T(8,128)(2,1)}, u32[]{:S(2)}, u32[]{:S(2)}) async-start(bf16[8,128,512]{1,2,0:T(8,128)(2,1)} %bitcast.33), calls=%async_computation | async-start | bytes 2097152 | tf_op jit(solution)/shard_map/all_to_all | solution.py:16
  22.6 24.2 %all-to-all-done = bf16[8,128,512]{1,2,0:T(8,128)(2,1)} async-done(((bf16[8,128,512]{1,2,0:T(8,128)(2,1)}), bf16[8,128,512]{1,2,0:T(8,128)(2,1)}, u32[]{:S(2)}, u32[]{:S(2)}) %all-to-all-start) | async-done | bytes 1048608 | tf_op jit(solution)/shard_map/all_to_all | solution.py:16
  50.1 4.9 %collective-permute-start.3 = (bf16[64,4096]{1,0:T(8,128)(2,1)}, bf16[64,4096]{1,0:T(8,128)(2,1)}, u32[]{:S(2)}, u32[]{:S(2)}) collective-permute-start(bf16[64,4096]{1,0:T(8,128)(2,1)} %slice.19), channel_id=1, source_target_pairs={{0,2},{2,4},{4,6},{6,32},{32,34},{34,36},{36,38},{38,0},{1,3},{3,5... | collective-permute-start | bytes 1572872 | tf_op jit(solution)/shard_map/ppermute | solution.py:12
  55.7 5.9 %convolution_convert_fusion.1 = bf16[512,2048]{1,0:T(8,128)(2,1)} fusion(bf16[1024,512]{1,0:T(8,128)(2,1)S(1)} %bitcast.40, bf16[1024,2048]{1,0:T(8,128)(2,1)} %all-gather.3.cloned.1.call-done), kind=kOutput, calls=%fused_computation.4 | convolution fusion | flops 2148532224 | bytes 7340032 | tf_op jit(solution)/shard_map/dot_general | solution.py:57
  61.6 31.1 %all-gather.5.cloned.1.call-done = bf16[1024,2048]{1,0:T(8,128)(2,1)} async-done(((bf16[128,2048]{1,0:T(8,128)(2,1)}), bf16[1024,2048]{1,0:T(8,128)(2,1)}) %all-gather.5.cloned.1.call-update) | async-done | bytes 4194320 | tf_op jit(solution)/shard_map/all_gather | solution.py:46
  92.7 4.6 %convolution_convert_fusion = bf16[2048,512]{0,1:T(8,128)(2,1)S(1)} fusion(bf16[1024,2048]{1,0:T(8,128)(2,1)} %all-gather.5.cloned.1.call-done, bf16[1024,512]{1,0:T(8,128)(2,1)S(1)} %bitcast.41), kind=kOutput, calls=%fused_computation.3 | convolution fusion | flops 2148532224 | bytes 7340032 | tf_op jit(solution)/shard_map/dot_general | solution.py:57
  98.9 4.2 %all-to-all-start.5 = ((bf16[4,4,32,2048]{3,2,1,0:T(8,128)(2,1)}), bf16[4,4,32,2048]{3,2,1,0:T(8,128)(2,1)S(1)}, u32[]{:S(2)}, u32[]{:S(2)}) async-start(bf16[4,4,32,2048]{3,2,1,0:T(8,128)(2,1)} %bitcast.31), calls=%async_computation.5 | async-start | bytes 4194304 | tf_op jit(solution)/shard_map/all_to_all | solution.py:16
  103.1 2.3 constant_dynamic-update-slice_fusion.8
  105.5 1.9 constant_dynamic-update-slice_fusion.7
  110.3 3.2 %copy.26 = bf16[4,4,32,2048]{3,2,0,1:T(8,128)(2,1)} copy(bf16[4,4,32,2048]{3,2,1,0:T(8,128)(2,1)} %bitcast.35) | data formatting | bytes 4194304 | tf_op jit(solution)/shard_map/reshape | solution.py:58
  113.5 16.4 %all-to-all-done.5 = bf16[4,4,32,2048]{3,2,1,0:T(8,128)(2,1)S(1)} async-done(((bf16[4,4,32,2048]{3,2,1,0:T(8,128)(2,1)}), bf16[4,4,32,2048]{3,2,1,0:T(8,128)(2,1)S(1)}, u32[]{:S(2)}, u32[]{:S(2)}) %all-to-all-start.5) | async-done | bytes 2097184 | tf_op jit(solution)/shard_map/all_to_all | solution.py:16
  129.9 4.5 %all-to-all-start.2 = ((bf16[4,4,32,2048]{3,2,1,0:T(8,128)(2,1)}), bf16[4,4,32,2048]{3,2,1,0:T(8,128)(2,1)}, u32[]{:S(2)}, u32[]{:S(2)}) async-start(bf16[4,4,32,2048]{3,2,1,0:T(8,128)(2,1)} %bitcast.32), calls=%async_computation.2 | async-start | bytes 4194304 | tf_op jit(solution)/shard_map/all_to_all | solution.py:16
  134.4 2.3 constant_dynamic-update-slice_fusion.4
  136.7 2.3 constant_dynamic-update-slice_fusion.3
  144.1 16.3 %all-to-all-done.2 = bf16[4,4,32,2048]{3,2,1,0:T(8,128)(2,1)} async-done(((bf16[4,4,32,2048]{3,2,1,0:T(8,128)(2,1)}), bf16[4,4,32,2048]{3,2,1,0:T(8,128)(2,1)}, u32[]{:S(2)}, u32[]{:S(2)}) %all-to-all-start.2) | async-done | bytes 2097184 | tf_op jit(solution)/shard_map/all_to_all | solution.py:16
  160.3 5.2 %all-to-all-start.6 = ((bf16[4,32,2048]{2,1,0:T(8,128)(2,1)}), bf16[4,32,2048]{2,1,0:T(8,128)(2,1)S(1)}, u32[]{:S(2)}, u32[]{:S(2)}) async-start(bf16[4,32,2048]{2,1,0:T(8,128)(2,1)} %reduce_sum.50), calls=%async_computation.6 | async-start | bytes 1048576 | tf_op jit(solution)/shard_map/all_to_all | solution.py:16
  166.6 7.8 %pad_maximum_fusion = bf16[1024,4096]{1,0:T(8,128)(2,1)} fusion(bf16[1024,2048]{1,0:T(8,128)(2,1)} %all-gather.5.cloned.1.call-done, bf16[1024,2048]{1,0:T(8,128)(2,1)} %all-gather.3.cloned.1.call-done), kind=kLoop, calls=%fused_computation | loop fusion | flops 16777216 | bytes 16777216 | tf_op jit(solution)/shard_map/concatenate | solution.py:67
  174.5 2.9 %reduce_sum.48 = bf16[4,32,2048]{2,1,0:T(8,128)(2,1)} reduce(bf16[4,4,32,2048]{3,2,1,0:T(8,128)(2,1)} %all-to-all-done.2, bf16[]{:T(256)} %constant.21.clone.1), dimensions={0}, to_apply=%region_0.0 | reduce | flops 786432 | bytes 2621442 | tf_op jit(solution)/shard_map/reduce_sum | solution.py:59
  177.4 5.1 %all-to-all-start.3 = ((bf16[4,32,2048]{2,1,0:T(8,128)(2,1)}), bf16[4,32,2048]{2,1,0:T(8,128)(2,1)S(1)}, u32[]{:S(2)}, u32[]{:S(2)}) async-start(bf16[4,32,2048]{2,1,0:T(8,128)(2,1)} %reduce_sum.48), calls=%async_computation.3 | async-start | bytes 1048576 | tf_op jit(solution)/shard_map/all_to_all | solution.py:16
  182.5 10.1 %fusion.2 = bf16[1024,512]{0,1:T(8,128)(2,1)} fusion(bf16[1024,4096]{1,0:T(8,128)(2,1)} %pad_maximum_fusion, bf16[1024,4096]{1,0:T(8,128)(2,1)} %constant_dynamic-update-slice_fusion, s32[]{:T(128)S(6)} %select_n.3), kind=kOutput, calls=%fused_computation.7 | convolution fusion | flops 4295491584 | bytes 13631492 | tf_op jit(solution)/shard_map/dot_general | solution.py:68
  192.5 5.7 %all-to-all-start.1 = ((bf16[4,1024,128]{1,2,0:T(8,128)(2,1)}), bf16[4,1024,128]{1,2,0:T(8,128)(2,1)S(1)}, u32[]{:S(2)}, u32[]{:S(2)}) async-start(bf16[4,1024,128]{1,2,0:T(8,128)(2,1)} %bitcast.9), calls=%async_computation.1 | async-start | bytes 2097152 | tf_op jit(solution)/shard_map/all_to_all | solution.py:16
  198.3 5.1 %collective-permute-start.5 = (bf16[32,2048]{1,0:T(8,128)(2,1)S(1)}, bf16[32,2048]{1,0:T(8,128)(2,1)S(1)}, u32[]{:S(2)}, u32[]{:S(2)}) collective-permute-start(bf16[32,2048]{1,0:T(8,128)(2,1)S(1)} %reduce_sum.51), channel_id=1, source_target_pairs={{0,32},{32,0},{1,33},{33,1},{2,34},{34,2},{3,35},{35,3},{4,36},{36... | collective-permute-start | bytes 393224 | tf_op jit(solution)/shard_map/ppermute | solution.py:12
  204.5 14.2 %collective-permute-done.5 = bf16[32,2048]{1,0:T(8,128)(2,1)S(1)} collective-permute-done((bf16[32,2048]{1,0:T(8,128)(2,1)S(1)}, bf16[32,2048]{1,0:T(8,128)(2,1)S(1)}, u32[]{:S(2)}, u32[]{:S(2)}) %collective-permute-start.5) | collective-permute-done | bytes 131104 | tf_op jit(solution)/shard_map/ppermute | solution.py:12
  218.7 10.9 %all-to-all-done.1 = bf16[4,1024,128]{1,2,0:T(8,128)(2,1)S(1)} async-done(((bf16[4,1024,128]{1,2,0:T(8,128)(2,1)}), bf16[4,1024,128]{1,2,0:T(8,128)(2,1)S(1)}, u32[]{:S(2)}, u32[]{:S(2)}) %all-to-all-start.1) | async-done | bytes 1048608 | tf_op jit(solution)/shard_map/all_to_all | solution.py:16
  230.5 3.5 %all-to-all-start.7 = ((bf16[4,32,2048]{2,1,0:T(8,128)(2,1)}), bf16[4,32,2048]{2,1,0:T(8,128)(2,1)S(1)}, u32[]{:S(2)}, u32[]{:S(2)}) async-start(bf16[4,32,2048]{2,1,0:T(8,128)(2,1)} %broadcast_in_dim.5), calls=%async_computation.7 | async-start | bytes 1048576 | tf_op jit(solution)/shard_map/all_to_all | solution.py:16
  234.1 8.9 %all-to-all-done.7 = bf16[4,32,2048]{2,1,0:T(8,128)(2,1)S(1)} async-done(((bf16[4,32,2048]{2,1,0:T(8,128)(2,1)}), bf16[4,32,2048]{2,1,0:T(8,128)(2,1)S(1)}, u32[]{:S(2)}, u32[]{:S(2)}) %all-to-all-start.7) | async-done | bytes 524320 | tf_op jit(solution)/shard_map/all_to_all | solution.py:16
  243.8 3.5 %all-to-all-start.4 = ((bf16[4,32,2048]{2,1,0:T(8,128)(2,1)}), bf16[4,32,2048]{2,1,0:T(8,128)(2,1)S(1)}, u32[]{:S(2)}, u32[]{:S(2)}) async-start(bf16[4,32,2048]{2,1,0:T(8,128)(2,1)} %broadcast_in_dim.4), calls=%async_computation.4 | async-start | bytes 1048576 | tf_op jit(solution)/shard_map/all_to_all | solution.py:16
  249.5 5.8 %all-to-all-done.4 = bf16[4,32,2048]{2,1,0:T(8,128)(2,1)S(1)} async-done(((bf16[4,32,2048]{2,1,0:T(8,128)(2,1)}), bf16[4,32,2048]{2,1,0:T(8,128)(2,1)S(1)}, u32[]{:S(2)}, u32[]{:S(2)}) %all-to-all-start.4) | async-done | bytes 524320 | tf_op jit(solution)/shard_map/all_to_all | solution.py:16
  (39 shorter events, 23.0 us)
Async XLA Ops:
  7.2 14.3 %copy-start.1 = (bf16[128,4096]{1,0:T(8,128)(2,1)S(1)}, bf16[128,4096]{1,0:T(8,128)(2,1)}, u32[]{:S(2)}) copy-start(bf16[128,4096]{1,0:T(8,128)(2,1)} %param.5) | copy-start | bytes 3145732
  7.2 48.5 %all-gather.3.cloned.1.call-start = ((), (), s32[]{:S(2)}) async-start(), calls=%async_computation.8 | async-start | bytes 4718592 | tf_op jit(solution)/shard_map/all_gather | solution.py:46
  9.6 83.1 %all-gather.5.cloned.1.call-start = ((), (), s32[]{:S(2)}) async-start(), calls=%async_computation.9 | async-start | bytes 4718592 | tf_op jit(solution)/shard_map/all_gather | solution.py:46
  10.4 37.9 %collective-permute-start = (bf16[128,4096]{1,0:T(8,128)(2,1)}, bf16[128,4096]{1,0:T(8,128)(2,1)S(1)}, u32[]{:S(2)}, u32[]{:S(2)}) collective-permute-start(bf16[128,4096]{1,0:T(8,128)(2,1)} %param.5), channel_id=1, source_target_pairs={{0,38},{2,0},{4,2},{6,4},{32,6},{34,32},{36,34},{38,36},{1,39},{3,... | collective-permute-start | bytes 3145736 | tf_op jit(solution)/shard_map/ppermute | solution.py:12
  10.5 38.7 %collective-permute-start.2 = (bf16[128,4096]{1,0:T(8,128)(2,1)}, bf16[128,4096]{1,0:T(8,128)(2,1)S(1)}, u32[]{:S(2)}, u32[]{:S(2)}) collective-permute-start(bf16[128,4096]{1,0:T(8,128)(2,1)} %param.5), channel_id=1, source_target_pairs={{0,2},{2,4},{4,6},{6,32},{32,34},{34,36},{36,38},{38,0},{1,3},{3,5... | collective-permute-start | bytes 3145736 | tf_op jit(solution)/shard_map/ppermute | solution.py:12
  17.0 29.8 %all-to-all-start = ((bf16[8,128,512]{1,2,0:T(8,128)(2,1)}), bf16[8,128,512]{1,2,0:T(8,128)(2,1)}, u32[]{:S(2)}, u32[]{:S(2)}) async-start(bf16[8,128,512]{1,2,0:T(8,128)(2,1)} %bitcast.33), calls=%async_computation | async-start | bytes 2097152 | tf_op jit(solution)/shard_map/all_to_all | solution.py:16
  48.3 49.0 %copy-start = (bf16[128,4096]{1,0:T(8,128)(2,1)}, bf16[128,4096]{1,0:T(8,128)(2,1)S(1)}, u32[]{:S(2)}) copy-start(bf16[128,4096]{1,0:T(8,128)(2,1)S(1)} %collective-permute-done) | copy-start | bytes 3145732
  49.2 56.2 %collective-permute-start.1 = (bf16[64,4096]{1,0:T(8,128)(2,1)}, bf16[64,4096]{1,0:T(8,128)(2,1)}, u32[]{:S(2)}, u32[]{:S(2)}) collective-permute-start(bf16[64,4096]{1,0:T(8,128)(2,1)} %slice.18), channel_id=1, source_target_pairs={{0,38},{2,0},{4,2},{6,4},{32,6},{34,32},{36,34},{38,36},{1,39},{3,... | collective-permute-start | bytes 1572872 | tf_op jit(solution)/shard_map/ppermute | solution.py:12
  50.1 57.3 %collective-permute-start.3 = (bf16[64,4096]{1,0:T(8,128)(2,1)}, bf16[64,4096]{1,0:T(8,128)(2,1)}, u32[]{:S(2)}, u32[]{:S(2)}) collective-permute-start(bf16[64,4096]{1,0:T(8,128)(2,1)} %slice.19), channel_id=1, source_target_pairs={{0,2},{2,4},{4,6},{6,32},{32,34},{34,36},{36,38},{38,0},{1,3},{3,5... | collective-permute-start | bytes 1572872 | tf_op jit(solution)/shard_map/ppermute | solution.py:12
  98.9 31.0 %all-to-all-start.5 = ((bf16[4,4,32,2048]{3,2,1,0:T(8,128)(2,1)}), bf16[4,4,32,2048]{3,2,1,0:T(8,128)(2,1)S(1)}, u32[]{:S(2)}, u32[]{:S(2)}) async-start(bf16[4,4,32,2048]{3,2,1,0:T(8,128)(2,1)} %bitcast.31), calls=%async_computation.5 | async-start | bytes 4194304 | tf_op jit(solution)/shard_map/all_to_all | solution.py:16
  129.9 30.5 %all-to-all-start.2 = ((bf16[4,4,32,2048]{3,2,1,0:T(8,128)(2,1)}), bf16[4,4,32,2048]{3,2,1,0:T(8,128)(2,1)}, u32[]{:S(2)}, u32[]{:S(2)}) async-start(bf16[4,4,32,2048]{3,2,1,0:T(8,128)(2,1)} %bitcast.32), calls=%async_computation.2 | async-start | bytes 4194304 | tf_op jit(solution)/shard_map/all_to_all | solution.py:16
  160.3 17.0 %all-to-all-start.6 = ((bf16[4,32,2048]{2,1,0:T(8,128)(2,1)}), bf16[4,32,2048]{2,1,0:T(8,128)(2,1)S(1)}, u32[]{:S(2)}, u32[]{:S(2)}) async-start(bf16[4,32,2048]{2,1,0:T(8,128)(2,1)} %reduce_sum.50), calls=%async_computation.6 | async-start | bytes 1048576 | tf_op jit(solution)/shard_map/all_to_all | solution.py:16
  177.4 15.2 %all-to-all-start.3 = ((bf16[4,32,2048]{2,1,0:T(8,128)(2,1)}), bf16[4,32,2048]{2,1,0:T(8,128)(2,1)S(1)}, u32[]{:S(2)}, u32[]{:S(2)}) async-start(bf16[4,32,2048]{2,1,0:T(8,128)(2,1)} %reduce_sum.48), calls=%async_computation.3 | async-start | bytes 1048576 | tf_op jit(solution)/shard_map/all_to_all | solution.py:16
  192.5 37.1 %all-to-all-start.1 = ((bf16[4,1024,128]{1,2,0:T(8,128)(2,1)}), bf16[4,1024,128]{1,2,0:T(8,128)(2,1)S(1)}, u32[]{:S(2)}, u32[]{:S(2)}) async-start(bf16[4,1024,128]{1,2,0:T(8,128)(2,1)} %bitcast.9), calls=%async_computation.1 | async-start | bytes 2097152 | tf_op jit(solution)/shard_map/all_to_all | solution.py:16
  198.3 20.4 %collective-permute-start.5 = (bf16[32,2048]{1,0:T(8,128)(2,1)S(1)}, bf16[32,2048]{1,0:T(8,128)(2,1)S(1)}, u32[]{:S(2)}, u32[]{:S(2)}) collective-permute-start(bf16[32,2048]{1,0:T(8,128)(2,1)S(1)} %reduce_sum.51), channel_id=1, source_target_pairs={{0,32},{32,0},{1,33},{33,1},{2,34},{34,2},{3,35},{35,3},{4,36},{36... | collective-permute-start | bytes 393224 | tf_op jit(solution)/shard_map/ppermute | solution.py:12
  203.5 30.5 %collective-permute-start.4 = (bf16[32,2048]{1,0:T(8,128)(2,1)S(1)}, bf16[32,2048]{1,0:T(8,128)(2,1)S(1)}, u32[]{:S(2)}, u32[]{:S(2)}) collective-permute-start(bf16[32,2048]{1,0:T(8,128)(2,1)S(1)} %reduce_sum.49), channel_id=1, source_target_pairs={{0,32},{32,0},{1,33},{33,1},{2,34},{34,2},{3,35},{35,3},{4,36},{36... | collective-permute-start | bytes 393224 | tf_op jit(solution)/shard_map/ppermute | solution.py:12
  230.5 12.4 %all-to-all-start.7 = ((bf16[4,32,2048]{2,1,0:T(8,128)(2,1)}), bf16[4,32,2048]{2,1,0:T(8,128)(2,1)S(1)}, u32[]{:S(2)}, u32[]{:S(2)}) async-start(bf16[4,32,2048]{2,1,0:T(8,128)(2,1)} %broadcast_in_dim.5), calls=%async_computation.7 | async-start | bytes 1048576 | tf_op jit(solution)/shard_map/all_to_all | solution.py:16
  243.8 11.5 %all-to-all-start.4 = ((bf16[4,32,2048]{2,1,0:T(8,128)(2,1)}), bf16[4,32,2048]{2,1,0:T(8,128)(2,1)S(1)}, u32[]{:S(2)}, u32[]{:S(2)}) async-start(bf16[4,32,2048]{2,1,0:T(8,128)(2,1)} %broadcast_in_dim.4), calls=%async_computation.4 | async-start | bytes 1048576 | tf_op jit(solution)/shard_map/all_to_all | solution.py:16
Sparse Core Ops, SparseCore 0:
  9.9 45.7 all-gather.2
  57.6 35.1 all-gather.4

commit v2 on v1

v2 whole, which is shorter than its diff:
```python
import jax
import jax.numpy as jnp
from jax import lax
from jax.experimental import pallas as pl
from jax.experimental.pallas import tpu as pltpu
from jax.sharding import Mesh, PartitionSpec as P

CHUNKS = (2048, 2048)
RING8 = ("h", "l")
F32, BF16 = jnp.float32, jnp.bfloat16


def shift(v, axis, by):
    n = lax.axis_size(axis)
    return lax.ppermute(v, axis, [(i, (i + by) % n) for i in range(n)])


def exchange(v, axis):
    return lax.all_to_all(v, axis, split_axis=0, concat_axis=0, tiled=True)


def after(v, *others):
    return lax.optimization_barrier((v, *others))[0]


def pick(v, index):
    return lax.dynamic_index_in_dim(v, index, 0, keepdims=False)


def gathered(acc):
    return exchange(jnp.broadcast_to(acc[None], (4,) + acc.shape), "x")


def partial_kernel(at, acts, own, sib, *refs):
    outs, total_ref = refs[:-1], refs[-1]
    x, c = at[0], at[2]
    blocks, rows, _ = outs[0].shape
    total = 0.0
    for which, tokens in ((c, own), (1 - c, sib)):
        lhs = jnp.concatenate([acts[i, which] for i in range(acts.shape[0])], axis=1)
        total = total + jnp.dot(lhs, tokens[...], preferred_element_type=F32)
    total_ref[...] = total.reshape(total_ref.shape)
    for r, out in enumerate(outs):
        out[...] = total_ref[:, (x + r) & 3].astype(out.dtype)


def partial(at, acts, own, sib):
    y, _, heads, toks = acts.shape
    cols = own.shape[1]
    wide = min(512, cols)
    rows = heads // 16
    return pl.pallas_call(
        partial_kernel,
        grid_spec=pltpu.PrefetchScalarGridSpec(
            num_scalar_prefetch=1,
            grid=(cols // wide,),
            in_specs=[
                pl.BlockSpec(acts.shape, lambda i, at: (0, 0, 0, 0)),
                pl.BlockSpec((y * toks, wide), lambda i, at: (0, i)),
                pl.BlockSpec((y * toks, wide), lambda i, at: (0, i)),
            ],
            out_specs=[pl.BlockSpec((4, rows, wide), lambda i, at: (0, 0, i))] * 4,
            scratch_shapes=[pltpu.VMEM((4, 4, rows, wide), F32)],
        ),
        out_shape=[jax.ShapeDtypeStruct((4, rows, cols), BF16)] * 4,
        cost_estimate=pl.CostEstimate(
            flops=4 * heads * y * toks * cols, transcendentals=0,
            bytes_accessed=4 * y * toks * cols + 2 * heads * cols + 2 * acts.size),
        name="partial_grad_w",
    )(at, acts, own, sib)


def inputs_kernel(chunks, at, *refs):
    owns, sibs = refs[:chunks], refs[chunks:2 * chunks]
    w0, w1, w2a, w2b, w3, out = refs[2 * chunks:]
    l, c = at[1], at[2]
    heads = w0.shape[0]
    weights = jnp.concatenate([w0[...], w1[...], w2a[...], w2b[...], w3[...]], axis=0)
    for which, tokens in ((c, owns), (1 - c, sibs)):
        total, lo = 0.0, 0
        for ref in tokens:
            hi = lo + ref.shape[1]
            total = total + lax.dot_general(
                ref[...], weights[:, lo:hi], (((1,), (1,)), ((), ())), preferred_element_type=F32)
            lo = hi
        total = total.astype(out.dtype).reshape(out.shape[1], out.shape[3], 4, heads)
        for d in range(4):
            out[(l + d) & 3, :, which] = total[:, :, d]


def inputs_grad(at, owns, sibs, w_parts):
    heads, feats = w_parts[0].shape
    toks = owns[0].shape[0] // 4
    steps = 2
    tall = owns[0].shape[0] // steps
    whole = lambda w: pl.BlockSpec(w.shape, lambda i, at: (0, 0))
    rows = [pl.BlockSpec((tall, o.shape[1]), lambda i, at: (i, 0)) for o in owns]
    return pl.pallas_call(
        lambda at, *refs: inputs_kernel(len(owns), at, *refs),
        grid_spec=pltpu.PrefetchScalarGridSpec(
            num_scalar_prefetch=1,
            grid=(steps,),
            in_specs=rows + rows + [whole(w) for w in w_parts],
            out_specs=pl.BlockSpec((4, 4 // steps, 2, toks, heads), lambda i, at: (0, i, 0, 0, 0)),
        ),
        out_shape=jax.ShapeDtypeStruct((4, 4, 2, toks, heads), BF16),
        cost_estimate=pl.CostEstimate(
            flops=2 * 8 * toks * feats * 4 * heads, transcendentals=0,
            bytes_accessed=2 * (8 * toks * feats + 4 * heads * feats + 32 * toks * heads)),
        name="grad_attn",
    )(at, *owns, *sibs, *w_parts)


def local(grad_out, attn, w_out):
    g = grad_out[0]
    a = attn[0]
    toks, feats = g.shape
    heads = w_out.shape[0]
    at = jnp.stack([lax.axis_index(n) for n in ("x", "l", "c")]).astype(jnp.int32)

    cuts, lo = [], 0
    for size in CHUNKS:
        size = size * feats // sum(CHUNKS)
        cuts.append((lo, lo + size))
        lo += size
    owns = [lax.all_gather(g[:, lo:hi], "y", axis=0, tiled=True) for lo, hi in cuts]

    a = a.reshape(toks, 4, 4, 2, heads).transpose(1, 3, 2, 4, 0).reshape(8, 4 * heads, toks)
    acts = exchange(a, ("y", "c")).reshape(4, 2, 4 * heads, toks)

    above, below = shift(w_out, RING8, -1), shift(w_out, RING8, 1)

    l = lax.axis_index("l")
    owns[0] = after(owns[0], acts, above, below)
    sums, sibs, part, far = [], [], None, None
    for j, own in enumerate(owns):
        if part is not None:
            owns[j] = own = after(own, *moved, *far)
        sib = shift(own, "c", 1)
        sibs.append(sib)
        part = partial(at, acts, own, sib)
        if j == 0:
            half = heads // 2
            far = [shift(after(above[:half], part[0]), RING8, -1), shift(after(below[half:], part[0]), RING8, 1)]
        moved = [shift(part[d], "x", d) for d in (1, 3, 2)]
        tot = part[0].astype(F32)
        for other in moved:
            tot = tot + other.astype(F32)
        tot = tot.astype(BF16)
        acc = pick(tot, l).astype(F32)
        for d in (1, -1, -2 if j % 2 else 2):
            acc = acc + shift(pick(tot, (l + d) & 3), RING8, d).astype(F32)
        acc = acc.astype(BF16)
        sums.append((acc.astype(F32) + shift(acc, "h", 1).astype(F32)).astype(BF16))
    grad_w = jnp.concatenate([gathered(acc).reshape(heads, -1) for acc in sums], 1)

    owns[0] = after(owns[0], part[0])
    res = inputs_grad(at, owns, sibs, [w_out, above, *far, below])
    pieces = [pick(res, l)] + [shift(pick(res, (l + d) & 3), "l", d) for d in (1, 2, 3)]
    out = jnp.zeros((4, 4, 2, toks, heads), BF16)
    for d, piece in enumerate(pieces):
        out = lax.dynamic_update_slice_in_dim(out, piece[:, None], (l - d) & 3, 1)
    out = out.reshape(1, 4 * 8 * toks, heads)
    return out, grad_w


def solution(mesh):
    fine = Mesh(mesh.devices.reshape(4, 2, 4, 4, 2), ("x", "h", "y", "l", "c"))
    dp, context = ("x", "h"), ("y", "l", "c")
    in_specs = (P(dp, context, None), P(dp, context, None), P(context, None))
    out_specs = (P(dp, None, context), P(context, None))
    return jax.shard_map(local, mesh=fine, in_specs=in_specs, out_specs=out_specs, check_vma=False)
```

time: 267 us -> 201 us (0.75)
  the two profiles are of different devices: /device:TPU:64 before, /device:TPU:2 now
where the time goes in v2:
time: 201 us
  waiting for transfers between devices  91.7 us (46%)
  starting transfers between devices  56.3 us (28%)
  Pallas kernels  25.3 us (13%)
  between operations  14.3 us (7%)
  local copies, waits for them, and re-layouts  9.6 us (5%)
  other arithmetic  3.63 us (2%)
    ppermute x23, starting transfers between devices, shift(): return lax.ppermute(v, axis, [(i, (i + by) % n) for i in range(n)])  39.2 us
    ppermute x23, waiting for transfers between devices, shift(): return lax.ppermute(v, axis, [(i, (i + by) % n) for i in range(n)])  38.5 us
    all_to_all x3, waiting for transfers between devices, exchange(): return lax.all_to_all(v, axis, split_axis=0, concat_axis=0, tiled=True)  31.8 us
    all_gather x2, waiting for transfers between devices, local(): lax.all_gather(g[:, lo:hi], 'y', axis=0, tiled=True)  20.6 us
    all_to_all x3, starting transfers between devices, exchange(): return lax.all_to_all(v, axis, split_axis=0, concat_axis=0, tiled=True)  17 us
    pallas_call x2, Pallas kernels, partial(): pl.pallas_call(partial_kernel, grid_spec=pltpu.PrefetchScalarGridSpec(num...  13.9 us
    pallas_call x1, Pallas kernels, inputs_grad(): pl.pallas_call(lambda at, *refs: inputs_kernel(len(owns), at, *refs), gri...  11.4 us
  transfers between devices with their start and end apart: 28, of which 13 were waited for; matrix products, arithmetic and copies ran while one was open for 5% of the time, Pallas kernels for 13%

profile of v2, /device:TPU:2, one launch (start us, length us, event | category | flops | bytes accessed | tf_op | source)
XLA Modules:
  0.0 200.8 jit_solution(3613150245367303605)
XLA Ops:
  7.2 2.4 %fusion.6 = (bf16[128,2048]{1,0:T(8,128)(2,1)}, bf16[128,2048]{1,0:T(8,128)(2,1)}) fusion(bf16[128,4096]{1,0:T(8,128)(2,1)} %bitcast.45), kind=kLoop, calls=%fused_computation.27 | loop fusion | bytes 2097152 | tf_op jit(solution)/shard_map/slice | solution.py:126
  9.6 5.9 %collective-permute-start = (bf16[128,4096]{1,0:T(8,128)(2,1)}, bf16[128,4096]{1,0:T(8,128)(2,1)S(1)}, u32[]{:S(2)}, u32[]{:S(2)}) collective-permute-start(bf16[128,4096]{1,0:T(8,128)(2,1)} %refs_4_.1), channel_id=1, source_target_pairs={{0,38},{2,0},{4,2},{6,4},{32,6},{34,32},{36,34},{38,36},{1,39},{3,... | collective-permute-start | bytes 3145736 | tf_op jit(solution)/shard_map/ppermute | solution.py:15
  16.3 2.1 %copy.5 = bf16[4,2,4,128,128]{4,3,2,1,0:T(8,128)(2,1)} copy(bf16[4,2,4,128,128]{3,1,2,0,4:T(2,128)(2,1)S(1)} %bitcast.42) | data formatting | bytes 2097152 | tf_op jit(solution)/shard_map/transpose | solution.py:128
  18.4 4.5 %all-to-all-start = ((bf16[8,512,128]{2,1,0:T(8,128)(2,1)}), bf16[8,512,128]{2,1,0:T(8,128)(2,1)S(1)}, u32[]{:S(2)}, u32[]{:S(2)}) async-start(bf16[8,512,128]{2,1,0:T(8,128)(2,1)} %bitcast.5), calls=%async_computation | async-start | bytes 2097152 | tf_op jit(solution)/shard_map/all_to_all | solution.py:19
  23.6 25.3 %all-to-all-done = bf16[8,512,128]{2,1,0:T(8,128)(2,1)S(1)} async-done(((bf16[8,512,128]{2,1,0:T(8,128)(2,1)}), bf16[8,512,128]{2,1,0:T(8,128)(2,1)S(1)}, u32[]{:S(2)}, u32[]{:S(2)}) %all-to-all-start) | async-done | bytes 1048608 | tf_op jit(solution)/shard_map/all_to_all | solution.py:19
  48.9 6.9 %all-gather.3.cloned.1.call-done.own.refs_0_ = bf16[512,2048]{1,0:T(8,128)(2,1)} async-done(((bf16[128,2048]{1,0:T(8,128)(2,1)}), bf16[512,2048]{1,0:T(8,128)(2,1)}) %all-gather.3.cloned.1.call-update) | async-done | bytes 2097168 | tf_op jit(solution)/shard_map/all_gather | solution.py:126
  58.6 1.7 collective-permute-done.2.sib.refs_2_
  60.3 6.9 %partial_grad_w.2 = (bf16[4,32,2048]{2,1,0:T(8,128)(2,1)}, bf16[4,32,2048]{2,1,0:T(8,128)(2,1)}, bf16[4,32,2048]{2,1,0:T(8,128)(2,1)}, bf16[4,32,2048]{2,1,0:T(8,128)(2,1)}) custom-call(s32[3]{0:T(128)} %pad_add_fusion.at, bf16[4,2,512,128]{3,2,1,0:T(8,128)(2,1)} %bitcast.46, bf16[512,2048]{1,0:T(8,128)(2,1)} %all-gather.3.cloned.1.call-done.own.refs_0_, ...), custom_call_target="tpu_custom_call" | custom-call | flops 2147483648 | bytes 7340032 | tf_op jit(solution)/shard_map/partial_grad_w/pallas_call | solution.py:52
  67.2 1.5 collective-permute-start.3
  69.3 2.1 %collective-permute-start.5 = (bf16[4,32,2048]{2,1,0:T(8,128)(2,1)}, bf16[4,32,2048]{2,1,0:T(8,128)(2,1)S(1)}, u32[]{:S(2)}, u32[]{:S(2)}) collective-permute-start(bf16[4,32,2048]{2,1,0:T(8,128)(2,1)} %get-tuple-element.18), channel_id=1, source_target_pairs={{0,128},{64,192},{128,0},{192,64},{1,129},{65,193},{129,1},{193,65... | collective-permute-start | bytes 1572872 | tf_op jit(solution)/shard_map/ppermute | solution.py:15
  71.4 3.2 %collective-permute-start.6 = (bf16[64,4096]{1,0:T(8,128)(2,1)S(1)}, bf16[64,4096]{1,0:T(8,128)(2,1)S(1)}, u32[]{:S(2)}, u32[]{:S(2)}) collective-permute-start(bf16[64,4096]{1,0:T(8,128)(2,1)S(1)} %slice.18), channel_id=1, source_target_pairs={{0,38},{2,0},{4,2},{6,4},{32,6},{34,32},{36,34},{38,36},{1,39},{3,... | collective-permute-start | bytes 1572872 | tf_op jit(solution)/shard_map/ppermute | solution.py:15
  74.7 13.7 %all-gather.5.cloned.1.call-done.own.refs_1_ = bf16[512,2048]{1,0:T(8,128)(2,1)} async-done(((bf16[128,2048]{1,0:T(8,128)(2,1)}), bf16[512,2048]{1,0:T(8,128)(2,1)}) %all-gather.5.cloned.1.call-update) | async-done | bytes 2097168 | tf_op jit(solution)/shard_map/all_gather | solution.py:126
  88.4 6.1 %collective-permute-done.5 = bf16[4,32,2048]{2,1,0:T(8,128)(2,1)S(1)} collective-permute-done((bf16[4,32,2048]{2,1,0:T(8,128)(2,1)}, bf16[4,32,2048]{2,1,0:T(8,128)(2,1)S(1)}, u32[]{:S(2)}, u32[]{:S(2)}) %collective-permute-start.5) | collective-permute-done | bytes 524320 | tf_op jit(solution)/shard_map/ppermute | solution.py:15
  96.2 3.3 %collective-permute-start.13 = (bf16[32,2048]{1,0:T(8,128)(2,1)S(1)}, bf16[32,2048]{1,0:T(8,128)(2,1)S(1)}, u32[]{:S(2)}, u32[]{:S(2)}) collective-permute-start(bf16[32,2048]{1,0:T(8,128)(2,1)S(1)} %get-tuple-element.35), channel_id=1, source_target_pairs={{0,38},{2,0},{4,2},{6,4},{32,6},{34,32},{36,34},{38,36},{1,39},{3,... | collective-permute-start | bytes 393224 | tf_op jit(solution)/shard_map/ppermute | solution.py:15
  99.6 4.3 %collective-permute-done.12 = bf16[32,2048]{1,0:T(8,128)(2,1)S(1)} collective-permute-done((bf16[32,2048]{1,0:T(8,128)(2,1)S(1)}, bf16[32,2048]{1,0:T(8,128)(2,1)S(1)}, u32[]{:S(2)}, u32[]{:S(2)}) %collective-permute-start.12) | collective-permute-done | bytes 131104 | tf_op jit(solution)/shard_map/ppermute | solution.py:15
  103.8 6.5 %collective-permute-done.14 = bf16[32,2048]{1,0:T(8,128)(2,1)S(1)} collective-permute-done((bf16[32,2048]{1,0:T(8,128)(2,1)S(1)}, bf16[32,2048]{1,0:T(8,128)(2,1)S(1)}, u32[]{:S(2)}, u32[]{:S(2)}) %collective-permute-start.14) | collective-permute-done | bytes 131104 | tf_op jit(solution)/shard_map/ppermute | solution.py:15
  110.4 2.1 %collective-permute-start.15 = (bf16[32,2048]{1,0:T(8,128)(2,1)S(1)}, bf16[32,2048]{1,0:T(8,128)(2,1)S(1)}, u32[]{:S(2)}, u32[]{:S(2)}) collective-permute-start(bf16[32,2048]{1,0:T(8,128)(2,1)S(1)} %fusion.5), channel_id=1, source_target_pairs={{0,32},{32,0},{1,33},{33,1},{2,34},{34,2},{3,35},{35,3},{4,36},{36... | collective-permute-start | bytes 393224 | tf_op jit(solution)/shard_map/ppermute | solution.py:15
  112.5 7.0 %partial_grad_w.3 = (bf16[4,32,2048]{2,1,0:T(8,128)(2,1)}, bf16[4,32,2048]{2,1,0:T(8,128)(2,1)}, bf16[4,32,2048]{2,1,0:T(8,128)(2,1)}, bf16[4,32,2048]{2,1,0:T(8,128)(2,1)}) custom-call(s32[3]{0:T(128)} %pad_add_fusion.at, bf16[4,2,512,128]{3,2,1,0:T(8,128)(2,1)} %bitcast.47, bf16[512,2048]{1,0:T(8,128)(2,1)} %all-gather.5.cloned.1.call-done.own.refs_1_, ...), custom_call_target="tpu_custom_call" | custom-call | flops 2147483648 | bytes 7340032 | tf_op jit(solution)/shard_map/partial_grad_w/pallas_call | solution.py:52
  119.8 2.0 %collective-permute-start.17 = (bf16[4,32,2048]{2,1,0:T(8,128)(2,1)}, bf16[4,32,2048]{2,1,0:T(8,128)(2,1)S(1)}, u32[]{:S(2)}, u32[]{:S(2)}) collective-permute-start(bf16[4,32,2048]{2,1,0:T(8,128)(2,1)} %get-tuple-element.26), channel_id=1, source_target_pairs={{0,192},{64,0},{128,64},{192,128},{1,193},{65,1},{129,65},{193,129... | collective-permute-start | bytes 1572872 | tf_op jit(solution)/shard_map/ppermute | solution.py:15
  121.8 1.7 collective-permute-start.18
  124.4 5.2 %all-to-all-start.1 = ((bf16[4,32,2048]{2,1,0:T(8,128)(2,1)}), bf16[4,32,2048]{2,1,0:T(8,128)(2,1)S(1)}, u32[]{:S(2)}, u32[]{:S(2)}) async-start(bf16[4,32,2048]{2,1,0:T(8,128)(2,1)} %broadcast_in_dim.32), calls=%async_computation.1 | async-start | bytes 1048576 | tf_op jit(solution)/shard_map/all_to_all | solution.py:19
  129.6 11.4 %grad_attn.1 = bf16[4,4,2,128,128]{4,3,2,1,0:T(8,128)(2,1)} custom-call(s32[3]{0:T(128)} %pad_add_fusion.at, bf16[512,2048]{1,0:T(8,128)(2,1)} %all-gather.3.cloned.1.call-done.own.refs_0_, bf16[512,2048]{1,0:T(8,128)(2,1)} %all-gather.5.cloned.1.call-done.own.refs_1_, bf16[512,2048]{1,0:T(8,128)(2,1)} %collective-permute-done.2.sib.refs_2_, ...), custom_call_target="tpu_custom_call" | custom-call | flops 4294967296 | bytes 13631488 | tf_op jit(solution)/shard_map/grad_attn/pallas_call | solution.py:98
  141.5 5.8 %collective-permute-done.18 = bf16[4,32,2048]{2,1,0:T(8,128)(2,1)S(1)} collective-permute-done((bf16[4,32,2048]{2,1,0:T(8,128)(2,1)}, bf16[4,32,2048]{2,1,0:T(8,128)(2,1)S(1)}, u32[]{:S(2)}, u32[]{:S(2)}) %collective-permute-start.18) | collective-permute-done | bytes 524320 | tf_op jit(solution)/shard_map/ppermute | solution.py:15
  148.8 2.3 %collective-permute-start.20 = (bf16[32,2048]{1,0:T(8,128)(2,1)S(1)}, bf16[32,2048]{1,0:T(8,128)(2,1)S(1)}, u32[]{:S(2)}, u32[]{:S(2)}) collective-permute-start(bf16[32,2048]{1,0:T(8,128)(2,1)S(1)} %get-tuple-element.38), channel_id=1, source_target_pairs={{0,38},{2,0},{4,2},{6,4},{32,6},{34,32},{36,34},{38,36},{1,39},{3,... | collective-permute-start | bytes 393224 | tf_op jit(solution)/shard_map/ppermute | solution.py:15
  152.7 1.6 collective-permute-start.10
  154.5 2.9 %collective-permute-start.11 = (bf16[4,2,128,128]{3,2,1,0:T(8,128)(2,1)S(1)}, bf16[4,2,128,128]{3,2,1,0:T(8,128)(2,1)S(1)}, u32[]{:S(2)}, u32[]{:S(2)}) collective-permute-start(bf16[4,2,128,128]{3,2,1,0:T(8,128)(2,1)S(1)} %get-tuple-element.28), channel_id=1, source_target_pairs={{0,6},{2,0},{4,2},{6,4},{1,7},{3,1},{5,3},{7,5},{8,14},{10,8},{12,... | collective-permute-start | bytes 786440 | tf_op jit(solution)/shard_map/ppermute | solution.py:15
  157.4 3.3 %collective-permute-done.20 = bf16[32,2048]{1,0:T(8,128)(2,1)S(1)} collective-permute-done((bf16[32,2048]{1,0:T(8,128)(2,1)S(1)}, bf16[32,2048]{1,0:T(8,128)(2,1)S(1)}, u32[]{:S(2)}, u32[]{:S(2)}) %collective-permute-start.20) | collective-permute-done | bytes 131104 | tf_op jit(solution)/shard_map/ppermute | solution.py:15
  160.8 7.2 %collective-permute-done.21 = bf16[32,2048]{1,0:T(8,128)(2,1)S(1)} collective-permute-done((bf16[32,2048]{1,0:T(8,128)(2,1)S(1)}, bf16[32,2048]{1,0:T(8,128)(2,1)S(1)}, u32[]{:S(2)}, u32[]{:S(2)}) %collective-permute-start.21) | collective-permute-done | bytes 131104 | tf_op jit(solution)/shard_map/ppermute | solution.py:15
  168.1 6.9 %collective-permute-start.22 = (bf16[32,2048]{1,0:T(8,128)(2,1)S(1)}, bf16[32,2048]{1,0:T(8,128)(2,1)S(1)}, u32[]{:S(2)}, u32[]{:S(2)}) collective-permute-start(bf16[32,2048]{1,0:T(8,128)(2,1)S(1)} %fusion.2), channel_id=1, source_target_pairs={{0,32},{32,0},{1,33},{33,1},{2,34},{34,2},{3,35},{35,3},{4,36},{36... | collective-permute-start | bytes 393224 | tf_op jit(solution)/shard_map/ppermute | solution.py:15
  175.0 3.0 %collective-permute-done.22 = bf16[32,2048]{1,0:T(8,128)(2,1)S(1)} collective-permute-done((bf16[32,2048]{1,0:T(8,128)(2,1)S(1)}, bf16[32,2048]{1,0:T(8,128)(2,1)S(1)}, u32[]{:S(2)}, u32[]{:S(2)}) %collective-permute-start.22) | collective-permute-done | bytes 131104 | tf_op jit(solution)/shard_map/ppermute | solution.py:15
  178.9 7.3 %all-to-all-start.2 = ((bf16[4,32,2048]{2,1,0:T(8,128)(2,1)}), bf16[4,32,2048]{2,1,0:T(8,128)(2,1)S(1)}, u32[]{:S(2)}, u32[]{:S(2)}) async-start(bf16[4,32,2048]{2,1,0:T(8,128)(2,1)} %broadcast_in_dim.33), calls=%async_computation.2 | async-start | bytes 1048576 | tf_op jit(solution)/shard_map/all_to_all | solution.py:19
  186.4 6.5 %all-to-all-done.2 = bf16[4,32,2048]{2,1,0:T(8,128)(2,1)S(1)} async-done(((bf16[4,32,2048]{2,1,0:T(8,128)(2,1)}), bf16[4,32,2048]{2,1,0:T(8,128)(2,1)S(1)}, u32[]{:S(2)}, u32[]{:S(2)}) %all-to-all-start.2) | async-done | bytes 524320 | tf_op jit(solution)/shard_map/all_to_all | solution.py:19
  (66 shorter events, 13.8 us)
Async XLA Ops:
  7.2 48.6 %all-gather.3.cloned.1.call-start = ((), (), s32[]{:S(2)}) async-start(), calls=%async_computation.3 | async-start | bytes 2621440 | tf_op jit(solution)/shard_map/all_gather | solution.py:126
  9.6 39.3 %collective-permute-start = (bf16[128,4096]{1,0:T(8,128)(2,1)}, bf16[128,4096]{1,0:T(8,128)(2,1)S(1)}, u32[]{:S(2)}, u32[]{:S(2)}) collective-permute-start(bf16[128,4096]{1,0:T(8,128)(2,1)} %refs_4_.1), channel_id=1, source_target_pairs={{0,38},{2,0},{4,2},{6,4},{32,6},{34,32},{36,34},{38,36},{1,39},{3,... | collective-permute-start | bytes 3145736 | tf_op jit(solution)/shard_map/ppermute | solution.py:15
  15.5 33.4 %collective-permute-start.1 = (bf16[128,4096]{1,0:T(8,128)(2,1)}, bf16[128,4096]{1,0:T(8,128)(2,1)}, u32[]{:S(2)}, u32[]{:S(2)}) collective-permute-start(bf16[128,4096]{1,0:T(8,128)(2,1)} %refs_4_.1), channel_id=1, source_target_pairs={{0,2},{2,4},{4,6},{6,32},{32,34},{34,36},{36,38},{38,0},{1,3},{3,5... | collective-permute-start | bytes 3145736 | tf_op jit(solution)/shard_map/ppermute | solution.py:15
  18.4 30.5 %all-to-all-start = ((bf16[8,512,128]{2,1,0:T(8,128)(2,1)}), bf16[8,512,128]{2,1,0:T(8,128)(2,1)S(1)}, u32[]{:S(2)}, u32[]{:S(2)}) async-start(bf16[8,512,128]{2,1,0:T(8,128)(2,1)} %bitcast.5), calls=%async_computation | async-start | bytes 2097152 | tf_op jit(solution)/shard_map/all_to_all | solution.py:19
  22.9 65.5 %all-gather.5.cloned.1.call-start = ((), (), s32[]{:S(2)}) async-start(), calls=%async_computation.4 | async-start | bytes 2621440 | tf_op jit(solution)/shard_map/all_gather | solution.py:126
  48.9 11.4 %copy-start.2 = (bf16[8,512,128]{2,1,0:T(8,128)(2,1)}, bf16[8,512,128]{2,1,0:T(8,128)(2,1)S(1)}, u32[]{:S(2)}) copy-start(bf16[8,512,128]{2,1,0:T(8,128)(2,1)S(1)} %all-to-all-done) | copy-start | bytes 3145732
  55.8 4.5 %collective-permute-start.2 = (bf16[512,2048]{1,0:T(8,128)(2,1)}, bf16[512,2048]{1,0:T(8,128)(2,1)}, u32[]{:S(2)}, u32[]{:S(2)}) collective-permute-start(bf16[512,2048]{1,0:T(8,128)(2,1)} %all-gather.3.cloned.1.call-done.own.refs_0_), channel_id=1, source_target_pairs={{0,1},{1,0},{2,3},{3,2},{4,5},{5,4},{6,7},{7,6},{8,9},{9,8},{10,11... | collective-permute-start | bytes 6291464 | tf_op jit(solution)/shard_map/ppermute | solution.py:15
  67.2 21.2 %collective-permute-start.3 = (bf16[4,32,2048]{2,1,0:T(8,128)(2,1)}, bf16[4,32,2048]{2,1,0:T(8,128)(2,1)S(1)}, u32[]{:S(2)}, u32[]{:S(2)}) collective-permute-start(bf16[4,32,2048]{2,1,0:T(8,128)(2,1)} %get-tuple-element.16), channel_id=1, source_target_pairs={{0,64},{64,128},{128,192},{192,0},{1,65},{65,129},{129,193},{193,1... | collective-permute-start | bytes 1572872 | tf_op jit(solution)/shard_map/ppermute | solution.py:15
  68.8 19.7 %collective-permute-start.4 = (bf16[4,32,2048]{2,1,0:T(8,128)(2,1)}, bf16[4,32,2048]{2,1,0:T(8,128)(2,1)S(1)}, u32[]{:S(2)}, u32[]{:S(2)}) collective-permute-start(bf16[4,32,2048]{2,1,0:T(8,128)(2,1)} %get-tuple-element.17), channel_id=1, source_target_pairs={{0,192},{64,0},{128,64},{192,128},{1,193},{65,1},{129,65},{193,129... | collective-permute-start | bytes 1572872 | tf_op jit(solution)/shard_map/ppermute | solution.py:15
  69.3 25.2 %collective-permute-start.5 = (bf16[4,32,2048]{2,1,0:T(8,128)(2,1)}, bf16[4,32,2048]{2,1,0:T(8,128)(2,1)S(1)}, u32[]{:S(2)}, u32[]{:S(2)}) collective-permute-start(bf16[4,32,2048]{2,1,0:T(8,128)(2,1)} %get-tuple-element.18), channel_id=1, source_target_pairs={{0,128},{64,192},{128,0},{192,64},{1,129},{65,193},{129,1},{193,65... | collective-permute-start | bytes 1572872 | tf_op jit(solution)/shard_map/ppermute | solution.py:15
  71.4 23.1 %collective-permute-start.6 = (bf16[64,4096]{1,0:T(8,128)(2,1)S(1)}, bf16[64,4096]{1,0:T(8,128)(2,1)S(1)}, u32[]{:S(2)}, u32[]{:S(2)}) collective-permute-start(bf16[64,4096]{1,0:T(8,128)(2,1)S(1)} %slice.18), channel_id=1, source_target_pairs={{0,38},{2,0},{4,2},{6,4},{32,6},{34,32},{36,34},{38,36},{1,39},{3,... | collective-permute-start | bytes 1572872 | tf_op jit(solution)/shard_map/ppermute | solution.py:15
  74.7 19.9 %collective-permute-start.7 = (bf16[64,4096]{1,0:T(8,128)(2,1)S(1)}, bf16[64,4096]{1,0:T(8,128)(2,1)}, u32[]{:S(2)}, u32[]{:S(2)}) collective-permute-start(bf16[64,4096]{1,0:T(8,128)(2,1)S(1)} %slice.19), channel_id=1, source_target_pairs={{0,2},{2,4},{4,6},{6,32},{32,34},{34,36},{36,38},{38,0},{1,3},{3,5... | collective-permute-start | bytes 1572872 | tf_op jit(solution)/shard_map/ppermute | solution.py:15
  94.5 25.0 %copy-start.6 = (bf16[64,4096]{1,0:T(8,128)(2,1)}, bf16[64,4096]{1,0:T(8,128)(2,1)S(1)}, u32[]{:S(2)}) copy-start(bf16[64,4096]{1,0:T(8,128)(2,1)S(1)} %collective-permute-done.6.refs_6_) | copy-start | bytes 1572868
  94.5 18.0 %collective-permute-start.8 = (bf16[512,2048]{1,0:T(8,128)(2,1)}, bf16[512,2048]{1,0:T(8,128)(2,1)}, u32[]{:S(2)}, u32[]{:S(2)}) collective-permute-start(bf16[512,2048]{1,0:T(8,128)(2,1)} %all-gather.5.cloned.1.call-done.own.refs_1_), channel_id=1, source_target_pairs={{0,1},{1,0},{2,3},{3,2},{4,5},{5,4},{6,7},{7,6},{8,9},{9,8},{10,11... | collective-permute-start | bytes 6291464 | tf_op jit(solution)/shard_map/ppermute | solution.py:15
  96.2 7.7 %collective-permute-start.12 = (bf16[32,2048]{1,0:T(8,128)(2,1)S(1)}, bf16[32,2048]{1,0:T(8,128)(2,1)S(1)}, u32[]{:S(2)}, u32[]{:S(2)}) collective-permute-start(bf16[32,2048]{1,0:T(8,128)(2,1)S(1)} %get-tuple-element.33), channel_id=1, source_target_pairs={{0,2},{2,4},{4,6},{6,32},{32,34},{34,36},{36,38},{38,0},{1,3},{3,5... | collective-permute-start | bytes 393224 | tf_op jit(solution)/shard_map/ppermute | solution.py:15
  96.2 7.6 %collective-permute-start.13 = (bf16[32,2048]{1,0:T(8,128)(2,1)S(1)}, bf16[32,2048]{1,0:T(8,128)(2,1)S(1)}, u32[]{:S(2)}, u32[]{:S(2)}) collective-permute-start(bf16[32,2048]{1,0:T(8,128)(2,1)S(1)} %get-tuple-element.35), channel_id=1, source_target_pairs={{0,38},{2,0},{4,2},{6,4},{32,6},{34,32},{36,34},{38,36},{1,39},{3,... | collective-permute-start | bytes 393224 | tf_op jit(solution)/shard_map/ppermute | solution.py:15
  99.5 10.8 %collective-permute-start.14 = (bf16[32,2048]{1,0:T(8,128)(2,1)S(1)}, bf16[32,2048]{1,0:T(8,128)(2,1)S(1)}, u32[]{:S(2)}, u32[]{:S(2)}) collective-permute-start(bf16[32,2048]{1,0:T(8,128)(2,1)S(1)} %get-tuple-element.34), channel_id=1, source_target_pairs={{0,4},{2,6},{4,32},{6,34},{32,36},{34,38},{36,0},{38,2},{1,5},{3,7... | collective-permute-start | bytes 393224 | tf_op jit(solution)/shard_map/ppermute | solution.py:15
  110.4 13.1 %collective-permute-start.15 = (bf16[32,2048]{1,0:T(8,128)(2,1)S(1)}, bf16[32,2048]{1,0:T(8,128)(2,1)S(1)}, u32[]{:S(2)}, u32[]{:S(2)}) collective-permute-start(bf16[32,2048]{1,0:T(8,128)(2,1)S(1)} %fusion.5), channel_id=1, source_target_pairs={{0,32},{32,0},{1,33},{33,1},{2,34},{34,2},{3,35},{35,3},{4,36},{36... | collective-permute-start | bytes 393224 | tf_op jit(solution)/shard_map/ppermute | solution.py:15
  119.5 21.5 %collective-permute-start.16 = (bf16[4,32,2048]{2,1,0:T(8,128)(2,1)}, bf16[4,32,2048]{2,1,0:T(8,128)(2,1)S(1)}, u32[]{:S(2)}, u32[]{:S(2)}) collective-permute-start(bf16[4,32,2048]{2,1,0:T(8,128)(2,1)} %get-tuple-element.25), channel_id=1, source_target_pairs={{0,64},{64,128},{128,192},{192,0},{1,65},{65,129},{129,193},{193,1... | collective-permute-start | bytes 1572872 | tf_op jit(solution)/shard_map/ppermute | solution.py:15
  119.8 21.8 %collective-permute-start.17 = (bf16[4,32,2048]{2,1,0:T(8,128)(2,1)}, bf16[4,32,2048]{2,1,0:T(8,128)(2,1)S(1)}, u32[]{:S(2)}, u32[]{:S(2)}) collective-permute-start(bf16[4,32,2048]{2,1,0:T(8,128)(2,1)} %get-tuple-element.26), channel_id=1, source_target_pairs={{0,192},{64,0},{128,64},{192,128},{1,193},{65,1},{129,65},{193,129... | collective-permute-start | bytes 1572872 | tf_op jit(solution)/shard_map/ppermute | solution.py:15
  121.8 25.6 %collective-permute-start.18 = (bf16[4,32,2048]{2,1,0:T(8,128)(2,1)}, bf16[4,32,2048]{2,1,0:T(8,128)(2,1)S(1)}, u32[]{:S(2)}, u32[]{:S(2)}) collective-permute-start(bf16[4,32,2048]{2,1,0:T(8,128)(2,1)} %get-tuple-element.27), channel_id=1, source_target_pairs={{0,128},{64,192},{128,0},{192,64},{1,129},{65,193},{129,1},{193,65... | collective-permute-start | bytes 1572872 | tf_op jit(solution)/shard_map/ppermute | solution.py:15
  124.4 53.7 %all-to-all-start.1 = ((bf16[4,32,2048]{2,1,0:T(8,128)(2,1)}), bf16[4,32,2048]{2,1,0:T(8,128)(2,1)S(1)}, u32[]{:S(2)}, u32[]{:S(2)}) async-start(bf16[4,32,2048]{2,1,0:T(8,128)(2,1)} %broadcast_in_dim.32), calls=%async_computation.1 | async-start | bytes 1048576 | tf_op jit(solution)/shard_map/all_to_all | solution.py:19
  129.6 17.8 %copy-start.4 = (bf16[4,32,2048]{2,1,0:T(8,128)(2,1)S(1)}, bf16[4,32,2048]{2,1,0:T(8,128)(2,1)}, u32[]{:S(2)}) copy-start(bf16[4,32,2048]{2,1,0:T(8,128)(2,1)} %get-tuple-element.23) | copy-start | bytes 1572868
  141.0 10.3 %copy-start = (bf16[4,4,2,128,128]{4,3,2,1,0:T(8,128)(2,1)S(1)}, bf16[4,4,2,128,128]{4,3,2,1,0:T(8,128)(2,1)}, u32[]{:S(2)}) copy-start(bf16[4,4,2,128,128]{4,3,2,1,0:T(8,128)(2,1)} %grad_attn.1) | copy-start | bytes 3145732
  147.7 6.8 %collective-permute-start.19 = (bf16[32,2048]{1,0:T(8,128)(2,1)S(1)}, bf16[32,2048]{1,0:T(8,128)(2,1)S(1)}, u32[]{:S(2)}, u32[]{:S(2)}) collective-permute-start(bf16[32,2048]{1,0:T(8,128)(2,1)S(1)} %get-tuple-element.36), channel_id=1, source_target_pairs={{0,2},{2,4},{4,6},{6,32},{32,34},{34,36},{36,38},{38,0},{1,3},{3,5... | collective-permute-start | bytes 393224 | tf_op jit(solution)/shard_map/ppermute | solution.py:15
  148.8 12.0 %collective-permute-start.20 = (bf16[32,2048]{1,0:T(8,128)(2,1)S(1)}, bf16[32,2048]{1,0:T(8,128)(2,1)S(1)}, u32[]{:S(2)}, u32[]{:S(2)}) collective-permute-start(bf16[32,2048]{1,0:T(8,128)(2,1)S(1)} %get-tuple-element.38), channel_id=1, source_target_pairs={{0,38},{2,0},{4,2},{6,4},{32,6},{34,32},{36,34},{38,36},{1,39},{3,... | collective-permute-start | bytes 393224 | tf_op jit(solution)/shard_map/ppermute | solution.py:15
  151.1 16.9 %collective-permute-start.21 = (bf16[32,2048]{1,0:T(8,128)(2,1)S(1)}, bf16[32,2048]{1,0:T(8,128)(2,1)S(1)}, u32[]{:S(2)}, u32[]{:S(2)}) collective-permute-start(bf16[32,2048]{1,0:T(8,128)(2,1)S(1)} %get-tuple-element.37), channel_id=1, source_target_pairs={{0,36},{2,38},{4,0},{6,2},{32,4},{34,6},{36,32},{38,34},{1,37},{3,... | collective-permute-start | bytes 393224 | tf_op jit(solution)/shard_map/ppermute | solution.py:15
  151.3 23.7 %collective-permute-start.9 = (bf16[4,2,128,128]{3,2,1,0:T(8,128)(2,1)S(1)}, bf16[4,2,128,128]{3,2,1,0:T(8,128)(2,1)S(1)}, u32[]{:S(2)}, u32[]{:S(2)}) collective-permute-start(bf16[4,2,128,128]{3,2,1,0:T(8,128)(2,1)S(1)} %get-tuple-element.30), channel_id=1, source_target_pairs={{0,2},{2,4},{4,6},{6,0},{1,3},{3,5},{5,7},{7,1},{8,10},{10,12},{12... | collective-permute-start | bytes 786440 | tf_op jit(solution)/shard_map/ppermute | solution.py:15
  152.7 33.6 %collective-permute-start.10 = (bf16[4,2,128,128]{3,2,1,0:T(8,128)(2,1)S(1)}, bf16[4,2,128,128]{3,2,1,0:T(8,128)(2,1)S(1)}, u32[]{:S(2)}, u32[]{:S(2)}) collective-permute-start(bf16[4,2,128,128]{3,2,1,0:T(8,128)(2,1)S(1)} %get-tuple-element.29), channel_id=1, source_target_pairs={{0,4},{2,6},{4,0},{6,2},{1,5},{3,7},{5,1},{7,3},{8,12},{10,14},{12... | collective-permute-start | bytes 786440 | tf_op jit(solution)/shard_map/ppermute | solution.py:15
  154.5 31.8 %collective-permute-start.11 = (bf16[4,2,128,128]{3,2,1,0:T(8,128)(2,1)S(1)}, bf16[4,2,128,128]{3,2,1,0:T(8,128)(2,1)S(1)}, u32[]{:S(2)}, u32[]{:S(2)}) collective-permute-start(bf16[4,2,128,128]{3,2,1,0:T(8,128)(2,1)S(1)} %get-tuple-element.28), channel_id=1, source_target_pairs={{0,6},{2,0},{4,2},{6,4},{1,7},{3,1},{5,3},{7,5},{8,14},{10,8},{12,... | collective-permute-start | bytes 786440 | tf_op jit(solution)/shard_map/ppermute | solution.py:15
  168.1 10.0 %collective-permute-start.22 = (bf16[32,2048]{1,0:T(8,128)(2,1)S(1)}, bf16[32,2048]{1,0:T(8,128)(2,1)S(1)}, u32[]{:S(2)}, u32[]{:S(2)}) collective-permute-start(bf16[32,2048]{1,0:T(8,128)(2,1)S(1)} %fusion.2), channel_id=1, source_target_pairs={{0,32},{32,0},{1,33},{33,1},{2,34},{34,2},{3,35},{35,3},{4,36},{36... | collective-permute-start | bytes 393224 | tf_op jit(solution)/shard_map/ppermute | solution.py:15
  178.9 14.0 %all-to-all-start.2 = ((bf16[4,32,2048]{2,1,0:T(8,128)(2,1)}), bf16[4,32,2048]{2,1,0:T(8,128)(2,1)S(1)}, u32[]{:S(2)}, u32[]{:S(2)}) async-start(bf16[4,32,2048]{2,1,0:T(8,128)(2,1)} %broadcast_in_dim.33), calls=%async_computation.2 | async-start | bytes 1048576 | tf_op jit(solution)/shard_map/all_to_all | solution.py:19
  (3 other events, 22.9 us)
Sparse Core Ops, SparseCore 0:
  9.8 45.9 all-gather.2
  57.6 30.7 all-gather.4

commit v3 on v1

v3 whole, which is shorter than its diff:
```python
import jax
import jax.numpy as jnp
from jax import lax
from jax.experimental import pallas as pl
from jax.experimental.pallas import tpu as pltpu
from jax.sharding import Mesh, PartitionSpec as P

CHUNKS = (5, 3)
RING8 = ("h", "l")
F32, BF16 = jnp.float32, jnp.bfloat16


def shift(v, axis, by):
    n = lax.axis_size(axis)
    return lax.ppermute(v, axis, [(i, (i + by) % n) for i in range(n)])


def exchange(v, axis):
    return lax.all_to_all(v, axis, split_axis=0, concat_axis=0, tiled=True)


def after(v, *others):
    return lax.optimization_barrier((v, *others))[0]


def pick(v, index):
    return lax.dynamic_index_in_dim(v, index, 0, keepdims=False)


def partial_kernel(at, acts, *refs):
    pieces, out, lhs = refs[:10], refs[10], refs[11]
    y, c = at[1], at[3]

    @pl.when(pl.program_id(0) == 0)
    def _():
        toks = acts.shape[3]
        for e in range(2):
            for d in range(4):
                k = 4 * e + d
                lhs[:, k * toks:(k + 1) * toks] = acts[(y + d) & 3, (c + e) & 1]

    rhs = jnp.concatenate([p[...] for p in pieces], axis=0)
    total = jnp.dot(lhs[...], rhs, preferred_element_type=F32).astype(out.dtype)
    parts, blocks, rows, _ = out.shape
    for b in range(blocks):
        for q in range(parts):
            r = (b * parts + q) * rows
            out[q, b] = total[r:r + rows]


def partial(at, acts, pieces, lo, hi):
    y, _, heads, toks = acts.shape
    wide = pieces[0].shape[1] // 8
    rows = heads // 16
    return pl.pallas_call(
        partial_kernel,
        grid_spec=pltpu.PrefetchScalarGridSpec(
            num_scalar_prefetch=1,
            grid=((hi - lo) // wide,),
            in_specs=[pl.BlockSpec(acts.shape, lambda i, at: (0, 0, 0, 0))]
            + [pl.BlockSpec((p.shape[0], wide), lambda i, at: (0, i + lo // wide)) for p in pieces],
            out_specs=pl.BlockSpec((4, 4, rows, wide), lambda i, at: (0, 0, 0, i)),
            scratch_shapes=[pltpu.VMEM((heads, 8 * toks), BF16)],
        ),
        out_shape=jax.ShapeDtypeStruct((4, 4, rows, hi - lo), BF16),
        cost_estimate=pl.CostEstimate(
            flops=2 * heads * 8 * toks * (hi - lo), transcendentals=0,
            bytes_accessed=16 * toks * (hi - lo) + 2 * heads * (hi - lo) + 2 * acts.size),
        name="partial_grad_w",
    )(at, acts, *pieces)


def inputs_kernel(at, *refs):
    pieces, weights, out, acc = refs[:10], refs[10:14], refs[14], refs[15]
    y, l, c = at[1], at[2], at[3]
    k = pl.program_id(0)
    lhs = jnp.concatenate([p[...] for p in pieces], axis=0)
    rhs = jnp.concatenate([w[...] for w in weights], axis=0)
    prod = lax.dot_general(lhs, rhs, (((1,), (1,)), ((), ())), preferred_element_type=F32)

    @pl.when(k == 0)
    def _():
        acc[...] = prod

    @pl.when(k > 0)
    def _():
        acc[...] += prod

    @pl.when(k == pl.num_programs(0) - 1)
    def _():
        toks, heads = out.shape[3:]
        for e in range(2):
            for d in range(4):
                t = (4 * e + d) * toks
                for r in range(4):
                    out[(l + r) & 3, (y + d) & 3, (c + e) & 1] = acc[
                        t:t + toks, r * heads:(r + 1) * heads].astype(out.dtype)


def inputs_grad(at, pieces, weights):
    heads, feats = weights[0].shape
    toks = pieces[0].shape[0]
    deep = feats // 4
    return pl.pallas_call(
        inputs_kernel,
        grid_spec=pltpu.PrefetchScalarGridSpec(
            num_scalar_prefetch=1,
            grid=(4,),
            in_specs=[pl.BlockSpec((p.shape[0], deep), lambda k, at: (0, k)) for p in (*pieces, *weights)],
            out_specs=pl.BlockSpec((4, 4, 2, toks, heads), lambda k, at: (0, 0, 0, 0, 0)),
            scratch_shapes=[pltpu.VMEM((8 * toks, 4 * heads), F32)],
        ),
        out_shape=jax.ShapeDtypeStruct((4, 4, 2, toks, heads), BF16),
        cost_estimate=pl.CostEstimate(
            flops=2 * 8 * toks * feats * 4 * heads, transcendentals=0,
            bytes_accessed=2 * (8 * toks * feats + 4 * heads * feats + 32 * toks * heads)),
        name="grad_attn",
    )(at, *pieces, *weights)


def local(grad_out, attn, w_out):
    g = grad_out[0]
    a = attn[0]
    toks, feats = g.shape
    heads = w_out.shape[0]
    at = jnp.stack([lax.axis_index(n) for n in ("x", "y", "l", "c")]).astype(jnp.int32)
    l = at[2]

    cuts, lo = [], 0
    for size in CHUNKS:
        size = size * feats // sum(CHUNKS)
        cuts.append((lo, lo + size))
        lo += size

    a = a.reshape(toks, 4, 4, 2, heads).transpose(1, 3, 2, 4, 0).reshape(8, 4 * heads, toks)
    acts = exchange(a, ("y", "c")).reshape(4, 2, 4 * heads, toks)

    w_above, w_below = shift(w_out, RING8, -1), shift(w_out, RING8, 1)
    w_far = shift(w_below, RING8, 1)
    weights = [w_out, w_above, w_far, w_below]

    half = toks // 2
    above, below = shift(g, "y", -1), shift(g, "y", 1)
    pieces = [g, above, shift(after(above[:half], acts), "y", -1), shift(after(below[half:], acts), "y", 1), below]
    pieces += [shift(p, "c", 1) for p in pieces]

    x = at[0]
    first = [after(g, *weights[1:])] + pieces[1:]
    tots = []
    for lo, hi in cuts:
        part = partial(at, acts, first, lo, hi)
        first = [after(g, part)] + pieces[1:]
        tots.append(exchange(part, "x").astype(F32).sum(0).astype(BF16))

    res = inputs_grad(at, first, weights)
    back = [pick(res, l)] + [shift(pick(res, (l + d) & 3), "l", d) for d in (1, 2, 3)]

    grad_w = jnp.zeros((4, heads // 4, feats), BF16)
    for j, ((lo, hi), tot) in enumerate(zip(cuts, tots)):
        acc = pick(tot, l).astype(F32)
        for d in (1, -1, -2 if j % 2 else 2):
            acc = acc + shift(pick(tot, (l + d) & 3), RING8, d).astype(F32)
        acc = acc.astype(BF16)
        acc = (acc.astype(F32) + shift(acc, "h", 1).astype(F32)).astype(BF16)
        for d in range(4):
            grad_w = lax.dynamic_update_slice(
                grad_w, (shift(acc, "x", d) if d else acc)[None], ((x - d) & 3, 0, lo))
    grad_w = grad_w.reshape(heads, feats)

    out = jnp.zeros((4, 4, 2, toks, heads), BF16)
    for d, piece in enumerate(back):
        out = lax.dynamic_update_slice_in_dim(out, piece[:, None], (l - d) & 3, 1)
    out = out.reshape(1, 4 * 8 * toks, heads)
    return out, grad_w


def solution(mesh):
    fine = Mesh(mesh.devices.reshape(4, 2, 4, 4, 2), ("x", "h", "y", "l", "c"))
    dp, context = ("x", "h"), ("y", "l", "c")
    in_specs = (P(dp, context, None), P(dp, context, None), P(context, None))
    out_specs = (P(dp, None, context), P(context, None))
    return jax.shard_map(local, mesh=fine, in_specs=in_specs, out_specs=out_specs, check_vma=False)
```

time: 267 us -> 198 us (0.74); the launches traced: 263 us -> 197 us
  waiting for transfers between devices: 129 us -> 98.8 us
  Pallas kernels: 0 us -> 25.3 us
  local copies, waits for them, and re-layouts: 36.6 us -> 14.9 us
  matrix products: 20.5 us -> 0 us
  between operations: 14.2 us -> 0.86 us
  other arithmetic: 13.3 us -> 2.97 us
  starting transfers between devices: 49.3 us -> 54.3 us
    ppermute x6 -> x29, waiting for transfers between devices: 14.2 us -> 75.3 us  [shift(): return lax.ppermute(v, axis, [(i, (i + by) % n) for i in range(n)])]
    all_to_all x8 -> x3, waiting for transfers between devices: 82.5 us -> 23.5 us  [exchange(): return lax.all_to_all(v, axis, split_axis=0, concat_axis=0, tiled=True)]
    all_gather x2 -> x0, waiting for transfers between devices: 31.9 us -> none  [local(): lax.all_gather(g[:, lo:hi], ('y', 'c'), axis=0, tiled=True)]
    ppermute x6 -> x29, starting transfers between devices: 13.1 us -> 42.1 us  [shift(): return lax.ppermute(v, axis, [(i, (i + by) % n) for i in range(n)])]
    pallas_call x0 -> x3, Pallas kernels: none -> 25.3 us  [the longest x2 15.3 us: partial(): pl.pallas_call(partial_kernel, grid_spec=pltpu.PrefetchScalarGridSpec(num...]
    all_to_all x8 -> x3, starting transfers between devices: 36.1 us -> 12.2 us  [exchange(): return lax.all_to_all(v, axis, split_axis=0, concat_axis=0, tiled=True)]
    dot_general x3 -> x0, matrix products: 20.5 us -> none  [the longest x2 10.5 us: local(): lax.dot_general(acts, gj, (((0,), (0,)), ((), ())), preferred_element_typ...]
    unnamed x14 -> x8, local copies, waits for them, and re-layouts: 18.8 us -> 0.98 us
  transfers between devices with their start and end apart: 16 -> 32, of which waited for: 9 -> 18; matrix products, arithmetic and copies ran while one was open for 25% -> 9% of each run, Pallas kernels for 0% -> 8%
where the time goes in v3:
time: 198 us; the launch traced here: 197 us
  waiting for transfers between devices  98.8 us (50%)
  starting transfers between devices  54.3 us (27%)
  Pallas kernels  25.3 us (13%)
  local copies, waits for them, and re-layouts  14.9 us (8%)
  other arithmetic  2.97 us (2%)
    ppermute x29, waiting for transfers between devices, shift(): return lax.ppermute(v, axis, [(i, (i + by) % n) for i in range(n)])  75.3 us
    ppermute x29, starting transfers between devices, shift(): return lax.ppermute(v, axis, [(i, (i + by) % n) for i in range(n)])  42.1 us
    all_to_all x3, waiting for transfers between devices, exchange(): return lax.all_to_all(v, axis, split_axis=0, concat_axis=0, tiled=True)  23.5 us
    pallas_call x2, Pallas kernels, partial(): pl.pallas_call(partial_kernel, grid_spec=pltpu.PrefetchScalarGridSpec(num...  15.3 us
    all_to_all x3, starting transfers between devices, exchange(): return lax.all_to_all(v, axis, split_axis=0, concat_axis=0, tiled=True)  12.2 us
    pallas_call x1, Pallas kernels, inputs_grad(): pl.pallas_call(inputs_kernel, grid_spec=pltpu.PrefetchScalarGridSpec(num_...  9.97 us
    dynamic_update_slice x4, local copies, waits for them, and re-layouts, local(): out = lax.dynamic_update_slice_in_dim(out, piece[:, None], l - d & 3, 1)  5.85 us
  transfers between devices with their start and end apart: 32, of which 18 were waited for; matrix products, arithmetic and copies ran while one was open for 9% of the time, Pallas kernels for 8%

profile of v3, /device:TPU:64, one launch (start us, length us, event | category | flops | bytes accessed | tf_op | source)
XLA Modules:
  0.0 197.1 jit_solution(9141302261394633992)
XLA Ops:
  0.6 3.1 %collective-permute-start.3 = (bf16[128,4096]{1,0:T(8,128)(2,1)}, bf16[128,4096]{1,0:T(8,128)(2,1)S(1)}, u32[]{:S(2)}, u32[]{:S(2)}) collective-permute-start(bf16[128,4096]{1,0:T(8,128)(2,1)} %bitcast.61), channel_id=1, source_target_pairs={{0,24},{8,0},{16,8},{24,16},{1,25},{9,1},{17,9},{25,17},{2,26},{10... | collective-permute-start | bytes 3145736 | tf_op jit(solution)/shard_map/ppermute | solution.py:15
  3.7 1.9 collective-permute-start.1
  7.4 2.1 %copy.5 = bf16[4,2,4,128,128]{4,3,2,1,0:T(8,128)(2,1)} copy(bf16[4,2,4,128,128]{3,1,2,0,4:T(2,128)(2,1)S(1)} %bitcast.60) | data formatting | bytes 2097152 | tf_op jit(solution)/shard_map/transpose | solution.py:135
  9.5 3.6 %all-to-all-start = ((bf16[8,512,128]{2,1,0:T(8,128)(2,1)}), bf16[8,512,128]{2,1,0:T(8,128)(2,1)S(1)}, u32[]{:S(2)}, u32[]{:S(2)}) async-start(bf16[8,512,128]{2,1,0:T(8,128)(2,1)} %bitcast.6), calls=%async_computation | async-start | bytes 2097152 | tf_op jit(solution)/shard_map/all_to_all | solution.py:19
  13.1 1.9 collective-permute-start.5
  15.1 13.9 %collective-permute-done.3.refs_1_ = bf16[128,4096]{1,0:T(8,128)(2,1)S(1)} collective-permute-done((bf16[128,4096]{1,0:T(8,128)(2,1)}, bf16[128,4096]{1,0:T(8,128)(2,1)S(1)}, u32[]{:S(2)}, u32[]{:S(2)}) %collective-permute-start.3) | collective-permute-done | bytes 1048608 | tf_op jit(solution)/shard_map/ppermute | solution.py:15
  29.9 7.8 %all-to-all-done = bf16[8,512,128]{2,1,0:T(8,128)(2,1)S(1)} async-done(((bf16[8,512,128]{2,1,0:T(8,128)(2,1)}), bf16[8,512,128]{2,1,0:T(8,128)(2,1)S(1)}, u32[]{:S(2)}, u32[]{:S(2)}) %all-to-all-start) | async-done | bytes 1048608 | tf_op jit(solution)/shard_map/all_to_all | solution.py:19
  37.7 1.9 collective-permute-start.2
  39.6 3.6 %collective-permute-start.4 = (bf16[64,4096]{1,0:T(8,128)(2,1)}, bf16[64,4096]{1,0:T(8,128)(2,1)}, u32[]{:S(2)}, u32[]{:S(2)}) collective-permute-start(bf16[64,4096]{1,0:T(8,128)(2,1)} %slice.8), channel_id=1, source_target_pairs={{0,24},{8,0},{16,8},{24,16},{1,25},{9,1},{17,9},{25,17},{2,26},{10... | collective-permute-start | bytes 1572872 | tf_op jit(solution)/shard_map/ppermute | solution.py:15
  43.2 8.0 %collective-permute-done.5.refs_4_ = bf16[128,4096]{1,0:T(8,128)(2,1)S(1)} collective-permute-done((bf16[128,4096]{1,0:T(8,128)(2,1)}, bf16[128,4096]{1,0:T(8,128)(2,1)S(1)}, u32[]{:S(2)}, u32[]{:S(2)}) %collective-permute-start.5) | collective-permute-done | bytes 1048608 | tf_op jit(solution)/shard_map/ppermute | solution.py:15
  52.8 13.5 %collective-permute-done.6.refs_3_ = bf16[64,4096]{1,0:T(8,128)(2,1)} collective-permute-done((bf16[64,4096]{1,0:T(8,128)(2,1)S(1)}, bf16[64,4096]{1,0:T(8,128)(2,1)}, u32[]{:S(2)}, u32[]{:S(2)}) %collective-permute-start.6) | collective-permute-done | bytes 524320 | tf_op jit(solution)/shard_map/ppermute | solution.py:15
  69.3 8.7 %partial_grad_w.2 = bf16[4,4,32,2560]{3,2,1,0:T(8,128)(2,1)} custom-call(s32[4]{0:T(128)} %pad_add_fusion.at, bf16[4,2,512,128]{3,2,1,0:T(8,128)(2,1)} %bitcast.58, bf16[128,4096]{1,0:T(8,128)(2,1)} %bitcast.64, bf16[128,4096]{1,0:T(8,128)(2,1)} %copy-done.1, bf16[64,4096]{1,0:T(8,128)(2,1)} %collective-permute-done.4.refs_2_, ...), custom_call_target="tpu_custom_call" | custom-call | flops 2684354560 | bytes 8912896 | tf_op jit(solution)/shard_map/partial_grad_w/pallas_call | solution.py:55
  78.0 4.3 %all-to-all-start.1 = ((bf16[4,4,32,2560]{3,2,1,0:T(8,128)(2,1)}), bf16[4,4,32,2560]{3,2,1,0:T(8,128)(2,1)S(1)}, u32[]{:S(2)}, u32[]{:S(2)}) async-start(bf16[4,4,32,2560]{3,2,1,0:T(8,128)(2,1)} %partial_grad_w.2), calls=%async_computation.1 | async-start | bytes 5242880 | tf_op jit(solution)/shard_map/all_to_all | solution.py:19
  82.3 6.6 %partial_grad_w.3 = bf16[4,4,32,1536]{3,2,1,0:T(8,128)(2,1)} custom-call(s32[4]{0:T(128)} %pad_add_fusion.at, bf16[4,2,512,128]{3,2,1,0:T(8,128)(2,1)} %bitcast.59, bf16[128,4096]{1,0:T(8,128)(2,1)} %bitcast.65, bf16[128,4096]{1,0:T(8,128)(2,1)} %copy-done.1, bf16[64,4096]{1,0:T(8,128)(2,1)} %collective-permute-done.4.refs_2_, ...), custom_call_target="tpu_custom_call" | custom-call | flops 1610612736 | bytes 5767168 | tf_op jit(solution)/shard_map/partial_grad_w/pallas_call | solution.py:55
  88.8 10.0 %grad_attn.1 = bf16[4,4,2,128,128]{4,3,2,1,0:T(8,128)(2,1)} custom-call(s32[4]{0:T(128)} %pad_add_fusion.at, bf16[128,4096]{1,0:T(8,128)(2,1)} %bitcast.66, bf16[128,4096]{1,0:T(8,128)(2,1)} %copy-done.1, bf16[64,4096]{1,0:T(8,128)(2,1)} %collective-permute-done.4.refs_2_, bf16[64,4096]{1,0:T(8,128)(2,1)} %collective-permute-done.6.refs_3_, ...), custom_call_target="tpu_custom_call" | custom-call | flops 4294967296 | bytes 13631488 | tf_op jit(solution)/shard_map/grad_attn/pallas_call | solution.py:104
  98.8 15.7 %all-to-all-done.1 = bf16[4,4,32,2560]{3,2,1,0:T(8,128)(2,1)S(1)} async-done(((bf16[4,4,32,2560]{3,2,1,0:T(8,128)(2,1)}), bf16[4,4,32,2560]{3,2,1,0:T(8,128)(2,1)S(1)}, u32[]{:S(2)}, u32[]{:S(2)}) %all-to-all-start.1) | async-done | bytes 2621472 | tf_op jit(solution)/shard_map/all_to_all | solution.py:19
  114.5 4.4 %all-to-all-start.2 = ((bf16[4,4,32,1536]{3,2,1,0:T(8,128)(2,1)}), bf16[4,4,32,1536]{3,2,1,0:T(8,128)(2,1)}, u32[]{:S(2)}, u32[]{:S(2)}) async-start(bf16[4,4,32,1536]{3,2,1,0:T(8,128)(2,1)} %partial_grad_w.3), calls=%async_computation.2 | async-start | bytes 3145728 | tf_op jit(solution)/shard_map/all_to_all | solution.py:19
  120.8 3.1 %collective-permute-start.12 = (bf16[4,2,128,128]{3,2,1,0:T(8,128)(2,1)S(1)}, bf16[4,2,128,128]{3,2,1,0:T(8,128)(2,1)S(1)}, u32[]{:S(2)}, u32[]{:S(2)}) collective-permute-start(bf16[4,2,128,128]{3,2,1,0:T(8,128)(2,1)S(1)} %get-tuple-element.18), channel_id=1, source_target_pairs={{0,2},{2,4},{4,6},{6,0},{1,3},{3,5},{5,7},{7,1},{8,10},{10,12},{12... | collective-permute-start | bytes 786440 | tf_op jit(solution)/shard_map/ppermute | solution.py:15
  128.3 14.8 %collective-permute-done.12 = bf16[4,2,128,128]{3,2,1,0:T(8,128)(2,1)S(1)} collective-permute-done((bf16[4,2,128,128]{3,2,1,0:T(8,128)(2,1)S(1)}, bf16[4,2,128,128]{3,2,1,0:T(8,128)(2,1)S(1)}, u32[]{:S(2)}, u32[]{:S(2)}) %collective-permute-start.12) | collective-permute-done | bytes 262176 | tf_op jit(solution)/shard_map/ppermute | solution.py:15
  144.5 2.0 %collective-permute-start.15 = (bf16[32,2560]{1,0:T(8,128)(2,1)S(1)}, bf16[32,2560]{1,0:T(8,128)(2,1)S(1)}, u32[]{:S(2)}, u32[]{:S(2)}) collective-permute-start(bf16[32,2560]{1,0:T(8,128)(2,1)S(1)} %get-tuple-element.19), channel_id=1, source_target_pairs={{0,2},{2,4},{4,6},{6,32},{32,34},{34,36},{36,38},{38,0},{1,3},{3,5... | collective-permute-start | bytes 491528 | tf_op jit(solution)/shard_map/ppermute | solution.py:15
  149.9 2.6 %collective-permute-done.17 = bf16[32,2560]{1,0:T(8,128)(2,1)S(1)} collective-permute-done((bf16[32,2560]{1,0:T(8,128)(2,1)S(1)}, bf16[32,2560]{1,0:T(8,128)(2,1)S(1)}, u32[]{:S(2)}, u32[]{:S(2)}) %collective-permute-start.17) | collective-permute-done | bytes 163872 | tf_op jit(solution)/shard_map/ppermute | solution.py:15
  152.5 4.7 %collective-permute-done.15 = bf16[32,2560]{1,0:T(8,128)(2,1)S(1)} collective-permute-done((bf16[32,2560]{1,0:T(8,128)(2,1)S(1)}, bf16[32,2560]{1,0:T(8,128)(2,1)S(1)}, u32[]{:S(2)}, u32[]{:S(2)}) %collective-permute-start.15) | collective-permute-done | bytes 163872 | tf_op jit(solution)/shard_map/ppermute | solution.py:15
  157.3 4.5 %collective-permute-start.18 = (bf16[32,2560]{1,0:T(8,128)(2,1)S(1)}, bf16[32,2560]{1,0:T(8,128)(2,1)S(1)}, u32[]{:S(2)}, u32[]{:S(2)}) collective-permute-start(bf16[32,2560]{1,0:T(8,128)(2,1)S(1)} %fusion.2), channel_id=1, source_target_pairs={{0,32},{32,0},{1,33},{33,1},{2,34},{34,2},{3,35},{35,3},{4,36},{36... | collective-permute-start | bytes 491528 | tf_op jit(solution)/shard_map/ppermute | solution.py:15
  162.0 2.0 %collective-permute-start.22 = (bf16[32,1536]{1,0:T(8,128)(2,1)S(1)}, bf16[32,1536]{1,0:T(8,128)(2,1)S(1)}, u32[]{:S(2)}, u32[]{:S(2)}) collective-permute-start(bf16[32,1536]{1,0:T(8,128)(2,1)S(1)} %get-tuple-element.22), channel_id=1, source_target_pairs={{0,2},{2,4},{4,6},{6,32},{32,34},{34,36},{36,38},{38,0},{1,3},{3,5... | collective-permute-start | bytes 294920 | tf_op jit(solution)/shard_map/ppermute | solution.py:15
  164.0 2.8 %collective-permute-done.18 = bf16[32,2560]{1,0:T(8,128)(2,1)S(1)} collective-permute-done((bf16[32,2560]{1,0:T(8,128)(2,1)S(1)}, bf16[32,2560]{1,0:T(8,128)(2,1)S(1)}, u32[]{:S(2)}, u32[]{:S(2)}) %collective-permute-start.18) | collective-permute-done | bytes 163872 | tf_op jit(solution)/shard_map/ppermute | solution.py:15
  167.0 2.2 %collective-permute-start.19 = (bf16[32,2560]{1,0:T(8,128)(2,1)S(1)}, bf16[32,2560]{1,0:T(8,128)(2,1)S(1)}, u32[]{:S(2)}, u32[]{:S(2)}) collective-permute-start(bf16[32,2560]{1,0:T(8,128)(2,1)S(1)} %get-tuple-element.15), channel_id=1, source_target_pairs={{0,64},{64,128},{128,192},{192,0},{1,65},{65,129},{129,193},{193,1... | collective-permute-start | bytes 491528 | tf_op jit(solution)/shard_map/ppermute | solution.py:15
  171.1 4.2 %collective-permute-start.25 = (bf16[32,1536]{1,0:T(8,128)(2,1)S(1)}, bf16[32,1536]{1,0:T(8,128)(2,1)S(1)}, u32[]{:S(2)}, u32[]{:S(2)}) collective-permute-start(bf16[32,1536]{1,0:T(8,128)(2,1)S(1)} %fusion.5), channel_id=1, source_target_pairs={{0,32},{32,0},{1,33},{33,1},{2,34},{34,2},{3,35},{35,3},{4,36},{36... | collective-permute-start | bytes 294920 | tf_op jit(solution)/shard_map/ppermute | solution.py:15
  175.3 2.9 %collective-permute-start.20 = (bf16[32,2560]{1,0:T(8,128)(2,1)S(1)}, bf16[32,2560]{1,0:T(8,128)(2,1)S(1)}, u32[]{:S(2)}, u32[]{:S(2)}) collective-permute-start(bf16[32,2560]{1,0:T(8,128)(2,1)S(1)} %get-tuple-element.15), channel_id=1, source_target_pairs={{0,128},{64,192},{128,0},{192,64},{1,129},{65,193},{129,1},{193,65... | collective-permute-start | bytes 491528 | tf_op jit(solution)/shard_map/ppermute | solution.py:15
  179.4 3.8 %collective-permute-done.20 = bf16[32,2560]{1,0:T(8,128)(2,1)S(1)} collective-permute-done((bf16[32,2560]{1,0:T(8,128)(2,1)S(1)}, bf16[32,2560]{1,0:T(8,128)(2,1)S(1)}, u32[]{:S(2)}, u32[]{:S(2)}) %collective-permute-start.20) | collective-permute-done | bytes 163872 | tf_op jit(solution)/shard_map/ppermute | solution.py:15
  185.2 2.3 %collective-permute-start.26 = (bf16[32,1536]{1,0:T(8,128)(2,1)S(1)}, bf16[32,1536]{1,0:T(8,128)(2,1)S(1)}, u32[]{:S(2)}, u32[]{:S(2)}) collective-permute-start(bf16[32,1536]{1,0:T(8,128)(2,1)S(1)} %get-tuple-element.13), channel_id=1, source_target_pairs={{0,64},{64,128},{128,192},{192,0},{1,65},{65,129},{129,193},{193,1... | collective-permute-start | bytes 294920 | tf_op jit(solution)/shard_map/ppermute | solution.py:15
  189.2 2.3 %collective-permute-start.27 = (bf16[32,1536]{1,0:T(8,128)(2,1)S(1)}, bf16[32,1536]{1,0:T(8,128)(2,1)S(1)}, u32[]{:S(2)}, u32[]{:S(2)}) collective-permute-start(bf16[32,1536]{1,0:T(8,128)(2,1)S(1)} %get-tuple-element.13), channel_id=1, source_target_pairs={{0,128},{64,192},{128,0},{192,64},{1,129},{65,193},{129,1},{193,65... | collective-permute-start | bytes 294920 | tf_op jit(solution)/shard_map/ppermute | solution.py:15
  191.9 3.4 %collective-permute-done.27 = bf16[32,1536]{1,0:T(8,128)(2,1)S(1)} collective-permute-done((bf16[32,1536]{1,0:T(8,128)(2,1)S(1)}, bf16[32,1536]{1,0:T(8,128)(2,1)S(1)}, u32[]{:S(2)}, u32[]{:S(2)}) %collective-permute-start.27) | collective-permute-done | bytes 98336 | tf_op jit(solution)/shard_map/ppermute | solution.py:15
  (69 shorter events, 27.8 us)
Async XLA Ops:
  0.6 28.4 %collective-permute-start.3 = (bf16[128,4096]{1,0:T(8,128)(2,1)}, bf16[128,4096]{1,0:T(8,128)(2,1)S(1)}, u32[]{:S(2)}, u32[]{:S(2)}) collective-permute-start(bf16[128,4096]{1,0:T(8,128)(2,1)} %bitcast.61), channel_id=1, source_target_pairs={{0,24},{8,0},{16,8},{24,16},{1,25},{9,1},{17,9},{25,17},{2,26},{10... | collective-permute-start | bytes 3145736 | tf_op jit(solution)/shard_map/ppermute | solution.py:15
  3.7 34.0 %collective-permute-start.1 = (bf16[128,4096]{1,0:T(8,128)(2,1)}, bf16[128,4096]{1,0:T(8,128)(2,1)}, u32[]{:S(2)}, u32[]{:S(2)}) collective-permute-start(bf16[128,4096]{1,0:T(8,128)(2,1)} %refs_10_.1), channel_id=1, source_target_pairs={{0,2},{2,4},{4,6},{6,32},{32,34},{34,36},{36,38},{38,0},{1,3},{3,5... | collective-permute-start | bytes 3145736 | tf_op jit(solution)/shard_map/ppermute | solution.py:15
  9.5 28.2 %all-to-all-start = ((bf16[8,512,128]{2,1,0:T(8,128)(2,1)}), bf16[8,512,128]{2,1,0:T(8,128)(2,1)S(1)}, u32[]{:S(2)}, u32[]{:S(2)}) async-start(bf16[8,512,128]{2,1,0:T(8,128)(2,1)} %bitcast.6), calls=%async_computation | async-start | bytes 2097152 | tf_op jit(solution)/shard_map/all_to_all | solution.py:19
  13.1 38.1 %collective-permute-start.5 = (bf16[128,4096]{1,0:T(8,128)(2,1)}, bf16[128,4096]{1,0:T(8,128)(2,1)S(1)}, u32[]{:S(2)}, u32[]{:S(2)}) collective-permute-start(bf16[128,4096]{1,0:T(8,128)(2,1)} %bitcast.62), channel_id=1, source_target_pairs={{0,8},{8,16},{16,24},{24,0},{1,9},{9,17},{17,25},{25,1},{2,10},{10... | collective-permute-start | bytes 3145736 | tf_op jit(solution)/shard_map/ppermute | solution.py:15
  15.0 36.3 %collective-permute-start = (bf16[128,4096]{1,0:T(8,128)(2,1)}, bf16[128,4096]{1,0:T(8,128)(2,1)}, u32[]{:S(2)}, u32[]{:S(2)}) collective-permute-start(bf16[128,4096]{1,0:T(8,128)(2,1)} %refs_10_.1), channel_id=1, source_target_pairs={{0,38},{2,0},{4,2},{6,4},{32,6},{34,32},{36,34},{38,36},{1,39},{3,... | collective-permute-start | bytes 3145736 | tf_op jit(solution)/shard_map/ppermute | solution.py:15
  37.7 28.5 %collective-permute-start.2 = (bf16[128,4096]{1,0:T(8,128)(2,1)}, bf16[128,4096]{1,0:T(8,128)(2,1)}, u32[]{:S(2)}, u32[]{:S(2)}) collective-permute-start(bf16[128,4096]{1,0:T(8,128)(2,1)} %collective-permute-done.1.refs_13_), channel_id=1, source_target_pairs={{0,2},{2,4},{4,6},{6,32},{32,34},{34,36},{36,38},{38,0},{1,3},{3,5... | collective-permute-start | bytes 3145736 | tf_op jit(solution)/shard_map/ppermute | solution.py:15
  39.6 13.1 %collective-permute-start.4 = (bf16[64,4096]{1,0:T(8,128)(2,1)}, bf16[64,4096]{1,0:T(8,128)(2,1)}, u32[]{:S(2)}, u32[]{:S(2)}) collective-permute-start(bf16[64,4096]{1,0:T(8,128)(2,1)} %slice.8), channel_id=1, source_target_pairs={{0,24},{8,0},{16,8},{24,16},{1,25},{9,1},{17,9},{25,17},{2,26},{10... | collective-permute-start | bytes 1572872 | tf_op jit(solution)/shard_map/ppermute | solution.py:15
  43.2 24.2 %collective-permute-start.7 = (bf16[128,4096]{1,0:T(8,128)(2,1)}, bf16[128,4096]{1,0:T(8,128)(2,1)}, u32[]{:S(2)}, u32[]{:S(2)}) collective-permute-start(bf16[128,4096]{1,0:T(8,128)(2,1)} %bitcast.63), channel_id=1, source_target_pairs={{0,1},{1,0},{2,3},{3,2},{4,5},{5,4},{6,7},{7,6},{8,9},{9,8},{10,11... | collective-permute-start | bytes 3145736 | tf_op jit(solution)/shard_map/ppermute | solution.py:15
  51.2 15.0 %collective-permute-start.6 = (bf16[64,4096]{1,0:T(8,128)(2,1)S(1)}, bf16[64,4096]{1,0:T(8,128)(2,1)}, u32[]{:S(2)}, u32[]{:S(2)}) collective-permute-start(bf16[64,4096]{1,0:T(8,128)(2,1)S(1)} %slice.9), channel_id=1, source_target_pairs={{0,8},{8,16},{16,24},{24,0},{1,9},{9,17},{17,25},{25,1},{2,10},{10... | collective-permute-start | bytes 1572872 | tf_op jit(solution)/shard_map/ppermute | solution.py:15
  51.3 16.1 %collective-permute-start.8 = (bf16[128,4096]{1,0:T(8,128)(2,1)S(1)}, bf16[128,4096]{1,0:T(8,128)(2,1)}, u32[]{:S(2)}, u32[]{:S(2)}) collective-permute-start(bf16[128,4096]{1,0:T(8,128)(2,1)S(1)} %collective-permute-done.3.refs_1_), channel_id=1, source_target_pairs={{0,1},{1,0},{2,3},{3,2},{4,5},{5,4},{6,7},{7,6},{8,9},{9,8},{10,11... | collective-permute-start | bytes 3145736 | tf_op jit(solution)/shard_map/ppermute | solution.py:15
  52.8 16.5 %collective-permute-start.11 = (bf16[128,4096]{1,0:T(8,128)(2,1)S(1)}, bf16[128,4096]{1,0:T(8,128)(2,1)}, u32[]{:S(2)}, u32[]{:S(2)}) collective-permute-start(bf16[128,4096]{1,0:T(8,128)(2,1)S(1)} %collective-permute-done.5.refs_4_), channel_id=1, source_target_pairs={{0,1},{1,0},{2,3},{3,2},{4,5},{5,4},{6,7},{7,6},{8,9},{9,8},{10,11... | collective-permute-start | bytes 3145736 | tf_op jit(solution)/shard_map/ppermute | solution.py:15
  66.2 2.3 %collective-permute-start.9 = (bf16[64,4096]{1,0:T(8,128)(2,1)}, bf16[64,4096]{1,0:T(8,128)(2,1)}, u32[]{:S(2)}, u32[]{:S(2)}) collective-permute-start(bf16[64,4096]{1,0:T(8,128)(2,1)} %collective-permute-done.4.refs_2_), channel_id=1, source_target_pairs={{0,1},{1,0},{2,3},{3,2},{4,5},{5,4},{6,7},{7,6},{8,9},{9,8},{10,11... | collective-permute-start | bytes 1572872 | tf_op jit(solution)/shard_map/ppermute | solution.py:15
  66.2 3.0 %collective-permute-start.10 = (bf16[64,4096]{1,0:T(8,128)(2,1)}, bf16[64,4096]{1,0:T(8,128)(2,1)}, u32[]{:S(2)}, u32[]{:S(2)}) collective-permute-start(bf16[64,4096]{1,0:T(8,128)(2,1)} %collective-permute-done.6.refs_3_), channel_id=1, source_target_pairs={{0,1},{1,0},{2,3},{3,2},{4,5},{5,4},{6,7},{7,6},{8,9},{9,8},{10,11... | collective-permute-start | bytes 1572872 | tf_op jit(solution)/shard_map/ppermute | solution.py:15
  78.0 36.5 %all-to-all-start.1 = ((bf16[4,4,32,2560]{3,2,1,0:T(8,128)(2,1)}), bf16[4,4,32,2560]{3,2,1,0:T(8,128)(2,1)S(1)}, u32[]{:S(2)}, u32[]{:S(2)}) async-start(bf16[4,4,32,2560]{3,2,1,0:T(8,128)(2,1)} %partial_grad_w.2), calls=%async_computation.1 | async-start | bytes 5242880 | tf_op jit(solution)/shard_map/all_to_all | solution.py:19
  114.5 33.7 %all-to-all-start.2 = ((bf16[4,4,32,1536]{3,2,1,0:T(8,128)(2,1)}), bf16[4,4,32,1536]{3,2,1,0:T(8,128)(2,1)}, u32[]{:S(2)}, u32[]{:S(2)}) async-start(bf16[4,4,32,1536]{3,2,1,0:T(8,128)(2,1)} %partial_grad_w.3), calls=%async_computation.2 | async-start | bytes 3145728 | tf_op jit(solution)/shard_map/all_to_all | solution.py:19
  120.8 22.3 %collective-permute-start.12 = (bf16[4,2,128,128]{3,2,1,0:T(8,128)(2,1)S(1)}, bf16[4,2,128,128]{3,2,1,0:T(8,128)(2,1)S(1)}, u32[]{:S(2)}, u32[]{:S(2)}) collective-permute-start(bf16[4,2,128,128]{3,2,1,0:T(8,128)(2,1)S(1)} %get-tuple-element.18), channel_id=1, source_target_pairs={{0,2},{2,4},{4,6},{6,0},{1,3},{3,5},{5,7},{7,1},{8,10},{10,12},{12... | collective-permute-start | bytes 786440 | tf_op jit(solution)/shard_map/ppermute | solution.py:15
  123.9 22.6 %collective-permute-start.13 = (bf16[4,2,128,128]{3,2,1,0:T(8,128)(2,1)}, bf16[4,2,128,128]{3,2,1,0:T(8,128)(2,1)}, u32[]{:S(2)}, u32[]{:S(2)}) collective-permute-start(bf16[4,2,128,128]{3,2,1,0:T(8,128)(2,1)} %get-tuple-element.17), channel_id=1, source_target_pairs={{0,4},{2,6},{4,0},{6,2},{1,5},{3,7},{5,1},{7,3},{8,12},{10,14},{12... | collective-permute-start | bytes 786440 | tf_op jit(solution)/shard_map/ppermute | solution.py:15
  123.9 63.5 %collective-permute-start.14 = (bf16[4,2,128,128]{3,2,1,0:T(8,128)(2,1)S(1)}, bf16[4,2,128,128]{3,2,1,0:T(8,128)(2,1)}, u32[]{:S(2)}, u32[]{:S(2)}) collective-permute-start(bf16[4,2,128,128]{3,2,1,0:T(8,128)(2,1)S(1)} %get-tuple-element.16), channel_id=1, source_target_pairs={{0,6},{2,0},{4,2},{6,4},{1,7},{3,1},{5,3},{7,5},{8,14},{10,8},{12,... | collective-permute-start | bytes 786440 | tf_op jit(solution)/shard_map/ppermute | solution.py:15
  144.3 8.2 %collective-permute-start.17 = (bf16[32,2560]{1,0:T(8,128)(2,1)S(1)}, bf16[32,2560]{1,0:T(8,128)(2,1)S(1)}, u32[]{:S(2)}, u32[]{:S(2)}) collective-permute-start(bf16[32,2560]{1,0:T(8,128)(2,1)S(1)} %get-tuple-element.20), channel_id=1, source_target_pairs={{0,4},{2,6},{4,32},{6,34},{32,36},{34,38},{36,0},{38,2},{1,5},{3,7... | collective-permute-start | bytes 491528 | tf_op jit(solution)/shard_map/ppermute | solution.py:15
  144.4 8.1 %collective-permute-start.16 = (bf16[32,2560]{1,0:T(8,128)(2,1)S(1)}, bf16[32,2560]{1,0:T(8,128)(2,1)S(1)}, u32[]{:S(2)}, u32[]{:S(2)}) collective-permute-start(bf16[32,2560]{1,0:T(8,128)(2,1)S(1)} %get-tuple-element.21), channel_id=1, source_target_pairs={{0,38},{2,0},{4,2},{6,4},{32,6},{34,32},{36,34},{38,36},{1,39},{3,... | collective-permute-start | bytes 491528 | tf_op jit(solution)/shard_map/ppermute | solution.py:15
  144.5 12.7 %collective-permute-start.15 = (bf16[32,2560]{1,0:T(8,128)(2,1)S(1)}, bf16[32,2560]{1,0:T(8,128)(2,1)S(1)}, u32[]{:S(2)}, u32[]{:S(2)}) collective-permute-start(bf16[32,2560]{1,0:T(8,128)(2,1)S(1)} %get-tuple-element.19), channel_id=1, source_target_pairs={{0,2},{2,4},{4,6},{6,32},{32,34},{34,36},{36,38},{38,0},{1,3},{3,5... | collective-permute-start | bytes 491528 | tf_op jit(solution)/shard_map/ppermute | solution.py:15
  157.3 9.5 %collective-permute-start.18 = (bf16[32,2560]{1,0:T(8,128)(2,1)S(1)}, bf16[32,2560]{1,0:T(8,128)(2,1)S(1)}, u32[]{:S(2)}, u32[]{:S(2)}) collective-permute-start(bf16[32,2560]{1,0:T(8,128)(2,1)S(1)} %fusion.2), channel_id=1, source_target_pairs={{0,32},{32,0},{1,33},{33,1},{2,34},{34,2},{3,35},{35,3},{4,36},{36... | collective-permute-start | bytes 491528 | tf_op jit(solution)/shard_map/ppermute | solution.py:15
  161.8 9.0 %collective-permute-start.24 = (bf16[32,1536]{1,0:T(8,128)(2,1)S(1)}, bf16[32,1536]{1,0:T(8,128)(2,1)S(1)}, u32[]{:S(2)}, u32[]{:S(2)}) collective-permute-start(bf16[32,1536]{1,0:T(8,128)(2,1)S(1)} %get-tuple-element.23), channel_id=1, source_target_pairs={{0,36},{2,38},{4,0},{6,2},{32,4},{34,6},{36,32},{38,34},{1,37},{3,... | collective-permute-start | bytes 294920 | tf_op jit(solution)/shard_map/ppermute | solution.py:15
  161.9 9.2 %collective-permute-start.23 = (bf16[32,1536]{1,0:T(8,128)(2,1)S(1)}, bf16[32,1536]{1,0:T(8,128)(2,1)S(1)}, u32[]{:S(2)}, u32[]{:S(2)}) collective-permute-start(bf16[32,1536]{1,0:T(8,128)(2,1)S(1)} %get-tuple-element.24), channel_id=1, source_target_pairs={{0,38},{2,0},{4,2},{6,4},{32,6},{34,32},{36,34},{38,36},{1,39},{3,... | collective-permute-start | bytes 294920 | tf_op jit(solution)/shard_map/ppermute | solution.py:15
  162.0 9.1 %collective-permute-start.22 = (bf16[32,1536]{1,0:T(8,128)(2,1)S(1)}, bf16[32,1536]{1,0:T(8,128)(2,1)S(1)}, u32[]{:S(2)}, u32[]{:S(2)}) collective-permute-start(bf16[32,1536]{1,0:T(8,128)(2,1)S(1)} %get-tuple-element.22), channel_id=1, source_target_pairs={{0,2},{2,4},{4,6},{6,32},{32,34},{34,36},{36,38},{38,0},{1,3},{3,5... | collective-permute-start | bytes 294920 | tf_op jit(solution)/shard_map/ppermute | solution.py:15
  167.0 12.4 %collective-permute-start.19 = (bf16[32,2560]{1,0:T(8,128)(2,1)S(1)}, bf16[32,2560]{1,0:T(8,128)(2,1)S(1)}, u32[]{:S(2)}, u32[]{:S(2)}) collective-permute-start(bf16[32,2560]{1,0:T(8,128)(2,1)S(1)} %get-tuple-element.15), channel_id=1, source_target_pairs={{0,64},{64,128},{128,192},{192,0},{1,65},{65,129},{129,193},{193,1... | collective-permute-start | bytes 491528 | tf_op jit(solution)/shard_map/ppermute | solution.py:15
  171.1 14.0 %collective-permute-start.25 = (bf16[32,1536]{1,0:T(8,128)(2,1)S(1)}, bf16[32,1536]{1,0:T(8,128)(2,1)S(1)}, u32[]{:S(2)}, u32[]{:S(2)}) collective-permute-start(bf16[32,1536]{1,0:T(8,128)(2,1)S(1)} %fusion.5), channel_id=1, source_target_pairs={{0,32},{32,0},{1,33},{33,1},{2,34},{34,2},{3,35},{35,3},{4,36},{36... | collective-permute-start | bytes 294920 | tf_op jit(solution)/shard_map/ppermute | solution.py:15
  175.3 7.9 %collective-permute-start.20 = (bf16[32,2560]{1,0:T(8,128)(2,1)S(1)}, bf16[32,2560]{1,0:T(8,128)(2,1)S(1)}, u32[]{:S(2)}, u32[]{:S(2)}) collective-permute-start(bf16[32,2560]{1,0:T(8,128)(2,1)S(1)} %get-tuple-element.15), channel_id=1, source_target_pairs={{0,128},{64,192},{128,0},{192,64},{1,129},{65,193},{129,1},{193,65... | collective-permute-start | bytes 491528 | tf_op jit(solution)/shard_map/ppermute | solution.py:15
  178.2 6.9 %collective-permute-start.21 = (bf16[32,2560]{1,0:T(8,128)(2,1)S(1)}, bf16[32,2560]{1,0:T(8,128)(2,1)S(1)}, u32[]{:S(2)}, u32[]{:S(2)}) collective-permute-start(bf16[32,2560]{1,0:T(8,128)(2,1)S(1)} %get-tuple-element.15), channel_id=1, source_target_pairs={{0,192},{64,0},{128,64},{192,128},{1,193},{65,1},{129,65},{193,129... | collective-permute-start | bytes 491528 | tf_op jit(solution)/shard_map/ppermute | solution.py:15
  185.2 6.7 %collective-permute-start.26 = (bf16[32,1536]{1,0:T(8,128)(2,1)S(1)}, bf16[32,1536]{1,0:T(8,128)(2,1)S(1)}, u32[]{:S(2)}, u32[]{:S(2)}) collective-permute-start(bf16[32,1536]{1,0:T(8,128)(2,1)S(1)} %get-tuple-element.13), channel_id=1, source_target_pairs={{0,64},{64,128},{128,192},{192,0},{1,65},{65,129},{129,193},{193,1... | collective-permute-start | bytes 294920 | tf_op jit(solution)/shard_map/ppermute | solution.py:15
  189.2 6.1 %collective-permute-start.27 = (bf16[32,1536]{1,0:T(8,128)(2,1)S(1)}, bf16[32,1536]{1,0:T(8,128)(2,1)S(1)}, u32[]{:S(2)}, u32[]{:S(2)}) collective-permute-start(bf16[32,1536]{1,0:T(8,128)(2,1)S(1)} %get-tuple-element.13), channel_id=1, source_target_pairs={{0,128},{64,192},{128,0},{192,64},{1,129},{65,193},{129,1},{193,65... | collective-permute-start | bytes 294920 | tf_op jit(solution)/shard_map/ppermute | solution.py:15
  191.5 4.6 %collective-permute-start.28 = (bf16[32,1536]{1,0:T(8,128)(2,1)S(1)}, bf16[32,1536]{1,0:T(8,128)(2,1)S(1)}, u32[]{:S(2)}, u32[]{:S(2)}) collective-permute-start(bf16[32,1536]{1,0:T(8,128)(2,1)S(1)} %get-tuple-element.13), channel_id=1, source_target_pairs={{0,192},{64,0},{128,64},{192,128},{1,193},{65,1},{129,65},{193,129... | collective-permute-start | bytes 294920 | tf_op jit(solution)/shard_map/ppermute | solution.py:15
  (4 other events, 90.9 us)

commit v4 on v3

v4 whole, which is shorter than its diff:
```python
import jax
import jax.numpy as jnp
from jax import lax
from jax.experimental import pallas as pl
from jax.experimental.pallas import tpu as pltpu
from jax.sharding import Mesh, PartitionSpec as P

SPLIT = 4
RING8 = ("h", "l")
F32, BF16 = jnp.float32, jnp.bfloat16


def shift(v, axis, by):
    n = lax.axis_size(axis)
    return lax.ppermute(v, axis, [(i, (i + by) % n) for i in range(n)])


def exchange(v, axis):
    return lax.all_to_all(v, axis, split_axis=0, concat_axis=0, tiled=True)


def after(v, *others):
    return lax.optimization_barrier((v, *others))[0]


def pick(v, index):
    return lax.dynamic_index_in_dim(v, index, 0, keepdims=False)


def partial_kernel(at, acts, *refs):
    pieces, out, lhs = refs[:-2], refs[-2], refs[-1]
    y, c = (at[1], at[3]) if len(pieces) > 1 else (0, 0)

    @pl.when(pl.program_id(0) == 0)
    def _():
        toks = acts.shape[3]
        for d in range(4):
            for e in range(2):
                k = 4 * e + d if len(pieces) > 1 else 2 * d + e
                lhs[:, k * toks:(k + 1) * toks] = acts[(y + d) & 3, (c + e) & 1]

    rhs = jnp.concatenate([p[...] for p in pieces], axis=0)
    total = jnp.dot(lhs[...], rhs, preferred_element_type=F32).astype(out.dtype)
    parts, blocks, rows, _ = out.shape
    for b in range(blocks):
        for q in range(parts):
            r = (b * parts + q) * rows
            out[q, b] = total[r:r + rows]


def partial(at, acts, pieces, lo, hi):
    y, _, heads, toks = acts.shape
    wide = (hi - lo) // 2
    rows = heads // 16
    starts = [lo // wide if p.shape[1] > hi - lo else 0 for p in pieces]
    return pl.pallas_call(
        partial_kernel,
        grid_spec=pltpu.PrefetchScalarGridSpec(
            num_scalar_prefetch=1,
            grid=((hi - lo) // wide,),
            in_specs=[pl.BlockSpec(acts.shape, lambda i, at: (0, 0, 0, 0))]
            + [pl.BlockSpec((p.shape[0], wide), lambda i, at, s=s: (0, i + s)) for p, s in zip(pieces, starts)],
            out_specs=pl.BlockSpec((4, 4, rows, wide), lambda i, at: (0, 0, 0, i)),
            scratch_shapes=[pltpu.VMEM((heads, 8 * toks), BF16)],
        ),
        out_shape=jax.ShapeDtypeStruct((4, 4, rows, hi - lo), BF16),
        cost_estimate=pl.CostEstimate(
            flops=2 * heads * 8 * toks * (hi - lo), transcendentals=0,
            bytes_accessed=16 * toks * (hi - lo) + 2 * heads * (hi - lo) + 2 * acts.size),
        name="partial_grad_w",
    )(at, acts, *pieces)


def inputs_kernel(early, at, *refs):
    whole, pieces, weights, out, acc, lhs = refs[0], refs[1:11], refs[11:15], refs[15], refs[16], refs[17]
    y, l, c = at[1], at[2], at[3]
    k = pl.program_id(0)
    toks, heads = out.shape[3:]
    rhs = jnp.concatenate([w[...] for w in weights], axis=0)

    def product(tokens):
        return lax.dot_general(tokens, rhs, (((1,), (1,)), ((), ())), preferred_element_type=F32)

    @pl.when(k == 0)
    def _():
        acc[...] = product(whole[...])

    @pl.when((k > 0) & (k < early))
    def _():
        acc[...] += product(whole[...])

    @pl.when(k >= early)
    def _():
        for e in range(2):
            own, above, far_a, far_b, below = pieces[5 * e:5 * e + 5]
            for d, piece in ((0, own), (1, above), (3, below)):
                lhs[(y + d) & 3, (c + e) & 1] = piece[...]
            lhs[(y + 2) & 3, (c + e) & 1, :toks // 2] = far_a[...]
            lhs[(y + 2) & 3, (c + e) & 1, toks // 2:] = far_b[...]
        acc[...] += product(lhs[...].reshape(8 * toks, lhs.shape[3]))

    @pl.when(k == pl.num_programs(0) - 1)
    def _():
        for r in range(4):
            out[(l + r) & 3] = acc[:, r * heads:(r + 1) * heads].astype(out.dtype).reshape(4, 2, toks, heads)


def inputs_grad(at, whole, pieces, weights):
    heads, feats = weights[0].shape
    toks = pieces[0].shape[0]
    deep = feats // 8
    early = whole.shape[1] // deep
    late = [p.shape[1] // deep == 8 for p in pieces]
    return pl.pallas_call(
        lambda *refs: inputs_kernel(early, *refs),
        grid_spec=pltpu.PrefetchScalarGridSpec(
            num_scalar_prefetch=1,
            grid=(8,),
            in_specs=[pl.BlockSpec((8 * toks, deep), lambda k, at: (0, jnp.minimum(k, early - 1)))]
            + [pl.BlockSpec(
                (p.shape[0], deep), lambda k, at, s=early if full else 0: (0, jnp.maximum(k - early, 0) + s))
               for p, full in zip(pieces, late)]
            + [pl.BlockSpec((heads, deep), lambda k, at: (0, k)) for _ in weights],
            out_specs=pl.BlockSpec((4, 4, 2, toks, heads), lambda k, at: (0, 0, 0, 0, 0)),
            scratch_shapes=[pltpu.VMEM((8 * toks, 4 * heads), F32), pltpu.VMEM((4, 2, toks, deep), BF16)],
        ),
        out_shape=jax.ShapeDtypeStruct((4, 4, 2, toks, heads), BF16),
        cost_estimate=pl.CostEstimate(
            flops=2 * 8 * toks * feats * 4 * heads, transcendentals=0,
            bytes_accessed=2 * (8 * toks * feats + 4 * heads * feats + 32 * toks * heads)),
        name="grad_attn",
    )(at, whole, *pieces, *weights)


def local(grad_out, attn, w_out):
    g = grad_out[0]
    a = attn[0]
    toks, feats = g.shape
    heads = w_out.shape[0]
    at = jnp.stack([lax.axis_index(n) for n in ("x", "y", "l", "c")]).astype(jnp.int32)
    x, l = at[0], at[2]
    cut = SPLIT * feats // 8

    whole = lax.all_gather(g[:, :cut], ("y", "c"), axis=0, tiled=True)

    a = a.reshape(toks, 4, 4, 2, heads).transpose(1, 3, 2, 4, 0).reshape(8, 4 * heads, toks)
    acts = exchange(a, ("y", "c")).reshape(4, 2, 4 * heads, toks)

    w_above, w_below = shift(w_out, RING8, -1), shift(w_out, RING8, 1)

    half = toks // 2
    rest = g[:, cut:]
    above, below = shift(rest, "y", -1), shift(rest, "y", 1)

    acts = after(acts, w_above, w_below, above, below)
    part = partial(at, acts, [whole], 0, cut)
    w_far = shift(after(w_below, part), RING8, 1)
    weights = [w_out, w_above, w_far, w_below]
    tots = [lax.psum_scatter(part.reshape(16 * heads // 4, cut), "x", scatter_dimension=0, tiled=True)]

    pieces = [rest, above, shift(after(above[:half], part), "y", -1), shift(after(below[half:], part), "y", 1), below]
    pieces += [shift(p, "c", 1) for p in pieces]
    part = partial(at, after(acts, w_far), pieces, cut, feats)
    tots[0] = after(tots[0], part).reshape(4, heads // 4, cut)
    tots.append(exchange(part, "x"))

    res = inputs_grad(at, after(whole, part), pieces, weights)
    back = [pick(res, l)] + [shift(pick(res, (l + d) & 3), "l", d) for d in (1, 2, 3)]

    sums = []
    for j, tot in enumerate(tots):
        if j:
            tot = after(tot, acc).astype(F32).sum(0).astype(BF16)
        acc = pick(tot, l).astype(F32)
        for d in (1, -1, -2 if j % 2 else 2):
            acc = acc + shift(pick(tot, (l + d) & 3), RING8, d).astype(F32)
        acc = acc.astype(BF16)
        sums.append((acc.astype(F32) + shift(acc, "h", 1).astype(F32)).astype(BF16))
    acc = jnp.concatenate(sums, 1)
    grad_w = jnp.zeros((4, heads // 4, feats), BF16)
    for d in range(4):
        grad_w = lax.dynamic_update_slice_in_dim(
            grad_w, (shift(acc, "x", d) if d else acc)[None], (x - d) & 3, 0)
    grad_w = grad_w.reshape(heads, feats)

    out = jnp.zeros((4, 4, 2, toks, heads), BF16)
    for d, piece in enumerate(back):
        out = lax.dynamic_update_slice_in_dim(out, piece[:, None], (l - d) & 3, 1)
    out = out.reshape(1, 4 * 8 * toks, heads)
    return out, grad_w


def solution(mesh):
    fine = Mesh(mesh.devices.reshape(4, 2, 4, 4, 2), ("x", "h", "y", "l", "c"))
    dp, context = ("x", "h"), ("y", "l", "c")
    in_specs = (P(dp, context, None), P(dp, context, None), P(context, None))
    out_specs = (P(dp, None, context), P(context, None))
    return jax.shard_map(local, mesh=fine, in_specs=in_specs, out_specs=out_specs, check_vma=False)
```

time: 198 us -> 212 us (1.071); the launches traced: 197 us -> 209 us
  between operations: 0.86 us -> 14.3 us
  starting transfers between devices: 54.3 us -> 67.3 us
  waiting for transfers between devices: 98.8 us -> 85.8 us
    all_to_all x3 -> x2, waiting for transfers between devices: 23.5 us -> 0.01 us  [exchange(): return lax.all_to_all(v, axis, split_axis=0, concat_axis=0, tiled=True)]
    ppermute x29 -> x26, starting transfers between devices: 42.1 us -> 58.4 us  [shift(): return lax.ppermute(v, axis, [(i, (i + by) % n) for i in range(n)])]
    ppermute x29 -> x26, waiting for transfers between devices: 75.3 us -> 82.9 us  [shift(): return lax.ppermute(v, axis, [(i, (i + by) % n) for i in range(n)])]
    all_to_all x3 -> x2, starting transfers between devices: 12.2 us -> 8.76 us  [exchange(): return lax.all_to_all(v, axis, split_axis=0, concat_axis=0, tiled=True)]
    all_gather x0 -> x1, waiting for transfers between devices: none -> 2.83 us  [local(): whole = lax.all_gather(g[:, :cut], ('y', 'c'), axis=0, tiled=True)]
    slice x0 -> x1, local copies, waits for them, and re-layouts: none -> 2.16 us  [local(): rest = g[:, cut:]]
  transfers between devices with their start and end apart: 32 -> 30, of which waited for: 18 -> 13; matrix products, arithmetic and copies ran while one was open for 9% -> 6% of each run, Pallas kernels for 8% -> 9%
where the time goes in v4:
time: 212 us; the launch traced here: 209 us
  waiting for transfers between devices  85.8 us (40%)
  starting transfers between devices  67.3 us (32%)
  Pallas kernels  25.3 us (12%)
  between operations  14.3 us (7%)
  local copies, waits for them, and re-layouts  14.2 us (7%)
  other arithmetic  2.15 us (1%)
    ppermute x26, waiting for transfers between devices, shift(): return lax.ppermute(v, axis, [(i, (i + by) % n) for i in range(n)])  82.9 us
    ppermute x26, starting transfers between devices, shift(): return lax.ppermute(v, axis, [(i, (i + by) % n) for i in range(n)])  58.4 us
    pallas_call x2, Pallas kernels, partial(): pl.pallas_call(partial_kernel, grid_spec=pltpu.PrefetchScalarGridSpec(num...  13.3 us
    pallas_call x1, Pallas kernels, inputs_grad(): pl.pallas_call(lambda *refs: inputs_kernel(early, *refs), grid_spec=pltpu...  12 us
    all_to_all x2, starting transfers between devices, exchange(): return lax.all_to_all(v, axis, split_axis=0, concat_axis=0, tiled=True)  8.76 us
    dynamic_update_slice x4, local copies, waits for them, and re-layouts, local(): out = lax.dynamic_update_slice_in_dim(out, piece[:, None], l - d & 3, 1)  4.66 us
  transfers between devices with their start and end apart: 30, of which 13 were waited for; matrix products, arithmetic and copies ran while one was open for 6% of the time, Pallas kernels for 9%

profile of v4, /device:TPU:64, one launch (start us, length us, event | category | flops | bytes accessed | tf_op | source)
XLA Modules:
  0.0 209.0 jit_solution(8580980846353259473)
XLA Ops:
  7.2 2.2 %fusion.6 = (bf16[128,2048]{1,0:T(8,128)(2,1)S(1)}, bf16[128,2048]{1,0:T(8,128)(2,1)}) fusion(bf16[128,4096]{1,0:T(8,128)(2,1)} %bitcast.54), kind=kLoop, calls=%fused_computation.29 | loop fusion | bytes 2097152 | tf_op jit(solution)/shard_map/slice | solution.py:152
  9.4 2.0 collective-permute-start.1
  12.3 2.1 %copy.5 = bf16[4,2,4,128,128]{4,3,2,1,0:T(8,128)(2,1)} copy(bf16[4,2,4,128,128]{3,1,2,0,4:T(2,128)(2,1)S(1)} %bitcast.52) | data formatting | bytes 2097152 | tf_op jit(solution)/shard_map/transpose | solution.py:146
  14.4 4.5 %all-to-all-start = ((bf16[8,512,128]{2,1,0:T(8,128)(2,1)}), bf16[8,512,128]{2,1,0:T(8,128)(2,1)S(1)}, u32[]{:S(2)}, u32[]{:S(2)}) async-start(bf16[8,512,128]{2,1,0:T(8,128)(2,1)} %bitcast.6), calls=%async_computation | async-start | bytes 2097152 | tf_op jit(solution)/shard_map/all_to_all | solution.py:19
  18.9 3.2 %collective-permute-start.2 = (bf16[128,2048]{1,0:T(8,128)(2,1)S(1)}, bf16[128,2048]{1,0:T(8,128)(2,1)S(1)}, u32[]{:S(2)}, u32[]{:S(2)}) collective-permute-start(bf16[128,2048]{1,0:T(8,128)(2,1)S(1)} %get-tuple-element.21.refs_0_.refs_2_), channel_id=1, source_target_pairs={{0,24},{8,0},{16,8},{24,16},{1,25},{9,1},{17,9},{25,17},{2,26},{10... | collective-permute-start | bytes 1572872 | tf_op jit(solution)/shard_map/ppermute | solution.py:15
  22.6 38.8 %collective-permute-done.2.refs_1_.refs_3_ = bf16[128,2048]{1,0:T(8,128)(2,1)S(1)} collective-permute-done((bf16[128,2048]{1,0:T(8,128)(2,1)S(1)}, bf16[128,2048]{1,0:T(8,128)(2,1)S(1)}, u32[]{:S(2)}, u32[]{:S(2)}) %collective-permute-start.2) | collective-permute-done | bytes 524320 | tf_op jit(solution)/shard_map/ppermute | solution.py:15
  61.4 2.8 %all-gather.2.cloned.1.call-done.refs_0_.refs_1_ = bf16[1024,2048]{1,0:T(8,128)(2,1)} async-done(((bf16[128,2048]{1,0:T(8,128)(2,1)}), bf16[1024,2048]{1,0:T(8,128)(2,1)}) %all-gather.2.cloned.1.call-update) | async-done | bytes 4194320 | tf_op jit(solution)/shard_map/all_gather | solution.py:144
  64.3 6.4 %partial_grad_w.2 = bf16[4,4,32,2048]{3,2,1,0:T(8,128)(2,1)} custom-call(s32[4]{0:T(128)} %pad_add_fusion.at.refs_0_, bf16[4,2,512,128]{3,2,1,0:T(8,128)(2,1)} %bitcast.55, bf16[1024,2048]{1,0:T(8,128)(2,1)} %all-gather.2.cloned.1.call-done.refs_0_.refs_1_), custom_call_target="tpu_custom_call" | custom-call | flops 2147483648 | bytes 7340032 | tf_op jit(solution)/shard_map/partial_grad_w/pallas_call | solution.py:56
  70.7 3.1 %collective-permute-start.4 = (bf16[128,4096]{1,0:T(8,128)(2,1)}, bf16[128,4096]{1,0:T(8,128)(2,1)}, u32[]{:S(2)}, u32[]{:S(2)}) collective-permute-start(bf16[128,4096]{1,0:T(8,128)(2,1)} %collective-permute-done.1.refs_15_), channel_id=1, source_target_pairs={{0,2},{2,4},{4,6},{6,32},{32,34},{34,36},{36,38},{38,0},{1,3},{3,5... | collective-permute-start | bytes 3145736 | tf_op jit(solution)/shard_map/ppermute | solution.py:15
  74.7 3.1 %collective-permute-start.5 = (bf16[64,2048]{1,0:T(8,128)(2,1)S(1)}, bf16[64,2048]{1,0:T(8,128)(2,1)}, u32[]{:S(2)}, u32[]{:S(2)}) collective-permute-start(bf16[64,2048]{1,0:T(8,128)(2,1)S(1)} %slice.18), channel_id=1, source_target_pairs={{0,24},{8,0},{16,8},{24,16},{1,25},{9,1},{17,9},{25,17},{2,26},{10... | collective-permute-start | bytes 786440 | tf_op jit(solution)/shard_map/ppermute | solution.py:15
  77.7 5.5 %collective-permute-done.6.refs_3_.refs_5_ = bf16[64,2048]{1,0:T(8,128)(2,1)S(1)} collective-permute-done((bf16[64,2048]{1,0:T(8,128)(2,1)S(1)}, bf16[64,2048]{1,0:T(8,128)(2,1)S(1)}, u32[]{:S(2)}, u32[]{:S(2)}) %collective-permute-start.6) | collective-permute-done | bytes 262176 | tf_op jit(solution)/shard_map/ppermute | solution.py:15
  83.8 13.1 %collective-permute-done.4.refs_14_ = bf16[128,4096]{1,0:T(8,128)(2,1)} collective-permute-done((bf16[128,4096]{1,0:T(8,128)(2,1)}, bf16[128,4096]{1,0:T(8,128)(2,1)}, u32[]{:S(2)}, u32[]{:S(2)}) %collective-permute-start.4) | collective-permute-done | bytes 1048608 | tf_op jit(solution)/shard_map/ppermute | solution.py:15
  97.0 1.8 collective-permute-done.9.refs_7_.refs_9_
  98.9 6.9 %partial_grad_w.3 = bf16[4,4,32,2048]{3,2,1,0:T(8,128)(2,1)} custom-call(s32[4]{0:T(128)} %pad_add_fusion.at.refs_0_, bf16[4,2,512,128]{3,2,1,0:T(8,128)(2,1)} %bitcast.56, bf16[128,2048]{1,0:T(8,128)(2,1)} %copy-done.4, bf16[128,2048]{1,0:T(8,128)(2,1)} %copy-done.5, bf16[64,2048]{1,0:T(8,128)(2,1)} %collective-permute-done.5.refs_2_.refs_4_, ...), custom_call_target="tpu_custom_call" | custom-call | flops 2147483648 | bytes 7340032 | tf_op jit(solution)/shard_map/partial_grad_w/pallas_call | solution.py:56
  105.7 4.3 %all-to-all-start.1 = ((bf16[4,4,32,2048]{3,2,1,0:T(8,128)(2,1)}), bf16[4,4,32,2048]{3,2,1,0:T(8,128)(2,1)S(1)}, u32[]{:S(2)}, u32[]{:S(2)}) async-start(bf16[4,4,32,2048]{3,2,1,0:T(8,128)(2,1)} %partial_grad_w.3), calls=%async_computation.2 | async-start | bytes 4194304 | tf_op jit(solution)/shard_map/all_to_all | solution.py:19
  110.0 12.0 %grad_attn.1 = bf16[4,4,2,128,128]{4,3,2,1,0:T(8,128)(2,1)} custom-call(s32[4]{0:T(128)} %pad_add_fusion.at.refs_0_, bf16[1024,2048]{1,0:T(8,128)(2,1)} %all-gather.2.cloned.1.call-done.refs_0_.refs_1_, bf16[128,2048]{1,0:T(8,128)(2,1)} %copy-done.4, bf16[128,2048]{1,0:T(8,128)(2,1)} %copy-done.5, bf16[64,2048]{1,0:T(8,128)(2,1)} %collective-permute-done.5.refs_2_.refs_4_, ...), custom_call_target="tpu_custom_call" | custom-call | flops 4294967296 | bytes 13631488 | tf_op jit(solution)/shard_map/grad_attn/pallas_call | solution.py:114
  122.0 2.0 dynamic-slice_bitcast_fusion
  124.0 3.2 %collective-permute-start.12 = (bf16[4,2,128,128]{3,2,1,0:T(8,128)(2,1)}, bf16[4,2,128,128]{3,2,1,0:T(8,128)(2,1)}, u32[]{:S(2)}, u32[]{:S(2)}) collective-permute-start(bf16[4,2,128,128]{3,2,1,0:T(8,128)(2,1)} %get-tuple-element.20), channel_id=1, source_target_pairs={{0,2},{2,4},{4,6},{6,0},{1,3},{3,5},{5,7},{7,1},{8,10},{10,12},{12... | collective-permute-start | bytes 786440 | tf_op jit(solution)/shard_map/ppermute | solution.py:15
  128.2 2.9 %collective-permute-start.14 = (bf16[4,2,128,128]{3,2,1,0:T(8,128)(2,1)S(1)}, bf16[4,2,128,128]{3,2,1,0:T(8,128)(2,1)}, u32[]{:S(2)}, u32[]{:S(2)}) collective-permute-start(bf16[4,2,128,128]{3,2,1,0:T(8,128)(2,1)S(1)} %get-tuple-element.18), channel_id=1, source_target_pairs={{0,6},{2,0},{4,2},{6,4},{1,7},{3,1},{5,3},{7,5},{8,14},{10,8},{12,... | collective-permute-start | bytes 786440 | tf_op jit(solution)/shard_map/ppermute | solution.py:15
  132.4 3.2 %collective-permute-done.12 = bf16[4,2,128,128]{3,2,1,0:T(8,128)(2,1)} collective-permute-done((bf16[4,2,128,128]{3,2,1,0:T(8,128)(2,1)}, bf16[4,2,128,128]{3,2,1,0:T(8,128)(2,1)}, u32[]{:S(2)}, u32[]{:S(2)}) %collective-permute-start.12) | collective-permute-done | bytes 262176 | tf_op jit(solution)/shard_map/ppermute | solution.py:15
  137.7 2.6 %collective-permute-start.15 = (bf16[32,2048]{1,0:T(8,128)(2,1)S(1)}, bf16[32,2048]{1,0:T(8,128)(2,1)S(1)}, u32[]{:S(2)}, u32[]{:S(2)}) collective-permute-start(bf16[32,2048]{1,0:T(8,128)(2,1)S(1)} %get-tuple-element.26), channel_id=1, source_target_pairs={{0,2},{2,4},{4,6},{6,32},{32,34},{34,36},{36,38},{38,0},{1,3},{3,5... | collective-permute-start | bytes 393224 | tf_op jit(solution)/shard_map/ppermute | solution.py:15
  140.3 6.9 %collective-permute-start.17 = (bf16[32,2048]{1,0:T(8,128)(2,1)S(1)}, bf16[32,2048]{1,0:T(8,128)(2,1)S(1)}, u32[]{:S(2)}, u32[]{:S(2)}) collective-permute-start(bf16[32,2048]{1,0:T(8,128)(2,1)S(1)} %get-tuple-element.27), channel_id=1, source_target_pairs={{0,4},{2,6},{4,32},{6,34},{32,36},{34,38},{36,0},{38,2},{1,5},{3,7... | collective-permute-start | bytes 393224 | tf_op jit(solution)/shard_map/ppermute | solution.py:15
  148.2 7.6 %collective-permute-done.15 = bf16[32,2048]{1,0:T(8,128)(2,1)S(1)} collective-permute-done((bf16[32,2048]{1,0:T(8,128)(2,1)S(1)}, bf16[32,2048]{1,0:T(8,128)(2,1)S(1)}, u32[]{:S(2)}, u32[]{:S(2)}) %collective-permute-start.15) | collective-permute-done | bytes 131104 | tf_op jit(solution)/shard_map/ppermute | solution.py:15
  157.3 3.5 %collective-permute-start.19 = (bf16[32,2048]{1,0:T(8,128)(2,1)S(1)}, bf16[32,2048]{1,0:T(8,128)(2,1)S(1)}, u32[]{:S(2)}, u32[]{:S(2)}) collective-permute-start(bf16[32,2048]{1,0:T(8,128)(2,1)S(1)} %get-tuple-element.23), channel_id=1, source_target_pairs={{0,2},{2,4},{4,6},{6,32},{32,34},{34,36},{36,38},{38,0},{1,3},{3,5... | collective-permute-start | bytes 393224 | tf_op jit(solution)/shard_map/ppermute | solution.py:15
  160.8 3.9 %collective-permute-start.21 = (bf16[32,2048]{1,0:T(8,128)(2,1)S(1)}, bf16[32,2048]{1,0:T(8,128)(2,1)S(1)}, u32[]{:S(2)}, u32[]{:S(2)}) collective-permute-start(bf16[32,2048]{1,0:T(8,128)(2,1)S(1)} %get-tuple-element.24), channel_id=1, source_target_pairs={{0,36},{2,38},{4,0},{6,2},{32,4},{34,6},{36,32},{38,34},{1,37},{3,... | collective-permute-start | bytes 393224 | tf_op jit(solution)/shard_map/ppermute | solution.py:15
  164.7 1.7 bitcast_dynamic-update-slice_fusion.4
  168.0 3.7 %collective-permute-done.21 = bf16[32,2048]{1,0:T(8,128)(2,1)S(1)} collective-permute-done((bf16[32,2048]{1,0:T(8,128)(2,1)S(1)}, bf16[32,2048]{1,0:T(8,128)(2,1)S(1)}, u32[]{:S(2)}, u32[]{:S(2)}) %collective-permute-start.21) | collective-permute-done | bytes 131104 | tf_op jit(solution)/shard_map/ppermute | solution.py:15
  171.7 14.6 %collective-permute-start.22 = (bf16[32,2048]{1,0:T(8,128)(2,1)S(1)}, bf16[32,2048]{1,0:T(8,128)(2,1)S(1)}, u32[]{:S(2)}, u32[]{:S(2)}) collective-permute-start(bf16[32,2048]{1,0:T(8,128)(2,1)S(1)} %fusion.2), channel_id=1, source_target_pairs={{0,32},{32,0},{1,33},{33,1},{2,34},{34,2},{3,35},{35,3},{4,36},{36... | collective-permute-start | bytes 393224 | tf_op jit(solution)/shard_map/ppermute | solution.py:15
  186.4 2.9 %collective-permute-done.22 = bf16[32,2048]{1,0:T(8,128)(2,1)S(1)} collective-permute-done((bf16[32,2048]{1,0:T(8,128)(2,1)S(1)}, bf16[32,2048]{1,0:T(8,128)(2,1)S(1)}, u32[]{:S(2)}, u32[]{:S(2)}) %collective-permute-start.22) | collective-permute-done | bytes 131104 | tf_op jit(solution)/shard_map/ppermute | solution.py:15
  189.4 1.9 collective-permute-start.23
  191.3 2.7 %collective-permute-start.24 = (bf16[32,4096]{1,0:T(8,128)(2,1)S(1)}, bf16[32,4096]{1,0:T(8,128)(2,1)S(1)}, u32[]{:S(2)}, u32[]{:S(2)}) collective-permute-start(bf16[32,4096]{1,0:T(8,128)(2,1)S(1)} %pad_maximum_fusion), channel_id=1, source_target_pairs={{0,128},{64,192},{128,0},{192,64},{1,129},{65,193},{129,1},{193,65... | collective-permute-start | bytes 786440 | tf_op jit(solution)/shard_map/ppermute | solution.py:15
  197.0 4.0 %collective-permute-done.24 = bf16[32,4096]{1,0:T(8,128)(2,1)S(1)} collective-permute-done((bf16[32,4096]{1,0:T(8,128)(2,1)S(1)}, bf16[32,4096]{1,0:T(8,128)(2,1)S(1)}, u32[]{:S(2)}, u32[]{:S(2)}) %collective-permute-start.24) | collective-permute-done | bytes 262176 | tf_op jit(solution)/shard_map/ppermute | solution.py:15
  (80 shorter events, 15.5 us)
Async XLA Ops:
  7.2 57.1 %all-gather.2.cloned.1.call-start = ((), (), s32[]{:S(2)}) async-start(), calls=%async_computation.3 | async-start | bytes 4718592 | tf_op jit(solution)/shard_map/all_gather | solution.py:144
  9.4 64.7 %copy-start.4 = (bf16[128,2048]{1,0:T(8,128)(2,1)}, bf16[128,2048]{1,0:T(8,128)(2,1)S(1)}, u32[]{:S(2)}) copy-start(bf16[128,2048]{1,0:T(8,128)(2,1)S(1)} %get-tuple-element.21.refs_0_.refs_2_) | copy-start | bytes 1572868
  9.4 52.0 %collective-permute-start.1 = (bf16[128,4096]{1,0:T(8,128)(2,1)}, bf16[128,4096]{1,0:T(8,128)(2,1)}, u32[]{:S(2)}, u32[]{:S(2)}) collective-permute-start(bf16[128,4096]{1,0:T(8,128)(2,1)} %refs_12_.1), channel_id=1, source_target_pairs={{0,2},{2,4},{4,6},{6,32},{32,34},{34,36},{36,38},{38,0},{1,3},{3,5... | collective-permute-start | bytes 3145736 | tf_op jit(solution)/shard_map/ppermute | solution.py:15
  11.4 50.0 %collective-permute-start = (bf16[128,4096]{1,0:T(8,128)(2,1)}, bf16[128,4096]{1,0:T(8,128)(2,1)}, u32[]{:S(2)}, u32[]{:S(2)}) collective-permute-start(bf16[128,4096]{1,0:T(8,128)(2,1)} %refs_12_.1), channel_id=1, source_target_pairs={{0,38},{2,0},{4,2},{6,4},{32,6},{34,32},{36,34},{38,36},{1,39},{3,... | collective-permute-start | bytes 3145736 | tf_op jit(solution)/shard_map/ppermute | solution.py:15
  14.4 47.0 %all-to-all-start = ((bf16[8,512,128]{2,1,0:T(8,128)(2,1)}), bf16[8,512,128]{2,1,0:T(8,128)(2,1)S(1)}, u32[]{:S(2)}, u32[]{:S(2)}) async-start(bf16[8,512,128]{2,1,0:T(8,128)(2,1)} %bitcast.6), calls=%async_computation | async-start | bytes 2097152 | tf_op jit(solution)/shard_map/all_to_all | solution.py:19
  18.8 117.8 %reduce-scatter.2.cloned.1.call-start = ((), (), s32[]{:S(2)}) async-start(), calls=%async_computation.4 | async-start | bytes 2621440 | tf_op jit(solution)/shard_map/reduce_scatter | solution.py:159
  18.9 42.5 %collective-permute-start.2 = (bf16[128,2048]{1,0:T(8,128)(2,1)S(1)}, bf16[128,2048]{1,0:T(8,128)(2,1)S(1)}, u32[]{:S(2)}, u32[]{:S(2)}) collective-permute-start(bf16[128,2048]{1,0:T(8,128)(2,1)S(1)} %get-tuple-element.21.refs_0_.refs_2_), channel_id=1, source_target_pairs={{0,24},{8,0},{16,8},{24,16},{1,25},{9,1},{17,9},{25,17},{2,26},{10... | collective-permute-start | bytes 1572872 | tf_op jit(solution)/shard_map/ppermute | solution.py:15
  22.1 39.3 %collective-permute-start.3 = (bf16[128,2048]{1,0:T(8,128)(2,1)S(1)}, bf16[128,2048]{1,0:T(8,128)(2,1)S(1)}, u32[]{:S(2)}, u32[]{:S(2)}) collective-permute-start(bf16[128,2048]{1,0:T(8,128)(2,1)S(1)} %get-tuple-element.21.refs_0_.refs_2_), channel_id=1, source_target_pairs={{0,8},{8,16},{16,24},{24,0},{1,9},{9,17},{17,25},{25,1},{2,10},{10... | collective-permute-start | bytes 1572872 | tf_op jit(solution)/shard_map/ppermute | solution.py:15
  61.4 37.4 %copy-start.5 = (bf16[128,2048]{1,0:T(8,128)(2,1)}, bf16[128,2048]{1,0:T(8,128)(2,1)S(1)}, u32[]{:S(2)}) copy-start(bf16[128,2048]{1,0:T(8,128)(2,1)S(1)} %collective-permute-done.2.refs_1_.refs_3_) | copy-start | bytes 1572868
  70.7 26.3 %collective-permute-start.4 = (bf16[128,4096]{1,0:T(8,128)(2,1)}, bf16[128,4096]{1,0:T(8,128)(2,1)}, u32[]{:S(2)}, u32[]{:S(2)}) collective-permute-start(bf16[128,4096]{1,0:T(8,128)(2,1)} %collective-permute-done.1.refs_15_), channel_id=1, source_target_pairs={{0,2},{2,4},{4,6},{6,32},{32,34},{34,36},{36,38},{38,0},{1,3},{3,5... | collective-permute-start | bytes 3145736 | tf_op jit(solution)/shard_map/ppermute | solution.py:15
  73.8 9.5 %collective-permute-start.6 = (bf16[64,2048]{1,0:T(8,128)(2,1)S(1)}, bf16[64,2048]{1,0:T(8,128)(2,1)S(1)}, u32[]{:S(2)}, u32[]{:S(2)}) collective-permute-start(bf16[64,2048]{1,0:T(8,128)(2,1)S(1)} %slice.19), channel_id=1, source_target_pairs={{0,8},{8,16},{16,24},{24,0},{1,9},{9,17},{17,25},{25,1},{2,10},{10... | collective-permute-start | bytes 786440 | tf_op jit(solution)/shard_map/ppermute | solution.py:15
  74.1 22.9 %collective-permute-start.7 = (bf16[128,2048]{1,0:T(8,128)(2,1)S(1)}, bf16[128,2048]{1,0:T(8,128)(2,1)S(1)}, u32[]{:S(2)}, u32[]{:S(2)}) collective-permute-start(bf16[128,2048]{1,0:T(8,128)(2,1)S(1)} %get-tuple-element.21.refs_0_.refs_2_), channel_id=1, source_target_pairs={{0,1},{1,0},{2,3},{3,2},{4,5},{5,4},{6,7},{7,6},{8,9},{9,8},{10,11... | collective-permute-start | bytes 1572872 | tf_op jit(solution)/shard_map/ppermute | solution.py:15
  74.1 22.9 %collective-permute-start.11 = (bf16[128,2048]{1,0:T(8,128)(2,1)S(1)}, bf16[128,2048]{1,0:T(8,128)(2,1)S(1)}, u32[]{:S(2)}, u32[]{:S(2)}) collective-permute-start(bf16[128,2048]{1,0:T(8,128)(2,1)S(1)} %collective-permute-done.3.refs_4_.refs_6_), channel_id=1, source_target_pairs={{0,1},{1,0},{2,3},{3,2},{4,5},{5,4},{6,7},{7,6},{8,9},{9,8},{10,11... | collective-permute-start | bytes 1572872 | tf_op jit(solution)/shard_map/ppermute | solution.py:15
  74.7 8.9 %collective-permute-start.5 = (bf16[64,2048]{1,0:T(8,128)(2,1)S(1)}, bf16[64,2048]{1,0:T(8,128)(2,1)}, u32[]{:S(2)}, u32[]{:S(2)}) collective-permute-start(bf16[64,2048]{1,0:T(8,128)(2,1)S(1)} %slice.18), channel_id=1, source_target_pairs={{0,24},{8,0},{16,8},{24,16},{1,25},{9,1},{17,9},{25,17},{2,26},{10... | collective-permute-start | bytes 786440 | tf_op jit(solution)/shard_map/ppermute | solution.py:15
  83.3 13.7 %collective-permute-start.8 = (bf16[128,2048]{1,0:T(8,128)(2,1)S(1)}, bf16[128,2048]{1,0:T(8,128)(2,1)S(1)}, u32[]{:S(2)}, u32[]{:S(2)}) collective-permute-start(bf16[128,2048]{1,0:T(8,128)(2,1)S(1)} %collective-permute-done.2.refs_1_.refs_3_), channel_id=1, source_target_pairs={{0,1},{1,0},{2,3},{3,2},{4,5},{5,4},{6,7},{7,6},{8,9},{9,8},{10,11... | collective-permute-start | bytes 1572872 | tf_op jit(solution)/shard_map/ppermute | solution.py:15
  83.6 13.4 %collective-permute-start.10 = (bf16[64,2048]{1,0:T(8,128)(2,1)S(1)}, bf16[64,2048]{1,0:T(8,128)(2,1)}, u32[]{:S(2)}, u32[]{:S(2)}) collective-permute-start(bf16[64,2048]{1,0:T(8,128)(2,1)S(1)} %collective-permute-done.6.refs_3_.refs_5_), channel_id=1, source_target_pairs={{0,1},{1,0},{2,3},{3,2},{4,5},{5,4},{6,7},{7,6},{8,9},{9,8},{10,11... | collective-permute-start | bytes 786440 | tf_op jit(solution)/shard_map/ppermute | solution.py:15
  96.9 1.9 collective-permute-start.9
  105.7 51.0 %all-to-all-start.1 = ((bf16[4,4,32,2048]{3,2,1,0:T(8,128)(2,1)}), bf16[4,4,32,2048]{3,2,1,0:T(8,128)(2,1)S(1)}, u32[]{:S(2)}, u32[]{:S(2)}) async-start(bf16[4,4,32,2048]{3,2,1,0:T(8,128)(2,1)} %partial_grad_w.3), calls=%async_computation.2 | async-start | bytes 4194304 | tf_op jit(solution)/shard_map/all_to_all | solution.py:19
  124.0 11.6 %collective-permute-start.12 = (bf16[4,2,128,128]{3,2,1,0:T(8,128)(2,1)}, bf16[4,2,128,128]{3,2,1,0:T(8,128)(2,1)}, u32[]{:S(2)}, u32[]{:S(2)}) collective-permute-start(bf16[4,2,128,128]{3,2,1,0:T(8,128)(2,1)} %get-tuple-element.20), channel_id=1, source_target_pairs={{0,2},{2,4},{4,6},{6,0},{1,3},{3,5},{5,7},{7,1},{8,10},{10,12},{12... | collective-permute-start | bytes 786440 | tf_op jit(solution)/shard_map/ppermute | solution.py:15
  127.3 19.9 %collective-permute-start.13 = (bf16[4,2,128,128]{3,2,1,0:T(8,128)(2,1)}, bf16[4,2,128,128]{3,2,1,0:T(8,128)(2,1)}, u32[]{:S(2)}, u32[]{:S(2)}) collective-permute-start(bf16[4,2,128,128]{3,2,1,0:T(8,128)(2,1)} %get-tuple-element.19), channel_id=1, source_target_pairs={{0,4},{2,6},{4,0},{6,2},{1,5},{3,7},{5,1},{7,3},{8,12},{10,14},{12... | collective-permute-start | bytes 786440 | tf_op jit(solution)/shard_map/ppermute | solution.py:15
  128.2 36.4 %collective-permute-start.14 = (bf16[4,2,128,128]{3,2,1,0:T(8,128)(2,1)S(1)}, bf16[4,2,128,128]{3,2,1,0:T(8,128)(2,1)}, u32[]{:S(2)}, u32[]{:S(2)}) collective-permute-start(bf16[4,2,128,128]{3,2,1,0:T(8,128)(2,1)S(1)} %get-tuple-element.18), channel_id=1, source_target_pairs={{0,6},{2,0},{4,2},{6,4},{1,7},{3,1},{5,3},{7,5},{8,14},{10,8},{12,... | collective-permute-start | bytes 786440 | tf_op jit(solution)/shard_map/ppermute | solution.py:15
  137.7 18.1 %collective-permute-start.15 = (bf16[32,2048]{1,0:T(8,128)(2,1)S(1)}, bf16[32,2048]{1,0:T(8,128)(2,1)S(1)}, u32[]{:S(2)}, u32[]{:S(2)}) collective-permute-start(bf16[32,2048]{1,0:T(8,128)(2,1)S(1)} %get-tuple-element.26), channel_id=1, source_target_pairs={{0,2},{2,4},{4,6},{6,32},{32,34},{34,36},{36,38},{38,0},{1,3},{3,5... | collective-permute-start | bytes 393224 | tf_op jit(solution)/shard_map/ppermute | solution.py:15
  140.2 15.5 %collective-permute-start.16 = (bf16[32,2048]{1,0:T(8,128)(2,1)S(1)}, bf16[32,2048]{1,0:T(8,128)(2,1)S(1)}, u32[]{:S(2)}, u32[]{:S(2)}) collective-permute-start(bf16[32,2048]{1,0:T(8,128)(2,1)S(1)} %get-tuple-element.28), channel_id=1, source_target_pairs={{0,38},{2,0},{4,2},{6,4},{32,6},{34,32},{36,34},{38,36},{1,39},{3,... | collective-permute-start | bytes 393224 | tf_op jit(solution)/shard_map/ppermute | solution.py:15
  140.3 15.5 %collective-permute-start.17 = (bf16[32,2048]{1,0:T(8,128)(2,1)S(1)}, bf16[32,2048]{1,0:T(8,128)(2,1)S(1)}, u32[]{:S(2)}, u32[]{:S(2)}) collective-permute-start(bf16[32,2048]{1,0:T(8,128)(2,1)S(1)} %get-tuple-element.27), channel_id=1, source_target_pairs={{0,4},{2,6},{4,32},{6,34},{32,36},{34,38},{36,0},{38,2},{1,5},{3,7... | collective-permute-start | bytes 393224 | tf_op jit(solution)/shard_map/ppermute | solution.py:15
  157.3 10.3 %collective-permute-start.19 = (bf16[32,2048]{1,0:T(8,128)(2,1)S(1)}, bf16[32,2048]{1,0:T(8,128)(2,1)S(1)}, u32[]{:S(2)}, u32[]{:S(2)}) collective-permute-start(bf16[32,2048]{1,0:T(8,128)(2,1)S(1)} %get-tuple-element.23), channel_id=1, source_target_pairs={{0,2},{2,4},{4,6},{6,32},{32,34},{34,36},{36,38},{38,0},{1,3},{3,5... | collective-permute-start | bytes 393224 | tf_op jit(solution)/shard_map/ppermute | solution.py:15
  160.8 7.2 %collective-permute-start.20 = (bf16[32,2048]{1,0:T(8,128)(2,1)S(1)}, bf16[32,2048]{1,0:T(8,128)(2,1)S(1)}, u32[]{:S(2)}, u32[]{:S(2)}) collective-permute-start(bf16[32,2048]{1,0:T(8,128)(2,1)S(1)} %get-tuple-element.25), channel_id=1, source_target_pairs={{0,38},{2,0},{4,2},{6,4},{32,6},{34,32},{36,34},{38,36},{1,39},{3,... | collective-permute-start | bytes 393224 | tf_op jit(solution)/shard_map/ppermute | solution.py:15
  160.8 10.9 %collective-permute-start.21 = (bf16[32,2048]{1,0:T(8,128)(2,1)S(1)}, bf16[32,2048]{1,0:T(8,128)(2,1)S(1)}, u32[]{:S(2)}, u32[]{:S(2)}) collective-permute-start(bf16[32,2048]{1,0:T(8,128)(2,1)S(1)} %get-tuple-element.24), channel_id=1, source_target_pairs={{0,36},{2,38},{4,0},{6,2},{32,4},{34,6},{36,32},{38,34},{1,37},{3,... | collective-permute-start | bytes 393224 | tf_op jit(solution)/shard_map/ppermute | solution.py:15
  166.4 20.0 %collective-permute-start.18 = (bf16[32,2048]{1,0:T(8,128)(2,1)S(1)}, bf16[32,2048]{1,0:T(8,128)(2,1)S(1)}, u32[]{:S(2)}, u32[]{:S(2)}) collective-permute-start(bf16[32,2048]{1,0:T(8,128)(2,1)S(1)} %fusion.5), channel_id=1, source_target_pairs={{0,32},{32,0},{1,33},{33,1},{2,34},{34,2},{3,35},{35,3},{4,36},{36... | collective-permute-start | bytes 393224 | tf_op jit(solution)/shard_map/ppermute | solution.py:15
  171.7 17.6 %collective-permute-start.22 = (bf16[32,2048]{1,0:T(8,128)(2,1)S(1)}, bf16[32,2048]{1,0:T(8,128)(2,1)S(1)}, u32[]{:S(2)}, u32[]{:S(2)}) collective-permute-start(bf16[32,2048]{1,0:T(8,128)(2,1)S(1)} %fusion.2), channel_id=1, source_target_pairs={{0,32},{32,0},{1,33},{33,1},{2,34},{34,2},{3,35},{35,3},{4,36},{36... | collective-permute-start | bytes 393224 | tf_op jit(solution)/shard_map/ppermute | solution.py:15
  189.4 7.7 %collective-permute-start.23 = (bf16[32,4096]{1,0:T(8,128)(2,1)S(1)}, bf16[32,4096]{1,0:T(8,128)(2,1)S(1)}, u32[]{:S(2)}, u32[]{:S(2)}) collective-permute-start(bf16[32,4096]{1,0:T(8,128)(2,1)S(1)} %pad_maximum_fusion), channel_id=1, source_target_pairs={{0,64},{64,128},{128,192},{192,0},{1,65},{65,129},{129,193},{193,1... | collective-permute-start | bytes 786440 | tf_op jit(solution)/shard_map/ppermute | solution.py:15
  191.3 9.8 %collective-permute-start.24 = (bf16[32,4096]{1,0:T(8,128)(2,1)S(1)}, bf16[32,4096]{1,0:T(8,128)(2,1)S(1)}, u32[]{:S(2)}, u32[]{:S(2)}) collective-permute-start(bf16[32,4096]{1,0:T(8,128)(2,1)S(1)} %pad_maximum_fusion), channel_id=1, source_target_pairs={{0,128},{64,192},{128,0},{192,64},{1,129},{65,193},{129,1},{193,65... | collective-permute-start | bytes 786440 | tf_op jit(solution)/shard_map/ppermute | solution.py:15
  193.9 7.2 %collective-permute-start.25 = (bf16[32,4096]{1,0:T(8,128)(2,1)S(1)}, bf16[32,4096]{1,0:T(8,128)(2,1)S(1)}, u32[]{:S(2)}, u32[]{:S(2)}) collective-permute-start(bf16[32,4096]{1,0:T(8,128)(2,1)S(1)} %pad_maximum_fusion), channel_id=1, source_target_pairs={{0,192},{64,0},{128,64},{192,128},{1,193},{65,1},{129,65},{193,129... | collective-permute-start | bytes 786440 | tf_op jit(solution)/shard_map/ppermute | solution.py:15
  (9 other events, 75.4 us)
Sparse Core Ops, SparseCore 0:
  10.4 53.7 all-gather.1
  70.8 33.2 reduce-scatter.1

commit v5 on v3

--- a/solution.py
+++ b/solution.py
@@ -5,7 +5,7 @@
 from jax.experimental.pallas import tpu as pltpu
 from jax.sharding import Mesh, PartitionSpec as P
 
-CHUNKS = (5, 3)
+SPLIT = 4
 RING8 = ("h", "l")
 F32, BF16 = jnp.float32, jnp.bfloat16
 
@@ -27,40 +27,65 @@
     return lax.dynamic_index_in_dim(v, index, 0, keepdims=False)
 
 
-def partial_kernel(at, acts, *refs):
-    pieces, out, lhs = refs[:10], refs[10], refs[11]
+def partial_kernel(lo, at, acts, *refs):
+    pieces, (out, lhs, rhs, lhs_sems, rhs_sems) = refs[:10], refs[10:]
     y, c = at[1], at[3]
-
-    @pl.when(pl.program_id(0) == 0)
-    def _():
-        toks = acts.shape[3]
-        for e in range(2):
-            for d in range(4):
-                k = 4 * e + d
-                lhs[:, k * toks:(k + 1) * toks] = acts[(y + d) & 3, (c + e) & 1]
-
-    rhs = jnp.concatenate([p[...] for p in pieces], axis=0)
-    total = jnp.dot(lhs[...], rhs, preferred_element_type=F32).astype(out.dtype)
-    parts, blocks, rows, _ = out.shape
+    blocks, _, wide = rhs.shape
+    toks = acts.shape[3]
+
+    def lhs_copy(k):
+        e, d = divmod(k, 4)
+        return pltpu.make_async_copy(
+            acts.at[(y + d) & 3, (c + e) & 1], lhs.at[:, pl.ds(k * toks, toks)], lhs_sems.at[k])
+
+    def rhs_copies(i):
+        row = 0
+        for k, piece in enumerate(pieces):
+            yield pltpu.make_async_copy(
+                piece.at[:, pl.ds(lo + i * wide, wide)], rhs.at[i, pl.ds(row, piece.shape[0])], rhs_sems.at[i, k])
+            row += piece.shape[0]
+
+    i = pl.program_id(0)
+
+    @pl.when(i == 0)
+    def _():
+        for k in range(8):
+            lhs_copy(k).start()
+        for b in range(blocks):
+            for copy in rhs_copies(b):
+                copy.start()
+        for k in range(8):
+            lhs_copy(k).wait()
+
     for b in range(blocks):
+        @pl.when(i == b)
+        def _():
+            for copy in rhs_copies(b):
+                copy.wait()
+
+    total = jnp.dot(lhs[...], rhs[i], preferred_element_type=F32).astype(out.dtype)
+    parts, groups, rows, _ = out.shape
+    for g in range(groups):
         for q in range(parts):
-            r = (b * parts + q) * rows
-            out[q, b] = total[r:r + rows]
+            r = (g * parts + q) * rows
+            out[q, g] = total[r:r + rows]
 
 
 def partial(at, acts, pieces, lo, hi):
     y, _, heads, toks = acts.shape
     wide = pieces[0].shape[1] // 8
     rows = heads // 16
+    blocks = (hi - lo) // wide
     return pl.pallas_call(
-        partial_kernel,
+        lambda *refs: partial_kernel(lo, *refs),
         grid_spec=pltpu.PrefetchScalarGridSpec(
             num_scalar_prefetch=1,
-            grid=((hi - lo) // wide,),
-            in_specs=[pl.BlockSpec(acts.shape, lambda i, at: (0, 0, 0, 0))]
-            + [pl.BlockSpec((p.shape[0], wide), lambda i, at: (0, i + lo // wide)) for p in pieces],
+            grid=(blocks,),
+            in_specs=[pl.BlockSpec(memory_space=pl.ANY)] * 11,
             out_specs=pl.BlockSpec((4, 4, rows, wide), lambda i, at: (0, 0, 0, i)),
-            scratch_shapes=[pltpu.VMEM((heads, 8 * toks), BF16)],
+            scratch_shapes=[
+                pltpu.VMEM((heads, 8 * toks), BF16), pltpu.VMEM((blocks, 8 * toks, wide), BF16),
+                pltpu.SemaphoreType.DMA((8,)), pltpu.SemaphoreType.DMA((blocks, 10))],
         ),
         out_shape=jax.ShapeDtypeStruct((4, 4, rows, hi - lo), BF16),
         cost_estimate=pl.CostEstimate(
@@ -71,7 +96,7 @@
 
 
 def inputs_kernel(at, *refs):
-    pieces, weights, out, acc = refs[:10], refs[10:14], refs[14], refs[15]
+    pieces, weights, out, acc = refs[:10], refs[10:15], refs[15], refs[16]
     y, l, c = at[1], at[2], at[3]
     k = pl.program_id(0)
     lhs = jnp.concatenate([p[...] for p in pieces], axis=0)
@@ -126,45 +151,45 @@
     at = jnp.stack([lax.axis_index(n) for n in ("x", "y", "l", "c")]).astype(jnp.int32)
     l = at[2]
 
-    cuts, lo = [], 0
-    for size in CHUNKS:
-        size = size * feats // sum(CHUNKS)
-        cuts.append((lo, lo + size))
-        lo += size
+    cut = SPLIT * feats // 8
 
     a = a.reshape(toks, 4, 4, 2, heads).transpose(1, 3, 2, 4, 0).reshape(8, 4 * heads, toks)
     acts = exchange(a, ("y", "c")).reshape(4, 2, 4 * heads, toks)
-
-    w_above, w_below = shift(w_out, RING8, -1), shift(w_out, RING8, 1)
-    w_far = shift(w_below, RING8, 1)
-    weights = [w_out, w_above, w_far, w_below]
 
     half = toks // 2
     above, below = shift(g, "y", -1), shift(g, "y", 1)
     pieces = [g, above, shift(after(above[:half], acts), "y", -1), shift(after(below[half:], acts), "y", 1), below]
     pieces += [shift(p, "c", 1) for p in pieces]
 
+    half = heads // 2
+    w = after(w_out, a)
+    w_above, w_below = shift(w, RING8, -1), shift(w, RING8, 1)
+    w_far = [shift(w_above[:half], RING8, -1), shift(w_below[half:], RING8, 1)]
+
+    part = partial(at, after(acts, *w_far), pieces, 0, cut)
+    tot = lax.psum_scatter(part.reshape(4 * heads, cut), "x", scatter_dimension=0, tiled=True)
+    part = partial(at, after(acts, part), pieces, cut, feats)
+    other = exchange(part, "x")
+
+    weights = [after(w_out, part), w_above, *w_far, w_below]
+    res = inputs_grad(at, pieces, weights)
+    back = [pick(res, l)] + [shift(pick(res, (l + d) & 3), "l", d) for d in (1, 2, 3)]
+
+    other = after(other, *back[1:]).astype(F32).sum(0).astype(BF16)
+    tot = jnp.concatenate([tot.reshape(4, heads // 4, cut), other], 2)
     x = at[0]
-    first = [after(g, *weights[1:])] + pieces[1:]
-    tots = []
-    for lo, hi in cuts:
-        part = partial(at, acts, first, lo, hi)
-        first = [after(g, part)] + pieces[1:]
-        tots.append(exchange(part, "x").astype(F32).sum(0).astype(BF16))
-
-    res = inputs_grad(at, first, weights)
-    back = [pick(res, l)] + [shift(pick(res, (l + d) & 3), "l", d) for d in (1, 2, 3)]
-
+    half = heads // 8
+    far = pick(tot, (l + 2) & 3)
+    acc = pick(tot, l).astype(F32)
+    for d in (1, -1):
+        acc = acc + shift(pick(tot, (l + d) & 3), RING8, d).astype(F32)
+    acc = acc + jnp.concatenate([shift(far[:half], RING8, -2), shift(far[half:], RING8, 2)], 0).astype(F32)
+    acc = acc.astype(BF16)
+    acc = (acc.astype(F32) + shift(acc, "h", 1).astype(F32)).astype(BF16)
     grad_w = jnp.zeros((4, heads // 4, feats), BF16)
-    for j, ((lo, hi), tot) in enumerate(zip(cuts, tots)):
-        acc = pick(tot, l).astype(F32)
-        for d in (1, -1, -2 if j % 2 else 2):
-            acc = acc + shift(pick(tot, (l + d) & 3), RING8, d).astype(F32)
-        acc = acc.astype(BF16)
-        acc = (acc.astype(F32) + shift(acc, "h", 1).astype(F32)).astype(BF16)
-        for d in range(4):
-            grad_w = lax.dynamic_update_slice(
-                grad_w, (shift(acc, "x", d) if d else acc)[None], ((x - d) & 3, 0, lo))
+    for d in range(4):
+        grad_w = lax.dynamic_update_slice_in_dim(
+            grad_w, (shift(acc, "x", d) if d else acc)[None], (x - d) & 3, 0)
     grad_w = grad_w.reshape(heads, feats)
 
     out = jnp.zeros((4, 4, 2, toks, heads), BF16)

time: 198 us -> 189 us (0.955)
  starting transfers between devices: 54.3 us -> 39.4 us
  between operations: 0.86 us -> 14.3 us
  waiting for transfers between devices: 98.8 us -> 94.4 us
  local copies, waits for them, and re-layouts: 14.9 us -> 12.4 us
    ppermute x29 -> x24, starting transfers between devices: 42.1 us -> 30.5 us  [shift(): return lax.ppermute(v, axis, [(i, (i + by) % n) for i in range(n)])]
    all_to_all x3 -> x2, waiting for transfers between devices: 23.5 us -> 14.3 us  [exchange(): return lax.all_to_all(v, axis, split_axis=0, concat_axis=0, tiled=True)]
    ppermute x29 -> x24, waiting for transfers between devices: 75.3 us -> 80 us  [shift(): return lax.ppermute(v, axis, [(i, (i + by) % n) for i in range(n)])]
    dynamic_update_slice x4, local copies, waits for them, and re-layouts: 5.85 us -> 2.06 us  [local(): out = lax.dynamic_update_slice_in_dim(out, piece[:, None], l - d & 3, 1)]
    all_to_all x3 -> x2, starting transfers between devices: 12.2 us -> 8.82 us  [exchange(): return lax.all_to_all(v, axis, split_axis=0, concat_axis=0, tiled=True)]
    slice x0 -> x3, local copies, waits for them, and re-layouts: none -> 2.17 us  [the longest x2 2.15 us: local(): w_far = [shift(w_above[:half], RING8, -1), shift(w_below[half:], RING8, 1)]]
  transfers between devices with their start and end apart: 32 -> 27, of which waited for: 18 -> 15; matrix products, arithmetic and copies ran while one was open for 9% -> 6% of each run, Pallas kernels for 8% -> 9%
where the time goes in v5:
time: 189 us; the launch traced here: 188 us
  waiting for transfers between devices  94.4 us (50%)
  starting transfers between devices  39.4 us (21%)
  Pallas kernels  25.5 us (13%)
  between operations  14.3 us (8%)
  local copies, waits for them, and re-layouts  12.4 us (7%)
  other arithmetic  2.4 us (1%)
    ppermute x24, waiting for transfers between devices, shift(): return lax.ppermute(v, axis, [(i, (i + by) % n) for i in range(n)])  80 us
    ppermute x24, starting transfers between devices, shift(): return lax.ppermute(v, axis, [(i, (i + by) % n) for i in range(n)])  30.5 us
    pallas_call x2, Pallas kernels, partial(): pl.pallas_call(lambda *refs: partial_kernel(lo, *refs), grid_spec=pltpu.P...  15.2 us
    all_to_all x2, waiting for transfers between devices, exchange(): return lax.all_to_all(v, axis, split_axis=0, concat_axis=0, tiled=True)  14.3 us
    pallas_call x1, Pallas kernels, inputs_grad(): pl.pallas_call(inputs_kernel, grid_spec=pltpu.PrefetchScalarGridSpec(num_...  10.3 us
    all_to_all x2, starting transfers between devices, exchange(): return lax.all_to_all(v, axis, split_axis=0, concat_axis=0, tiled=True)  8.82 us
  transfers between devices with their start and end apart: 27, of which 15 were waited for; matrix products, arithmetic and copies ran while one was open for 6% of the time, Pallas kernels for 9%

profile of v5, /device:TPU:64, one launch (start us, length us, event | category | flops | bytes accessed | tf_op | source)
XLA Modules:
  0.0 188.3 jit_solution(11389694427654719104)
XLA Ops:
  7.2 3.1 %collective-permute-start = (bf16[128,4096]{1,0:T(8,128)(2,1)}, bf16[128,4096]{1,0:T(8,128)(2,1)S(1)}, u32[]{:S(2)}, u32[]{:S(2)}) collective-permute-start(bf16[128,4096]{1,0:T(8,128)(2,1)} %bitcast.50), channel_id=1, source_target_pairs={{0,24},{8,0},{16,8},{24,16},{1,25},{9,1},{17,9},{25,17},{2,26},{10... | collective-permute-start | bytes 3145736 | tf_op jit(solution)/shard_map/ppermute | solution.py:15
  10.3 1.8 reshape_squeeze.3
  12.1 2.1 %copy.5 = bf16[4,2,4,128,128]{4,3,2,1,0:T(8,128)(2,1)} copy(bf16[4,2,4,128,128]{3,1,2,0,4:T(2,128)(2,1)S(1)} %bitcast.57) | data formatting | bytes 2097152 | tf_op jit(solution)/shard_map/transpose | solution.py:156
  14.1 4.5 %all-to-all-start = ((bf16[8,512,128]{2,1,0:T(8,128)(2,1)}), bf16[8,512,128]{2,1,0:T(8,128)(2,1)S(1)}, u32[]{:S(2)}, u32[]{:S(2)}) async-start(bf16[8,512,128]{2,1,0:T(8,128)(2,1)} %bitcast.56), calls=%async_computation | async-start | bytes 2097152 | tf_op jit(solution)/shard_map/all_to_all | solution.py:19
  18.9 1.9 %collective-permute-start.11 = (bf16[128,4096]{1,0:T(8,128)(2,1)}, bf16[128,4096]{1,0:T(8,128)(2,1)}, u32[]{:S(2)}, u32[]{:S(2)}) collective-permute-start(bf16[128,4096]{1,0:T(8,128)(2,1)} %refs_10_), channel_id=1, source_target_pairs={{0,2},{2,4},{4,6},{6,32},{32,34},{34,36},{36,38},{38,0},{1,3},{3,5... | collective-permute-start | bytes 3145736 | tf_op jit(solution)/shard_map/ppermute | solution.py:15
  20.8 14.7 %collective-permute-done.refs_3_.refs_1_ = bf16[128,4096]{1,0:T(8,128)(2,1)S(1)} collective-permute-done((bf16[128,4096]{1,0:T(8,128)(2,1)}, bf16[128,4096]{1,0:T(8,128)(2,1)S(1)}, u32[]{:S(2)}, u32[]{:S(2)}) %collective-permute-start) | collective-permute-done | bytes 1048608 | tf_op jit(solution)/shard_map/ppermute | solution.py:15
  36.5 11.1 %all-to-all-done = bf16[8,512,128]{2,1,0:T(8,128)(2,1)S(1)} async-done(((bf16[8,512,128]{2,1,0:T(8,128)(2,1)}), bf16[8,512,128]{2,1,0:T(8,128)(2,1)S(1)}, u32[]{:S(2)}, u32[]{:S(2)}) %all-to-all-start) | async-done | bytes 1048608 | tf_op jit(solution)/shard_map/all_to_all | solution.py:19
  47.9 1.8 collective-permute-start.3
  52.0 2.0 %collective-permute-start.12 = (bf16[64,4096]{1,0:T(8,128)(2,1)S(1)}, bf16[64,4096]{1,0:T(8,128)(2,1)S(1)}, u32[]{:S(2)}, u32[]{:S(2)}) collective-permute-start(bf16[64,4096]{1,0:T(8,128)(2,1)S(1)} %slice.35), channel_id=1, source_target_pairs={{0,2},{2,4},{4,6},{6,32},{32,34},{34,36},{36,38},{38,0},{1,3},{3,5... | collective-permute-start | bytes 1572872 | tf_op jit(solution)/shard_map/ppermute | solution.py:15
  54.0 5.1 %collective-permute-done.1.refs_4_.refs_2_ = bf16[64,4096]{1,0:T(8,128)(2,1)} collective-permute-done((bf16[64,4096]{1,0:T(8,128)(2,1)}, bf16[64,4096]{1,0:T(8,128)(2,1)}, u32[]{:S(2)}, u32[]{:S(2)}) %collective-permute-start.1) | collective-permute-done | bytes 524320 | tf_op jit(solution)/shard_map/ppermute | solution.py:15
  59.2 1.1 collective-permute-done.3.refs_5_.refs_3_
  60.3 5.0 %collective-permute-done.10.refs_12_ = bf16[64,4096]{1,0:T(8,128)(2,1)S(1)} collective-permute-done((bf16[64,4096]{1,0:T(8,128)(2,1)S(1)}, bf16[64,4096]{1,0:T(8,128)(2,1)S(1)}, u32[]{:S(2)}, u32[]{:S(2)}) %collective-permute-start.10) | collective-permute-done | bytes 524320 | tf_op jit(solution)/shard_map/ppermute | solution.py:15
  68.7 7.6 %partial_grad_w.2 = bf16[4,4,32,2048]{3,2,1,0:T(8,128)(2,1)} custom-call(s32[4]{0:T(128)} %pad_add_fusion.refs_0_.at, bf16[4,2,512,128]{3,2,1,0:T(8,128)(2,1)} %bitcast.47, bf16[128,4096]{1,0:T(8,128)(2,1)} %bitcast.53, bf16[128,4096]{1,0:T(8,128)(2,1)} %copy-done.1, bf16[64,4096]{1,0:T(8,128)(2,1)} %collective-permute-done.1.refs_4_.refs_2_, ...), custom_call_target="tpu_custom_call" | custom-call | flops 2147483648 | bytes 7340032 | tf_op jit(solution)/shard_map/partial_grad_w/pallas_call | solution.py:79
  76.3 7.6 %partial_grad_w.3 = bf16[4,4,32,2048]{3,2,1,0:T(8,128)(2,1)} custom-call(s32[4]{0:T(128)} %pad_add_fusion.refs_0_.at, bf16[4,2,512,128]{3,2,1,0:T(8,128)(2,1)} %bitcast.48, bf16[128,4096]{1,0:T(8,128)(2,1)} %bitcast.54, bf16[128,4096]{1,0:T(8,128)(2,1)} %copy-done.1, bf16[64,4096]{1,0:T(8,128)(2,1)} %collective-permute-done.1.refs_4_.refs_2_, ...), custom_call_target="tpu_custom_call" | custom-call | flops 2147483648 | bytes 7340032 | tf_op jit(solution)/shard_map/partial_grad_w/pallas_call | solution.py:79
  83.9 4.3 %all-to-all-start.1 = ((bf16[4,4,32,2048]{3,2,1,0:T(8,128)(2,1)}), bf16[4,4,32,2048]{3,2,1,0:T(8,128)(2,1)S(1)}, u32[]{:S(2)}, u32[]{:S(2)}) async-start(bf16[4,4,32,2048]{3,2,1,0:T(8,128)(2,1)} %partial_grad_w.3), calls=%async_computation.2 | async-start | bytes 4194304 | tf_op jit(solution)/shard_map/all_to_all | solution.py:19
  88.2 10.3 %grad_attn.1 = bf16[4,4,2,128,128]{4,3,2,1,0:T(8,128)(2,1)} custom-call(s32[4]{0:T(128)} %pad_add_fusion.refs_0_.at, bf16[128,4096]{1,0:T(8,128)(2,1)} %bitcast.55, bf16[128,4096]{1,0:T(8,128)(2,1)} %copy-done.1, bf16[64,4096]{1,0:T(8,128)(2,1)} %collective-permute-done.1.refs_4_.refs_2_, bf16[64,4096]{1,0:T(8,128)(2,1)} %collective-permute-done.3.refs_5_.refs_3_, ...), custom_call_target="tpu_custom_call" | custom-call | flops 4294967296 | bytes 13631488 | tf_op jit(solution)/shard_map/grad_attn/pallas_call | solution.py:129
  98.5 1.2 dynamic-slice_bitcast_fusion
  99.7 2.7 %collective-permute-start.13 = (bf16[4,2,128,128]{3,2,1,0:T(8,128)(2,1)S(1)}, bf16[4,2,128,128]{3,2,1,0:T(8,128)(2,1)}, u32[]{:S(2)}, u32[]{:S(2)}) collective-permute-start(bf16[4,2,128,128]{3,2,1,0:T(8,128)(2,1)S(1)} %get-tuple-element.23), channel_id=1, source_target_pairs={{0,2},{2,4},{4,6},{6,0},{1,3},{3,5},{5,7},{7,1},{8,10},{10,12},{12... | collective-permute-start | bytes 786440 | tf_op jit(solution)/shard_map/ppermute | solution.py:15
  102.4 3.6 %collective-permute-start.14 = (bf16[4,2,128,128]{3,2,1,0:T(8,128)(2,1)S(1)}, bf16[4,2,128,128]{3,2,1,0:T(8,128)(2,1)S(1)}, u32[]{:S(2)}, u32[]{:S(2)}) collective-permute-start(bf16[4,2,128,128]{3,2,1,0:T(8,128)(2,1)S(1)} %get-tuple-element.22), channel_id=1, source_target_pairs={{0,4},{2,6},{4,0},{6,2},{1,5},{3,7},{5,1},{7,3},{8,12},{10,14},{12... | collective-permute-start | bytes 786440 | tf_op jit(solution)/shard_map/ppermute | solution.py:15
  106.0 2.8 %collective-permute-start.15 = (bf16[4,2,128,128]{3,2,1,0:T(8,128)(2,1)S(1)}, bf16[4,2,128,128]{3,2,1,0:T(8,128)(2,1)S(1)}, u32[]{:S(2)}, u32[]{:S(2)}) collective-permute-start(bf16[4,2,128,128]{3,2,1,0:T(8,128)(2,1)S(1)} %get-tuple-element.21), channel_id=1, source_target_pairs={{0,6},{2,0},{4,2},{6,4},{1,7},{3,1},{5,3},{7,5},{8,14},{10,8},{12,... | collective-permute-start | bytes 786440 | tf_op jit(solution)/shard_map/ppermute | solution.py:15
  108.8 1.9 %collective-permute-done.13 = bf16[4,2,128,128]{3,2,1,0:T(8,128)(2,1)} collective-permute-done((bf16[4,2,128,128]{3,2,1,0:T(8,128)(2,1)S(1)}, bf16[4,2,128,128]{3,2,1,0:T(8,128)(2,1)}, u32[]{:S(2)}, u32[]{:S(2)}) %collective-permute-start.13) | collective-permute-done | bytes 262176 | tf_op jit(solution)/shard_map/ppermute | solution.py:15
  110.7 13.0 %collective-permute-done.14 = bf16[4,2,128,128]{3,2,1,0:T(8,128)(2,1)S(1)} collective-permute-done((bf16[4,2,128,128]{3,2,1,0:T(8,128)(2,1)S(1)}, bf16[4,2,128,128]{3,2,1,0:T(8,128)(2,1)S(1)}, u32[]{:S(2)}, u32[]{:S(2)}) %collective-permute-start.14) | collective-permute-done | bytes 262176 | tf_op jit(solution)/shard_map/ppermute | solution.py:15
  123.7 4.7 %collective-permute-done.15 = bf16[4,2,128,128]{3,2,1,0:T(8,128)(2,1)S(1)} collective-permute-done((bf16[4,2,128,128]{3,2,1,0:T(8,128)(2,1)S(1)}, bf16[4,2,128,128]{3,2,1,0:T(8,128)(2,1)S(1)}, u32[]{:S(2)}, u32[]{:S(2)}) %collective-permute-start.15) | collective-permute-done | bytes 262176 | tf_op jit(solution)/shard_map/ppermute | solution.py:15
  128.4 3.2 %all-to-all-done.1 = bf16[4,4,32,2048]{3,2,1,0:T(8,128)(2,1)S(1)} async-done(((bf16[4,4,32,2048]{3,2,1,0:T(8,128)(2,1)}), bf16[4,4,32,2048]{3,2,1,0:T(8,128)(2,1)S(1)}, u32[]{:S(2)}, u32[]{:S(2)}) %all-to-all-start.1) | async-done | bytes 2097184 | tf_op jit(solution)/shard_map/all_to_all | solution.py:19
  132.1 1.1 fusion.3
  133.3 2.0 %collective-permute-start.16 = (bf16[32,4096]{1,0:T(8,128)(2,1)S(1)}, bf16[32,4096]{1,0:T(8,128)(2,1)S(1)}, u32[]{:S(2)}, u32[]{:S(2)}) collective-permute-start(bf16[32,4096]{1,0:T(8,128)(2,1)S(1)} %get-tuple-element.19), channel_id=1, source_target_pairs={{0,2},{2,4},{4,6},{6,32},{32,34},{34,36},{36,38},{38,0},{1,3},{3,5... | collective-permute-start | bytes 786440 | tf_op jit(solution)/shard_map/ppermute | solution.py:15
  135.4 2.2 %collective-permute-start.18 = (bf16[16,4096]{1,0:T(8,128)(2,1)S(1)}, bf16[16,4096]{1,0:T(8,128)(2,1)S(1)}, u32[]{:S(2)}, u32[]{:S(2)}) collective-permute-start(bf16[16,4096]{1,0:T(8,128)(2,1)S(1)} %get-tuple-element.24), channel_id=1, source_target_pairs={{0,36},{2,38},{4,0},{6,2},{32,4},{34,6},{36,32},{38,34},{1,37},{3,... | collective-permute-start | bytes 393224 | tf_op jit(solution)/shard_map/ppermute | solution.py:15
  137.7 3.3 %collective-permute-start.19 = (bf16[16,4096]{1,0:T(8,128)(2,1)S(1)}, bf16[16,4096]{1,0:T(8,128)(2,1)S(1)}, u32[]{:S(2)}, u32[]{:S(2)}) collective-permute-start(bf16[16,4096]{1,0:T(8,128)(2,1)S(1)} %get-tuple-element.25), channel_id=1, source_target_pairs={{0,4},{2,6},{4,32},{6,34},{32,36},{34,38},{36,0},{38,2},{1,5},{3,7... | collective-permute-start | bytes 393224 | tf_op jit(solution)/shard_map/ppermute | solution.py:15
  141.0 11.0 %collective-permute-done.18 = bf16[16,4096]{1,0:T(8,128)(2,1)S(1)} collective-permute-done((bf16[16,4096]{1,0:T(8,128)(2,1)S(1)}, bf16[16,4096]{1,0:T(8,128)(2,1)S(1)}, u32[]{:S(2)}, u32[]{:S(2)}) %collective-permute-start.18) | collective-permute-done | bytes 131104 | tf_op jit(solution)/shard_map/ppermute | solution.py:15
  155.2 10.3 %collective-permute-done.20 = bf16[32,4096]{1,0:T(8,128)(2,1)S(1)} collective-permute-done((bf16[32,4096]{1,0:T(8,128)(2,1)S(1)}, bf16[32,4096]{1,0:T(8,128)(2,1)S(1)}, u32[]{:S(2)}, u32[]{:S(2)}) %collective-permute-start.20) | collective-permute-done | bytes 262176 | tf_op jit(solution)/shard_map/ppermute | solution.py:15
  166.4 2.1 %collective-permute-start.22 = (bf16[32,4096]{1,0:T(8,128)(2,1)S(1)}, bf16[32,4096]{1,0:T(8,128)(2,1)S(1)}, u32[]{:S(2)}, u32[]{:S(2)}) collective-permute-start(bf16[32,4096]{1,0:T(8,128)(2,1)S(1)} %get-tuple-element.17), channel_id=1, source_target_pairs={{0,128},{64,192},{128,0},{192,64},{1,129},{65,193},{129,1},{193,65... | collective-permute-start | bytes 786440 | tf_op jit(solution)/shard_map/ppermute | solution.py:15
  169.3 10.4 %collective-permute-done.21 = bf16[32,4096]{1,0:T(8,128)(2,1)S(1)} collective-permute-done((bf16[32,4096]{1,0:T(8,128)(2,1)S(1)}, bf16[32,4096]{1,0:T(8,128)(2,1)S(1)}, u32[]{:S(2)}, u32[]{:S(2)}) %collective-permute-start.21) | collective-permute-done | bytes 262176 | tf_op jit(solution)/shard_map/ppermute | solution.py:15
  (64 shorter events, 14.2 us)
Async XLA Ops:
  7.2 28.4 %collective-permute-start = (bf16[128,4096]{1,0:T(8,128)(2,1)}, bf16[128,4096]{1,0:T(8,128)(2,1)S(1)}, u32[]{:S(2)}, u32[]{:S(2)}) collective-permute-start(bf16[128,4096]{1,0:T(8,128)(2,1)} %bitcast.50), channel_id=1, source_target_pairs={{0,24},{8,0},{16,8},{24,16},{1,25},{9,1},{17,9},{25,17},{2,26},{10... | collective-permute-start | bytes 3145736 | tf_op jit(solution)/shard_map/ppermute | solution.py:15
  10.3 37.6 %collective-permute-start.2 = (bf16[128,4096]{1,0:T(8,128)(2,1)}, bf16[128,4096]{1,0:T(8,128)(2,1)S(1)}, u32[]{:S(2)}, u32[]{:S(2)}) collective-permute-start(bf16[128,4096]{1,0:T(8,128)(2,1)} %bitcast.51), channel_id=1, source_target_pairs={{0,8},{8,16},{16,24},{24,0},{1,9},{9,17},{17,25},{25,1},{2,10},{10... | collective-permute-start | bytes 3145736 | tf_op jit(solution)/shard_map/ppermute | solution.py:15
  14.1 33.4 %all-to-all-start = ((bf16[8,512,128]{2,1,0:T(8,128)(2,1)}), bf16[8,512,128]{2,1,0:T(8,128)(2,1)S(1)}, u32[]{:S(2)}, u32[]{:S(2)}) async-start(bf16[8,512,128]{2,1,0:T(8,128)(2,1)} %bitcast.56), calls=%async_computation | async-start | bytes 2097152 | tf_op jit(solution)/shard_map/all_to_all | solution.py:19
  18.7 113.5 %reduce-scatter.2.cloned.1.call-start = ((), (), s32[]{:S(2)}) async-start(), calls=%async_computation.3 | async-start | bytes 2621440 | tf_op jit(solution)/shard_map/reduce_scatter | solution.py:170
  18.7 31.0 %collective-permute-start.9 = (bf16[128,4096]{1,0:T(8,128)(2,1)}, bf16[128,4096]{1,0:T(8,128)(2,1)}, u32[]{:S(2)}, u32[]{:S(2)}) collective-permute-start(bf16[128,4096]{1,0:T(8,128)(2,1)} %refs_10_), channel_id=1, source_target_pairs={{0,38},{2,0},{4,2},{6,4},{32,6},{34,32},{36,34},{38,36},{1,39},{3,... | collective-permute-start | bytes 3145736 | tf_op jit(solution)/shard_map/ppermute | solution.py:15
  18.9 32.0 %collective-permute-start.11 = (bf16[128,4096]{1,0:T(8,128)(2,1)}, bf16[128,4096]{1,0:T(8,128)(2,1)}, u32[]{:S(2)}, u32[]{:S(2)}) collective-permute-start(bf16[128,4096]{1,0:T(8,128)(2,1)} %refs_10_), channel_id=1, source_target_pairs={{0,2},{2,4},{4,6},{6,32},{32,34},{34,36},{36,38},{38,0},{1,3},{3,5... | collective-permute-start | bytes 3145736 | tf_op jit(solution)/shard_map/ppermute | solution.py:15
  35.5 23.6 %copy-start.1 = (bf16[128,4096]{1,0:T(8,128)(2,1)}, bf16[128,4096]{1,0:T(8,128)(2,1)S(1)}, u32[]{:S(2)}) copy-start(bf16[128,4096]{1,0:T(8,128)(2,1)S(1)} %collective-permute-done.refs_3_.refs_1_) | copy-start | bytes 3145732
  47.5 21.1 %copy-start = (bf16[8,512,128]{2,1,0:T(8,128)(2,1)}, bf16[8,512,128]{2,1,0:T(8,128)(2,1)S(1)}, u32[]{:S(2)}) copy-start(bf16[8,512,128]{2,1,0:T(8,128)(2,1)S(1)} %all-to-all-done) | copy-start | bytes 3145732
  47.5 11.6 %collective-permute-start.1 = (bf16[64,4096]{1,0:T(8,128)(2,1)}, bf16[64,4096]{1,0:T(8,128)(2,1)}, u32[]{:S(2)}, u32[]{:S(2)}) collective-permute-start(bf16[64,4096]{1,0:T(8,128)(2,1)} %slice.32), channel_id=1, source_target_pairs={{0,24},{8,0},{16,8},{24,16},{1,25},{9,1},{17,9},{25,17},{2,26},{10... | collective-permute-start | bytes 1572872 | tf_op jit(solution)/shard_map/ppermute | solution.py:15
  47.8 20.8 %copy-start.2 = (bf16[128,4096]{1,0:T(8,128)(2,1)}, bf16[128,4096]{1,0:T(8,128)(2,1)S(1)}, u32[]{:S(2)}) copy-start(bf16[128,4096]{1,0:T(8,128)(2,1)S(1)} %collective-permute-done.2.refs_6_.refs_4_) | copy-start | bytes 3145732
  47.9 12.4 %collective-permute-start.3 = (bf16[64,4096]{1,0:T(8,128)(2,1)S(1)}, bf16[64,4096]{1,0:T(8,128)(2,1)}, u32[]{:S(2)}, u32[]{:S(2)}) collective-permute-start(bf16[64,4096]{1,0:T(8,128)(2,1)S(1)} %slice.33), channel_id=1, source_target_pairs={{0,8},{8,16},{16,24},{24,0},{1,9},{9,17},{17,25},{25,1},{2,10},{10... | collective-permute-start | bytes 1572872 | tf_op jit(solution)/shard_map/ppermute | solution.py:15
  49.7 18.1 %collective-permute-start.4 = (bf16[128,4096]{1,0:T(8,128)(2,1)}, bf16[128,4096]{1,0:T(8,128)(2,1)}, u32[]{:S(2)}, u32[]{:S(2)}) collective-permute-start(bf16[128,4096]{1,0:T(8,128)(2,1)} %bitcast.52), channel_id=1, source_target_pairs={{0,1},{1,0},{2,3},{3,2},{4,5},{5,4},{6,7},{7,6},{8,9},{9,8},{10,11... | collective-permute-start | bytes 3145736 | tf_op jit(solution)/shard_map/ppermute | solution.py:15
  50.8 14.6 %collective-permute-start.10 = (bf16[64,4096]{1,0:T(8,128)(2,1)S(1)}, bf16[64,4096]{1,0:T(8,128)(2,1)S(1)}, u32[]{:S(2)}, u32[]{:S(2)}) collective-permute-start(bf16[64,4096]{1,0:T(8,128)(2,1)S(1)} %slice.34), channel_id=1, source_target_pairs={{0,38},{2,0},{4,2},{6,4},{32,6},{34,32},{36,34},{38,36},{1,39},{3,... | collective-permute-start | bytes 1572872 | tf_op jit(solution)/shard_map/ppermute | solution.py:15
  52.0 14.3 %collective-permute-start.12 = (bf16[64,4096]{1,0:T(8,128)(2,1)S(1)}, bf16[64,4096]{1,0:T(8,128)(2,1)S(1)}, u32[]{:S(2)}, u32[]{:S(2)}) collective-permute-start(bf16[64,4096]{1,0:T(8,128)(2,1)S(1)} %slice.35), channel_id=1, source_target_pairs={{0,2},{2,4},{4,6},{6,32},{32,34},{34,36},{36,38},{38,0},{1,3},{3,5... | collective-permute-start | bytes 1572872 | tf_op jit(solution)/shard_map/ppermute | solution.py:15
  59.2 9.5 %collective-permute-start.5 = (bf16[128,4096]{1,0:T(8,128)(2,1)S(1)}, bf16[128,4096]{1,0:T(8,128)(2,1)}, u32[]{:S(2)}, u32[]{:S(2)}) collective-permute-start(bf16[128,4096]{1,0:T(8,128)(2,1)S(1)} %collective-permute-done.refs_3_.refs_1_), channel_id=1, source_target_pairs={{0,1},{1,0},{2,3},{3,2},{4,5},{5,4},{6,7},{7,6},{8,9},{9,8},{10,11... | collective-permute-start | bytes 3145736 | tf_op jit(solution)/shard_map/ppermute | solution.py:15
  60.3 8.3 %collective-permute-start.8 = (bf16[128,4096]{1,0:T(8,128)(2,1)S(1)}, bf16[128,4096]{1,0:T(8,128)(2,1)}, u32[]{:S(2)}, u32[]{:S(2)}) collective-permute-start(bf16[128,4096]{1,0:T(8,128)(2,1)S(1)} %collective-permute-done.2.refs_6_.refs_4_), channel_id=1, source_target_pairs={{0,1},{1,0},{2,3},{3,2},{4,5},{5,4},{6,7},{7,6},{8,9},{9,8},{10,11... | collective-permute-start | bytes 3145736 | tf_op jit(solution)/shard_map/ppermute | solution.py:15
  65.4 2.4 %collective-permute-start.6 = (bf16[64,4096]{1,0:T(8,128)(2,1)}, bf16[64,4096]{1,0:T(8,128)(2,1)}, u32[]{:S(2)}, u32[]{:S(2)}) collective-permute-start(bf16[64,4096]{1,0:T(8,128)(2,1)} %collective-permute-done.1.refs_4_.refs_2_), channel_id=1, source_target_pairs={{0,1},{1,0},{2,3},{3,2},{4,5},{5,4},{6,7},{7,6},{8,9},{9,8},{10,11... | collective-permute-start | bytes 1572872 | tf_op jit(solution)/shard_map/ppermute | solution.py:15
  66.4 2.3 %collective-permute-start.7 = (bf16[64,4096]{1,0:T(8,128)(2,1)}, bf16[64,4096]{1,0:T(8,128)(2,1)}, u32[]{:S(2)}, u32[]{:S(2)}) collective-permute-start(bf16[64,4096]{1,0:T(8,128)(2,1)} %collective-permute-done.3.refs_5_.refs_3_), channel_id=1, source_target_pairs={{0,1},{1,0},{2,3},{3,2},{4,5},{5,4},{6,7},{7,6},{8,9},{9,8},{10,11... | collective-permute-start | bytes 1572872 | tf_op jit(solution)/shard_map/ppermute | solution.py:15
  83.9 47.8 %all-to-all-start.1 = ((bf16[4,4,32,2048]{3,2,1,0:T(8,128)(2,1)}), bf16[4,4,32,2048]{3,2,1,0:T(8,128)(2,1)S(1)}, u32[]{:S(2)}, u32[]{:S(2)}) async-start(bf16[4,4,32,2048]{3,2,1,0:T(8,128)(2,1)} %partial_grad_w.3), calls=%async_computation.2 | async-start | bytes 4194304 | tf_op jit(solution)/shard_map/all_to_all | solution.py:19
  99.7 11.0 %collective-permute-start.13 = (bf16[4,2,128,128]{3,2,1,0:T(8,128)(2,1)S(1)}, bf16[4,2,128,128]{3,2,1,0:T(8,128)(2,1)}, u32[]{:S(2)}, u32[]{:S(2)}) collective-permute-start(bf16[4,2,128,128]{3,2,1,0:T(8,128)(2,1)S(1)} %get-tuple-element.23), channel_id=1, source_target_pairs={{0,2},{2,4},{4,6},{6,0},{1,3},{3,5},{5,7},{7,1},{8,10},{10,12},{12... | collective-permute-start | bytes 786440 | tf_op jit(solution)/shard_map/ppermute | solution.py:15
  102.4 21.3 %collective-permute-start.14 = (bf16[4,2,128,128]{3,2,1,0:T(8,128)(2,1)S(1)}, bf16[4,2,128,128]{3,2,1,0:T(8,128)(2,1)S(1)}, u32[]{:S(2)}, u32[]{:S(2)}) collective-permute-start(bf16[4,2,128,128]{3,2,1,0:T(8,128)(2,1)S(1)} %get-tuple-element.22), channel_id=1, source_target_pairs={{0,4},{2,6},{4,0},{6,2},{1,5},{3,7},{5,1},{7,3},{8,12},{10,14},{12... | collective-permute-start | bytes 786440 | tf_op jit(solution)/shard_map/ppermute | solution.py:15
  106.0 22.5 %collective-permute-start.15 = (bf16[4,2,128,128]{3,2,1,0:T(8,128)(2,1)S(1)}, bf16[4,2,128,128]{3,2,1,0:T(8,128)(2,1)S(1)}, u32[]{:S(2)}, u32[]{:S(2)}) collective-permute-start(bf16[4,2,128,128]{3,2,1,0:T(8,128)(2,1)S(1)} %get-tuple-element.21), channel_id=1, source_target_pairs={{0,6},{2,0},{4,2},{6,4},{1,7},{3,1},{5,3},{7,5},{8,14},{10,8},{12,... | collective-permute-start | bytes 786440 | tf_op jit(solution)/shard_map/ppermute | solution.py:15
  132.1 19.9 %copy-start.3 = (bf16[128,2048]{1,0:T(8,128)(2,1)S(1)}, bf16[128,2048]{1,0:T(8,128)(2,1)}, u32[]{:S(2)}) copy-start(bf16[128,2048]{1,0:T(8,128)(2,1)} %reduce-scatter.2.cloned.1.call-done) | copy-start | bytes 1572868
  133.3 18.7 %collective-permute-start.16 = (bf16[32,4096]{1,0:T(8,128)(2,1)S(1)}, bf16[32,4096]{1,0:T(8,128)(2,1)S(1)}, u32[]{:S(2)}, u32[]{:S(2)}) collective-permute-start(bf16[32,4096]{1,0:T(8,128)(2,1)S(1)} %get-tuple-element.19), channel_id=1, source_target_pairs={{0,2},{2,4},{4,6},{6,32},{32,34},{34,36},{36,38},{38,0},{1,3},{3,5... | collective-permute-start | bytes 786440 | tf_op jit(solution)/shard_map/ppermute | solution.py:15
  135.3 16.7 %collective-permute-start.17 = (bf16[32,4096]{1,0:T(8,128)(2,1)S(1)}, bf16[32,4096]{1,0:T(8,128)(2,1)S(1)}, u32[]{:S(2)}, u32[]{:S(2)}) collective-permute-start(bf16[32,4096]{1,0:T(8,128)(2,1)S(1)} %get-tuple-element.20), channel_id=1, source_target_pairs={{0,38},{2,0},{4,2},{6,4},{32,6},{34,32},{36,34},{38,36},{1,39},{3,... | collective-permute-start | bytes 786440 | tf_op jit(solution)/shard_map/ppermute | solution.py:15
  135.4 16.6 %collective-permute-start.18 = (bf16[16,4096]{1,0:T(8,128)(2,1)S(1)}, bf16[16,4096]{1,0:T(8,128)(2,1)S(1)}, u32[]{:S(2)}, u32[]{:S(2)}) collective-permute-start(bf16[16,4096]{1,0:T(8,128)(2,1)S(1)} %get-tuple-element.24), channel_id=1, source_target_pairs={{0,36},{2,38},{4,0},{6,2},{32,4},{34,6},{36,32},{38,34},{1,37},{3,... | collective-permute-start | bytes 393224 | tf_op jit(solution)/shard_map/ppermute | solution.py:15
  137.7 14.3 %collective-permute-start.19 = (bf16[16,4096]{1,0:T(8,128)(2,1)S(1)}, bf16[16,4096]{1,0:T(8,128)(2,1)S(1)}, u32[]{:S(2)}, u32[]{:S(2)}) collective-permute-start(bf16[16,4096]{1,0:T(8,128)(2,1)S(1)} %get-tuple-element.25), channel_id=1, source_target_pairs={{0,4},{2,6},{4,32},{6,34},{32,36},{34,38},{36,0},{38,2},{1,5},{3,7... | collective-permute-start | bytes 393224 | tf_op jit(solution)/shard_map/ppermute | solution.py:15
  152.2 13.3 %collective-permute-start.20 = (bf16[32,4096]{1,0:T(8,128)(2,1)S(1)}, bf16[32,4096]{1,0:T(8,128)(2,1)S(1)}, u32[]{:S(2)}, u32[]{:S(2)}) collective-permute-start(bf16[32,4096]{1,0:T(8,128)(2,1)S(1)} %fusion.2), channel_id=1, source_target_pairs={{0,32},{32,0},{1,33},{33,1},{2,34},{34,2},{3,35},{35,3},{4,36},{36... | collective-permute-start | bytes 786440 | tf_op jit(solution)/shard_map/ppermute | solution.py:15
  165.7 13.9 %collective-permute-start.21 = (bf16[32,4096]{1,0:T(8,128)(2,1)S(1)}, bf16[32,4096]{1,0:T(8,128)(2,1)S(1)}, u32[]{:S(2)}, u32[]{:S(2)}) collective-permute-start(bf16[32,4096]{1,0:T(8,128)(2,1)S(1)} %get-tuple-element.17), channel_id=1, source_target_pairs={{0,64},{64,128},{128,192},{192,0},{1,65},{65,129},{129,193},{193,1... | collective-permute-start | bytes 786440 | tf_op jit(solution)/shard_map/ppermute | solution.py:15
  166.4 14.0 %copy-start.5 = (bf16[4,4,2,128,128]{4,3,2,1,0:T(8,128)(2,1)}, bf16[4,4,2,128,128]{4,3,2,1,0:T(8,128)(2,1)S(1)}, u32[]{:S(2)}) copy-start(bf16[4,4,2,128,128]{4,3,2,1,0:T(8,128)(2,1)S(1)} %bitcast_dynamic-update-slice_fusion.4) | copy-start | bytes 3145732
  166.4 13.2 %collective-permute-start.22 = (bf16[32,4096]{1,0:T(8,128)(2,1)S(1)}, bf16[32,4096]{1,0:T(8,128)(2,1)S(1)}, u32[]{:S(2)}, u32[]{:S(2)}) collective-permute-start(bf16[32,4096]{1,0:T(8,128)(2,1)S(1)} %get-tuple-element.17), channel_id=1, source_target_pairs={{0,128},{64,192},{128,0},{192,64},{1,129},{65,193},{129,1},{193,65... | collective-permute-start | bytes 786440 | tf_op jit(solution)/shard_map/ppermute | solution.py:15
  168.6 11.8 %collective-permute-start.23 = (bf16[32,4096]{1,0:T(8,128)(2,1)S(1)}, bf16[32,4096]{1,0:T(8,128)(2,1)S(1)}, u32[]{:S(2)}, u32[]{:S(2)}) collective-permute-start(bf16[32,4096]{1,0:T(8,128)(2,1)S(1)} %get-tuple-element.17), channel_id=1, source_target_pairs={{0,192},{64,0},{128,64},{192,128},{1,193},{65,1},{129,65},{193,129... | collective-permute-start | bytes 786440 | tf_op jit(solution)/shard_map/ppermute | solution.py:15
  (3 other events, 2.8 us)
Sparse Core Ops, SparseCore 0:
  76.4 50.3 reduce-scatter.1

commit v6 on v1

v6 whole, which is shorter than its diff:
```python
import jax
import jax.numpy as jnp
from jax import lax
from jax.sharding import Mesh, PartitionSpec as P

RING8 = ("h", "l")
F32, BF16 = jnp.float32, jnp.bfloat16


def shift(v, axis, by):
    n = lax.axis_size(axis)
    return lax.ppermute(v, axis, [(i, (i + by) % n) for i in range(n)])


def exchange(v, axis):
    return lax.all_to_all(v, axis, split_axis=0, concat_axis=0, tiled=True)


def after(v, *others):
    return lax.optimization_barrier((v, *others))[0]


def pick(v, index, axis=0):
    return lax.dynamic_index_in_dim(v, index, axis, keepdims=False)


def put(buffer, piece, *at):
    at = at + (0,) * (buffer.ndim - len(at))
    return lax.dynamic_update_slice(buffer, piece.reshape((1,) * (buffer.ndim - piece.ndim) + piece.shape), at)


def add(a, b):
    return (a.astype(F32) + b.astype(F32)).astype(BF16)


def local(grad_out, attn, w_out):
    g = grad_out[0]
    a = attn[0]
    toks, feats = g.shape
    heads = w_out.shape[0]
    x, y, l, c = (lax.axis_index(n) for n in ("x", "y", "l", "c"))

    a = a.reshape(toks, 4, 4, 2, heads).transpose(1, 3, 0, 2, 4).reshape(8, toks, 4 * heads)
    acts = exchange(a, ("y", "c")).reshape(8 * toks, 4 * heads)

    half = toks // 2
    above, below = shift(g, "y", -1), shift(g, "y", 1)
    far_a, far_b = shift(after(above[:half], acts), "y", -1), shift(after(below[half:], acts), "y", 1)
    tokens = jnp.zeros((4, 2, toks, feats), BF16)
    for piece, d, row in ((g, 0, 0), (above, 1, 0), (below, 3, 0), (far_a, 2, 0), (far_b, 2, half)):
        tokens = put(tokens, piece, (y + d) & 3, c, row)
        tokens = put(tokens, shift(piece, "c", 1), (y + d) & 3, 1 - c, row)
    tokens = tokens.reshape(8 * toks, feats)

    half = heads // 2
    w = after(w_out, a)
    weights = put(jnp.zeros((4, heads, feats), BF16), w_out, l)
    for d in (1, -1):
        weights = put(weights, shift(w, RING8, -d), (l + d) & 3)
    weights = put(weights, shift(w[:half], RING8, 2), (l + 2) & 3, 0)
    weights = put(weights, shift(w[half:], RING8, -2), (l + 2) & 3, half)
    weights = weights.reshape(4 * heads, feats)

    part = lax.dot_general(acts, tokens, (((0,), (0,)), ((), ())), preferred_element_type=F32).astype(BF16)
    part = part.reshape(4, 4, heads // 4, feats)
    own, near_a, far, near_b = (pick(part, (x + d) & 3, 1) for d in range(4))
    half = heads // 8
    far_a, far_b = shift(far[:, :half], "x", 1), shift(far[:, half:], "x", -1)

    res = lax.dot_general(
        after(tokens, part), weights, (((1,), (1,)), ((), ())), preferred_element_type=F32).astype(BF16)
    res = res.reshape(4, 2, toks, 4, heads)
    back = [pick(res, l, 3)] + [shift(pick(res, (l + d) & 3, 3), "l", d) for d in (1, 2, 3)]

    far_a = after(far_a, res)
    near_a = jnp.concatenate([add(near_a[:, :half], far_a), near_a[:, half:]], 1)
    near_b = jnp.concatenate([near_b[:, :half], add(near_b[:, half:], far_b)], 1)
    tot = [own, shift(near_a, "x", 1), shift(near_b, "x", -1)]
    tot[0] = after(tot[0], *back[1:])
    tot = sum(t.astype(F32) for t in tot).astype(BF16)
    half = heads // 8
    far = pick(tot, (l + 2) & 3)
    acc = pick(tot, l).astype(F32)
    for d in (1, -1):
        acc = acc + shift(pick(tot, (l + d) & 3), RING8, d).astype(F32)
    acc = acc + jnp.concatenate([shift(far[:half], RING8, -2), shift(far[half:], RING8, 2)], 0).astype(F32)
    acc = acc.astype(BF16)
    acc = add(acc, shift(acc, "h", 1))
    grad_w = jnp.zeros((4, heads // 4, feats), BF16)
    for d in range(4):
        grad_w = put(grad_w, shift(acc, "x", d) if d else acc, (x - d) & 3)
    grad_w = grad_w.reshape(heads, feats)

    out = jnp.zeros((4, 4, 2, toks, heads), BF16)
    for d, piece in enumerate(back):
        out = lax.dynamic_update_slice_in_dim(out, piece[:, None], (l - d) & 3, 1)
    out = out.reshape(1, 4 * 8 * toks, heads)
    return out, grad_w


def solution(mesh):
    fine = Mesh(mesh.devices.reshape(4, 2, 4, 4, 2), ("x", "h", "y", "l", "c"))
    dp, context = ("x", "h"), ("y", "l", "c")
    in_specs = (P(dp, context, None), P(dp, context, None), P(context, None))
    out_specs = (P(dp, None, context), P(context, None))
    return jax.shard_map(local, mesh=fine, in_specs=in_specs, out_specs=out_specs, check_vma=False)
```

time: 267 us -> 200 us (0.75); the launches traced: 263 us -> 200 us
  waiting for transfers between devices: 129 us -> 93.4 us
  between operations: 14.2 us -> 0.95 us
  starting transfers between devices: 49.3 us -> 39 us
  other arithmetic: 13.3 us -> 5.66 us
  local copies, waits for them, and re-layouts: 36.6 us -> 42.5 us
    all_to_all x8 -> x1, waiting for transfers between devices: 82.5 us -> 18.7 us  [exchange(): return lax.all_to_all(v, axis, split_axis=0, concat_axis=0, tiled=True)]
    ppermute x6 -> x28, waiting for transfers between devices: 14.2 us -> 74.7 us  [shift(): return lax.ppermute(v, axis, [(i, (i + by) % n) for i in range(n)])]
    all_gather x2 -> x0, waiting for transfers between devices: 31.9 us -> none  [local(): lax.all_gather(g[:, lo:hi], ('y', 'c'), axis=0, tiled=True)]
    all_to_all x8 -> x1, starting transfers between devices: 36.1 us -> 4.51 us  [exchange(): return lax.all_to_all(v, axis, split_axis=0, concat_axis=0, tiled=True)]
    dynamic_update_slice x0 -> x22, local copies, waits for them, and re-layouts: none -> 21.9 us  [the longest x18 19.8 us: put(): lax.dynamic_update_slice(buffer, piece.reshape((1,) * (buffer.ndim - piec...]
    ppermute x6 -> x28, starting transfers between devices: 13.1 us -> 34.5 us  [shift(): return lax.ppermute(v, axis, [(i, (i + by) % n) for i in range(n)])]
    unnamed x14 -> x16, local copies, waits for them, and re-layouts: 18.8 us -> 3.39 us
    concatenate x2, other arithmetic: 8.85 us -> 2.15 us  [the longest x1 1.09 us: local(): jnp.concatenate([add(near_a[:, :half], far_a), near_a[:, half:]], 1)]
  transfers between devices with their start and end apart: 16 -> 29, of which waited for: 9 -> 11; matrix products, arithmetic and copies ran while one was open for 25% -> 25% of each run, Pallas kernels for 0% -> 0%
where the time goes in v6:
time: 200 us
  waiting for transfers between devices  93.4 us (47%)
  local copies, waits for them, and re-layouts  42.5 us (21%)
  starting transfers between devices  39 us (20%)
  matrix products  18.3 us (9%)
  other arithmetic  5.66 us (3%)
    ppermute x28, waiting for transfers between devices, shift(): return lax.ppermute(v, axis, [(i, (i + by) % n) for i in range(n)])  74.7 us
    ppermute x28, starting transfers between devices, shift(): return lax.ppermute(v, axis, [(i, (i + by) % n) for i in range(n)])  34.5 us
    dynamic_update_slice x18, local copies, waits for them, and re-layouts, put(): lax.dynamic_update_slice(buffer, piece.reshape((1,) * (buffer.ndim - piec...  19.8 us
    all_to_all x1, waiting for transfers between devices, exchange(): return lax.all_to_all(v, axis, split_axis=0, concat_axis=0, tiled=True)  18.7 us
    dot_general x1, matrix products, local(): lax.dot_general(after(tokens, part), weights, (((1,), (1,)), ((), ())), p...  10.1 us
    dot_general x1, matrix products, local(): lax.dot_general(acts, tokens, (((0,), (0,)), ((), ())), preferred_element...  8.24 us
    all_to_all x1, starting transfers between devices, exchange(): return lax.all_to_all(v, axis, split_axis=0, concat_axis=0, tiled=True)  4.51 us
    broadcast_in_dim x1, local copies, waits for them, and re-layouts, local(): tokens = jnp.zeros((4, 2, toks, feats), BF16)  4.34 us
  transfers between devices with their start and end apart: 29, of which 11 were waited for; matrix products, arithmetic and copies ran while one was open for 25% of the time, Pallas kernels for 0%

profile of v6, /device:TPU:64, one launch (start us, length us, event | category | flops | bytes accessed | tf_op | source)
XLA Modules:
  0.0 199.9 jit_solution(20509780762494175)
XLA Ops:
  0.7 3.1 %collective-permute-start.1 = (bf16[128,4096]{1,0:T(8,128)(2,1)}, bf16[128,4096]{1,0:T(8,128)(2,1)}, u32[]{:S(2)}, u32[]{:S(2)}) collective-permute-start(bf16[128,4096]{1,0:T(8,128)(2,1)} %bitcast.107), channel_id=1, source_target_pairs={{0,24},{8,0},{16,8},{24,16},{1,25},{9,1},{17,9},{25,17},{2,26},{10... | collective-permute-start | bytes 3145736 | tf_op jit(solution)/shard_map/ppermute | solution.py:12
  3.8 1.6 copy.13
  6.5 4.5 %all-to-all-start = ((bf16[8,128,512]{1,2,0:T(8,128)(2,1)}), bf16[8,128,512]{1,2,0:T(8,128)(2,1)S(1)}, u32[]{:S(2)}, u32[]{:S(2)}) async-start(bf16[8,128,512]{1,2,0:T(8,128)(2,1)} %bitcast.9), calls=%async_computation | async-start | bytes 2097152 | tf_op jit(solution)/shard_map/all_to_all | solution.py:16
  11.1 1.9 collective-permute-start.10
  13.0 2.5 %broadcast_in_dim.26 = bf16[4,128,4096]{2,1,0:T(8,128)(2,1)} broadcast(bf16[]{:T(256)} %constant.60.clone.1), dimensions={} | broadcast | bytes 4194306 | tf_op jit(solution)/shard_map/broadcast_in_dim | solution.py:57
  16.6 4.3 %broadcast_in_dim.25 = bf16[4,2,128,4096]{3,2,1,0:T(8,128)(2,1)} broadcast(bf16[]{:T(256)} %constant.60.clone.1), dimensions={} | broadcast | bytes 8388610 | tf_op jit(solution)/shard_map/broadcast_in_dim | solution.py:49
  23.0 18.7 %all-to-all-done = bf16[8,128,512]{1,2,0:T(8,128)(2,1)S(1)} async-done(((bf16[8,128,512]{1,2,0:T(8,128)(2,1)}), bf16[8,128,512]{1,2,0:T(8,128)(2,1)S(1)}, u32[]{:S(2)}, u32[]{:S(2)}) %all-to-all-start) | async-done | bytes 1048608 | tf_op jit(solution)/shard_map/all_to_all | solution.py:16
  42.2 4.6 %collective-permute-start.11 = (bf16[64,4096]{1,0:T(8,128)(2,1)}, bf16[64,4096]{1,0:T(8,128)(2,1)S(1)}, u32[]{:S(2)}, u32[]{:S(2)}) collective-permute-start(bf16[64,4096]{1,0:T(8,128)(2,1)} %get-tuple-element.31), channel_id=1, source_target_pairs={{0,4},{2,6},{4,32},{6,34},{32,36},{34,38},{36,0},{38,2},{1,5},{3,7... | collective-permute-start | bytes 1572872 | tf_op jit(solution)/shard_map/ppermute | solution.py:12
  46.8 2.3 %bitcast_dynamic-update-slice_fusion.7 = bf16[4,2,128,4096]{3,2,1,0:T(8,128)(2,1)} fusion(bf16[4,2,128,4096]{3,2,1,0:T(8,128)(2,1)} %bitcast_dynamic-update-slice_fusion.8, s32[]{:T(128)S(6)} %select_n.90, s32[]{:T(128)S(6)} %select_n.92, bf16[128,4096]{1,0:T(8,128)(2,1)} %collective-permute-done), kind=kLoop, calls=%fused_computation.12 | loop fusion | bytes 2097160 | tf_op jit(solution)/shard_map/dynamic_update_slice | solution.py:29
  49.1 2.3 %bitcast_dynamic-update-slice_fusion.6 = bf16[4,2,128,4096]{3,2,1,0:T(8,128)(2,1)} fusion(bf16[4,2,128,4096]{3,2,1,0:T(8,128)(2,1)} %bitcast_dynamic-update-slice_fusion.7, s32[]{:T(128)S(6)} %select_n.93, s32[]{:T(128)S(6)} %select_n.91, bf16[128,4096]{1,0:T(8,128)(2,1)} %collective-permute-done.1), kind=kLoop, calls=%fused_computation.11 | loop fusion | bytes 2097160 | tf_op jit(solution)/shard_map/dynamic_update_slice | solution.py:29
  53.0 1.7 collective-permute-start.7
  54.8 2.3 %bitcast_dynamic-update-slice_fusion.1 = bf16[4,128,4096]{2,1,0:T(8,128)(2,1)} fusion(bf16[4,128,4096]{2,1,0:T(8,128)(2,1)} %bitcast_dynamic-update-slice_fusion.2, s32[]{:T(128)S(6)} %select_n.97, bf16[128,4096]{1,0:T(8,128)(2,1)} %collective-permute-done.9), kind=kLoop, calls=%fused_computation.6 | loop fusion | bytes 2097156 | tf_op jit(solution)/shard_map/dynamic_update_slice | solution.py:29
  57.1 2.3 %bitcast_dynamic-update-slice_fusion = bf16[4,128,4096]{2,1,0:T(8,128)(2,1)} fusion(bf16[4,128,4096]{2,1,0:T(8,128)(2,1)} %bitcast_dynamic-update-slice_fusion.1, s32[]{:T(128)S(6)} %select_n.98, bf16[128,4096]{1,0:T(8,128)(2,1)} %collective-permute-done.10), kind=kLoop, calls=%fused_computation.5 | loop fusion | bytes 2097156 | tf_op jit(solution)/shard_map/dynamic_update_slice | solution.py:29
  59.4 8.6 %collective-permute-done.11 = bf16[64,4096]{1,0:T(8,128)(2,1)S(1)} collective-permute-done((bf16[64,4096]{1,0:T(8,128)(2,1)}, bf16[64,4096]{1,0:T(8,128)(2,1)S(1)}, u32[]{:S(2)}, u32[]{:S(2)}) %collective-permute-start.11) | collective-permute-done | bytes 524320 | tf_op jit(solution)/shard_map/ppermute | solution.py:12
  68.8 5.5 %collective-permute-done.12 = bf16[64,4096]{1,0:T(8,128)(2,1)S(1)} collective-permute-done((bf16[64,4096]{1,0:T(8,128)(2,1)}, bf16[64,4096]{1,0:T(8,128)(2,1)S(1)}, u32[]{:S(2)}, u32[]{:S(2)}) %collective-permute-start.12) | collective-permute-done | bytes 524320 | tf_op jit(solution)/shard_map/ppermute | solution.py:12
  82.4 8.2 %convolution_convert_fusion = bf16[4096,512]{0,1:T(8,128)(2,1)S(1)} fusion(bf16[1024,4096]{1,0:T(8,128)(2,1)} %bitcast.15, bf16[1024,512]{1,0:T(8,128)(2,1)S(1)} %bitcast.103), kind=kOutput, calls=%fused_computation | convolution fusion | flops 4297064448 | bytes 13631488 | tf_op jit(solution)/shard_map/dot_general | solution.py:64
  94.6 10.1 %convolution_convert_fusion.1 = bf16[1024,512]{1,0:T(8,128)(2,1)} fusion(bf16[1024,4096]{1,0:T(8,128)(2,1)} %bitcast.15, bf16[512,4096]{1,0:T(8,128)(2,1)} %bitcast.23), kind=kOutput, calls=%fused_computation.2 | convolution fusion | flops 4295491584 | bytes 13631488 | tf_op jit(solution)/shard_map/dot_general | solution.py:70
  106.0 1.8 collective-permute-start.18
  111.3 8.9 %collective-permute-done.18 = bf16[4,16,4096]{2,1,0:T(8,128)(2,1)S(1)} collective-permute-done((bf16[4,16,4096]{2,1,0:T(8,128)(2,1)}, bf16[4,16,4096]{2,1,0:T(8,128)(2,1)S(1)}, u32[]{:S(2)}, u32[]{:S(2)}) %collective-permute-start.18) | collective-permute-done | bytes 524320 | tf_op jit(solution)/shard_map/ppermute | solution.py:12
  121.4 3.0 %collective-permute-start.19 = (bf16[4,32,4096]{2,1,0:T(8,128)(2,1)}, bf16[4,32,4096]{2,1,0:T(8,128)(2,1)}, u32[]{:S(2)}, u32[]{:S(2)}) collective-permute-start(bf16[4,32,4096]{2,1,0:T(8,128)(2,1)} %pad_maximum_fusion.1), channel_id=1, source_target_pairs={{0,192},{64,0},{128,64},{192,128},{1,193},{65,1},{129,65},{193,129... | collective-permute-start | bytes 3145736 | tf_op jit(solution)/shard_map/ppermute | solution.py:12
  124.3 2.5 %constant_dynamic-slice_fusion = (bf16[4,2,128,1,128]{4,3,2,1,0:T(2,128)(2,1)S(1)}, bf16[4,2,128,1,128]{4,3,2,1,0:T(2,128)(2,1)S(1)}, bf16[4,2,128,1,128]{4,3,2,...) fusion(bf16[4,2,128,4,128]{4,3,2,1,0:T(4,128)(2,1)S(1)} %reshape.106, s32[]{:T(128)S(6)} %select_n.102, s32[]{:T(128)S(6)} %select_n.99, ...), kind=kLoop, calls=%fused_computation.47 | loop fusion | bytes 2097168 | tf_op jit(solution)/shard_map/jit(dynamic_index_in_dim)/dynamic_slice | solution.py:24
  129.4 17.8 %collective-permute-done.13 = bf16[4,2,128,128]{3,2,1,0:T(8,128)(2,1)} collective-permute-done((bf16[4,2,128,128]{3,2,1,0:T(8,128)(2,1)S(1)}, bf16[4,2,128,128]{3,2,1,0:T(8,128)(2,1)}, u32[]{:S(2)}, u32[]{:S(2)}) %collective-permute-start.13) | collective-permute-done | bytes 262176 | tf_op jit(solution)/shard_map/ppermute | solution.py:12
  147.2 1.6 collective-permute-done.15
  149.6 2.0 %add_convert_fusion = bf16[4,32,4096]{2,1,0:T(8,128)(2,1)S(1)} fusion(bf16[4,32,4096]{2,1,0:T(8,128)(2,1)} %collective-permute-done.19, bf16[4,32,4096]{2,1,0:T(8,128)(2,1)} %collective-permute-done.17, bf16[4,32,4096]{2,1,0:T(8,128)(2,1)S(1)} %copy-done.1), kind=kLoop, calls=%fused_computation.1 | loop fusion | flops 3145728 | bytes 4194304 | tf_op jit(solution)/shard_map/convert_element_type | solution.py:80
  151.6 3.5 %collective-permute-start.20 = (bf16[32,4096]{1,0:T(8,128)(2,1)S(1)}, bf16[32,4096]{1,0:T(8,128)(2,1)S(1)}, u32[]{:S(2)}, u32[]{:S(2)}) collective-permute-start(bf16[32,4096]{1,0:T(8,128)(2,1)S(1)} %get-tuple-element.22), channel_id=1, source_target_pairs={{0,2},{2,4},{4,6},{6,32},{32,34},{34,36},{36,38},{38,0},{1,3},{3,5... | collective-permute-start | bytes 786440 | tf_op jit(solution)/shard_map/ppermute | solution.py:12
  155.8 3.6 %collective-permute-start.23 = (bf16[16,4096]{1,0:T(8,128)(2,1)S(1)}, bf16[16,4096]{1,0:T(8,128)(2,1)S(1)}, u32[]{:S(2)}, u32[]{:S(2)}) collective-permute-start(bf16[16,4096]{1,0:T(8,128)(2,1)S(1)} %get-tuple-element.21), channel_id=1, source_target_pairs={{0,4},{2,6},{4,32},{6,34},{32,36},{34,38},{36,0},{38,2},{1,5},{3,7... | collective-permute-start | bytes 393224 | tf_op jit(solution)/shard_map/ppermute | solution.py:12
  159.4 8.4 %collective-permute-done.22 = bf16[16,4096]{1,0:T(8,128)(2,1)S(1)} collective-permute-done((bf16[16,4096]{1,0:T(8,128)(2,1)S(1)}, bf16[16,4096]{1,0:T(8,128)(2,1)S(1)}, u32[]{:S(2)}, u32[]{:S(2)}) %collective-permute-start.22) | collective-permute-done | bytes 131104 | tf_op jit(solution)/shard_map/ppermute | solution.py:12
  168.0 1.8 collective-permute-start.24
  171.1 12.5 %collective-permute-done.24 = bf16[32,4096]{1,0:T(8,128)(2,1)S(1)} collective-permute-done((bf16[32,4096]{1,0:T(8,128)(2,1)S(1)}, bf16[32,4096]{1,0:T(8,128)(2,1)S(1)}, u32[]{:S(2)}, u32[]{:S(2)}) %collective-permute-start.24) | collective-permute-done | bytes 262176 | tf_op jit(solution)/shard_map/ppermute | solution.py:12
  185.0 2.0 collective-permute-start.26
  188.4 8.7 %collective-permute-done.25 = bf16[32,4096]{1,0:T(8,128)(2,1)S(1)} collective-permute-done((bf16[32,4096]{1,0:T(8,128)(2,1)S(1)}, bf16[32,4096]{1,0:T(8,128)(2,1)S(1)}, u32[]{:S(2)}, u32[]{:S(2)}) %collective-permute-start.25) | collective-permute-done | bytes 262176 | tf_op jit(solution)/shard_map/ppermute | solution.py:12
  197.2 1.7 collective-permute-done.27
  (90 shorter events, 34.4 us)
Async XLA Ops:
  0.6 15.0 %copy-start = (bf16[128,4096]{1,0:T(8,128)(2,1)S(1)}, bf16[128,4096]{1,0:T(8,128)(2,1)}, u32[]{:S(2)}) copy-start(bf16[128,4096]{1,0:T(8,128)(2,1)} %param.5) | copy-start | bytes 3145732
  0.6 41.6 %collective-permute-start = (bf16[128,4096]{1,0:T(8,128)(2,1)}, bf16[128,4096]{1,0:T(8,128)(2,1)}, u32[]{:S(2)}, u32[]{:S(2)}) collective-permute-start(bf16[128,4096]{1,0:T(8,128)(2,1)} %bitcast.106), channel_id=1, source_target_pairs={{0,1},{1,0},{2,3},{3,2},{4,5},{5,4},{6,7},{7,6},{8,9},{9,8},{10,11... | collective-permute-start | bytes 3145736 | tf_op jit(solution)/shard_map/ppermute | solution.py:12
  0.7 48.4 %collective-permute-start.1 = (bf16[128,4096]{1,0:T(8,128)(2,1)}, bf16[128,4096]{1,0:T(8,128)(2,1)}, u32[]{:S(2)}, u32[]{:S(2)}) collective-permute-start(bf16[128,4096]{1,0:T(8,128)(2,1)} %bitcast.107), channel_id=1, source_target_pairs={{0,24},{8,0},{16,8},{24,16},{1,25},{9,1},{17,9},{25,17},{2,26},{10... | collective-permute-start | bytes 3145736 | tf_op jit(solution)/shard_map/ppermute | solution.py:12
  3.8 48.7 %collective-permute-start.3 = (bf16[128,4096]{1,0:T(8,128)(2,1)}, bf16[128,4096]{1,0:T(8,128)(2,1)S(1)}, u32[]{:S(2)}, u32[]{:S(2)}) collective-permute-start(bf16[128,4096]{1,0:T(8,128)(2,1)} %bitcast.108), channel_id=1, source_target_pairs={{0,8},{8,16},{16,24},{24,0},{1,9},{9,17},{17,25},{25,1},{2,10},{10... | collective-permute-start | bytes 3145736 | tf_op jit(solution)/shard_map/ppermute | solution.py:12
  6.5 35.2 %all-to-all-start = ((bf16[8,128,512]{1,2,0:T(8,128)(2,1)}), bf16[8,128,512]{1,2,0:T(8,128)(2,1)S(1)}, u32[]{:S(2)}, u32[]{:S(2)}) async-start(bf16[8,128,512]{1,2,0:T(8,128)(2,1)} %bitcast.9), calls=%async_computation | async-start | bytes 2097152 | tf_op jit(solution)/shard_map/all_to_all | solution.py:16
  11.0 42.0 %collective-permute-start.9 = (bf16[128,4096]{1,0:T(8,128)(2,1)}, bf16[128,4096]{1,0:T(8,128)(2,1)}, u32[]{:S(2)}, u32[]{:S(2)}) collective-permute-start(bf16[128,4096]{1,0:T(8,128)(2,1)} %param.5), channel_id=1, source_target_pairs={{0,38},{2,0},{4,2},{6,4},{32,6},{34,32},{36,34},{38,36},{1,39},{3,... | collective-permute-start | bytes 3145736 | tf_op jit(solution)/shard_map/ppermute | solution.py:12
  11.1 46.0 %collective-permute-start.10 = (bf16[128,4096]{1,0:T(8,128)(2,1)}, bf16[128,4096]{1,0:T(8,128)(2,1)}, u32[]{:S(2)}, u32[]{:S(2)}) collective-permute-start(bf16[128,4096]{1,0:T(8,128)(2,1)} %param.5), channel_id=1, source_target_pairs={{0,2},{2,4},{4,6},{6,32},{32,34},{34,36},{36,38},{38,0},{1,3},{3,5... | collective-permute-start | bytes 3145736 | tf_op jit(solution)/shard_map/ppermute | solution.py:12
  42.2 25.7 %collective-permute-start.11 = (bf16[64,4096]{1,0:T(8,128)(2,1)}, bf16[64,4096]{1,0:T(8,128)(2,1)S(1)}, u32[]{:S(2)}, u32[]{:S(2)}) collective-permute-start(bf16[64,4096]{1,0:T(8,128)(2,1)} %get-tuple-element.31), channel_id=1, source_target_pairs={{0,4},{2,6},{4,32},{6,34},{32,36},{34,38},{36,0},{38,2},{1,5},{3,7... | collective-permute-start | bytes 1572872 | tf_op jit(solution)/shard_map/ppermute | solution.py:12
  49.1 25.3 %collective-permute-start.12 = (bf16[64,4096]{1,0:T(8,128)(2,1)}, bf16[64,4096]{1,0:T(8,128)(2,1)S(1)}, u32[]{:S(2)}, u32[]{:S(2)}) collective-permute-start(bf16[64,4096]{1,0:T(8,128)(2,1)} %get-tuple-element.30), channel_id=1, source_target_pairs={{0,36},{2,38},{4,0},{6,2},{32,4},{34,6},{36,32},{38,34},{1,37},{3,... | collective-permute-start | bytes 1572872 | tf_op jit(solution)/shard_map/ppermute | solution.py:12
  52.5 22.7 %collective-permute-start.5 = (bf16[64,4096]{1,0:T(8,128)(2,1)S(1)}, bf16[64,4096]{1,0:T(8,128)(2,1)S(1)}, u32[]{:S(2)}, u32[]{:S(2)}) collective-permute-start(bf16[64,4096]{1,0:T(8,128)(2,1)S(1)} %slice.56), channel_id=1, source_target_pairs={{0,24},{8,0},{16,8},{24,16},{1,25},{9,1},{17,9},{25,17},{2,26},{10... | collective-permute-start | bytes 1572872 | tf_op jit(solution)/shard_map/ppermute | solution.py:12
  53.0 22.2 %collective-permute-start.7 = (bf16[64,4096]{1,0:T(8,128)(2,1)S(1)}, bf16[64,4096]{1,0:T(8,128)(2,1)S(1)}, u32[]{:S(2)}, u32[]{:S(2)}) collective-permute-start(bf16[64,4096]{1,0:T(8,128)(2,1)S(1)} %slice.57), channel_id=1, source_target_pairs={{0,8},{8,16},{16,24},{24,0},{1,9},{9,17},{17,25},{25,1},{2,10},{10... | collective-permute-start | bytes 1572872 | tf_op jit(solution)/shard_map/ppermute | solution.py:12
  57.1 18.7 %collective-permute-start.2 = (bf16[128,4096]{1,0:T(8,128)(2,1)}, bf16[128,4096]{1,0:T(8,128)(2,1)S(1)}, u32[]{:S(2)}, u32[]{:S(2)}) collective-permute-start(bf16[128,4096]{1,0:T(8,128)(2,1)} %collective-permute-done.1), channel_id=1, source_target_pairs={{0,1},{1,0},{2,3},{3,2},{4,5},{5,4},{6,7},{7,6},{8,9},{9,8},{10,11... | collective-permute-start | bytes 3145736 | tf_op jit(solution)/shard_map/ppermute | solution.py:12
  67.9 9.9 %collective-permute-start.4 = (bf16[128,4096]{1,0:T(8,128)(2,1)S(1)}, bf16[128,4096]{1,0:T(8,128)(2,1)S(1)}, u32[]{:S(2)}, u32[]{:S(2)}) collective-permute-start(bf16[128,4096]{1,0:T(8,128)(2,1)S(1)} %collective-permute-done.3), channel_id=1, source_target_pairs={{0,1},{1,0},{2,3},{3,2},{4,5},{5,4},{6,7},{7,6},{8,9},{9,8},{10,11... | collective-permute-start | bytes 3145736 | tf_op jit(solution)/shard_map/ppermute | solution.py:12
  75.2 4.6 %collective-permute-start.6 = (bf16[64,4096]{1,0:T(8,128)(2,1)S(1)}, bf16[64,4096]{1,0:T(8,128)(2,1)S(1)}, u32[]{:S(2)}, u32[]{:S(2)}) collective-permute-start(bf16[64,4096]{1,0:T(8,128)(2,1)S(1)} %collective-permute-done.5), channel_id=1, source_target_pairs={{0,1},{1,0},{2,3},{3,2},{4,5},{5,4},{6,7},{7,6},{8,9},{9,8},{10,11... | collective-permute-start | bytes 1572872 | tf_op jit(solution)/shard_map/ppermute | solution.py:12
  75.2 6.3 %collective-permute-start.8 = (bf16[64,4096]{1,0:T(8,128)(2,1)S(1)}, bf16[64,4096]{1,0:T(8,128)(2,1)S(1)}, u32[]{:S(2)}, u32[]{:S(2)}) collective-permute-start(bf16[64,4096]{1,0:T(8,128)(2,1)S(1)} %collective-permute-done.7), channel_id=1, source_target_pairs={{0,1},{1,0},{2,3},{3,2},{4,5},{5,4},{6,7},{7,6},{8,9},{9,8},{10,11... | collective-permute-start | bytes 1572872 | tf_op jit(solution)/shard_map/ppermute | solution.py:12
  93.1 15.6 %collective-permute-start.16 = (bf16[4,16,4096]{2,1,0:T(8,128)(2,1)}, bf16[4,16,4096]{2,1,0:T(8,128)(2,1)}, u32[]{:S(2)}, u32[]{:S(2)}) collective-permute-start(bf16[4,16,4096]{2,1,0:T(8,128)(2,1)} %get-tuple-element.24), channel_id=1, source_target_pairs={{0,64},{64,128},{128,192},{192,0},{1,65},{65,129},{129,193},{193,1... | collective-permute-start | bytes 1572872 | tf_op jit(solution)/shard_map/ppermute | solution.py:12
  106.0 14.1 %collective-permute-start.18 = (bf16[4,16,4096]{2,1,0:T(8,128)(2,1)}, bf16[4,16,4096]{2,1,0:T(8,128)(2,1)S(1)}, u32[]{:S(2)}, u32[]{:S(2)}) collective-permute-start(bf16[4,16,4096]{2,1,0:T(8,128)(2,1)} %get-tuple-element.25), channel_id=1, source_target_pairs={{0,192},{64,0},{128,64},{192,128},{1,193},{65,1},{129,65},{193,129... | collective-permute-start | bytes 1572872 | tf_op jit(solution)/shard_map/ppermute | solution.py:12
  109.9 39.7 %copy-start.1 = (bf16[4,32,4096]{2,1,0:T(8,128)(2,1)S(1)}, bf16[4,32,4096]{2,1,0:T(8,128)(2,1)}, u32[]{:S(2)}) copy-start(bf16[4,32,4096]{2,1,0:T(8,128)(2,1)} %get-tuple-element.12) | copy-start | bytes 3145732
  111.0 37.9 %collective-permute-start.17 = (bf16[4,32,4096]{2,1,0:T(8,128)(2,1)}, bf16[4,32,4096]{2,1,0:T(8,128)(2,1)}, u32[]{:S(2)}, u32[]{:S(2)}) collective-permute-start(bf16[4,32,4096]{2,1,0:T(8,128)(2,1)} %pad_maximum_fusion), channel_id=1, source_target_pairs={{0,64},{64,128},{128,192},{192,0},{1,65},{65,129},{129,193},{193,1... | collective-permute-start | bytes 3145736 | tf_op jit(solution)/shard_map/ppermute | solution.py:12
  121.4 28.2 %collective-permute-start.19 = (bf16[4,32,4096]{2,1,0:T(8,128)(2,1)}, bf16[4,32,4096]{2,1,0:T(8,128)(2,1)}, u32[]{:S(2)}, u32[]{:S(2)}) collective-permute-start(bf16[4,32,4096]{2,1,0:T(8,128)(2,1)} %pad_maximum_fusion.1), channel_id=1, source_target_pairs={{0,192},{64,0},{128,64},{192,128},{1,193},{65,1},{129,65},{193,129... | collective-permute-start | bytes 3145736 | tf_op jit(solution)/shard_map/ppermute | solution.py:12
  126.8 20.4 %collective-permute-start.13 = (bf16[4,2,128,128]{3,2,1,0:T(8,128)(2,1)S(1)}, bf16[4,2,128,128]{3,2,1,0:T(8,128)(2,1)}, u32[]{:S(2)}, u32[]{:S(2)}) collective-permute-start(bf16[4,2,128,128]{3,2,1,0:T(8,128)(2,1)S(1)} %bitcast.109), channel_id=1, source_target_pairs={{0,2},{2,4},{4,6},{6,0},{1,3},{3,5},{5,7},{7,1},{8,10},{10,12},{12... | collective-permute-start | bytes 786440 | tf_op jit(solution)/shard_map/ppermute | solution.py:12
  127.7 19.5 %collective-permute-start.14 = (bf16[4,2,128,128]{3,2,1,0:T(8,128)(2,1)S(1)}, bf16[4,2,128,128]{3,2,1,0:T(8,128)(2,1)S(1)}, u32[]{:S(2)}, u32[]{:S(2)}) collective-permute-start(bf16[4,2,128,128]{3,2,1,0:T(8,128)(2,1)S(1)} %bitcast.110), channel_id=1, source_target_pairs={{0,4},{2,6},{4,0},{6,2},{1,5},{3,7},{5,1},{7,3},{8,12},{10,14},{12... | collective-permute-start | bytes 786440 | tf_op jit(solution)/shard_map/ppermute | solution.py:12
  127.9 21.0 %collective-permute-start.15 = (bf16[4,2,128,128]{3,2,1,0:T(8,128)(2,1)S(1)}, bf16[4,2,128,128]{3,2,1,0:T(8,128)(2,1)S(1)}, u32[]{:S(2)}, u32[]{:S(2)}) collective-permute-start(bf16[4,2,128,128]{3,2,1,0:T(8,128)(2,1)S(1)} %bitcast.111), channel_id=1, source_target_pairs={{0,6},{2,0},{4,2},{6,4},{1,7},{3,1},{5,3},{7,5},{8,14},{10,8},{12,... | collective-permute-start | bytes 786440 | tf_op jit(solution)/shard_map/ppermute | solution.py:12
  151.6 16.2 %collective-permute-start.20 = (bf16[32,4096]{1,0:T(8,128)(2,1)S(1)}, bf16[32,4096]{1,0:T(8,128)(2,1)S(1)}, u32[]{:S(2)}, u32[]{:S(2)}) collective-permute-start(bf16[32,4096]{1,0:T(8,128)(2,1)S(1)} %get-tuple-element.22), channel_id=1, source_target_pairs={{0,2},{2,4},{4,6},{6,32},{32,34},{34,36},{36,38},{38,0},{1,3},{3,5... | collective-permute-start | bytes 786440 | tf_op jit(solution)/shard_map/ppermute | solution.py:12
  155.2 12.7 %collective-permute-start.21 = (bf16[32,4096]{1,0:T(8,128)(2,1)S(1)}, bf16[32,4096]{1,0:T(8,128)(2,1)S(1)}, u32[]{:S(2)}, u32[]{:S(2)}) collective-permute-start(bf16[32,4096]{1,0:T(8,128)(2,1)S(1)} %get-tuple-element.23), channel_id=1, source_target_pairs={{0,38},{2,0},{4,2},{6,4},{32,6},{34,32},{36,34},{38,36},{1,39},{3,... | collective-permute-start | bytes 786440 | tf_op jit(solution)/shard_map/ppermute | solution.py:12
  155.2 12.7 %collective-permute-start.22 = (bf16[16,4096]{1,0:T(8,128)(2,1)S(1)}, bf16[16,4096]{1,0:T(8,128)(2,1)S(1)}, u32[]{:S(2)}, u32[]{:S(2)}) collective-permute-start(bf16[16,4096]{1,0:T(8,128)(2,1)S(1)} %get-tuple-element.20), channel_id=1, source_target_pairs={{0,36},{2,38},{4,0},{6,2},{32,4},{34,6},{36,32},{38,34},{1,37},{3,... | collective-permute-start | bytes 393224 | tf_op jit(solution)/shard_map/ppermute | solution.py:12
  155.8 12.0 %collective-permute-start.23 = (bf16[16,4096]{1,0:T(8,128)(2,1)S(1)}, bf16[16,4096]{1,0:T(8,128)(2,1)S(1)}, u32[]{:S(2)}, u32[]{:S(2)}) collective-permute-start(bf16[16,4096]{1,0:T(8,128)(2,1)S(1)} %get-tuple-element.21), channel_id=1, source_target_pairs={{0,4},{2,6},{4,32},{6,34},{32,36},{34,38},{36,0},{38,2},{1,5},{3,7... | collective-permute-start | bytes 393224 | tf_op jit(solution)/shard_map/ppermute | solution.py:12
  168.0 15.6 %collective-permute-start.24 = (bf16[32,4096]{1,0:T(8,128)(2,1)S(1)}, bf16[32,4096]{1,0:T(8,128)(2,1)S(1)}, u32[]{:S(2)}, u32[]{:S(2)}) collective-permute-start(bf16[32,4096]{1,0:T(8,128)(2,1)S(1)} %fusion.2), channel_id=1, source_target_pairs={{0,32},{32,0},{1,33},{33,1},{2,34},{34,2},{3,35},{35,3},{4,36},{36... | collective-permute-start | bytes 786440 | tf_op jit(solution)/shard_map/ppermute | solution.py:12
  183.8 13.3 %collective-permute-start.25 = (bf16[32,4096]{1,0:T(8,128)(2,1)S(1)}, bf16[32,4096]{1,0:T(8,128)(2,1)S(1)}, u32[]{:S(2)}, u32[]{:S(2)}) collective-permute-start(bf16[32,4096]{1,0:T(8,128)(2,1)S(1)} %get-tuple-element.15), channel_id=1, source_target_pairs={{0,64},{64,128},{128,192},{192,0},{1,65},{65,129},{129,193},{193,1... | collective-permute-start | bytes 786440 | tf_op jit(solution)/shard_map/ppermute | solution.py:12
  184.9 14.0 %copy-start.3 = (bf16[4,4,2,128,128]{4,3,2,1,0:T(8,128)(2,1)}, bf16[4,4,2,128,128]{4,3,2,1,0:T(8,128)(2,1)S(1)}, u32[]{:S(2)}) copy-start(bf16[4,4,2,128,128]{4,3,2,1,0:T(8,128)(2,1)S(1)} %bitcast_dynamic-update-slice_fusion.15) | copy-start | bytes 3145732
  185.0 12.2 %collective-permute-start.26 = (bf16[32,4096]{1,0:T(8,128)(2,1)S(1)}, bf16[32,4096]{1,0:T(8,128)(2,1)S(1)}, u32[]{:S(2)}, u32[]{:S(2)}) collective-permute-start(bf16[32,4096]{1,0:T(8,128)(2,1)S(1)} %get-tuple-element.15), channel_id=1, source_target_pairs={{0,128},{64,192},{128,0},{192,64},{1,129},{65,193},{129,1},{193,65... | collective-permute-start | bytes 786440 | tf_op jit(solution)/shard_map/ppermute | solution.py:12
  186.9 11.9 %collective-permute-start.27 = (bf16[32,4096]{1,0:T(8,128)(2,1)S(1)}, bf16[32,4096]{1,0:T(8,128)(2,1)S(1)}, u32[]{:S(2)}, u32[]{:S(2)}) collective-permute-start(bf16[32,4096]{1,0:T(8,128)(2,1)S(1)} %get-tuple-element.15), channel_id=1, source_target_pairs={{0,192},{64,0},{128,64},{192,128},{1,193},{65,1},{129,65},{193,129... | collective-permute-start | bytes 786440 | tf_op jit(solution)/shard_map/ppermute | solution.py:12
  (3 other events, 9.6 us)

commit v7 on v6

v7 whole, which is shorter than its diff:
```python
import jax
import jax.numpy as jnp
from jax import lax
from jax.sharding import Mesh, PartitionSpec as P

RING8 = ("h", "l")
F32, BF16 = jnp.float32, jnp.bfloat16


def shift(v, axis, by):
    n = lax.axis_size(axis)
    return lax.ppermute(v, axis, [(i, (i + by) % n) for i in range(n)])


def exchange(v, axis):
    return lax.all_to_all(v, axis, split_axis=0, concat_axis=0, tiled=True)


def after(v, *others):
    return lax.optimization_barrier((v, *others))[0]


def pick(v, index, axis=0):
    return lax.dynamic_index_in_dim(v, index, axis, keepdims=False)


def put(buffer, piece, *at):
    at = at + (0,) * (buffer.ndim - len(at))
    return lax.dynamic_update_slice(buffer, piece.reshape((1,) * (buffer.ndim - piece.ndim) + piece.shape), at)


def add(a, b):
    return (a.astype(F32) + b.astype(F32)).astype(BF16)


def local(grad_out, attn, w_out):
    g = grad_out[0]
    a = attn[0]
    toks, feats = g.shape
    heads = w_out.shape[0]
    x, y, l, c = (lax.axis_index(n) for n in ("x", "y", "l", "c"))

    a = a.reshape(toks, 4, 4, 2, heads).transpose(1, 3, 0, 2, 4).reshape(8, toks, 4 * heads)
    acts = exchange(a, ("y", "c")).reshape(8 * toks, 4 * heads)

    half = toks // 2
    above, below = shift(g, "y", -1), shift(g, "y", 1)
    far_a, far_b = shift(after(above[:half], acts), "y", -1), shift(after(below[half:], acts), "y", 1)
    tokens = jnp.zeros((4, 2, toks, feats), BF16)
    for piece, d, row in ((g, 0, 0), (above, 1, 0), (below, 3, 0), (far_a, 2, 0), (far_b, 2, half)):
        tokens = put(tokens, piece, (y + d) & 3, c, row)
        tokens = put(tokens, shift(piece, "c", 1), (y + d) & 3, 1 - c, row)
    tokens = tokens.reshape(8 * toks, feats)

    def partial(r, source):
        columns = lax.dynamic_slice_in_dim(source, ((x + r) & 3) * cols, cols, 1)
        return lax.dot_general(columns, acts, (((0,), (0,)), ((), ())), preferred_element_type=F32).astype(BF16)

    cols = feats // 4
    far = partial(2, tokens)
    top, bottom = shift(far[:cols // 2], "x", 1), shift(far[cols // 2:], "x", -1)

    half = heads // 2
    w = after(w_out, a)
    w_above, w_below = shift(w, RING8, -1), shift(w, RING8, 1)
    weights = jnp.zeros((4, heads, feats), BF16)
    for piece, d in ((w_out, 0), (w_above, 1), (w_below, 3)):
        weights = put(weights, piece, (l + d) & 3)
    w_far_a = shift(after(w_above[:half], far_a), RING8, -1)
    w_far_b = shift(after(w_below[half:], far_a), RING8, 1)
    weights = put(weights, after(w_far_a, top), (l + 2) & 3, 0)
    weights = put(weights, after(w_far_b, top), (l + 2) & 3, half)
    weights = weights.reshape(4 * heads, feats)

    res = lax.dot_general(
        after(tokens, far), weights, (((1,), (1,)), ((), ())), preferred_element_type=F32).astype(BF16)

    def block(v, k):
        return lax.dynamic_slice_in_dim(v, (k & 3) * heads, heads, 1)

    back = [block(res, l)] + [shift(block(res, l + d), "l", d) for d in (1, 2, 3)]

    near_a, near_b = partial(1, after(tokens, top)), partial(3, after(tokens, bottom))
    near_a = lax.dynamic_update_slice(near_a, add(near_a[:cols // 2], top), (0, 0))
    near_b = lax.dynamic_update_slice(near_b, add(near_b[cols // 2:], bottom), (cols // 2, 0))
    own = partial(0, after(tokens, near_b))
    tot = [after(own, *back[1:]), shift(near_a, "x", 1), shift(near_b, "x", -1)]
    tot = sum(t.astype(F32) for t in tot).astype(BF16)
    far = block(tot, l + 2)
    acc = block(tot, l).astype(F32)
    for d in (1, -1):
        acc = acc + shift(block(tot, l + d), RING8, d).astype(F32)
    acc = acc + jnp.concatenate(
        [shift(far[:cols // 2], RING8, -2), shift(far[cols // 2:], RING8, 2)], 0).astype(F32)
    acc = acc.astype(BF16)
    acc = add(acc, shift(acc, "h", 1)).T
    grad_w = jnp.zeros((heads, feats), BF16)
    for d in range(4):
        grad_w = lax.dynamic_update_slice(
            grad_w, shift(acc, "x", d) if d else acc, (0, ((x - d) & 3) * cols))

    out = jnp.zeros((4, 4, 2 * toks, heads), BF16)
    for d, piece in enumerate(back):
        out = lax.dynamic_update_slice_in_dim(out, piece.reshape(4, 1, 2 * toks, heads), (l - d) & 3, 1)
    out = out.reshape(1, 4 * 8 * toks, heads)
    return out, grad_w


def solution(mesh):
    fine = Mesh(mesh.devices.reshape(4, 2, 4, 4, 2), ("x", "h", "y", "l", "c"))
    dp, context = ("x", "h"), ("y", "l", "c")
    in_specs = (P(dp, context, None), P(dp, context, None), P(context, None))
    out_specs = (P(dp, None, context), P(context, None))
    return jax.shard_map(local, mesh=fine, in_specs=in_specs, out_specs=out_specs, check_vma=False)
```

time: 200 us -> 183 us (0.915)
  the two profiles are of different devices: /device:TPU:64 before, /device:TPU:6 now
where the time goes in v7:
time: 183 us; the launch traced here: 182 us
  waiting for transfers between devices  76.9 us (42%)
  starting transfers between devices  47.1 us (26%)
  local copies, waits for them, and re-layouts  35.2 us (19%)
  matrix products  20.6 us (11%)
    ppermute x28, waiting for transfers between devices, shift(): return lax.ppermute(v, axis, [(i, (i + by) % n) for i in range(n)])  62.3 us
    ppermute x28, starting transfers between devices, shift(): return lax.ppermute(v, axis, [(i, (i + by) % n) for i in range(n)])  42.6 us
    dynamic_update_slice x15, local copies, waits for them, and re-layouts, put(): lax.dynamic_update_slice(buffer, piece.reshape((1,) * (buffer.ndim - piec...  19.7 us
    all_to_all x1, waiting for transfers between devices, exchange(): return lax.all_to_all(v, axis, split_axis=0, concat_axis=0, tiled=True)  14.6 us
    dot_general x4, matrix products, partial(): lax.dot_general(columns, acts, (((0,), (0,)), ((), ())), preferred_elemen...  11.6 us
    dot_general x1, matrix products, local(): lax.dot_general(after(tokens, far), weights, (((1,), (1,)), ((), ())), pr...  9.09 us
    all_to_all x1, starting transfers between devices, exchange(): return lax.all_to_all(v, axis, split_axis=0, concat_axis=0, tiled=True)  4.51 us
    broadcast_in_dim x1, local copies, waits for them, and re-layouts, local(): tokens = jnp.zeros((4, 2, toks, feats), BF16)  4.32 us
  transfers between devices with their start and end apart: 29, of which 11 were waited for; matrix products, arithmetic and copies ran while one was open for 29% of the time, Pallas kernels for 0%

profile of v7, /device:TPU:6, one launch (start us, length us, event | category | flops | bytes accessed | tf_op | source)
XLA Modules:
  0.0 182.0 jit_solution(11655045122227183970)
XLA Ops:
  0.7 3.1 %collective-permute-start.1 = (bf16[128,4096]{1,0:T(8,128)(2,1)}, bf16[128,4096]{1,0:T(8,128)(2,1)}, u32[]{:S(2)}, u32[]{:S(2)}) collective-permute-start(bf16[128,4096]{1,0:T(8,128)(2,1)} %bitcast.65), channel_id=1, source_target_pairs={{0,24},{8,0},{16,8},{24,16},{1,25},{9,1},{17,9},{25,17},{2,26},{10... | collective-permute-start | bytes 3145736 | tf_op jit(solution)/shard_map/ppermute | solution.py:12
  3.8 1.6 copy.19
  6.5 4.5 %all-to-all-start = ((bf16[8,128,512]{1,2,0:T(8,128)(2,1)}), bf16[8,128,512]{1,2,0:T(8,128)(2,1)S(1)}, u32[]{:S(2)}, u32[]{:S(2)}) async-start(bf16[8,128,512]{1,2,0:T(8,128)(2,1)} %bitcast.9), calls=%async_computation | async-start | bytes 2097152 | tf_op jit(solution)/shard_map/all_to_all | solution.py:16
  11.0 5.9 %collective-permute-start.9 = (bf16[128,4096]{1,0:T(8,128)(2,1)}, bf16[128,4096]{1,0:T(8,128)(2,1)S(1)}, u32[]{:S(2)}, u32[]{:S(2)}) collective-permute-start(bf16[128,4096]{1,0:T(8,128)(2,1)} %param.5), channel_id=1, source_target_pairs={{0,38},{2,0},{4,2},{6,4},{32,6},{34,32},{36,34},{38,36},{1,39},{3,... | collective-permute-start | bytes 3145736 | tf_op jit(solution)/shard_map/ppermute | solution.py:12
  16.9 2.5 %broadcast_in_dim.14 = bf16[4,128,4096]{2,1,0:T(8,128)(2,1)} broadcast(bf16[]{:T(256)} %constant.17.clone.1), dimensions={} | broadcast | bytes 4194306 | tf_op jit(solution)/shard_map/broadcast_in_dim | solution.py:66
  19.4 2.3 %bitcast_dynamic-update-slice_fusion.2 = bf16[4,128,4096]{2,1,0:T(8,128)(2,1)} fusion(bf16[4,128,4096]{2,1,0:T(8,128)(2,1)} %broadcast_in_dim.14, s32[]{:T(128)S(6)} %select_n.102, bf16[128,4096]{1,0:T(8,128)(2,1)} %param.5), kind=kLoop, calls=%fused_computation.16 | loop fusion | bytes 2097156 | tf_op jit(solution)/shard_map/dynamic_update_slice | solution.py:29
  21.7 4.3 %broadcast_in_dim.13 = bf16[4,2,128,4096]{3,2,1,0:T(8,128)(2,1)} broadcast(bf16[]{:T(256)} %constant.17.clone.1), dimensions={} | broadcast | bytes 8388610 | tf_op jit(solution)/shard_map/broadcast_in_dim | solution.py:49
  27.1 14.6 %all-to-all-done = bf16[8,128,512]{1,2,0:T(8,128)(2,1)S(1)} async-done(((bf16[8,128,512]{1,2,0:T(8,128)(2,1)}), bf16[8,128,512]{1,2,0:T(8,128)(2,1)S(1)}, u32[]{:S(2)}, u32[]{:S(2)}) %all-to-all-start) | async-done | bytes 1048608 | tf_op jit(solution)/shard_map/all_to_all | solution.py:16
  45.5 1.8 %collective-permute-start.7 = (bf16[64,4096]{1,0:T(8,128)(2,1)S(1)}, bf16[64,4096]{1,0:T(8,128)(2,1)S(1)}, u32[]{:S(2)}, u32[]{:S(2)}) collective-permute-start(bf16[64,4096]{1,0:T(8,128)(2,1)S(1)} %slice.41), channel_id=1, source_target_pairs={{0,8},{8,16},{16,24},{24,0},{1,9},{9,17},{17,25},{25,1},{2,10},{10... | collective-permute-start | bytes 1572872 | tf_op jit(solution)/shard_map/ppermute | solution.py:12
  47.4 2.3 %bitcast_dynamic-update-slice_fusion.7 = bf16[4,2,128,4096]{3,2,1,0:T(8,128)(2,1)} fusion(bf16[4,2,128,4096]{3,2,1,0:T(8,128)(2,1)} %bitcast_dynamic-update-slice_fusion.8, s32[]{:T(128)S(6)} %select_n.95, s32[]{:T(128)S(6)} %select_n.97, bf16[128,4096]{1,0:T(8,128)(2,1)} %collective-permute-done), kind=kLoop, calls=%fused_computation.21 | loop fusion | bytes 2097160 | tf_op jit(solution)/shard_map/dynamic_update_slice | solution.py:29
  49.6 2.4 %bitcast_dynamic-update-slice_fusion.6 = bf16[4,2,128,4096]{3,2,1,0:T(8,128)(2,1)} fusion(bf16[4,2,128,4096]{3,2,1,0:T(8,128)(2,1)} %bitcast_dynamic-update-slice_fusion.7, s32[]{:T(128)S(6)} %select_n.98, s32[]{:T(128)S(6)} %select_n.96, bf16[128,4096]{1,0:T(8,128)(2,1)} %collective-permute-done.1), kind=kLoop, calls=%fused_computation.20 | loop fusion | bytes 2097160 | tf_op jit(solution)/shard_map/dynamic_update_slice | solution.py:29
  53.7 2.6 %collective-permute-done.5 = bf16[64,4096]{1,0:T(8,128)(2,1)S(1)} collective-permute-done((bf16[64,4096]{1,0:T(8,128)(2,1)S(1)}, bf16[64,4096]{1,0:T(8,128)(2,1)S(1)}, u32[]{:S(2)}, u32[]{:S(2)}) %collective-permute-start.5) | collective-permute-done | bytes 524320 | tf_op jit(solution)/shard_map/ppermute | solution.py:12
  56.3 5.9 %collective-permute-start.11 = (bf16[64,4096]{1,0:T(8,128)(2,1)S(1)}, bf16[64,4096]{1,0:T(8,128)(2,1)S(1)}, u32[]{:S(2)}, u32[]{:S(2)}) collective-permute-start(bf16[64,4096]{1,0:T(8,128)(2,1)S(1)} %slice.42), channel_id=1, source_target_pairs={{0,38},{2,0},{4,2},{6,4},{32,6},{34,32},{36,34},{38,36},{1,39},{3,... | collective-permute-start | bytes 1572872 | tf_op jit(solution)/shard_map/ppermute | solution.py:12
  63.8 2.3 %bitcast_dynamic-update-slice_fusion.4 = bf16[4,2,128,4096]{3,2,1,0:T(8,128)(2,1)} fusion(bf16[4,2,128,4096]{3,2,1,0:T(8,128)(2,1)} %bitcast_dynamic-update-slice_fusion.5, s32[]{:T(128)S(6)} %select_n.99, s32[]{:T(128)S(6)} %select_n.96, bf16[128,4096]{1,0:T(8,128)(2,1)} %collective-permute-done.3), kind=kLoop, calls=%fused_computation.18 | loop fusion | bytes 2097160 | tf_op jit(solution)/shard_map/dynamic_update_slice | solution.py:29
  70.5 2.9 %fusion.8 = bf16[1024,512]{1,0:T(8,128)(2,1)S(1)} fusion(bf16[1024,512]{1,0:T(8,128)(2,1)S(1)} %bitcast.59, bf16[1024,4096]{1,0:T(8,128)(2,1)} %bitcast.15, s32[]{:T(128)S(6)} %select_n.101), kind=kOutput, calls=%fused_computation.10 | convolution fusion | flops 1074266112 | bytes 4194308 | tf_op jit(solution)/shard_map/dot_general | solution.py:57
  76.7 11.0 %collective-permute-done.12 = bf16[512,512]{1,0:T(8,128)(2,1)S(1)} collective-permute-done((bf16[512,512]{1,0:T(8,128)(2,1)S(1)}, bf16[512,512]{1,0:T(8,128)(2,1)S(1)}, u32[]{:S(2)}, u32[]{:S(2)}) %collective-permute-start.12) | collective-permute-done | bytes 524320 | tf_op jit(solution)/shard_map/ppermute | solution.py:12
  89.1 2.9 %fusion.11 = bf16[1024,512]{1,0:T(8,128)(2,1)S(1)} fusion(bf16[1024,512]{1,0:T(8,128)(2,1)S(1)} %bitcast.60, bf16[1024,4096]{1,0:T(8,128)(2,1)} %bitcast.15, s32[]{:T(128)S(6)} %select_n.113), kind=kOutput, calls=%fused_computation.11 | convolution fusion | flops 1074266112 | bytes 4194308 | tf_op jit(solution)/shard_map/dot_general | solution.py:57
  92.7 2.9 %fusion.17 = bf16[1024,512]{1,0:T(8,128)(2,1)S(1)} fusion(bf16[1024,512]{1,0:T(8,128)(2,1)S(1)} %bitcast.61, bf16[1024,4096]{1,0:T(8,128)(2,1)} %bitcast.15, s32[]{:T(128)S(6)} %select_n.115), kind=kOutput, calls=%fused_computation.13 | convolution fusion | flops 1074266112 | bytes 4194308 | tf_op jit(solution)/shard_map/dot_general | solution.py:57
  95.8 3.0 %collective-permute-start.18 = (bf16[1024,512]{1,0:T(8,128)(2,1)S(1)}, bf16[1024,512]{1,0:T(8,128)(2,1)S(1)}, u32[]{:S(2)}, u32[]{:S(2)}) collective-permute-start(bf16[1024,512]{1,0:T(8,128)(2,1)S(1)} %fusion.21), channel_id=1, source_target_pairs={{0,64},{64,128},{128,192},{192,0},{1,65},{65,129},{129,193},{193,1... | collective-permute-start | bytes 3145736 | tf_op jit(solution)/shard_map/ppermute | solution.py:12
  100.4 9.1 %convolution_convert_fusion = bf16[1024,512]{1,0:T(8,128)(2,1)S(1)} fusion(bf16[1024,4096]{1,0:T(8,128)(2,1)} %bitcast.15, bf16[512,4096]{1,0:T(8,128)(2,1)} %bitcast.21), kind=kOutput, calls=%fused_computation.9 | convolution fusion | flops 4295491584 | bytes 13631488 | tf_op jit(solution)/shard_map/dot_general | solution.py:75
  109.8 2.6 %collective-permute-start.15 = (bf16[1024,128]{1,0:T(8,128)(2,1)S(1)}, bf16[1024,128]{1,0:T(8,128)(2,1)S(1)}, u32[]{:S(2)}, u32[]{:S(2)}) collective-permute-start(bf16[1024,128]{1,0:T(8,128)(2,1)S(1)} %get-tuple-element.33), channel_id=1, source_target_pairs={{0,4},{2,6},{4,0},{6,2},{1,5},{3,7},{5,1},{7,3},{8,12},{10,14},{12... | collective-permute-start | bytes 786440 | tf_op jit(solution)/shard_map/ppermute | solution.py:12
  113.6 2.9 %fusion.14 = bf16[1024,512]{1,0:T(8,128)(2,1)S(1)} fusion(bf16[1024,512]{1,0:T(8,128)(2,1)S(1)} %bitcast.62, bf16[1024,4096]{1,0:T(8,128)(2,1)} %bitcast.15, s32[]{:T(128)S(6)} %select_n.114), kind=kOutput, calls=%fused_computation.12 | convolution fusion | flops 1074266112 | bytes 4194308 | tf_op jit(solution)/shard_map/dot_general | solution.py:57
  116.5 4.4 %collective-permute-done.14 = bf16[1024,128]{1,0:T(8,128)(2,1)S(1)} collective-permute-done((bf16[1024,128]{1,0:T(8,128)(2,1)S(1)}, bf16[1024,128]{1,0:T(8,128)(2,1)S(1)}, u32[]{:S(2)}, u32[]{:S(2)}) %collective-permute-start.14) | collective-permute-done | bytes 262176 | tf_op jit(solution)/shard_map/ppermute | solution.py:12
  121.0 8.9 %collective-permute-done.15 = bf16[1024,128]{1,0:T(8,128)(2,1)S(1)} collective-permute-done((bf16[1024,128]{1,0:T(8,128)(2,1)S(1)}, bf16[1024,128]{1,0:T(8,128)(2,1)S(1)}, u32[]{:S(2)}, u32[]{:S(2)}) %collective-permute-start.15) | collective-permute-done | bytes 262176 | tf_op jit(solution)/shard_map/ppermute | solution.py:12
  130.4 6.1 %collective-permute-start.21 = (bf16[1024,128]{1,0:T(8,128)(2,1)S(1)}, bf16[1024,128]{1,0:T(8,128)(2,1)S(1)}, u32[]{:S(2)}, u32[]{:S(2)}) collective-permute-start(bf16[1024,128]{1,0:T(8,128)(2,1)S(1)} %get-tuple-element.29), channel_id=1, source_target_pairs={{0,38},{2,0},{4,2},{6,4},{32,6},{34,32},{36,34},{38,36},{1,39},{3,... | collective-permute-start | bytes 786440 | tf_op jit(solution)/shard_map/ppermute | solution.py:12
  137.5 3.3 %collective-permute-start.22 = (bf16[512,128]{1,0:T(8,128)(2,1)S(1)}, bf16[512,128]{1,0:T(8,128)(2,1)S(1)}, u32[]{:S(2)}, u32[]{:S(2)}) collective-permute-start(bf16[512,128]{1,0:T(8,128)(2,1)S(1)} %get-tuple-element.26), channel_id=1, source_target_pairs={{0,36},{2,38},{4,0},{6,2},{32,4},{34,6},{36,32},{38,34},{1,37},{3,... | collective-permute-start | bytes 393224 | tf_op jit(solution)/shard_map/ppermute | solution.py:12
  140.8 9.7 %collective-permute-done.23 = bf16[512,128]{1,0:T(8,128)(2,1)S(1)} collective-permute-done((bf16[512,128]{1,0:T(8,128)(2,1)S(1)}, bf16[512,128]{1,0:T(8,128)(2,1)S(1)}, u32[]{:S(2)}, u32[]{:S(2)}) %collective-permute-start.23) | collective-permute-done | bytes 131104 | tf_op jit(solution)/shard_map/ppermute | solution.py:12
  150.7 2.6 %collective-permute-start.24 = (bf16[1024,128]{1,0:T(8,128)(2,1)S(1)}, bf16[1024,128]{1,0:T(8,128)(2,1)S(1)}, u32[]{:S(2)}, u32[]{:S(2)}) collective-permute-start(bf16[1024,128]{1,0:T(8,128)(2,1)S(1)} %add_convert_fusion.4), channel_id=1, source_target_pairs={{0,32},{32,0},{1,33},{33,1},{2,34},{34,2},{3,35},{35,3},{4,36},{36... | collective-permute-start | bytes 786440 | tf_op jit(solution)/shard_map/ppermute | solution.py:12
  153.6 13.4 %collective-permute-done.24 = bf16[1024,128]{1,0:T(8,128)(2,1)S(1)} collective-permute-done((bf16[1024,128]{1,0:T(8,128)(2,1)S(1)}, bf16[1024,128]{1,0:T(8,128)(2,1)S(1)}, u32[]{:S(2)}, u32[]{:S(2)}) %collective-permute-start.24) | collective-permute-done | bytes 262176 | tf_op jit(solution)/shard_map/ppermute | solution.py:12
  169.6 6.8 %collective-permute-done.25 = bf16[128,1024]{0,1:T(8,128)(2,1)S(1)} collective-permute-done((bf16[128,1024]{0,1:T(8,128)(2,1)S(1)}, bf16[128,1024]{0,1:T(8,128)(2,1)S(1)}, u32[]{:S(2)}, u32[]{:S(2)}) %collective-permute-start.25) | collective-permute-done | bytes 262176 | tf_op jit(solution)/shard_map/ppermute | solution.py:12
  176.5 1.6 collective-permute-done.26
  178.3 2.6 %collective-permute-done.27 = bf16[128,1024]{0,1:T(8,128)(2,1)S(1)} collective-permute-done((bf16[128,1024]{0,1:T(8,128)(2,1)S(1)}, bf16[128,1024]{0,1:T(8,128)(2,1)S(1)}, u32[]{:S(2)}, u32[]{:S(2)}) %collective-permute-start.27) | collective-permute-done | bytes 262176 | tf_op jit(solution)/shard_map/ppermute | solution.py:12
  (86 shorter events, 28.5 us)
Async XLA Ops:
  0.6 46.7 %collective-permute-start = (bf16[128,4096]{1,0:T(8,128)(2,1)}, bf16[128,4096]{1,0:T(8,128)(2,1)}, u32[]{:S(2)}, u32[]{:S(2)}) collective-permute-start(bf16[128,4096]{1,0:T(8,128)(2,1)} %bitcast.64), channel_id=1, source_target_pairs={{0,1},{1,0},{2,3},{3,2},{4,5},{5,4},{6,7},{7,6},{8,9},{9,8},{10,11... | collective-permute-start | bytes 3145736 | tf_op jit(solution)/shard_map/ppermute | solution.py:12
  0.7 42.3 %collective-permute-start.1 = (bf16[128,4096]{1,0:T(8,128)(2,1)}, bf16[128,4096]{1,0:T(8,128)(2,1)}, u32[]{:S(2)}, u32[]{:S(2)}) collective-permute-start(bf16[128,4096]{1,0:T(8,128)(2,1)} %bitcast.65), channel_id=1, source_target_pairs={{0,24},{8,0},{16,8},{24,16},{1,25},{9,1},{17,9},{25,17},{2,26},{10... | collective-permute-start | bytes 3145736 | tf_op jit(solution)/shard_map/ppermute | solution.py:12
  3.8 40.6 %collective-permute-start.3 = (bf16[128,4096]{1,0:T(8,128)(2,1)}, bf16[128,4096]{1,0:T(8,128)(2,1)}, u32[]{:S(2)}, u32[]{:S(2)}) collective-permute-start(bf16[128,4096]{1,0:T(8,128)(2,1)} %bitcast.66), channel_id=1, source_target_pairs={{0,8},{8,16},{16,24},{24,0},{1,9},{9,17},{17,25},{25,1},{2,10},{10... | collective-permute-start | bytes 3145736 | tf_op jit(solution)/shard_map/ppermute | solution.py:12
  6.5 35.2 %all-to-all-start = ((bf16[8,128,512]{1,2,0:T(8,128)(2,1)}), bf16[8,128,512]{1,2,0:T(8,128)(2,1)S(1)}, u32[]{:S(2)}, u32[]{:S(2)}) async-start(bf16[8,128,512]{1,2,0:T(8,128)(2,1)} %bitcast.9), calls=%async_computation | async-start | bytes 2097152 | tf_op jit(solution)/shard_map/all_to_all | solution.py:16
  11.0 41.0 %collective-permute-start.9 = (bf16[128,4096]{1,0:T(8,128)(2,1)}, bf16[128,4096]{1,0:T(8,128)(2,1)S(1)}, u32[]{:S(2)}, u32[]{:S(2)}) collective-permute-start(bf16[128,4096]{1,0:T(8,128)(2,1)} %param.5), channel_id=1, source_target_pairs={{0,38},{2,0},{4,2},{6,4},{32,6},{34,32},{36,34},{38,36},{1,39},{3,... | collective-permute-start | bytes 3145736 | tf_op jit(solution)/shard_map/ppermute | solution.py:12
  16.9 35.7 %collective-permute-start.10 = (bf16[128,4096]{1,0:T(8,128)(2,1)}, bf16[128,4096]{1,0:T(8,128)(2,1)S(1)}, u32[]{:S(2)}, u32[]{:S(2)}) collective-permute-start(bf16[128,4096]{1,0:T(8,128)(2,1)} %param.5), channel_id=1, source_target_pairs={{0,2},{2,4},{4,6},{6,32},{32,34},{34,36},{36,38},{38,0},{1,3},{3,5... | collective-permute-start | bytes 3145736 | tf_op jit(solution)/shard_map/ppermute | solution.py:12
  21.7 4.3 %copy-start.3 = (bf16[1,128,4096]{2,1,0:T(8,128)(2,1)S(1)}, bf16[1,128,4096]{2,1,0:T(8,128)(2,1)}, u32[]{:S(2)}) copy-start(bf16[1,128,4096]{2,1,0:T(8,128)(2,1)} %param.3) | copy-start | bytes 3145732
  44.1 12.2 %collective-permute-start.5 = (bf16[64,4096]{1,0:T(8,128)(2,1)S(1)}, bf16[64,4096]{1,0:T(8,128)(2,1)S(1)}, u32[]{:S(2)}, u32[]{:S(2)}) collective-permute-start(bf16[64,4096]{1,0:T(8,128)(2,1)S(1)} %slice.40), channel_id=1, source_target_pairs={{0,24},{8,0},{16,8},{24,16},{1,25},{9,1},{17,9},{25,17},{2,26},{10... | collective-permute-start | bytes 1572872 | tf_op jit(solution)/shard_map/ppermute | solution.py:12
  45.5 16.7 %collective-permute-start.7 = (bf16[64,4096]{1,0:T(8,128)(2,1)S(1)}, bf16[64,4096]{1,0:T(8,128)(2,1)S(1)}, u32[]{:S(2)}, u32[]{:S(2)}) collective-permute-start(bf16[64,4096]{1,0:T(8,128)(2,1)S(1)} %slice.41), channel_id=1, source_target_pairs={{0,8},{8,16},{16,24},{24,0},{1,9},{9,17},{17,25},{25,1},{2,10},{10... | collective-permute-start | bytes 1572872 | tf_op jit(solution)/shard_map/ppermute | solution.py:12
  47.4 14.9 %collective-permute-start.2 = (bf16[128,4096]{1,0:T(8,128)(2,1)}, bf16[128,4096]{1,0:T(8,128)(2,1)S(1)}, u32[]{:S(2)}, u32[]{:S(2)}) collective-permute-start(bf16[128,4096]{1,0:T(8,128)(2,1)} %collective-permute-done.1), channel_id=1, source_target_pairs={{0,1},{1,0},{2,3},{3,2},{4,5},{5,4},{6,7},{7,6},{8,9},{9,8},{10,11... | collective-permute-start | bytes 3145736 | tf_op jit(solution)/shard_map/ppermute | solution.py:12
  49.6 20.9 %copy-start = (bf16[8,128,512]{2,1,0:T(8,128)(2,1)S(1)}, bf16[8,128,512]{2,1,0:T(8,128)(2,1)}, u32[]{:S(2)}) copy-start(bf16[8,128,512]{2,1,0:T(8,128)(2,1)} %copy.21) | copy-start | bytes 3145732
  52.0 14.0 %collective-permute-start.4 = (bf16[128,4096]{1,0:T(8,128)(2,1)}, bf16[128,4096]{1,0:T(8,128)(2,1)S(1)}, u32[]{:S(2)}, u32[]{:S(2)}) collective-permute-start(bf16[128,4096]{1,0:T(8,128)(2,1)} %collective-permute-done.3), channel_id=1, source_target_pairs={{0,1},{1,0},{2,3},{3,2},{4,5},{5,4},{6,7},{7,6},{8,9},{9,8},{10,11... | collective-permute-start | bytes 3145736 | tf_op jit(solution)/shard_map/ppermute | solution.py:12
  56.3 20.4 %collective-permute-start.11 = (bf16[64,4096]{1,0:T(8,128)(2,1)S(1)}, bf16[64,4096]{1,0:T(8,128)(2,1)S(1)}, u32[]{:S(2)}, u32[]{:S(2)}) collective-permute-start(bf16[64,4096]{1,0:T(8,128)(2,1)S(1)} %slice.42), channel_id=1, source_target_pairs={{0,38},{2,0},{4,2},{6,4},{32,6},{34,32},{36,34},{38,36},{1,39},{3,... | collective-permute-start | bytes 1572872 | tf_op jit(solution)/shard_map/ppermute | solution.py:12
  62.2 25.5 %collective-permute-start.13 = (bf16[64,4096]{1,0:T(8,128)(2,1)S(1)}, bf16[64,4096]{1,0:T(8,128)(2,1)S(1)}, u32[]{:S(2)}, u32[]{:S(2)}) collective-permute-start(bf16[64,4096]{1,0:T(8,128)(2,1)S(1)} %slice.44), channel_id=1, source_target_pairs={{0,2},{2,4},{4,6},{6,32},{32,34},{34,36},{36,38},{38,0},{1,3},{3,5... | collective-permute-start | bytes 1572872 | tf_op jit(solution)/shard_map/ppermute | solution.py:12
  62.2 5.8 %collective-permute-start.6 = (bf16[64,4096]{1,0:T(8,128)(2,1)S(1)}, bf16[64,4096]{1,0:T(8,128)(2,1)S(1)}, u32[]{:S(2)}, u32[]{:S(2)}) collective-permute-start(bf16[64,4096]{1,0:T(8,128)(2,1)S(1)} %collective-permute-done.5), channel_id=1, source_target_pairs={{0,1},{1,0},{2,3},{3,2},{4,5},{5,4},{6,7},{7,6},{8,9},{9,8},{10,11... | collective-permute-start | bytes 1572872 | tf_op jit(solution)/shard_map/ppermute | solution.py:12
  62.2 7.5 %collective-permute-start.8 = (bf16[64,4096]{1,0:T(8,128)(2,1)S(1)}, bf16[64,4096]{1,0:T(8,128)(2,1)S(1)}, u32[]{:S(2)}, u32[]{:S(2)}) collective-permute-start(bf16[64,4096]{1,0:T(8,128)(2,1)S(1)} %collective-permute-done.7), channel_id=1, source_target_pairs={{0,1},{1,0},{2,3},{3,2},{4,5},{5,4},{6,7},{7,6},{8,9},{9,8},{10,11... | collective-permute-start | bytes 1572872 | tf_op jit(solution)/shard_map/ppermute | solution.py:12
  73.5 14.2 %collective-permute-start.12 = (bf16[512,512]{1,0:T(8,128)(2,1)S(1)}, bf16[512,512]{1,0:T(8,128)(2,1)S(1)}, u32[]{:S(2)}, u32[]{:S(2)}) collective-permute-start(bf16[512,512]{1,0:T(8,128)(2,1)S(1)} %get-tuple-element.31), channel_id=1, source_target_pairs={{0,64},{64,128},{128,192},{192,0},{1,65},{65,129},{129,193},{193,1... | collective-permute-start | bytes 1572872 | tf_op jit(solution)/shard_map/ppermute | solution.py:12
  74.1 15.1 %collective-permute-start.17 = (bf16[512,512]{1,0:T(8,128)(2,1)S(1)}, bf16[512,512]{1,0:T(8,128)(2,1)S(1)}, u32[]{:S(2)}, u32[]{:S(2)}) collective-permute-start(bf16[512,512]{1,0:T(8,128)(2,1)S(1)} %get-tuple-element.30), channel_id=1, source_target_pairs={{0,192},{64,0},{128,64},{192,128},{1,193},{65,1},{129,65},{193,129... | collective-permute-start | bytes 1572872 | tf_op jit(solution)/shard_map/ppermute | solution.py:12
  92.3 37.6 %collective-permute-start.19 = (bf16[1024,512]{1,0:T(8,128)(2,1)S(1)}, bf16[1024,512]{1,0:T(8,128)(2,1)S(1)}, u32[]{:S(2)}, u32[]{:S(2)}) collective-permute-start(bf16[1024,512]{1,0:T(8,128)(2,1)S(1)} %fusion.20), channel_id=1, source_target_pairs={{0,192},{64,0},{128,64},{192,128},{1,193},{65,1},{129,65},{193,129... | collective-permute-start | bytes 3145736 | tf_op jit(solution)/shard_map/ppermute | solution.py:12
  95.8 34.0 %collective-permute-start.18 = (bf16[1024,512]{1,0:T(8,128)(2,1)S(1)}, bf16[1024,512]{1,0:T(8,128)(2,1)S(1)}, u32[]{:S(2)}, u32[]{:S(2)}) collective-permute-start(bf16[1024,512]{1,0:T(8,128)(2,1)S(1)} %fusion.21), channel_id=1, source_target_pairs={{0,64},{64,128},{128,192},{192,0},{1,65},{65,129},{129,193},{193,1... | collective-permute-start | bytes 3145736 | tf_op jit(solution)/shard_map/ppermute | solution.py:12
  109.7 11.2 %collective-permute-start.14 = (bf16[1024,128]{1,0:T(8,128)(2,1)S(1)}, bf16[1024,128]{1,0:T(8,128)(2,1)S(1)}, u32[]{:S(2)}, u32[]{:S(2)}) collective-permute-start(bf16[1024,128]{1,0:T(8,128)(2,1)S(1)} %get-tuple-element.34), channel_id=1, source_target_pairs={{0,2},{2,4},{4,6},{6,0},{1,3},{3,5},{5,7},{7,1},{8,10},{10,12},{12... | collective-permute-start | bytes 786440 | tf_op jit(solution)/shard_map/ppermute | solution.py:12
  109.8 20.0 %collective-permute-start.15 = (bf16[1024,128]{1,0:T(8,128)(2,1)S(1)}, bf16[1024,128]{1,0:T(8,128)(2,1)S(1)}, u32[]{:S(2)}, u32[]{:S(2)}) collective-permute-start(bf16[1024,128]{1,0:T(8,128)(2,1)S(1)} %get-tuple-element.33), channel_id=1, source_target_pairs={{0,4},{2,6},{4,0},{6,2},{1,5},{3,7},{5,1},{7,3},{8,12},{10,14},{12... | collective-permute-start | bytes 786440 | tf_op jit(solution)/shard_map/ppermute | solution.py:12
  112.4 17.5 %collective-permute-start.16 = (bf16[1024,128]{1,0:T(8,128)(2,1)S(1)}, bf16[1024,128]{1,0:T(8,128)(2,1)S(1)}, u32[]{:S(2)}, u32[]{:S(2)}) collective-permute-start(bf16[1024,128]{1,0:T(8,128)(2,1)S(1)} %get-tuple-element.32), channel_id=1, source_target_pairs={{0,6},{2,0},{4,2},{6,4},{1,7},{3,1},{5,3},{7,5},{8,14},{10,8},{12,... | collective-permute-start | bytes 786440 | tf_op jit(solution)/shard_map/ppermute | solution.py:12
  130.4 20.1 %collective-permute-start.21 = (bf16[1024,128]{1,0:T(8,128)(2,1)S(1)}, bf16[1024,128]{1,0:T(8,128)(2,1)S(1)}, u32[]{:S(2)}, u32[]{:S(2)}) collective-permute-start(bf16[1024,128]{1,0:T(8,128)(2,1)S(1)} %get-tuple-element.29), channel_id=1, source_target_pairs={{0,38},{2,0},{4,2},{6,4},{32,6},{34,32},{36,34},{38,36},{1,39},{3,... | collective-permute-start | bytes 786440 | tf_op jit(solution)/shard_map/ppermute | solution.py:12
  136.5 14.0 %collective-permute-start.20 = (bf16[1024,128]{1,0:T(8,128)(2,1)S(1)}, bf16[1024,128]{1,0:T(8,128)(2,1)S(1)}, u32[]{:S(2)}, u32[]{:S(2)}) collective-permute-start(bf16[1024,128]{1,0:T(8,128)(2,1)S(1)} %get-tuple-element.28), channel_id=1, source_target_pairs={{0,2},{2,4},{4,6},{6,32},{32,34},{34,36},{36,38},{38,0},{1,3},{3,5... | collective-permute-start | bytes 786440 | tf_op jit(solution)/shard_map/ppermute | solution.py:12
  136.6 13.9 %collective-permute-start.23 = (bf16[512,128]{1,0:T(8,128)(2,1)S(1)}, bf16[512,128]{1,0:T(8,128)(2,1)S(1)}, u32[]{:S(2)}, u32[]{:S(2)}) collective-permute-start(bf16[512,128]{1,0:T(8,128)(2,1)S(1)} %get-tuple-element.27), channel_id=1, source_target_pairs={{0,4},{2,6},{4,32},{6,34},{32,36},{34,38},{36,0},{38,2},{1,5},{3,7... | collective-permute-start | bytes 393224 | tf_op jit(solution)/shard_map/ppermute | solution.py:12
  137.5 13.0 %collective-permute-start.22 = (bf16[512,128]{1,0:T(8,128)(2,1)S(1)}, bf16[512,128]{1,0:T(8,128)(2,1)S(1)}, u32[]{:S(2)}, u32[]{:S(2)}) collective-permute-start(bf16[512,128]{1,0:T(8,128)(2,1)S(1)} %get-tuple-element.26), channel_id=1, source_target_pairs={{0,36},{2,38},{4,0},{6,2},{32,4},{34,6},{36,32},{38,34},{1,37},{3,... | collective-permute-start | bytes 393224 | tf_op jit(solution)/shard_map/ppermute | solution.py:12
  150.7 16.3 %collective-permute-start.24 = (bf16[1024,128]{1,0:T(8,128)(2,1)S(1)}, bf16[1024,128]{1,0:T(8,128)(2,1)S(1)}, u32[]{:S(2)}, u32[]{:S(2)}) collective-permute-start(bf16[1024,128]{1,0:T(8,128)(2,1)S(1)} %add_convert_fusion.4), channel_id=1, source_target_pairs={{0,32},{32,0},{1,33},{33,1},{2,34},{34,2},{3,35},{35,3},{4,36},{36... | collective-permute-start | bytes 786440 | tf_op jit(solution)/shard_map/ppermute | solution.py:12
  167.0 9.3 %collective-permute-start.25 = (bf16[128,1024]{0,1:T(8,128)(2,1)S(1)}, bf16[128,1024]{0,1:T(8,128)(2,1)S(1)}, u32[]{:S(2)}, u32[]{:S(2)}) collective-permute-start(bf16[128,1024]{0,1:T(8,128)(2,1)S(1)} %fusion.22), channel_id=1, source_target_pairs={{0,64},{64,128},{128,192},{192,0},{1,65},{65,129},{129,193},{193,1... | collective-permute-start | bytes 786440 | tf_op jit(solution)/shard_map/ppermute | solution.py:12
  167.4 10.6 %collective-permute-start.26 = (bf16[128,1024]{0,1:T(8,128)(2,1)S(1)}, bf16[128,1024]{0,1:T(8,128)(2,1)S(1)}, u32[]{:S(2)}, u32[]{:S(2)}) collective-permute-start(bf16[128,1024]{0,1:T(8,128)(2,1)S(1)} %fusion.22), channel_id=1, source_target_pairs={{0,128},{64,192},{128,0},{192,64},{1,129},{65,193},{129,1},{193,65... | collective-permute-start | bytes 786440 | tf_op jit(solution)/shard_map/ppermute | solution.py:12
  168.5 12.5 %copy-start.2 = (bf16[4,4,256,128]{3,2,1,0:T(8,128)(2,1)}, bf16[4,4,256,128]{3,2,1,0:T(8,128)(2,1)S(1)}, u32[]{:S(2)}) copy-start(bf16[4,4,256,128]{3,2,1,0:T(8,128)(2,1)S(1)} %constant_dynamic-update-slice_fusion.4) | copy-start | bytes 3145732
  168.7 12.2 %collective-permute-start.27 = (bf16[128,1024]{0,1:T(8,128)(2,1)S(1)}, bf16[128,1024]{0,1:T(8,128)(2,1)S(1)}, u32[]{:S(2)}, u32[]{:S(2)}) collective-permute-start(bf16[128,1024]{0,1:T(8,128)(2,1)S(1)} %fusion.22), channel_id=1, source_target_pairs={{0,192},{64,0},{128,64},{192,128},{1,193},{65,1},{129,65},{193,129... | collective-permute-start | bytes 786440 | tf_op jit(solution)/shard_map/ppermute | solution.py:12
  (1 other events, 1.0 us)

commit v8 on v7

--- a/solution.py
+++ b/solution.py
@@ -68,8 +68,8 @@
         weights = put(weights, piece, (l + d) & 3)
     w_far_a = shift(after(w_above[:half], far_a), RING8, -1)
     w_far_b = shift(after(w_below[half:], far_a), RING8, 1)
-    weights = put(weights, after(w_far_a, top), (l + 2) & 3, 0)
-    weights = put(weights, after(w_far_b, top), (l + 2) & 3, half)
+    weights = put(weights, after(w_far_a, far), (l + 2) & 3, 0)
+    weights = put(weights, after(w_far_b, far), (l + 2) & 3, half)
     weights = weights.reshape(4 * heads, feats)
 
     res = lax.dot_general(
@@ -80,7 +80,7 @@
 
     back = [block(res, l)] + [shift(block(res, l + d), "l", d) for d in (1, 2, 3)]
 
-    near_a, near_b = partial(1, after(tokens, top)), partial(3, after(tokens, bottom))
+    near_a, near_b = partial(1, after(tokens, top, res)), partial(3, after(tokens, bottom, res))
     near_a = lax.dynamic_update_slice(near_a, add(near_a[:cols // 2], top), (0, 0))
     near_b = lax.dynamic_update_slice(near_b, add(near_b[cols // 2:], bottom), (cols // 2, 0))
     own = partial(0, after(tokens, near_b))

time: 183 us -> 181 us (0.989)
  the two profiles are of different devices: /device:TPU:6 before, /device:TPU:64 now
where the time goes in v8:
time: 181 us; the launch traced here: 180 us
  waiting for transfers between devices  74.2 us (41%)
  starting transfers between devices  40.1 us (22%)
  local copies, waits for them, and re-layouts  36 us (20%)
  matrix products  22.5 us (12%)
  other arithmetic  6.13 us (3%)
    ppermute x28, waiting for transfers between devices, shift(): return lax.ppermute(v, axis, [(i, (i + by) % n) for i in range(n)])  55.7 us
    ppermute x28, starting transfers between devices, shift(): return lax.ppermute(v, axis, [(i, (i + by) % n) for i in range(n)])  35.6 us
    dynamic_update_slice x15, local copies, waits for them, and re-layouts, put(): lax.dynamic_update_slice(buffer, piece.reshape((1,) * (buffer.ndim - piec...  19.6 us
    all_to_all x1, waiting for transfers between devices, exchange(): return lax.all_to_all(v, axis, split_axis=0, concat_axis=0, tiled=True)  18.5 us
    dot_general x4, matrix products, partial(): lax.dot_general(columns, acts, (((0,), (0,)), ((), ())), preferred_elemen...  13.4 us
    dot_general x1, matrix products, local(): lax.dot_general(after(tokens, far), weights, (((1,), (1,)), ((), ())), pr...  9.09 us
    all_to_all x1, starting transfers between devices, exchange(): return lax.all_to_all(v, axis, split_axis=0, concat_axis=0, tiled=True)  4.51 us
    broadcast_in_dim x1, local copies, waits for them, and re-layouts, local(): tokens = jnp.zeros((4, 2, toks, feats), BF16)  4.32 us
  transfers between devices with their start and end apart: 29, of which 10 were waited for; matrix products, arithmetic and copies ran while one was open for 31% of the time, Pallas kernels for 0%

profile of v8, /device:TPU:64, one launch (start us, length us, event | category | flops | bytes accessed | tf_op | source)
XLA Modules:
  0.0 179.9 jit_solution(4366778720986639545)
XLA Ops:
  0.7 3.1 %collective-permute-start.1 = (bf16[128,4096]{1,0:T(8,128)(2,1)}, bf16[128,4096]{1,0:T(8,128)(2,1)}, u32[]{:S(2)}, u32[]{:S(2)}) collective-permute-start(bf16[128,4096]{1,0:T(8,128)(2,1)} %bitcast.65), channel_id=1, source_target_pairs={{0,24},{8,0},{16,8},{24,16},{1,25},{9,1},{17,9},{25,17},{2,26},{10... | collective-permute-start | bytes 3145736 | tf_op jit(solution)/shard_map/ppermute | solution.py:12
  6.5 4.5 %all-to-all-start = ((bf16[8,128,512]{1,2,0:T(8,128)(2,1)}), bf16[8,128,512]{1,2,0:T(8,128)(2,1)S(1)}, u32[]{:S(2)}, u32[]{:S(2)}) async-start(bf16[8,128,512]{1,2,0:T(8,128)(2,1)} %bitcast.9), calls=%async_computation | async-start | bytes 2097152 | tf_op jit(solution)/shard_map/all_to_all | solution.py:16
  11.1 1.9 %collective-permute-start.10 = (bf16[128,4096]{1,0:T(8,128)(2,1)}, bf16[128,4096]{1,0:T(8,128)(2,1)S(1)}, u32[]{:S(2)}, u32[]{:S(2)}) collective-permute-start(bf16[128,4096]{1,0:T(8,128)(2,1)} %param.5), channel_id=1, source_target_pairs={{0,2},{2,4},{4,6},{6,32},{32,34},{34,36},{36,38},{38,0},{1,3},{3,5... | collective-permute-start | bytes 3145736 | tf_op jit(solution)/shard_map/ppermute | solution.py:12
  13.0 2.5 %broadcast_in_dim.14 = bf16[4,128,4096]{2,1,0:T(8,128)(2,1)} broadcast(bf16[]{:T(256)} %constant.17.clone.1), dimensions={} | broadcast | bytes 4194306 | tf_op jit(solution)/shard_map/broadcast_in_dim | solution.py:66
  15.5 2.3 %bitcast_dynamic-update-slice_fusion.2 = bf16[4,128,4096]{2,1,0:T(8,128)(2,1)} fusion(bf16[4,128,4096]{2,1,0:T(8,128)(2,1)} %broadcast_in_dim.14, s32[]{:T(128)S(6)} %select_n.102, bf16[128,4096]{1,0:T(8,128)(2,1)} %param.5), kind=kLoop, calls=%fused_computation.16 | loop fusion | bytes 2097156 | tf_op jit(solution)/shard_map/dynamic_update_slice | solution.py:29
  17.8 4.3 %broadcast_in_dim.13 = bf16[4,2,128,4096]{3,2,1,0:T(8,128)(2,1)} broadcast(bf16[]{:T(256)} %constant.17.clone.1), dimensions={} | broadcast | bytes 8388610 | tf_op jit(solution)/shard_map/broadcast_in_dim | solution.py:49
  23.2 18.5 %all-to-all-done = bf16[8,128,512]{1,2,0:T(8,128)(2,1)S(1)} async-done(((bf16[8,128,512]{1,2,0:T(8,128)(2,1)}), bf16[8,128,512]{1,2,0:T(8,128)(2,1)S(1)}, u32[]{:S(2)}, u32[]{:S(2)}) %all-to-all-start) | async-done | bytes 1048608 | tf_op jit(solution)/shard_map/all_to_all | solution.py:16
  47.4 2.3 %bitcast_dynamic-update-slice_fusion.7 = bf16[4,2,128,4096]{3,2,1,0:T(8,128)(2,1)} fusion(bf16[4,2,128,4096]{3,2,1,0:T(8,128)(2,1)} %bitcast_dynamic-update-slice_fusion.8, s32[]{:T(128)S(6)} %select_n.95, s32[]{:T(128)S(6)} %select_n.97, bf16[128,4096]{1,0:T(8,128)(2,1)} %collective-permute-done), kind=kLoop, calls=%fused_computation.21 | loop fusion | bytes 2097160 | tf_op jit(solution)/shard_map/dynamic_update_slice | solution.py:29
  49.6 2.3 %bitcast_dynamic-update-slice_fusion.6 = bf16[4,2,128,4096]{3,2,1,0:T(8,128)(2,1)} fusion(bf16[4,2,128,4096]{3,2,1,0:T(8,128)(2,1)} %bitcast_dynamic-update-slice_fusion.7, s32[]{:T(128)S(6)} %select_n.98, s32[]{:T(128)S(6)} %select_n.96, bf16[128,4096]{1,0:T(8,128)(2,1)} %collective-permute-done.1), kind=kLoop, calls=%fused_computation.20 | loop fusion | bytes 2097160 | tf_op jit(solution)/shard_map/dynamic_update_slice | solution.py:29
  56.4 1.9 %collective-permute-start.12 = (bf16[64,4096]{1,0:T(8,128)(2,1)S(1)}, bf16[64,4096]{1,0:T(8,128)(2,1)S(1)}, u32[]{:S(2)}, u32[]{:S(2)}) collective-permute-start(bf16[64,4096]{1,0:T(8,128)(2,1)S(1)} %slice.43), channel_id=1, source_target_pairs={{0,2},{2,4},{4,6},{6,32},{32,34},{34,36},{36,38},{38,0},{1,3},{3,5... | collective-permute-start | bytes 1572872 | tf_op jit(solution)/shard_map/ppermute | solution.py:12
  60.3 2.3 %bitcast_dynamic-update-slice_fusion.4 = bf16[4,2,128,4096]{3,2,1,0:T(8,128)(2,1)} fusion(bf16[4,2,128,4096]{3,2,1,0:T(8,128)(2,1)} %bitcast_dynamic-update-slice_fusion.5, s32[]{:T(128)S(6)} %select_n.99, s32[]{:T(128)S(6)} %select_n.96, bf16[128,4096]{1,0:T(8,128)(2,1)} %collective-permute-done.3), kind=kLoop, calls=%fused_computation.18 | loop fusion | bytes 2097160 | tf_op jit(solution)/shard_map/dynamic_update_slice | solution.py:29
  67.1 2.9 %fusion.8 = bf16[1024,512]{1,0:T(8,128)(2,1)S(1)} fusion(bf16[1024,512]{1,0:T(8,128)(2,1)S(1)} %bitcast.59, bf16[1024,4096]{1,0:T(8,128)(2,1)} %bitcast.15, s32[]{:T(128)S(6)} %select_n.101), kind=kOutput, calls=%fused_computation.10 | convolution fusion | flops 1074266112 | bytes 4194308 | tf_op jit(solution)/shard_map/dot_general | solution.py:57
  70.0 2.8 %collective-permute-start.16 = (bf16[512,512]{1,0:T(8,128)(2,1)S(1)}, bf16[512,512]{1,0:T(8,128)(2,1)S(1)}, u32[]{:S(2)}, u32[]{:S(2)}) collective-permute-start(bf16[512,512]{1,0:T(8,128)(2,1)S(1)} %get-tuple-element.31), channel_id=1, source_target_pairs={{0,192},{64,0},{128,64},{192,128},{1,193},{65,1},{129,65},{193,129... | collective-permute-start | bytes 1572872 | tf_op jit(solution)/shard_map/ppermute | solution.py:12
  74.6 9.1 %convolution_convert_fusion = bf16[1024,512]{1,0:T(8,128)(2,1)S(1)} fusion(bf16[1024,4096]{1,0:T(8,128)(2,1)} %bitcast.15, bf16[512,4096]{1,0:T(8,128)(2,1)} %bitcast.21), kind=kOutput, calls=%fused_computation.9 | convolution fusion | flops 4295491584 | bytes 13631488 | tf_op jit(solution)/shard_map/dot_general | solution.py:75
  84.3 3.4 %collective-permute-done.17 = bf16[512,512]{1,0:T(8,128)(2,1)S(1)} collective-permute-done((bf16[512,512]{1,0:T(8,128)(2,1)S(1)}, bf16[512,512]{1,0:T(8,128)(2,1)S(1)}, u32[]{:S(2)}, u32[]{:S(2)}) %collective-permute-start.17) | collective-permute-done | bytes 524320 | tf_op jit(solution)/shard_map/ppermute | solution.py:12
  87.7 3.8 %fusion.17 = bf16[1024,512]{1,0:T(8,128)(2,1)} fusion(bf16[1024,512]{1,0:T(8,128)(2,1)S(1)} %bitcast.60, bf16[1024,4096]{1,0:T(8,128)(2,1)} %bitcast.15, s32[]{:T(128)S(6)} %select_n.115), kind=kOutput, calls=%fused_computation.13 | convolution fusion | flops 1074266112 | bytes 4194308 | tf_op jit(solution)/shard_map/dot_general | solution.py:57
  91.6 2.0 %fusion.21 = bf16[1024,512]{1,0:T(8,128)(2,1)} fusion(bf16[1024,512]{1,0:T(8,128)(2,1)} %fusion.17, bf16[512,512]{1,0:T(8,128)(2,1)S(1)} %collective-permute-done.17), kind=kLoop, calls=%fused_computation.26 | loop fusion | flops 1048576 | bytes 1572864 | tf_op jit(solution)/shard_map/dynamic_update_slice | solution.py:84
  93.5 3.9 %fusion.11 = bf16[1024,512]{1,0:T(8,128)(2,1)} fusion(bf16[1024,512]{1,0:T(8,128)(2,1)S(1)} %bitcast.61, bf16[1024,4096]{1,0:T(8,128)(2,1)} %bitcast.15, s32[]{:T(128)S(6)} %select_n.113), kind=kOutput, calls=%fused_computation.11 | convolution fusion | flops 1074266112 | bytes 4194308 | tf_op jit(solution)/shard_map/dot_general | solution.py:57
  97.4 2.0 %fusion.20 = bf16[1024,512]{1,0:T(8,128)(2,1)} fusion(bf16[1024,512]{1,0:T(8,128)(2,1)} %fusion.11, bf16[512,512]{1,0:T(8,128)(2,1)S(1)} %collective-permute-done.16), kind=kLoop, calls=%fused_computation.25 | loop fusion | flops 1048576 | bytes 1572864 | tf_op jit(solution)/shard_map/dynamic_update_slice | solution.py:85
  99.4 3.2 %collective-permute-start.19 = (bf16[1024,512]{1,0:T(8,128)(2,1)}, bf16[1024,512]{1,0:T(8,128)(2,1)}, u32[]{:S(2)}, u32[]{:S(2)}) collective-permute-start(bf16[1024,512]{1,0:T(8,128)(2,1)} %fusion.20), channel_id=1, source_target_pairs={{0,192},{64,0},{128,64},{192,128},{1,193},{65,1},{129,65},{193,129... | collective-permute-start | bytes 3145736 | tf_op jit(solution)/shard_map/ppermute | solution.py:12
  102.8 3.0 %collective-permute-start.13 = (bf16[1024,128]{1,0:T(8,128)(2,1)S(1)}, bf16[1024,128]{1,0:T(8,128)(2,1)S(1)}, u32[]{:S(2)}, u32[]{:S(2)}) collective-permute-start(bf16[1024,128]{1,0:T(8,128)(2,1)S(1)} %get-tuple-element.34), channel_id=1, source_target_pairs={{0,2},{2,4},{4,6},{6,0},{1,3},{3,5},{5,7},{7,1},{8,10},{10,12},{12... | collective-permute-start | bytes 786440 | tf_op jit(solution)/shard_map/ppermute | solution.py:12
  106.5 2.6 %collective-permute-start.15 = (bf16[1024,128]{1,0:T(8,128)(2,1)S(1)}, bf16[1024,128]{1,0:T(8,128)(2,1)S(1)}, u32[]{:S(2)}, u32[]{:S(2)}) collective-permute-start(bf16[1024,128]{1,0:T(8,128)(2,1)S(1)} %get-tuple-element.32), channel_id=1, source_target_pairs={{0,6},{2,0},{4,2},{6,4},{1,7},{3,1},{5,3},{7,5},{8,14},{10,8},{12,... | collective-permute-start | bytes 786440 | tf_op jit(solution)/shard_map/ppermute | solution.py:12
  109.1 2.9 %fusion.14 = bf16[1024,512]{1,0:T(8,128)(2,1)S(1)} fusion(bf16[1024,512]{1,0:T(8,128)(2,1)S(1)} %bitcast.62, bf16[1024,4096]{1,0:T(8,128)(2,1)} %bitcast.15, s32[]{:T(128)S(6)} %select_n.114), kind=kOutput, calls=%fused_computation.12 | convolution fusion | flops 1074266112 | bytes 4194308 | tf_op jit(solution)/shard_map/dot_general | solution.py:57
  112.0 11.4 %collective-permute-done.13 = bf16[1024,128]{1,0:T(8,128)(2,1)S(1)} collective-permute-done((bf16[1024,128]{1,0:T(8,128)(2,1)S(1)}, bf16[1024,128]{1,0:T(8,128)(2,1)S(1)}, u32[]{:S(2)}, u32[]{:S(2)}) %collective-permute-start.13) | collective-permute-done | bytes 262176 | tf_op jit(solution)/shard_map/ppermute | solution.py:12
  123.3 3.4 %collective-permute-done.15 = bf16[1024,128]{1,0:T(8,128)(2,1)S(1)} collective-permute-done((bf16[1024,128]{1,0:T(8,128)(2,1)S(1)}, bf16[1024,128]{1,0:T(8,128)(2,1)S(1)}, u32[]{:S(2)}, u32[]{:S(2)}) %collective-permute-start.15) | collective-permute-done | bytes 262176 | tf_op jit(solution)/shard_map/ppermute | solution.py:12
  126.7 2.0 %add_convert_fusion = bf16[1024,512]{1,0:T(8,128)(2,1)S(1)} fusion(bf16[1024,512]{1,0:T(8,128)(2,1)} %collective-permute-done.19, bf16[1024,512]{1,0:T(8,128)(2,1)} %collective-permute-done.18, bf16[1024,512]{1,0:T(8,128)(2,1)S(1)} %fusion.14), kind=kLoop, calls=%fused_computation | loop fusion | flops 3145728 | bytes 4194304 | tf_op jit(solution)/shard_map/convert_element_type | solution.py:88
  131.5 3.1 %collective-permute-start.22 = (bf16[512,128]{1,0:T(8,128)(2,1)S(1)}, bf16[512,128]{1,0:T(8,128)(2,1)S(1)}, u32[]{:S(2)}, u32[]{:S(2)}) collective-permute-start(bf16[512,128]{1,0:T(8,128)(2,1)S(1)} %get-tuple-element.26), channel_id=1, source_target_pairs={{0,36},{2,38},{4,0},{6,2},{32,4},{34,6},{36,32},{38,34},{1,37},{3,... | collective-permute-start | bytes 393224 | tf_op jit(solution)/shard_map/ppermute | solution.py:12
  135.7 11.2 %collective-permute-done.22 = bf16[512,128]{1,0:T(8,128)(2,1)S(1)} collective-permute-done((bf16[512,128]{1,0:T(8,128)(2,1)S(1)}, bf16[512,128]{1,0:T(8,128)(2,1)S(1)}, u32[]{:S(2)}, u32[]{:S(2)}) %collective-permute-start.22) | collective-permute-done | bytes 131104 | tf_op jit(solution)/shard_map/ppermute | solution.py:12
  147.1 2.5 %collective-permute-start.24 = (bf16[1024,128]{1,0:T(8,128)(2,1)S(1)}, bf16[1024,128]{1,0:T(8,128)(2,1)S(1)}, u32[]{:S(2)}, u32[]{:S(2)}) collective-permute-start(bf16[1024,128]{1,0:T(8,128)(2,1)S(1)} %add_convert_fusion.4), channel_id=1, source_target_pairs={{0,32},{32,0},{1,33},{33,1},{2,34},{34,2},{3,35},{35,3},{4,36},{36... | collective-permute-start | bytes 786440 | tf_op jit(solution)/shard_map/ppermute | solution.py:12
  149.9 12.6 %collective-permute-done.24 = bf16[1024,128]{1,0:T(8,128)(2,1)S(1)} collective-permute-done((bf16[1024,128]{1,0:T(8,128)(2,1)S(1)}, bf16[1024,128]{1,0:T(8,128)(2,1)S(1)}, u32[]{:S(2)}, u32[]{:S(2)}) %collective-permute-start.24) | collective-permute-done | bytes 262176 | tf_op jit(solution)/shard_map/ppermute | solution.py:12
  163.0 3.2 %collective-permute-start.27 = (bf16[128,1024]{0,1:T(8,128)(2,1)S(1)}, bf16[128,1024]{0,1:T(8,128)(2,1)S(1)}, u32[]{:S(2)}, u32[]{:S(2)}) collective-permute-start(bf16[128,1024]{0,1:T(8,128)(2,1)S(1)} %fusion.22), channel_id=1, source_target_pairs={{0,192},{64,0},{128,64},{192,128},{1,193},{65,1},{129,65},{193,129... | collective-permute-start | bytes 786440 | tf_op jit(solution)/shard_map/ppermute | solution.py:12
  166.3 11.1 %collective-permute-done.25 = bf16[128,1024]{0,1:T(8,128)(2,1)} collective-permute-done((bf16[128,1024]{0,1:T(8,128)(2,1)S(1)}, bf16[128,1024]{0,1:T(8,128)(2,1)}, u32[]{:S(2)}, u32[]{:S(2)}) %collective-permute-start.25) | collective-permute-done | bytes 262176 | tf_op jit(solution)/shard_map/ppermute | solution.py:12
  (86 shorter events, 31.1 us)
Async XLA Ops:
  0.6 46.7 %collective-permute-start = (bf16[128,4096]{1,0:T(8,128)(2,1)}, bf16[128,4096]{1,0:T(8,128)(2,1)}, u32[]{:S(2)}, u32[]{:S(2)}) collective-permute-start(bf16[128,4096]{1,0:T(8,128)(2,1)} %bitcast.64), channel_id=1, source_target_pairs={{0,1},{1,0},{2,3},{3,2},{4,5},{5,4},{6,7},{7,6},{8,9},{9,8},{10,11... | collective-permute-start | bytes 3145736 | tf_op jit(solution)/shard_map/ppermute | solution.py:12
  0.7 42.3 %collective-permute-start.1 = (bf16[128,4096]{1,0:T(8,128)(2,1)}, bf16[128,4096]{1,0:T(8,128)(2,1)}, u32[]{:S(2)}, u32[]{:S(2)}) collective-permute-start(bf16[128,4096]{1,0:T(8,128)(2,1)} %bitcast.65), channel_id=1, source_target_pairs={{0,24},{8,0},{16,8},{24,16},{1,25},{9,1},{17,9},{25,17},{2,26},{10... | collective-permute-start | bytes 3145736 | tf_op jit(solution)/shard_map/ppermute | solution.py:12
  3.8 40.6 %collective-permute-start.3 = (bf16[128,4096]{1,0:T(8,128)(2,1)}, bf16[128,4096]{1,0:T(8,128)(2,1)}, u32[]{:S(2)}, u32[]{:S(2)}) collective-permute-start(bf16[128,4096]{1,0:T(8,128)(2,1)} %bitcast.66), channel_id=1, source_target_pairs={{0,8},{8,16},{16,24},{24,0},{1,9},{9,17},{17,25},{25,1},{2,10},{10... | collective-permute-start | bytes 3145736 | tf_op jit(solution)/shard_map/ppermute | solution.py:12
  6.5 35.2 %all-to-all-start = ((bf16[8,128,512]{1,2,0:T(8,128)(2,1)}), bf16[8,128,512]{1,2,0:T(8,128)(2,1)S(1)}, u32[]{:S(2)}, u32[]{:S(2)}) async-start(bf16[8,128,512]{1,2,0:T(8,128)(2,1)} %bitcast.9), calls=%async_computation | async-start | bytes 2097152 | tf_op jit(solution)/shard_map/all_to_all | solution.py:16
  11.0 41.0 %collective-permute-start.9 = (bf16[128,4096]{1,0:T(8,128)(2,1)}, bf16[128,4096]{1,0:T(8,128)(2,1)S(1)}, u32[]{:S(2)}, u32[]{:S(2)}) collective-permute-start(bf16[128,4096]{1,0:T(8,128)(2,1)} %param.5), channel_id=1, source_target_pairs={{0,38},{2,0},{4,2},{6,4},{32,6},{34,32},{36,34},{38,36},{1,39},{3,... | collective-permute-start | bytes 3145736 | tf_op jit(solution)/shard_map/ppermute | solution.py:12
  11.1 42.5 %collective-permute-start.10 = (bf16[128,4096]{1,0:T(8,128)(2,1)}, bf16[128,4096]{1,0:T(8,128)(2,1)S(1)}, u32[]{:S(2)}, u32[]{:S(2)}) collective-permute-start(bf16[128,4096]{1,0:T(8,128)(2,1)} %param.5), channel_id=1, source_target_pairs={{0,2},{2,4},{4,6},{6,32},{32,34},{34,36},{36,38},{38,0},{1,3},{3,5... | collective-permute-start | bytes 3145736 | tf_op jit(solution)/shard_map/ppermute | solution.py:12
  17.8 4.3 %copy-start.3 = (bf16[1,128,4096]{2,1,0:T(8,128)(2,1)S(1)}, bf16[1,128,4096]{2,1,0:T(8,128)(2,1)}, u32[]{:S(2)}) copy-start(bf16[1,128,4096]{2,1,0:T(8,128)(2,1)} %param.3) | copy-start | bytes 3145732
  44.1 12.2 %collective-permute-start.5 = (bf16[64,4096]{1,0:T(8,128)(2,1)S(1)}, bf16[64,4096]{1,0:T(8,128)(2,1)S(1)}, u32[]{:S(2)}, u32[]{:S(2)}) collective-permute-start(bf16[64,4096]{1,0:T(8,128)(2,1)S(1)} %slice.40), channel_id=1, source_target_pairs={{0,24},{8,0},{16,8},{24,16},{1,25},{9,1},{17,9},{25,17},{2,26},{10... | collective-permute-start | bytes 1572872 | tf_op jit(solution)/shard_map/ppermute | solution.py:12
  45.5 13.2 %collective-permute-start.7 = (bf16[64,4096]{1,0:T(8,128)(2,1)S(1)}, bf16[64,4096]{1,0:T(8,128)(2,1)S(1)}, u32[]{:S(2)}, u32[]{:S(2)}) collective-permute-start(bf16[64,4096]{1,0:T(8,128)(2,1)S(1)} %slice.41), channel_id=1, source_target_pairs={{0,8},{8,16},{16,24},{24,0},{1,9},{9,17},{17,25},{25,1},{2,10},{10... | collective-permute-start | bytes 1572872 | tf_op jit(solution)/shard_map/ppermute | solution.py:12
  47.4 11.4 %collective-permute-start.2 = (bf16[128,4096]{1,0:T(8,128)(2,1)}, bf16[128,4096]{1,0:T(8,128)(2,1)S(1)}, u32[]{:S(2)}, u32[]{:S(2)}) collective-permute-start(bf16[128,4096]{1,0:T(8,128)(2,1)} %collective-permute-done.1), channel_id=1, source_target_pairs={{0,1},{1,0},{2,3},{3,2},{4,5},{5,4},{6,7},{7,6},{8,9},{9,8},{10,11... | collective-permute-start | bytes 3145736 | tf_op jit(solution)/shard_map/ppermute | solution.py:12
  52.0 15.1 %copy-start = (bf16[8,128,512]{2,1,0:T(8,128)(2,1)S(1)}, bf16[8,128,512]{2,1,0:T(8,128)(2,1)}, u32[]{:S(2)}) copy-start(bf16[8,128,512]{2,1,0:T(8,128)(2,1)} %copy.21) | copy-start | bytes 3145732
  52.0 10.6 %collective-permute-start.4 = (bf16[128,4096]{1,0:T(8,128)(2,1)}, bf16[128,4096]{1,0:T(8,128)(2,1)S(1)}, u32[]{:S(2)}, u32[]{:S(2)}) collective-permute-start(bf16[128,4096]{1,0:T(8,128)(2,1)} %collective-permute-done.3), channel_id=1, source_target_pairs={{0,1},{1,0},{2,3},{3,2},{4,5},{5,4},{6,7},{7,6},{8,9},{9,8},{10,11... | collective-permute-start | bytes 3145736 | tf_op jit(solution)/shard_map/ppermute | solution.py:12
  56.3 13.6 %collective-permute-start.11 = (bf16[64,4096]{1,0:T(8,128)(2,1)S(1)}, bf16[64,4096]{1,0:T(8,128)(2,1)S(1)}, u32[]{:S(2)}, u32[]{:S(2)}) collective-permute-start(bf16[64,4096]{1,0:T(8,128)(2,1)S(1)} %slice.42), channel_id=1, source_target_pairs={{0,38},{2,0},{4,2},{6,4},{32,6},{34,32},{36,34},{38,36},{1,39},{3,... | collective-permute-start | bytes 1572872 | tf_op jit(solution)/shard_map/ppermute | solution.py:12
  56.4 13.6 %collective-permute-start.12 = (bf16[64,4096]{1,0:T(8,128)(2,1)S(1)}, bf16[64,4096]{1,0:T(8,128)(2,1)S(1)}, u32[]{:S(2)}, u32[]{:S(2)}) collective-permute-start(bf16[64,4096]{1,0:T(8,128)(2,1)S(1)} %slice.43), channel_id=1, source_target_pairs={{0,2},{2,4},{4,6},{6,32},{32,34},{34,36},{36,38},{38,0},{1,3},{3,5... | collective-permute-start | bytes 1572872 | tf_op jit(solution)/shard_map/ppermute | solution.py:12
  58.7 5.8 %collective-permute-start.6 = (bf16[64,4096]{1,0:T(8,128)(2,1)S(1)}, bf16[64,4096]{1,0:T(8,128)(2,1)S(1)}, u32[]{:S(2)}, u32[]{:S(2)}) collective-permute-start(bf16[64,4096]{1,0:T(8,128)(2,1)S(1)} %collective-permute-done.5), channel_id=1, source_target_pairs={{0,1},{1,0},{2,3},{3,2},{4,5},{5,4},{6,7},{7,6},{8,9},{9,8},{10,11... | collective-permute-start | bytes 1572872 | tf_op jit(solution)/shard_map/ppermute | solution.py:12
  58.7 7.5 %collective-permute-start.8 = (bf16[64,4096]{1,0:T(8,128)(2,1)S(1)}, bf16[64,4096]{1,0:T(8,128)(2,1)S(1)}, u32[]{:S(2)}, u32[]{:S(2)}) collective-permute-start(bf16[64,4096]{1,0:T(8,128)(2,1)S(1)} %collective-permute-done.7), channel_id=1, source_target_pairs={{0,1},{1,0},{2,3},{3,2},{4,5},{5,4},{6,7},{7,6},{8,9},{9,8},{10,11... | collective-permute-start | bytes 1572872 | tf_op jit(solution)/shard_map/ppermute | solution.py:12
  70.0 14.3 %collective-permute-start.16 = (bf16[512,512]{1,0:T(8,128)(2,1)S(1)}, bf16[512,512]{1,0:T(8,128)(2,1)S(1)}, u32[]{:S(2)}, u32[]{:S(2)}) collective-permute-start(bf16[512,512]{1,0:T(8,128)(2,1)S(1)} %get-tuple-element.31), channel_id=1, source_target_pairs={{0,192},{64,0},{128,64},{192,128},{1,193},{65,1},{129,65},{193,129... | collective-permute-start | bytes 1572872 | tf_op jit(solution)/shard_map/ppermute | solution.py:12
  72.9 14.8 %collective-permute-start.17 = (bf16[512,512]{1,0:T(8,128)(2,1)S(1)}, bf16[512,512]{1,0:T(8,128)(2,1)S(1)}, u32[]{:S(2)}, u32[]{:S(2)}) collective-permute-start(bf16[512,512]{1,0:T(8,128)(2,1)S(1)} %get-tuple-element.30), channel_id=1, source_target_pairs={{0,64},{64,128},{128,192},{192,0},{1,65},{65,129},{129,193},{193,1... | collective-permute-start | bytes 1572872 | tf_op jit(solution)/shard_map/ppermute | solution.py:12
  93.5 33.2 %collective-permute-start.18 = (bf16[1024,512]{1,0:T(8,128)(2,1)}, bf16[1024,512]{1,0:T(8,128)(2,1)}, u32[]{:S(2)}, u32[]{:S(2)}) collective-permute-start(bf16[1024,512]{1,0:T(8,128)(2,1)} %fusion.21), channel_id=1, source_target_pairs={{0,64},{64,128},{128,192},{192,0},{1,65},{65,129},{129,193},{193,1... | collective-permute-start | bytes 3145736 | tf_op jit(solution)/shard_map/ppermute | solution.py:12
  99.4 27.4 %collective-permute-start.19 = (bf16[1024,512]{1,0:T(8,128)(2,1)}, bf16[1024,512]{1,0:T(8,128)(2,1)}, u32[]{:S(2)}, u32[]{:S(2)}) collective-permute-start(bf16[1024,512]{1,0:T(8,128)(2,1)} %fusion.20), channel_id=1, source_target_pairs={{0,192},{64,0},{128,64},{192,128},{1,193},{65,1},{129,65},{193,129... | collective-permute-start | bytes 3145736 | tf_op jit(solution)/shard_map/ppermute | solution.py:12
  102.8 20.6 %collective-permute-start.13 = (bf16[1024,128]{1,0:T(8,128)(2,1)S(1)}, bf16[1024,128]{1,0:T(8,128)(2,1)S(1)}, u32[]{:S(2)}, u32[]{:S(2)}) collective-permute-start(bf16[1024,128]{1,0:T(8,128)(2,1)S(1)} %get-tuple-element.34), channel_id=1, source_target_pairs={{0,2},{2,4},{4,6},{6,0},{1,3},{3,5},{5,7},{7,1},{8,10},{10,12},{12... | collective-permute-start | bytes 786440 | tf_op jit(solution)/shard_map/ppermute | solution.py:12
  105.8 17.5 %collective-permute-start.14 = (bf16[1024,128]{1,0:T(8,128)(2,1)S(1)}, bf16[1024,128]{1,0:T(8,128)(2,1)S(1)}, u32[]{:S(2)}, u32[]{:S(2)}) collective-permute-start(bf16[1024,128]{1,0:T(8,128)(2,1)S(1)} %get-tuple-element.33), channel_id=1, source_target_pairs={{0,4},{2,6},{4,0},{6,2},{1,5},{3,7},{5,1},{7,3},{8,12},{10,14},{12... | collective-permute-start | bytes 786440 | tf_op jit(solution)/shard_map/ppermute | solution.py:12
  106.5 20.2 %collective-permute-start.15 = (bf16[1024,128]{1,0:T(8,128)(2,1)S(1)}, bf16[1024,128]{1,0:T(8,128)(2,1)S(1)}, u32[]{:S(2)}, u32[]{:S(2)}) collective-permute-start(bf16[1024,128]{1,0:T(8,128)(2,1)S(1)} %get-tuple-element.32), channel_id=1, source_target_pairs={{0,6},{2,0},{4,2},{6,4},{1,7},{3,1},{5,3},{7,5},{8,14},{10,8},{12,... | collective-permute-start | bytes 786440 | tf_op jit(solution)/shard_map/ppermute | solution.py:12
  128.8 18.1 %collective-permute-start.20 = (bf16[1024,128]{1,0:T(8,128)(2,1)S(1)}, bf16[1024,128]{1,0:T(8,128)(2,1)S(1)}, u32[]{:S(2)}, u32[]{:S(2)}) collective-permute-start(bf16[1024,128]{1,0:T(8,128)(2,1)S(1)} %get-tuple-element.28), channel_id=1, source_target_pairs={{0,2},{2,4},{4,6},{6,32},{32,34},{34,36},{36,38},{38,0},{1,3},{3,5... | collective-permute-start | bytes 786440 | tf_op jit(solution)/shard_map/ppermute | solution.py:12
  129.9 17.0 %collective-permute-start.21 = (bf16[1024,128]{1,0:T(8,128)(2,1)S(1)}, bf16[1024,128]{1,0:T(8,128)(2,1)S(1)}, u32[]{:S(2)}, u32[]{:S(2)}) collective-permute-start(bf16[1024,128]{1,0:T(8,128)(2,1)S(1)} %get-tuple-element.29), channel_id=1, source_target_pairs={{0,38},{2,0},{4,2},{6,4},{32,6},{34,32},{36,34},{38,36},{1,39},{3,... | collective-permute-start | bytes 786440 | tf_op jit(solution)/shard_map/ppermute | solution.py:12
  131.5 15.4 %collective-permute-start.22 = (bf16[512,128]{1,0:T(8,128)(2,1)S(1)}, bf16[512,128]{1,0:T(8,128)(2,1)S(1)}, u32[]{:S(2)}, u32[]{:S(2)}) collective-permute-start(bf16[512,128]{1,0:T(8,128)(2,1)S(1)} %get-tuple-element.26), channel_id=1, source_target_pairs={{0,36},{2,38},{4,0},{6,2},{32,4},{34,6},{36,32},{38,34},{1,37},{3,... | collective-permute-start | bytes 393224 | tf_op jit(solution)/shard_map/ppermute | solution.py:12
  134.6 12.3 %collective-permute-start.23 = (bf16[512,128]{1,0:T(8,128)(2,1)S(1)}, bf16[512,128]{1,0:T(8,128)(2,1)S(1)}, u32[]{:S(2)}, u32[]{:S(2)}) collective-permute-start(bf16[512,128]{1,0:T(8,128)(2,1)S(1)} %get-tuple-element.27), channel_id=1, source_target_pairs={{0,4},{2,6},{4,32},{6,34},{32,36},{34,38},{36,0},{38,2},{1,5},{3,7... | collective-permute-start | bytes 393224 | tf_op jit(solution)/shard_map/ppermute | solution.py:12
  147.1 15.4 %collective-permute-start.24 = (bf16[1024,128]{1,0:T(8,128)(2,1)S(1)}, bf16[1024,128]{1,0:T(8,128)(2,1)S(1)}, u32[]{:S(2)}, u32[]{:S(2)}) collective-permute-start(bf16[1024,128]{1,0:T(8,128)(2,1)S(1)} %add_convert_fusion.4), channel_id=1, source_target_pairs={{0,32},{32,0},{1,33},{33,1},{2,34},{34,2},{3,35},{35,3},{4,36},{36... | collective-permute-start | bytes 786440 | tf_op jit(solution)/shard_map/ppermute | solution.py:12
  162.5 14.8 %collective-permute-start.25 = (bf16[128,1024]{0,1:T(8,128)(2,1)S(1)}, bf16[128,1024]{0,1:T(8,128)(2,1)}, u32[]{:S(2)}, u32[]{:S(2)}) collective-permute-start(bf16[128,1024]{0,1:T(8,128)(2,1)S(1)} %fusion.22), channel_id=1, source_target_pairs={{0,64},{64,128},{128,192},{192,0},{1,65},{65,129},{129,193},{193,1... | collective-permute-start | bytes 786440 | tf_op jit(solution)/shard_map/ppermute | solution.py:12
  162.6 15.8 %collective-permute-start.26 = (bf16[128,1024]{0,1:T(8,128)(2,1)S(1)}, bf16[128,1024]{0,1:T(8,128)(2,1)S(1)}, u32[]{:S(2)}, u32[]{:S(2)}) collective-permute-start(bf16[128,1024]{0,1:T(8,128)(2,1)S(1)} %fusion.22), channel_id=1, source_target_pairs={{0,128},{64,192},{128,0},{192,64},{1,129},{65,193},{129,1},{193,65... | collective-permute-start | bytes 786440 | tf_op jit(solution)/shard_map/ppermute | solution.py:12
  162.8 16.1 %copy-start.2 = (bf16[4,4,256,128]{3,2,1,0:T(8,128)(2,1)}, bf16[4,4,256,128]{3,2,1,0:T(8,128)(2,1)S(1)}, u32[]{:S(2)}) copy-start(bf16[4,4,256,128]{3,2,1,0:T(8,128)(2,1)S(1)} %constant_dynamic-update-slice_fusion.4) | copy-start | bytes 3145732
  163.0 15.7 %collective-permute-start.27 = (bf16[128,1024]{0,1:T(8,128)(2,1)S(1)}, bf16[128,1024]{0,1:T(8,128)(2,1)S(1)}, u32[]{:S(2)}, u32[]{:S(2)}) collective-permute-start(bf16[128,1024]{0,1:T(8,128)(2,1)S(1)} %fusion.22), channel_id=1, source_target_pairs={{0,192},{64,0},{128,64},{192,128},{1,193},{65,1},{129,65},{193,129... | collective-permute-start | bytes 786440 | tf_op jit(solution)/shard_map/ppermute | solution.py:12
  (1 other events, 1.0 us)

commit v9 on v8

--- a/solution.py
+++ b/solution.py
@@ -52,9 +52,10 @@
         tokens = put(tokens, shift(piece, "c", 1), (y + d) & 3, 1 - c, row)
     tokens = tokens.reshape(8 * toks, feats)
 
-    def partial(r, source):
+    def partial(r, source, more=0.0):
         columns = lax.dynamic_slice_in_dim(source, ((x + r) & 3) * cols, cols, 1)
-        return lax.dot_general(columns, acts, (((0,), (0,)), ((), ())), preferred_element_type=F32).astype(BF16)
+        total = lax.dot_general(columns, acts, (((0,), (0,)), ((), ())), preferred_element_type=F32)
+        return (total + more).astype(BF16)
 
     cols = feats // 4
     far = partial(2, tokens)
@@ -80,9 +81,10 @@
 
     back = [block(res, l)] + [shift(block(res, l + d), "l", d) for d in (1, 2, 3)]
 
-    near_a, near_b = partial(1, after(tokens, top, res)), partial(3, after(tokens, bottom, res))
-    near_a = lax.dynamic_update_slice(near_a, add(near_a[:cols // 2], top), (0, 0))
-    near_b = lax.dynamic_update_slice(near_b, add(near_b[cols // 2:], bottom), (cols // 2, 0))
+    none = jnp.zeros((), BF16)
+    top = lax.pad(top, none, ((0, cols // 2, 0), (0, 0, 0))).astype(F32)
+    bottom = lax.pad(bottom, none, ((cols // 2, 0, 0), (0, 0, 0))).astype(F32)
+    near_a, near_b = partial(1, after(tokens, res), top), partial(3, after(tokens, res), bottom)
     own = partial(0, after(tokens, near_b))
     tot = [after(own, *back[1:]), shift(near_a, "x", 1), shift(near_b, "x", -1)]
     tot = sum(t.astype(F32) for t in tot).astype(BF16)

time: 181 us -> 177 us (0.978)
  other arithmetic: 6.13 us -> 2.19 us
    dynamic_update_slice x2 -> x0, other arithmetic: 3.94 us -> none  [the longest x1 1.97 us: local(): lax.dynamic_update_slice(near_a, add(near_a[:cols // 2], top), (0, 0))]
  transfers between devices with their start and end apart: 29 -> 29, of which waited for: 10 -> 9; matrix products, arithmetic and copies ran while one was open for 31% -> 33% of each run, Pallas kernels for 0% -> 0%
where the time goes in v9:
time: 177 us; the launch traced here: 176 us
  waiting for transfers between devices  74.2 us (42%)
  starting transfers between devices  40.1 us (23%)
  local copies, waits for them, and re-layouts  36 us (20%)
  matrix products  22.5 us (13%)
  other arithmetic  2.19 us (1%)
    ppermute x28, waiting for transfers between devices, shift(): return lax.ppermute(v, axis, [(i, (i + by) % n) for i in range(n)])  55.7 us
    ppermute x28, starting transfers between devices, shift(): return lax.ppermute(v, axis, [(i, (i + by) % n) for i in range(n)])  35.6 us
    dynamic_update_slice x15, local copies, waits for them, and re-layouts, put(): lax.dynamic_update_slice(buffer, piece.reshape((1,) * (buffer.ndim - piec...  19.6 us
    all_to_all x1, waiting for transfers between devices, exchange(): return lax.all_to_all(v, axis, split_axis=0, concat_axis=0, tiled=True)  18.5 us
    dot_general x4, matrix products, partial(): lax.dot_general(columns, acts, (((0,), (0,)), ((), ())), preferred_elemen...  13.4 us
    dot_general x1, matrix products, local(): lax.dot_general(after(tokens, far), weights, (((1,), (1,)), ((), ())), pr...  9.09 us
    all_to_all x1, starting transfers between devices, exchange(): return lax.all_to_all(v, axis, split_axis=0, concat_axis=0, tiled=True)  4.51 us
    broadcast_in_dim x1, local copies, waits for them, and re-layouts, local(): tokens = jnp.zeros((4, 2, toks, feats), BF16)  4.32 us
  transfers between devices with their start and end apart: 29, of which 9 were waited for; matrix products, arithmetic and copies ran while one was open for 33% of the time, Pallas kernels for 0%

profile of v9, /device:TPU:64, one launch (start us, length us, event | category | flops | bytes accessed | tf_op | source)
XLA Modules:
  0.0 175.9 jit_solution(3680886692210145930)
XLA Ops:
  0.7 3.1 %collective-permute-start.1 = (bf16[128,4096]{1,0:T(8,128)(2,1)}, bf16[128,4096]{1,0:T(8,128)(2,1)}, u32[]{:S(2)}, u32[]{:S(2)}) collective-permute-start(bf16[128,4096]{1,0:T(8,128)(2,1)} %bitcast.65), channel_id=1, source_target_pairs={{0,24},{8,0},{16,8},{24,16},{1,25},{9,1},{17,9},{25,17},{2,26},{10... | collective-permute-start | bytes 3145736 | tf_op jit(solution)/shard_map/ppermute | solution.py:12
  6.5 4.5 %all-to-all-start = ((bf16[8,128,512]{1,2,0:T(8,128)(2,1)}), bf16[8,128,512]{1,2,0:T(8,128)(2,1)S(1)}, u32[]{:S(2)}, u32[]{:S(2)}) async-start(bf16[8,128,512]{1,2,0:T(8,128)(2,1)} %bitcast.9), calls=%async_computation | async-start | bytes 2097152 | tf_op jit(solution)/shard_map/all_to_all | solution.py:16
  11.1 1.9 %collective-permute-start.10 = (bf16[128,4096]{1,0:T(8,128)(2,1)}, bf16[128,4096]{1,0:T(8,128)(2,1)S(1)}, u32[]{:S(2)}, u32[]{:S(2)}) collective-permute-start(bf16[128,4096]{1,0:T(8,128)(2,1)} %param.5), channel_id=1, source_target_pairs={{0,2},{2,4},{4,6},{6,32},{32,34},{34,36},{36,38},{38,0},{1,3},{3,5... | collective-permute-start | bytes 3145736 | tf_op jit(solution)/shard_map/ppermute | solution.py:12
  13.0 2.5 %broadcast_in_dim.14 = bf16[4,128,4096]{2,1,0:T(8,128)(2,1)} broadcast(bf16[]{:T(256)} %constant.17.clone.1), dimensions={} | broadcast | bytes 4194306 | tf_op jit(solution)/shard_map/broadcast_in_dim | solution.py:67
  15.5 2.3 %bitcast_dynamic-update-slice_fusion.2 = bf16[4,128,4096]{2,1,0:T(8,128)(2,1)} fusion(bf16[4,128,4096]{2,1,0:T(8,128)(2,1)} %broadcast_in_dim.14, s32[]{:T(128)S(6)} %select_n.102, bf16[128,4096]{1,0:T(8,128)(2,1)} %param.5), kind=kLoop, calls=%fused_computation.16 | loop fusion | bytes 2097156 | tf_op jit(solution)/shard_map/dynamic_update_slice | solution.py:29
  17.8 4.3 %broadcast_in_dim.13 = bf16[4,2,128,4096]{3,2,1,0:T(8,128)(2,1)} broadcast(bf16[]{:T(256)} %constant.17.clone.1), dimensions={} | broadcast | bytes 8388610 | tf_op jit(solution)/shard_map/broadcast_in_dim | solution.py:49
  23.2 18.5 %all-to-all-done = bf16[8,128,512]{1,2,0:T(8,128)(2,1)S(1)} async-done(((bf16[8,128,512]{1,2,0:T(8,128)(2,1)}), bf16[8,128,512]{1,2,0:T(8,128)(2,1)S(1)}, u32[]{:S(2)}, u32[]{:S(2)}) %all-to-all-start) | async-done | bytes 1048608 | tf_op jit(solution)/shard_map/all_to_all | solution.py:16
  45.5 1.8 %collective-permute-start.7 = (bf16[64,4096]{1,0:T(8,128)(2,1)S(1)}, bf16[64,4096]{1,0:T(8,128)(2,1)S(1)}, u32[]{:S(2)}, u32[]{:S(2)}) collective-permute-start(bf16[64,4096]{1,0:T(8,128)(2,1)S(1)} %slice.33), channel_id=1, source_target_pairs={{0,8},{8,16},{16,24},{24,0},{1,9},{9,17},{17,25},{25,1},{2,10},{10... | collective-permute-start | bytes 1572872 | tf_op jit(solution)/shard_map/ppermute | solution.py:12
  47.4 2.3 %bitcast_dynamic-update-slice_fusion.7 = bf16[4,2,128,4096]{3,2,1,0:T(8,128)(2,1)} fusion(bf16[4,2,128,4096]{3,2,1,0:T(8,128)(2,1)} %bitcast_dynamic-update-slice_fusion.8, s32[]{:T(128)S(6)} %select_n.95, s32[]{:T(128)S(6)} %select_n.97, bf16[128,4096]{1,0:T(8,128)(2,1)} %collective-permute-done), kind=kLoop, calls=%fused_computation.21 | loop fusion | bytes 2097160 | tf_op jit(solution)/shard_map/dynamic_update_slice | solution.py:29
  49.6 2.3 %bitcast_dynamic-update-slice_fusion.6 = bf16[4,2,128,4096]{3,2,1,0:T(8,128)(2,1)} fusion(bf16[4,2,128,4096]{3,2,1,0:T(8,128)(2,1)} %bitcast_dynamic-update-slice_fusion.7, s32[]{:T(128)S(6)} %select_n.98, s32[]{:T(128)S(6)} %select_n.96, bf16[128,4096]{1,0:T(8,128)(2,1)} %collective-permute-done.1), kind=kLoop, calls=%fused_computation.20 | loop fusion | bytes 2097160 | tf_op jit(solution)/shard_map/dynamic_update_slice | solution.py:29
  54.7 1.6 collective-permute-done.5
  56.4 1.9 %collective-permute-start.12 = (bf16[64,4096]{1,0:T(8,128)(2,1)S(1)}, bf16[64,4096]{1,0:T(8,128)(2,1)S(1)}, u32[]{:S(2)}, u32[]{:S(2)}) collective-permute-start(bf16[64,4096]{1,0:T(8,128)(2,1)S(1)} %slice.35), channel_id=1, source_target_pairs={{0,2},{2,4},{4,6},{6,32},{32,34},{34,36},{36,38},{38,0},{1,3},{3,5... | collective-permute-start | bytes 1572872 | tf_op jit(solution)/shard_map/ppermute | solution.py:12
  60.3 2.3 %bitcast_dynamic-update-slice_fusion.4 = bf16[4,2,128,4096]{3,2,1,0:T(8,128)(2,1)} fusion(bf16[4,2,128,4096]{3,2,1,0:T(8,128)(2,1)} %bitcast_dynamic-update-slice_fusion.5, s32[]{:T(128)S(6)} %select_n.99, s32[]{:T(128)S(6)} %select_n.96, bf16[128,4096]{1,0:T(8,128)(2,1)} %collective-permute-done.3), kind=kLoop, calls=%fused_computation.18 | loop fusion | bytes 2097160 | tf_op jit(solution)/shard_map/dynamic_update_slice | solution.py:29
  67.1 2.9 %fusion.8 = bf16[1024,512]{1,0:T(8,128)(2,1)S(1)} fusion(bf16[1024,512]{1,0:T(8,128)(2,1)S(1)} %bitcast.59, bf16[1024,4096]{1,0:T(8,128)(2,1)} %bitcast.15, s32[]{:T(128)S(6)} %select_n.101), kind=kOutput, calls=%fused_computation.12 | convolution fusion | flops 1074266112 | bytes 4194308 | tf_op jit(solution)/shard_map/dot_general | solution.py:57
  70.0 2.8 %collective-permute-start.16 = (bf16[512,512]{1,0:T(8,128)(2,1)S(1)}, bf16[512,512]{1,0:T(8,128)(2,1)S(1)}, u32[]{:S(2)}, u32[]{:S(2)}) collective-permute-start(bf16[512,512]{1,0:T(8,128)(2,1)S(1)} %get-tuple-element.29), channel_id=1, source_target_pairs={{0,192},{64,0},{128,64},{192,128},{1,193},{65,1},{129,65},{193,129... | collective-permute-start | bytes 1572872 | tf_op jit(solution)/shard_map/ppermute | solution.py:12
  74.6 9.1 %convolution_convert_fusion = bf16[1024,512]{1,0:T(8,128)(2,1)S(1)} fusion(bf16[1024,4096]{1,0:T(8,128)(2,1)} %bitcast.15, bf16[512,4096]{1,0:T(8,128)(2,1)} %bitcast.21), kind=kOutput, calls=%fused_computation.11 | convolution fusion | flops 4295491584 | bytes 13631488 | tf_op jit(solution)/shard_map/dot_general | solution.py:76
  83.6 4.1 %collective-permute-done.17 = bf16[512,512]{1,0:T(8,128)(2,1)S(1)} collective-permute-done((bf16[512,512]{1,0:T(8,128)(2,1)S(1)}, bf16[512,512]{1,0:T(8,128)(2,1)S(1)}, u32[]{:S(2)}, u32[]{:S(2)}) %collective-permute-start.17) | collective-permute-done | bytes 524320 | tf_op jit(solution)/shard_map/ppermute | solution.py:12
  87.7 3.8 %add_convert_fusion.1 = bf16[1024,512]{1,0:T(8,128)(2,1)} fusion(bf16[512,512]{1,0:T(8,128)(2,1)S(1)} %collective-permute-done.17, bf16[1024,512]{1,0:T(8,128)(2,1)S(1)} %bitcast.60, bf16[1024,4096]{1,0:T(8,128)(2,1)} %bitcast.15, s32[]{:T(128)S(6)} %select_n.115), kind=kOutput, calls=%fused_computation.1 | convolution fusion | flops 1075314688 | bytes 4718596 | tf_op jit(solution)/shard_map/dot_general | solution.py:57
  91.6 3.8 %add_convert_fusion.2 = bf16[1024,512]{1,0:T(8,128)(2,1)} fusion(bf16[512,512]{1,0:T(8,128)(2,1)S(1)} %collective-permute-done.16, bf16[1024,512]{1,0:T(8,128)(2,1)S(1)} %bitcast.61, bf16[1024,4096]{1,0:T(8,128)(2,1)} %bitcast.15, s32[]{:T(128)S(6)} %select_n.113), kind=kOutput, calls=%fused_computation.6 | convolution fusion | flops 1075314688 | bytes 4718596 | tf_op jit(solution)/shard_map/dot_general | solution.py:57
  95.4 3.2 %collective-permute-start.19 = (bf16[1024,512]{1,0:T(8,128)(2,1)}, bf16[1024,512]{1,0:T(8,128)(2,1)}, u32[]{:S(2)}, u32[]{:S(2)}) collective-permute-start(bf16[1024,512]{1,0:T(8,128)(2,1)} %add_convert_fusion.2), channel_id=1, source_target_pairs={{0,192},{64,0},{128,64},{192,128},{1,193},{65,1},{129,65},{193,129... | collective-permute-start | bytes 3145736 | tf_op jit(solution)/shard_map/ppermute | solution.py:12
  98.8 3.0 %collective-permute-start.13 = (bf16[1024,128]{1,0:T(8,128)(2,1)S(1)}, bf16[1024,128]{1,0:T(8,128)(2,1)S(1)}, u32[]{:S(2)}, u32[]{:S(2)}) collective-permute-start(bf16[1024,128]{1,0:T(8,128)(2,1)S(1)} %get-tuple-element.32), channel_id=1, source_target_pairs={{0,2},{2,4},{4,6},{6,0},{1,3},{3,5},{5,7},{7,1},{8,10},{10,12},{12... | collective-permute-start | bytes 786440 | tf_op jit(solution)/shard_map/ppermute | solution.py:12
  102.4 2.8 %collective-permute-start.15 = (bf16[1024,128]{1,0:T(8,128)(2,1)S(1)}, bf16[1024,128]{1,0:T(8,128)(2,1)S(1)}, u32[]{:S(2)}, u32[]{:S(2)}) collective-permute-start(bf16[1024,128]{1,0:T(8,128)(2,1)S(1)} %get-tuple-element.30), channel_id=1, source_target_pairs={{0,6},{2,0},{4,2},{6,4},{1,7},{3,1},{5,3},{7,5},{8,14},{10,8},{12,... | collective-permute-start | bytes 786440 | tf_op jit(solution)/shard_map/ppermute | solution.py:12
  105.2 2.9 %fusion.11 = bf16[1024,512]{1,0:T(8,128)(2,1)S(1)} fusion(bf16[1024,512]{1,0:T(8,128)(2,1)S(1)} %bitcast.62, bf16[1024,4096]{1,0:T(8,128)(2,1)} %bitcast.15, s32[]{:T(128)S(6)} %select_n.114), kind=kOutput, calls=%fused_computation.13 | convolution fusion | flops 1074266112 | bytes 4194308 | tf_op jit(solution)/shard_map/dot_general | solution.py:57
  108.1 11.3 %collective-permute-done.13 = bf16[1024,128]{1,0:T(8,128)(2,1)S(1)} collective-permute-done((bf16[1024,128]{1,0:T(8,128)(2,1)S(1)}, bf16[1024,128]{1,0:T(8,128)(2,1)S(1)}, u32[]{:S(2)}, u32[]{:S(2)}) %collective-permute-start.13) | collective-permute-done | bytes 262176 | tf_op jit(solution)/shard_map/ppermute | solution.py:12
  119.4 3.4 %collective-permute-done.15 = bf16[1024,128]{1,0:T(8,128)(2,1)S(1)} collective-permute-done((bf16[1024,128]{1,0:T(8,128)(2,1)S(1)}, bf16[1024,128]{1,0:T(8,128)(2,1)S(1)}, u32[]{:S(2)}, u32[]{:S(2)}) %collective-permute-start.15) | collective-permute-done | bytes 262176 | tf_op jit(solution)/shard_map/ppermute | solution.py:12
  122.8 2.0 %add_convert_fusion = bf16[1024,512]{1,0:T(8,128)(2,1)S(1)} fusion(bf16[1024,512]{1,0:T(8,128)(2,1)} %collective-permute-done.19, bf16[1024,512]{1,0:T(8,128)(2,1)} %collective-permute-done.18, bf16[1024,512]{1,0:T(8,128)(2,1)S(1)} %fusion.11), kind=kLoop, calls=%fused_computation | loop fusion | flops 3145728 | bytes 4194304 | tf_op jit(solution)/shard_map/convert_element_type | solution.py:90
  127.5 3.1 %collective-permute-start.22 = (bf16[512,128]{1,0:T(8,128)(2,1)S(1)}, bf16[512,128]{1,0:T(8,128)(2,1)S(1)}, u32[]{:S(2)}, u32[]{:S(2)}) collective-permute-start(bf16[512,128]{1,0:T(8,128)(2,1)S(1)} %get-tuple-element.24), channel_id=1, source_target_pairs={{0,36},{2,38},{4,0},{6,2},{32,4},{34,6},{36,32},{38,34},{1,37},{3,... | collective-permute-start | bytes 393224 | tf_op jit(solution)/shard_map/ppermute | solution.py:12
  131.8 11.2 %collective-permute-done.22 = bf16[512,128]{1,0:T(8,128)(2,1)S(1)} collective-permute-done((bf16[512,128]{1,0:T(8,128)(2,1)S(1)}, bf16[512,128]{1,0:T(8,128)(2,1)S(1)}, u32[]{:S(2)}, u32[]{:S(2)}) %collective-permute-start.22) | collective-permute-done | bytes 131104 | tf_op jit(solution)/shard_map/ppermute | solution.py:12
  143.1 2.5 %collective-permute-start.24 = (bf16[1024,128]{1,0:T(8,128)(2,1)S(1)}, bf16[1024,128]{1,0:T(8,128)(2,1)S(1)}, u32[]{:S(2)}, u32[]{:S(2)}) collective-permute-start(bf16[1024,128]{1,0:T(8,128)(2,1)S(1)} %add_convert_fusion.4), channel_id=1, source_target_pairs={{0,32},{32,0},{1,33},{33,1},{2,34},{34,2},{3,35},{35,3},{4,36},{36... | collective-permute-start | bytes 786440 | tf_op jit(solution)/shard_map/ppermute | solution.py:12
  146.0 12.6 %collective-permute-done.24 = bf16[1024,128]{1,0:T(8,128)(2,1)S(1)} collective-permute-done((bf16[1024,128]{1,0:T(8,128)(2,1)S(1)}, bf16[1024,128]{1,0:T(8,128)(2,1)S(1)}, u32[]{:S(2)}, u32[]{:S(2)}) %collective-permute-start.24) | collective-permute-done | bytes 262176 | tf_op jit(solution)/shard_map/ppermute | solution.py:12
  159.1 3.2 %collective-permute-start.27 = (bf16[128,1024]{0,1:T(8,128)(2,1)S(1)}, bf16[128,1024]{0,1:T(8,128)(2,1)S(1)}, u32[]{:S(2)}, u32[]{:S(2)}) collective-permute-start(bf16[128,1024]{0,1:T(8,128)(2,1)S(1)} %fusion.14), channel_id=1, source_target_pairs={{0,192},{64,0},{128,64},{192,128},{1,193},{65,1},{129,65},{193,129... | collective-permute-start | bytes 786440 | tf_op jit(solution)/shard_map/ppermute | solution.py:12
  162.4 11.1 %collective-permute-done.25 = bf16[128,1024]{0,1:T(8,128)(2,1)} collective-permute-done((bf16[128,1024]{0,1:T(8,128)(2,1)S(1)}, bf16[128,1024]{0,1:T(8,128)(2,1)}, u32[]{:S(2)}, u32[]{:S(2)}) %collective-permute-start.25) | collective-permute-done | bytes 262176 | tf_op jit(solution)/shard_map/ppermute | solution.py:12
  (84 shorter events, 26.8 us)
Async XLA Ops:
  0.6 46.7 %collective-permute-start = (bf16[128,4096]{1,0:T(8,128)(2,1)}, bf16[128,4096]{1,0:T(8,128)(2,1)}, u32[]{:S(2)}, u32[]{:S(2)}) collective-permute-start(bf16[128,4096]{1,0:T(8,128)(2,1)} %bitcast.64), channel_id=1, source_target_pairs={{0,1},{1,0},{2,3},{3,2},{4,5},{5,4},{6,7},{7,6},{8,9},{9,8},{10,11... | collective-permute-start | bytes 3145736 | tf_op jit(solution)/shard_map/ppermute | solution.py:12
  0.7 42.3 %collective-permute-start.1 = (bf16[128,4096]{1,0:T(8,128)(2,1)}, bf16[128,4096]{1,0:T(8,128)(2,1)}, u32[]{:S(2)}, u32[]{:S(2)}) collective-permute-start(bf16[128,4096]{1,0:T(8,128)(2,1)} %bitcast.65), channel_id=1, source_target_pairs={{0,24},{8,0},{16,8},{24,16},{1,25},{9,1},{17,9},{25,17},{2,26},{10... | collective-permute-start | bytes 3145736 | tf_op jit(solution)/shard_map/ppermute | solution.py:12
  3.8 40.6 %collective-permute-start.3 = (bf16[128,4096]{1,0:T(8,128)(2,1)}, bf16[128,4096]{1,0:T(8,128)(2,1)}, u32[]{:S(2)}, u32[]{:S(2)}) collective-permute-start(bf16[128,4096]{1,0:T(8,128)(2,1)} %bitcast.66), channel_id=1, source_target_pairs={{0,8},{8,16},{16,24},{24,0},{1,9},{9,17},{17,25},{25,1},{2,10},{10... | collective-permute-start | bytes 3145736 | tf_op jit(solution)/shard_map/ppermute | solution.py:12
  6.5 35.2 %all-to-all-start = ((bf16[8,128,512]{1,2,0:T(8,128)(2,1)}), bf16[8,128,512]{1,2,0:T(8,128)(2,1)S(1)}, u32[]{:S(2)}, u32[]{:S(2)}) async-start(bf16[8,128,512]{1,2,0:T(8,128)(2,1)} %bitcast.9), calls=%async_computation | async-start | bytes 2097152 | tf_op jit(solution)/shard_map/all_to_all | solution.py:16
  11.0 41.0 %collective-permute-start.9 = (bf16[128,4096]{1,0:T(8,128)(2,1)}, bf16[128,4096]{1,0:T(8,128)(2,1)S(1)}, u32[]{:S(2)}, u32[]{:S(2)}) collective-permute-start(bf16[128,4096]{1,0:T(8,128)(2,1)} %param.5), channel_id=1, source_target_pairs={{0,38},{2,0},{4,2},{6,4},{32,6},{34,32},{36,34},{38,36},{1,39},{3,... | collective-permute-start | bytes 3145736 | tf_op jit(solution)/shard_map/ppermute | solution.py:12
  11.1 42.5 %collective-permute-start.10 = (bf16[128,4096]{1,0:T(8,128)(2,1)}, bf16[128,4096]{1,0:T(8,128)(2,1)S(1)}, u32[]{:S(2)}, u32[]{:S(2)}) collective-permute-start(bf16[128,4096]{1,0:T(8,128)(2,1)} %param.5), channel_id=1, source_target_pairs={{0,2},{2,4},{4,6},{6,32},{32,34},{34,36},{36,38},{38,0},{1,3},{3,5... | collective-permute-start | bytes 3145736 | tf_op jit(solution)/shard_map/ppermute | solution.py:12
  17.8 4.3 %copy-start.3 = (bf16[1,128,4096]{2,1,0:T(8,128)(2,1)S(1)}, bf16[1,128,4096]{2,1,0:T(8,128)(2,1)}, u32[]{:S(2)}) copy-start(bf16[1,128,4096]{2,1,0:T(8,128)(2,1)} %param.3) | copy-start | bytes 3145732
  44.1 12.2 %collective-permute-start.5 = (bf16[64,4096]{1,0:T(8,128)(2,1)S(1)}, bf16[64,4096]{1,0:T(8,128)(2,1)S(1)}, u32[]{:S(2)}, u32[]{:S(2)}) collective-permute-start(bf16[64,4096]{1,0:T(8,128)(2,1)S(1)} %slice.32), channel_id=1, source_target_pairs={{0,24},{8,0},{16,8},{24,16},{1,25},{9,1},{17,9},{25,17},{2,26},{10... | collective-permute-start | bytes 1572872 | tf_op jit(solution)/shard_map/ppermute | solution.py:12
  45.5 13.2 %collective-permute-start.7 = (bf16[64,4096]{1,0:T(8,128)(2,1)S(1)}, bf16[64,4096]{1,0:T(8,128)(2,1)S(1)}, u32[]{:S(2)}, u32[]{:S(2)}) collective-permute-start(bf16[64,4096]{1,0:T(8,128)(2,1)S(1)} %slice.33), channel_id=1, source_target_pairs={{0,8},{8,16},{16,24},{24,0},{1,9},{9,17},{17,25},{25,1},{2,10},{10... | collective-permute-start | bytes 1572872 | tf_op jit(solution)/shard_map/ppermute | solution.py:12
  47.4 11.4 %collective-permute-start.2 = (bf16[128,4096]{1,0:T(8,128)(2,1)}, bf16[128,4096]{1,0:T(8,128)(2,1)S(1)}, u32[]{:S(2)}, u32[]{:S(2)}) collective-permute-start(bf16[128,4096]{1,0:T(8,128)(2,1)} %collective-permute-done.1), channel_id=1, source_target_pairs={{0,1},{1,0},{2,3},{3,2},{4,5},{5,4},{6,7},{7,6},{8,9},{9,8},{10,11... | collective-permute-start | bytes 3145736 | tf_op jit(solution)/shard_map/ppermute | solution.py:12
  52.0 15.1 %copy-start = (bf16[8,128,512]{2,1,0:T(8,128)(2,1)S(1)}, bf16[8,128,512]{2,1,0:T(8,128)(2,1)}, u32[]{:S(2)}) copy-start(bf16[8,128,512]{2,1,0:T(8,128)(2,1)} %copy.21) | copy-start | bytes 3145732
  52.0 10.6 %collective-permute-start.4 = (bf16[128,4096]{1,0:T(8,128)(2,1)}, bf16[128,4096]{1,0:T(8,128)(2,1)S(1)}, u32[]{:S(2)}, u32[]{:S(2)}) collective-permute-start(bf16[128,4096]{1,0:T(8,128)(2,1)} %collective-permute-done.3), channel_id=1, source_target_pairs={{0,1},{1,0},{2,3},{3,2},{4,5},{5,4},{6,7},{7,6},{8,9},{9,8},{10,11... | collective-permute-start | bytes 3145736 | tf_op jit(solution)/shard_map/ppermute | solution.py:12
  56.3 13.6 %collective-permute-start.11 = (bf16[64,4096]{1,0:T(8,128)(2,1)S(1)}, bf16[64,4096]{1,0:T(8,128)(2,1)S(1)}, u32[]{:S(2)}, u32[]{:S(2)}) collective-permute-start(bf16[64,4096]{1,0:T(8,128)(2,1)S(1)} %slice.34), channel_id=1, source_target_pairs={{0,38},{2,0},{4,2},{6,4},{32,6},{34,32},{36,34},{38,36},{1,39},{3,... | collective-permute-start | bytes 1572872 | tf_op jit(solution)/shard_map/ppermute | solution.py:12
  56.4 13.6 %collective-permute-start.12 = (bf16[64,4096]{1,0:T(8,128)(2,1)S(1)}, bf16[64,4096]{1,0:T(8,128)(2,1)S(1)}, u32[]{:S(2)}, u32[]{:S(2)}) collective-permute-start(bf16[64,4096]{1,0:T(8,128)(2,1)S(1)} %slice.35), channel_id=1, source_target_pairs={{0,2},{2,4},{4,6},{6,32},{32,34},{34,36},{36,38},{38,0},{1,3},{3,5... | collective-permute-start | bytes 1572872 | tf_op jit(solution)/shard_map/ppermute | solution.py:12
  58.7 5.8 %collective-permute-start.6 = (bf16[64,4096]{1,0:T(8,128)(2,1)S(1)}, bf16[64,4096]{1,0:T(8,128)(2,1)S(1)}, u32[]{:S(2)}, u32[]{:S(2)}) collective-permute-start(bf16[64,4096]{1,0:T(8,128)(2,1)S(1)} %collective-permute-done.5), channel_id=1, source_target_pairs={{0,1},{1,0},{2,3},{3,2},{4,5},{5,4},{6,7},{7,6},{8,9},{9,8},{10,11... | collective-permute-start | bytes 1572872 | tf_op jit(solution)/shard_map/ppermute | solution.py:12
  58.7 7.5 %collective-permute-start.8 = (bf16[64,4096]{1,0:T(8,128)(2,1)S(1)}, bf16[64,4096]{1,0:T(8,128)(2,1)S(1)}, u32[]{:S(2)}, u32[]{:S(2)}) collective-permute-start(bf16[64,4096]{1,0:T(8,128)(2,1)S(1)} %collective-permute-done.7), channel_id=1, source_target_pairs={{0,1},{1,0},{2,3},{3,2},{4,5},{5,4},{6,7},{7,6},{8,9},{9,8},{10,11... | collective-permute-start | bytes 1572872 | tf_op jit(solution)/shard_map/ppermute | solution.py:12
  70.0 21.5 %collective-permute-start.16 = (bf16[512,512]{1,0:T(8,128)(2,1)S(1)}, bf16[512,512]{1,0:T(8,128)(2,1)S(1)}, u32[]{:S(2)}, u32[]{:S(2)}) collective-permute-start(bf16[512,512]{1,0:T(8,128)(2,1)S(1)} %get-tuple-element.29), channel_id=1, source_target_pairs={{0,192},{64,0},{128,64},{192,128},{1,193},{65,1},{129,65},{193,129... | collective-permute-start | bytes 1572872 | tf_op jit(solution)/shard_map/ppermute | solution.py:12
  72.9 14.8 %collective-permute-start.17 = (bf16[512,512]{1,0:T(8,128)(2,1)S(1)}, bf16[512,512]{1,0:T(8,128)(2,1)S(1)}, u32[]{:S(2)}, u32[]{:S(2)}) collective-permute-start(bf16[512,512]{1,0:T(8,128)(2,1)S(1)} %get-tuple-element.28), channel_id=1, source_target_pairs={{0,64},{64,128},{128,192},{192,0},{1,65},{65,129},{129,193},{193,1... | collective-permute-start | bytes 1572872 | tf_op jit(solution)/shard_map/ppermute | solution.py:12
  91.6 31.2 %collective-permute-start.18 = (bf16[1024,512]{1,0:T(8,128)(2,1)}, bf16[1024,512]{1,0:T(8,128)(2,1)}, u32[]{:S(2)}, u32[]{:S(2)}) collective-permute-start(bf16[1024,512]{1,0:T(8,128)(2,1)} %add_convert_fusion.1), channel_id=1, source_target_pairs={{0,64},{64,128},{128,192},{192,0},{1,65},{65,129},{129,193},{193,1... | collective-permute-start | bytes 3145736 | tf_op jit(solution)/shard_map/ppermute | solution.py:12
  95.4 27.4 %collective-permute-start.19 = (bf16[1024,512]{1,0:T(8,128)(2,1)}, bf16[1024,512]{1,0:T(8,128)(2,1)}, u32[]{:S(2)}, u32[]{:S(2)}) collective-permute-start(bf16[1024,512]{1,0:T(8,128)(2,1)} %add_convert_fusion.2), channel_id=1, source_target_pairs={{0,192},{64,0},{128,64},{192,128},{1,193},{65,1},{129,65},{193,129... | collective-permute-start | bytes 3145736 | tf_op jit(solution)/shard_map/ppermute | solution.py:12
  98.8 20.6 %collective-permute-start.13 = (bf16[1024,128]{1,0:T(8,128)(2,1)S(1)}, bf16[1024,128]{1,0:T(8,128)(2,1)S(1)}, u32[]{:S(2)}, u32[]{:S(2)}) collective-permute-start(bf16[1024,128]{1,0:T(8,128)(2,1)S(1)} %get-tuple-element.32), channel_id=1, source_target_pairs={{0,2},{2,4},{4,6},{6,0},{1,3},{3,5},{5,7},{7,1},{8,10},{10,12},{12... | collective-permute-start | bytes 786440 | tf_op jit(solution)/shard_map/ppermute | solution.py:12
  101.9 17.5 %collective-permute-start.14 = (bf16[1024,128]{1,0:T(8,128)(2,1)S(1)}, bf16[1024,128]{1,0:T(8,128)(2,1)S(1)}, u32[]{:S(2)}, u32[]{:S(2)}) collective-permute-start(bf16[1024,128]{1,0:T(8,128)(2,1)S(1)} %get-tuple-element.31), channel_id=1, source_target_pairs={{0,4},{2,6},{4,0},{6,2},{1,5},{3,7},{5,1},{7,3},{8,12},{10,14},{12... | collective-permute-start | bytes 786440 | tf_op jit(solution)/shard_map/ppermute | solution.py:12
  102.4 20.5 %collective-permute-start.15 = (bf16[1024,128]{1,0:T(8,128)(2,1)S(1)}, bf16[1024,128]{1,0:T(8,128)(2,1)S(1)}, u32[]{:S(2)}, u32[]{:S(2)}) collective-permute-start(bf16[1024,128]{1,0:T(8,128)(2,1)S(1)} %get-tuple-element.30), channel_id=1, source_target_pairs={{0,6},{2,0},{4,2},{6,4},{1,7},{3,1},{5,3},{7,5},{8,14},{10,8},{12,... | collective-permute-start | bytes 786440 | tf_op jit(solution)/shard_map/ppermute | solution.py:12
  124.9 18.1 %collective-permute-start.20 = (bf16[1024,128]{1,0:T(8,128)(2,1)S(1)}, bf16[1024,128]{1,0:T(8,128)(2,1)S(1)}, u32[]{:S(2)}, u32[]{:S(2)}) collective-permute-start(bf16[1024,128]{1,0:T(8,128)(2,1)S(1)} %get-tuple-element.26), channel_id=1, source_target_pairs={{0,2},{2,4},{4,6},{6,32},{32,34},{34,36},{36,38},{38,0},{1,3},{3,5... | collective-permute-start | bytes 786440 | tf_op jit(solution)/shard_map/ppermute | solution.py:12
  125.9 17.0 %collective-permute-start.21 = (bf16[1024,128]{1,0:T(8,128)(2,1)S(1)}, bf16[1024,128]{1,0:T(8,128)(2,1)S(1)}, u32[]{:S(2)}, u32[]{:S(2)}) collective-permute-start(bf16[1024,128]{1,0:T(8,128)(2,1)S(1)} %get-tuple-element.27), channel_id=1, source_target_pairs={{0,38},{2,0},{4,2},{6,4},{32,6},{34,32},{36,34},{38,36},{1,39},{3,... | collective-permute-start | bytes 786440 | tf_op jit(solution)/shard_map/ppermute | solution.py:12
  127.5 15.4 %collective-permute-start.22 = (bf16[512,128]{1,0:T(8,128)(2,1)S(1)}, bf16[512,128]{1,0:T(8,128)(2,1)S(1)}, u32[]{:S(2)}, u32[]{:S(2)}) collective-permute-start(bf16[512,128]{1,0:T(8,128)(2,1)S(1)} %get-tuple-element.24), channel_id=1, source_target_pairs={{0,36},{2,38},{4,0},{6,2},{32,4},{34,6},{36,32},{38,34},{1,37},{3,... | collective-permute-start | bytes 393224 | tf_op jit(solution)/shard_map/ppermute | solution.py:12
  130.6 12.3 %collective-permute-start.23 = (bf16[512,128]{1,0:T(8,128)(2,1)S(1)}, bf16[512,128]{1,0:T(8,128)(2,1)S(1)}, u32[]{:S(2)}, u32[]{:S(2)}) collective-permute-start(bf16[512,128]{1,0:T(8,128)(2,1)S(1)} %get-tuple-element.25), channel_id=1, source_target_pairs={{0,4},{2,6},{4,32},{6,34},{32,36},{34,38},{36,0},{38,2},{1,5},{3,7... | collective-permute-start | bytes 393224 | tf_op jit(solution)/shard_map/ppermute | solution.py:12
  143.1 15.4 %collective-permute-start.24 = (bf16[1024,128]{1,0:T(8,128)(2,1)S(1)}, bf16[1024,128]{1,0:T(8,128)(2,1)S(1)}, u32[]{:S(2)}, u32[]{:S(2)}) collective-permute-start(bf16[1024,128]{1,0:T(8,128)(2,1)S(1)} %add_convert_fusion.4), channel_id=1, source_target_pairs={{0,32},{32,0},{1,33},{33,1},{2,34},{34,2},{3,35},{35,3},{4,36},{36... | collective-permute-start | bytes 786440 | tf_op jit(solution)/shard_map/ppermute | solution.py:12
  158.6 14.8 %collective-permute-start.25 = (bf16[128,1024]{0,1:T(8,128)(2,1)S(1)}, bf16[128,1024]{0,1:T(8,128)(2,1)}, u32[]{:S(2)}, u32[]{:S(2)}) collective-permute-start(bf16[128,1024]{0,1:T(8,128)(2,1)S(1)} %fusion.14), channel_id=1, source_target_pairs={{0,64},{64,128},{128,192},{192,0},{1,65},{65,129},{129,193},{193,1... | collective-permute-start | bytes 786440 | tf_op jit(solution)/shard_map/ppermute | solution.py:12
  158.7 15.8 %collective-permute-start.26 = (bf16[128,1024]{0,1:T(8,128)(2,1)S(1)}, bf16[128,1024]{0,1:T(8,128)(2,1)S(1)}, u32[]{:S(2)}, u32[]{:S(2)}) collective-permute-start(bf16[128,1024]{0,1:T(8,128)(2,1)S(1)} %fusion.14), channel_id=1, source_target_pairs={{0,128},{64,192},{128,0},{192,64},{1,129},{65,193},{129,1},{193,65... | collective-permute-start | bytes 786440 | tf_op jit(solution)/shard_map/ppermute | solution.py:12
  158.9 16.1 %copy-start.2 = (bf16[4,4,256,128]{3,2,1,0:T(8,128)(2,1)}, bf16[4,4,256,128]{3,2,1,0:T(8,128)(2,1)S(1)}, u32[]{:S(2)}) copy-start(bf16[4,4,256,128]{3,2,1,0:T(8,128)(2,1)S(1)} %constant_dynamic-update-slice_fusion.4) | copy-start | bytes 3145732
  159.1 15.7 %collective-permute-start.27 = (bf16[128,1024]{0,1:T(8,128)(2,1)S(1)}, bf16[128,1024]{0,1:T(8,128)(2,1)S(1)}, u32[]{:S(2)}, u32[]{:S(2)}) collective-permute-start(bf16[128,1024]{0,1:T(8,128)(2,1)S(1)} %fusion.14), channel_id=1, source_target_pairs={{0,192},{64,0},{128,64},{192,128},{1,193},{65,1},{129,65},{193,129... | collective-permute-start | bytes 786440 | tf_op jit(solution)/shard_map/ppermute | solution.py:12
  (1 other events, 1.0 us)

commit v10 on v9

--- a/solution.py
+++ b/solution.py
@@ -45,11 +45,12 @@
 
     half = toks // 2
     above, below = shift(g, "y", -1), shift(g, "y", 1)
-    far_a, far_b = shift(after(above[:half], acts), "y", -1), shift(after(below[half:], acts), "y", 1)
+    half_a, half_b = after(above[:half], acts), after(below[half:], acts)
+    far_a, far_b = shift(half_a, "y", -1), shift(half_b, "y", 1)
     tokens = jnp.zeros((4, 2, toks, feats), BF16)
-    for piece, d, row in ((g, 0, 0), (above, 1, 0), (below, 3, 0), (far_a, 2, 0), (far_b, 2, half)):
-        tokens = put(tokens, piece, (y + d) & 3, c, row)
-        tokens = put(tokens, shift(piece, "c", 1), (y + d) & 3, 1 - c, row)
+    for piece, d in ((g, 0), (above, 1), (below, 3), (jnp.concatenate([far_a, far_b]), 2)):
+        tokens = put(tokens, piece, (y + d) & 3, c)
+        tokens = put(tokens, shift(piece, "c", 1), (y + d) & 3, 1 - c)
     tokens = tokens.reshape(8 * toks, feats)
 
     def partial(r, source, more=0.0):
@@ -67,8 +68,8 @@
     weights = jnp.zeros((4, heads, feats), BF16)
     for piece, d in ((w_out, 0), (w_above, 1), (w_below, 3)):
         weights = put(weights, piece, (l + d) & 3)
-    w_far_a = shift(after(w_above[:half], far_a), RING8, -1)
-    w_far_b = shift(after(w_below[half:], far_a), RING8, 1)
+    w_far_a = shift(after(w_above[:half], half_a, half_b), RING8, -1)
+    w_far_b = shift(after(w_below[half:], half_a, half_b), RING8, 1)
     weights = put(weights, after(w_far_a, far), (l + 2) & 3, 0)
     weights = put(weights, after(w_far_b, far), (l + 2) & 3, half)
     weights = weights.reshape(4 * heads, feats)

time: 177 us -> 175 us (0.989)
    dynamic_update_slice x15 -> x13, local copies, waits for them, and re-layouts: 19.6 us -> 18.5 us  [put(): lax.dynamic_update_slice(buffer, piece.reshape((1,) * (buffer.ndim - piec...]
    ppermute x28 -> x27, starting transfers between devices: 35.6 us -> 34.6 us  [shift(): return lax.ppermute(v, axis, [(i, (i + by) % n) for i in range(n)])]
    ppermute x28 -> x27, waiting for transfers between devices: 55.7 us -> 56.3 us  [shift(): return lax.ppermute(v, axis, [(i, (i + by) % n) for i in range(n)])]
  transfers between devices with their start and end apart: 29 -> 28, of which waited for: 9 -> 8; matrix products, arithmetic and copies ran while one was open for 33% -> 32% of each run, Pallas kernels for 0% -> 0%
where the time goes in v10:
time: 175 us
  waiting for transfers between devices  74.8 us (43%)
  starting transfers between devices  39.1 us (22%)
  local copies, waits for them, and re-layouts  35 us (20%)
  matrix products  22.5 us (13%)
  other arithmetic  2.19 us (1%)
    ppermute x27, waiting for transfers between devices, shift(): return lax.ppermute(v, axis, [(i, (i + by) % n) for i in range(n)])  56.3 us
    ppermute x27, starting transfers between devices, shift(): return lax.ppermute(v, axis, [(i, (i + by) % n) for i in range(n)])  34.6 us
    all_to_all x1, waiting for transfers between devices, exchange(): return lax.all_to_all(v, axis, split_axis=0, concat_axis=0, tiled=True)  18.5 us
    dynamic_update_slice x13, local copies, waits for them, and re-layouts, put(): lax.dynamic_update_slice(buffer, piece.reshape((1,) * (buffer.ndim - piec...  18.5 us
    dot_general x4, matrix products, partial(): lax.dot_general(columns, acts, (((0,), (0,)), ((), ())), preferred_elemen...  13.4 us
    dot_general x1, matrix products, local(): lax.dot_general(after(tokens, far), weights, (((1,), (1,)), ((), ())), pr...  9.09 us
    all_to_all x1, starting transfers between devices, exchange(): return lax.all_to_all(v, axis, split_axis=0, concat_axis=0, tiled=True)  4.51 us
    broadcast_in_dim x1, local copies, waits for them, and re-layouts, local(): tokens = jnp.zeros((4, 2, toks, feats), BF16)  4.33 us
  transfers between devices with their start and end apart: 28, of which 8 were waited for; matrix products, arithmetic and copies ran while one was open for 32% of the time, Pallas kernels for 0%

profile of v10, /device:TPU:64, one launch (start us, length us, event | category | flops | bytes accessed | tf_op | source)
XLA Modules:
  0.0 174.5 jit_solution(1519235514181731557)
XLA Ops:
  0.7 3.1 %collective-permute-start.1 = (bf16[128,4096]{1,0:T(8,128)(2,1)}, bf16[128,4096]{1,0:T(8,128)(2,1)}, u32[]{:S(2)}, u32[]{:S(2)}) collective-permute-start(bf16[128,4096]{1,0:T(8,128)(2,1)} %bitcast.61), channel_id=1, source_target_pairs={{0,24},{8,0},{16,8},{24,16},{1,25},{9,1},{17,9},{25,17},{2,26},{10... | collective-permute-start | bytes 3145736 | tf_op jit(solution)/shard_map/ppermute | solution.py:12
  6.5 4.5 %all-to-all-start = ((bf16[8,128,512]{1,2,0:T(8,128)(2,1)}), bf16[8,128,512]{1,2,0:T(8,128)(2,1)S(1)}, u32[]{:S(2)}, u32[]{:S(2)}) async-start(bf16[8,128,512]{1,2,0:T(8,128)(2,1)} %bitcast.9), calls=%async_computation | async-start | bytes 2097152 | tf_op jit(solution)/shard_map/all_to_all | solution.py:16
  11.1 1.9 %collective-permute-start.9 = (bf16[128,4096]{1,0:T(8,128)(2,1)}, bf16[128,4096]{1,0:T(8,128)(2,1)S(1)}, u32[]{:S(2)}, u32[]{:S(2)}) collective-permute-start(bf16[128,4096]{1,0:T(8,128)(2,1)} %param.5), channel_id=1, source_target_pairs={{0,2},{2,4},{4,6},{6,32},{32,34},{34,36},{36,38},{38,0},{1,3},{3,5... | collective-permute-start | bytes 3145736 | tf_op jit(solution)/shard_map/ppermute | solution.py:12
  13.0 2.5 %broadcast_in_dim.14 = bf16[4,128,4096]{2,1,0:T(8,128)(2,1)} broadcast(bf16[]{:T(256)} %constant.17.clone.1), dimensions={} | broadcast | bytes 4194306 | tf_op jit(solution)/shard_map/broadcast_in_dim | solution.py:68
  15.5 2.3 %bitcast_dynamic-update-slice_fusion.2 = bf16[4,128,4096]{2,1,0:T(8,128)(2,1)} fusion(bf16[4,128,4096]{2,1,0:T(8,128)(2,1)} %broadcast_in_dim.14, s32[]{:T(128)S(6)} %select_n.98, bf16[128,4096]{1,0:T(8,128)(2,1)} %param.5), kind=kLoop, calls=%fused_computation.16 | loop fusion | bytes 2097156 | tf_op jit(solution)/shard_map/dynamic_update_slice | solution.py:29
  17.8 4.3 %broadcast_in_dim.13 = bf16[4,2,128,4096]{3,2,1,0:T(8,128)(2,1)} broadcast(bf16[]{:T(256)} %constant.17.clone.1), dimensions={} | broadcast | bytes 8388610 | tf_op jit(solution)/shard_map/broadcast_in_dim | solution.py:50
  23.2 18.5 %all-to-all-done = bf16[8,128,512]{1,2,0:T(8,128)(2,1)S(1)} async-done(((bf16[8,128,512]{1,2,0:T(8,128)(2,1)}), bf16[8,128,512]{1,2,0:T(8,128)(2,1)S(1)}, u32[]{:S(2)}, u32[]{:S(2)}) %all-to-all-start) | async-done | bytes 1048608 | tf_op jit(solution)/shard_map/all_to_all | solution.py:16
  47.6 2.0 %collective-permute-start.11 = (bf16[64,4096]{1,0:T(8,128)(2,1)S(1)}, bf16[64,4096]{1,0:T(8,128)(2,1)S(1)}, u32[]{:S(2)}, u32[]{:S(2)}) collective-permute-start(bf16[64,4096]{1,0:T(8,128)(2,1)S(1)} %slice.35), channel_id=1, source_target_pairs={{0,2},{2,4},{4,6},{6,32},{32,34},{34,36},{36,38},{38,0},{1,3},{3,5... | collective-permute-start | bytes 1572872 | tf_op jit(solution)/shard_map/ppermute | solution.py:12
  49.6 2.3 %bitcast_dynamic-update-slice_fusion.9 = bf16[4,2,128,4096]{3,2,1,0:T(8,128)(2,1)} fusion(bf16[4,2,128,4096]{3,2,1,0:T(8,128)(2,1)} %bitcast_dynamic-update-slice_fusion.10, s32[]{:T(128)S(6)} %select_n.91, s32[]{:T(128)S(6)} %select_n.93, bf16[128,4096]{1,0:T(8,128)(2,1)} %collective-permute-done), kind=kLoop, calls=%fused_computation.23 | loop fusion | bytes 2097160 | tf_op jit(solution)/shard_map/dynamic_update_slice | solution.py:29
  51.9 2.3 %bitcast_dynamic-update-slice_fusion.8 = bf16[4,2,128,4096]{3,2,1,0:T(8,128)(2,1)} fusion(bf16[4,2,128,4096]{3,2,1,0:T(8,128)(2,1)} %bitcast_dynamic-update-slice_fusion.9, s32[]{:T(128)S(6)} %select_n.94, s32[]{:T(128)S(6)} %select_n.92, bf16[128,4096]{1,0:T(8,128)(2,1)} %collective-permute-done.1), kind=kLoop, calls=%fused_computation.22 | loop fusion | bytes 2097160 | tf_op jit(solution)/shard_map/dynamic_update_slice | solution.py:29
  56.9 1.8 %collective-permute-done.6 = bf16[64,4096]{1,0:T(8,128)(2,1)S(1)} collective-permute-done((bf16[64,4096]{1,0:T(8,128)(2,1)S(1)}, bf16[64,4096]{1,0:T(8,128)(2,1)S(1)}, u32[]{:S(2)}, u32[]{:S(2)}) %collective-permute-start.6) | collective-permute-done | bytes 524320 | tf_op jit(solution)/shard_map/ppermute | solution.py:12
  60.1 2.4 %bitcast_dynamic-update-slice_fusion.6 = bf16[4,2,128,4096]{3,2,1,0:T(8,128)(2,1)} fusion(bf16[4,2,128,4096]{3,2,1,0:T(8,128)(2,1)} %bitcast_dynamic-update-slice_fusion.7, s32[]{:T(128)S(6)} %select_n.95, s32[]{:T(128)S(6)} %select_n.92, bf16[128,4096]{1,0:T(8,128)(2,1)} %collective-permute-done.3), kind=kLoop, calls=%fused_computation.20 | loop fusion | bytes 2097160 | tf_op jit(solution)/shard_map/dynamic_update_slice | solution.py:29
  65.8 2.9 %fusion.8 = bf16[1024,512]{1,0:T(8,128)(2,1)S(1)} fusion(bf16[1024,512]{1,0:T(8,128)(2,1)S(1)} %bitcast.55, bf16[1024,4096]{1,0:T(8,128)(2,1)} %bitcast.13, s32[]{:T(128)S(6)} %select_n.97), kind=kOutput, calls=%fused_computation.12 | convolution fusion | flops 1074266112 | bytes 4194308 | tf_op jit(solution)/shard_map/dot_general | solution.py:58
  68.8 2.8 %collective-permute-start.15 = (bf16[512,512]{1,0:T(8,128)(2,1)S(1)}, bf16[512,512]{1,0:T(8,128)(2,1)S(1)}, u32[]{:S(2)}, u32[]{:S(2)}) collective-permute-start(bf16[512,512]{1,0:T(8,128)(2,1)S(1)} %get-tuple-element.29), channel_id=1, source_target_pairs={{0,192},{64,0},{128,64},{192,128},{1,193},{65,1},{129,65},{193,129... | collective-permute-start | bytes 1572872 | tf_op jit(solution)/shard_map/ppermute | solution.py:12
  73.3 9.1 %convolution_convert_fusion = bf16[1024,512]{1,0:T(8,128)(2,1)S(1)} fusion(bf16[1024,4096]{1,0:T(8,128)(2,1)} %bitcast.13, bf16[512,4096]{1,0:T(8,128)(2,1)} %bitcast.19), kind=kOutput, calls=%fused_computation.11 | convolution fusion | flops 4295491584 | bytes 13631488 | tf_op jit(solution)/shard_map/dot_general | solution.py:77
  82.4 4.5 %collective-permute-done.16 = bf16[512,512]{1,0:T(8,128)(2,1)S(1)} collective-permute-done((bf16[512,512]{1,0:T(8,128)(2,1)S(1)}, bf16[512,512]{1,0:T(8,128)(2,1)S(1)}, u32[]{:S(2)}, u32[]{:S(2)}) %collective-permute-start.16) | collective-permute-done | bytes 524320 | tf_op jit(solution)/shard_map/ppermute | solution.py:12
  86.9 3.8 %add_convert_fusion.1 = bf16[1024,512]{1,0:T(8,128)(2,1)} fusion(bf16[512,512]{1,0:T(8,128)(2,1)S(1)} %collective-permute-done.16, bf16[1024,512]{1,0:T(8,128)(2,1)S(1)} %bitcast.56, bf16[1024,4096]{1,0:T(8,128)(2,1)} %bitcast.13, s32[]{:T(128)S(6)} %select_n.111), kind=kOutput, calls=%fused_computation.1 | convolution fusion | flops 1075314688 | bytes 4718596 | tf_op jit(solution)/shard_map/dot_general | solution.py:58
  90.7 3.8 %add_convert_fusion.2 = bf16[1024,512]{1,0:T(8,128)(2,1)} fusion(bf16[512,512]{1,0:T(8,128)(2,1)S(1)} %collective-permute-done.15, bf16[1024,512]{1,0:T(8,128)(2,1)S(1)} %bitcast.57, bf16[1024,4096]{1,0:T(8,128)(2,1)} %bitcast.13, s32[]{:T(128)S(6)} %select_n.109), kind=kOutput, calls=%fused_computation.6 | convolution fusion | flops 1075314688 | bytes 4718596 | tf_op jit(solution)/shard_map/dot_general | solution.py:58
  94.6 3.2 %collective-permute-start.18 = (bf16[1024,512]{1,0:T(8,128)(2,1)}, bf16[1024,512]{1,0:T(8,128)(2,1)}, u32[]{:S(2)}, u32[]{:S(2)}) collective-permute-start(bf16[1024,512]{1,0:T(8,128)(2,1)} %add_convert_fusion.2), channel_id=1, source_target_pairs={{0,192},{64,0},{128,64},{192,128},{1,193},{65,1},{129,65},{193,129... | collective-permute-start | bytes 3145736 | tf_op jit(solution)/shard_map/ppermute | solution.py:12
  98.0 2.0 %collective-permute-start.12 = (bf16[1024,128]{1,0:T(8,128)(2,1)S(1)}, bf16[1024,128]{1,0:T(8,128)(2,1)S(1)}, u32[]{:S(2)}, u32[]{:S(2)}) collective-permute-start(bf16[1024,128]{1,0:T(8,128)(2,1)S(1)} %get-tuple-element.32), channel_id=1, source_target_pairs={{0,2},{2,4},{4,6},{6,0},{1,3},{3,5},{5,7},{7,1},{8,10},{10,12},{12... | collective-permute-start | bytes 786440 | tf_op jit(solution)/shard_map/ppermute | solution.py:12
  100.0 2.8 %collective-permute-start.14 = (bf16[1024,128]{1,0:T(8,128)(2,1)S(1)}, bf16[1024,128]{1,0:T(8,128)(2,1)S(1)}, u32[]{:S(2)}, u32[]{:S(2)}) collective-permute-start(bf16[1024,128]{1,0:T(8,128)(2,1)S(1)} %get-tuple-element.30), channel_id=1, source_target_pairs={{0,6},{2,0},{4,2},{6,4},{1,7},{3,1},{5,3},{7,5},{8,14},{10,8},{12,... | collective-permute-start | bytes 786440 | tf_op jit(solution)/shard_map/ppermute | solution.py:12
  102.8 2.9 %fusion.11 = bf16[1024,512]{1,0:T(8,128)(2,1)S(1)} fusion(bf16[1024,512]{1,0:T(8,128)(2,1)S(1)} %bitcast.58, bf16[1024,4096]{1,0:T(8,128)(2,1)} %bitcast.13, s32[]{:T(128)S(6)} %select_n.110), kind=kOutput, calls=%fused_computation.13 | convolution fusion | flops 1074266112 | bytes 4194308 | tf_op jit(solution)/shard_map/dot_general | solution.py:58
  105.6 12.9 %collective-permute-done.12 = bf16[1024,128]{1,0:T(8,128)(2,1)S(1)} collective-permute-done((bf16[1024,128]{1,0:T(8,128)(2,1)S(1)}, bf16[1024,128]{1,0:T(8,128)(2,1)S(1)}, u32[]{:S(2)}, u32[]{:S(2)}) %collective-permute-start.12) | collective-permute-done | bytes 262176 | tf_op jit(solution)/shard_map/ppermute | solution.py:12
  118.5 2.9 %collective-permute-done.14 = bf16[1024,128]{1,0:T(8,128)(2,1)S(1)} collective-permute-done((bf16[1024,128]{1,0:T(8,128)(2,1)S(1)}, bf16[1024,128]{1,0:T(8,128)(2,1)S(1)}, u32[]{:S(2)}, u32[]{:S(2)}) %collective-permute-start.14) | collective-permute-done | bytes 262176 | tf_op jit(solution)/shard_map/ppermute | solution.py:12
  121.5 2.0 %add_convert_fusion = bf16[1024,512]{1,0:T(8,128)(2,1)S(1)} fusion(bf16[1024,512]{1,0:T(8,128)(2,1)} %collective-permute-done.18, bf16[1024,512]{1,0:T(8,128)(2,1)} %collective-permute-done.17, bf16[1024,512]{1,0:T(8,128)(2,1)S(1)} %fusion.11), kind=kLoop, calls=%fused_computation | loop fusion | flops 3145728 | bytes 4194304 | tf_op jit(solution)/shard_map/convert_element_type | solution.py:91
  123.5 2.1 %collective-permute-start.19 = (bf16[1024,128]{1,0:T(8,128)(2,1)S(1)}, bf16[1024,128]{1,0:T(8,128)(2,1)S(1)}, u32[]{:S(2)}, u32[]{:S(2)}) collective-permute-start(bf16[1024,128]{1,0:T(8,128)(2,1)S(1)} %get-tuple-element.26), channel_id=1, source_target_pairs={{0,2},{2,4},{4,6},{6,32},{32,34},{34,36},{36,38},{38,0},{1,3},{3,5... | collective-permute-start | bytes 786440 | tf_op jit(solution)/shard_map/ppermute | solution.py:12
  126.2 4.1 %collective-permute-start.21 = (bf16[512,128]{1,0:T(8,128)(2,1)S(1)}, bf16[512,128]{1,0:T(8,128)(2,1)S(1)}, u32[]{:S(2)}, u32[]{:S(2)}) collective-permute-start(bf16[512,128]{1,0:T(8,128)(2,1)S(1)} %get-tuple-element.24), channel_id=1, source_target_pairs={{0,36},{2,38},{4,0},{6,2},{32,4},{34,6},{36,32},{38,34},{1,37},{3,... | collective-permute-start | bytes 393224 | tf_op jit(solution)/shard_map/ppermute | solution.py:12
  131.1 11.4 %collective-permute-done.21 = bf16[512,128]{1,0:T(8,128)(2,1)S(1)} collective-permute-done((bf16[512,128]{1,0:T(8,128)(2,1)S(1)}, bf16[512,128]{1,0:T(8,128)(2,1)S(1)}, u32[]{:S(2)}, u32[]{:S(2)}) %collective-permute-start.21) | collective-permute-done | bytes 131104 | tf_op jit(solution)/shard_map/ppermute | solution.py:12
  142.6 2.5 %collective-permute-start.23 = (bf16[1024,128]{1,0:T(8,128)(2,1)S(1)}, bf16[1024,128]{1,0:T(8,128)(2,1)S(1)}, u32[]{:S(2)}, u32[]{:S(2)}) collective-permute-start(bf16[1024,128]{1,0:T(8,128)(2,1)S(1)} %add_convert_fusion.4), channel_id=1, source_target_pairs={{0,32},{32,0},{1,33},{33,1},{2,34},{34,2},{3,35},{35,3},{4,36},{36... | collective-permute-start | bytes 786440 | tf_op jit(solution)/shard_map/ppermute | solution.py:12
  145.4 11.9 %collective-permute-done.23 = bf16[1024,128]{1,0:T(8,128)(2,1)S(1)} collective-permute-done((bf16[1024,128]{1,0:T(8,128)(2,1)S(1)}, bf16[1024,128]{1,0:T(8,128)(2,1)S(1)}, u32[]{:S(2)}, u32[]{:S(2)}) %collective-permute-start.23) | collective-permute-done | bytes 262176 | tf_op jit(solution)/shard_map/ppermute | solution.py:12
  158.0 3.0 %collective-permute-start.26 = (bf16[128,1024]{0,1:T(8,128)(2,1)S(1)}, bf16[128,1024]{0,1:T(8,128)(2,1)S(1)}, u32[]{:S(2)}, u32[]{:S(2)}) collective-permute-start(bf16[128,1024]{0,1:T(8,128)(2,1)S(1)} %fusion.14), channel_id=1, source_target_pairs={{0,192},{64,0},{128,64},{192,128},{1,193},{65,1},{129,65},{193,129... | collective-permute-start | bytes 786440 | tf_op jit(solution)/shard_map/ppermute | solution.py:12
  161.2 10.9 %collective-permute-done.24 = bf16[128,1024]{0,1:T(8,128)(2,1)} collective-permute-done((bf16[128,1024]{0,1:T(8,128)(2,1)S(1)}, bf16[128,1024]{0,1:T(8,128)(2,1)}, u32[]{:S(2)}, u32[]{:S(2)}) %collective-permute-start.24) | collective-permute-done | bytes 262176 | tf_op jit(solution)/shard_map/ppermute | solution.py:12
  (82 shorter events, 24.3 us)
Async XLA Ops:
  0.6 49.0 %collective-permute-start = (bf16[128,4096]{1,0:T(8,128)(2,1)}, bf16[128,4096]{1,0:T(8,128)(2,1)}, u32[]{:S(2)}, u32[]{:S(2)}) collective-permute-start(bf16[128,4096]{1,0:T(8,128)(2,1)} %bitcast.60), channel_id=1, source_target_pairs={{0,1},{1,0},{2,3},{3,2},{4,5},{5,4},{6,7},{7,6},{8,9},{9,8},{10,11... | collective-permute-start | bytes 3145736 | tf_op jit(solution)/shard_map/ppermute | solution.py:12
  0.7 42.3 %collective-permute-start.1 = (bf16[128,4096]{1,0:T(8,128)(2,1)}, bf16[128,4096]{1,0:T(8,128)(2,1)}, u32[]{:S(2)}, u32[]{:S(2)}) collective-permute-start(bf16[128,4096]{1,0:T(8,128)(2,1)} %bitcast.61), channel_id=1, source_target_pairs={{0,24},{8,0},{16,8},{24,16},{1,25},{9,1},{17,9},{25,17},{2,26},{10... | collective-permute-start | bytes 3145736 | tf_op jit(solution)/shard_map/ppermute | solution.py:12
  3.8 40.6 %collective-permute-start.3 = (bf16[128,4096]{1,0:T(8,128)(2,1)}, bf16[128,4096]{1,0:T(8,128)(2,1)}, u32[]{:S(2)}, u32[]{:S(2)}) collective-permute-start(bf16[128,4096]{1,0:T(8,128)(2,1)} %bitcast.62), channel_id=1, source_target_pairs={{0,8},{8,16},{16,24},{24,0},{1,9},{9,17},{17,25},{25,1},{2,10},{10... | collective-permute-start | bytes 3145736 | tf_op jit(solution)/shard_map/ppermute | solution.py:12
  6.5 35.2 %all-to-all-start = ((bf16[8,128,512]{1,2,0:T(8,128)(2,1)}), bf16[8,128,512]{1,2,0:T(8,128)(2,1)S(1)}, u32[]{:S(2)}, u32[]{:S(2)}) async-start(bf16[8,128,512]{1,2,0:T(8,128)(2,1)} %bitcast.9), calls=%async_computation | async-start | bytes 2097152 | tf_op jit(solution)/shard_map/all_to_all | solution.py:16
  11.0 36.4 %collective-permute-start.8 = (bf16[128,4096]{1,0:T(8,128)(2,1)}, bf16[128,4096]{1,0:T(8,128)(2,1)S(1)}, u32[]{:S(2)}, u32[]{:S(2)}) collective-permute-start(bf16[128,4096]{1,0:T(8,128)(2,1)} %param.5), channel_id=1, source_target_pairs={{0,38},{2,0},{4,2},{6,4},{32,6},{34,32},{36,34},{38,36},{1,39},{3,... | collective-permute-start | bytes 3145736 | tf_op jit(solution)/shard_map/ppermute | solution.py:12
  11.1 36.5 %collective-permute-start.9 = (bf16[128,4096]{1,0:T(8,128)(2,1)}, bf16[128,4096]{1,0:T(8,128)(2,1)S(1)}, u32[]{:S(2)}, u32[]{:S(2)}) collective-permute-start(bf16[128,4096]{1,0:T(8,128)(2,1)} %param.5), channel_id=1, source_target_pairs={{0,2},{2,4},{4,6},{6,32},{32,34},{34,36},{36,38},{38,0},{1,3},{3,5... | collective-permute-start | bytes 3145736 | tf_op jit(solution)/shard_map/ppermute | solution.py:12
  17.8 4.3 %copy-start.3 = (bf16[1,128,4096]{2,1,0:T(8,128)(2,1)S(1)}, bf16[1,128,4096]{2,1,0:T(8,128)(2,1)}, u32[]{:S(2)}) copy-start(bf16[1,128,4096]{2,1,0:T(8,128)(2,1)} %param.3) | copy-start | bytes 3145732
  44.1 12.2 %collective-permute-start.5 = (bf16[64,4096]{1,0:T(8,128)(2,1)S(1)}, bf16[64,4096]{1,0:T(8,128)(2,1)S(1)}, u32[]{:S(2)}, u32[]{:S(2)}) collective-permute-start(bf16[64,4096]{1,0:T(8,128)(2,1)S(1)} %slice.32), channel_id=1, source_target_pairs={{0,24},{8,0},{16,8},{24,16},{1,25},{9,1},{17,9},{25,17},{2,26},{10... | collective-permute-start | bytes 1572872 | tf_op jit(solution)/shard_map/ppermute | solution.py:12
  45.5 13.2 %collective-permute-start.6 = (bf16[64,4096]{1,0:T(8,128)(2,1)S(1)}, bf16[64,4096]{1,0:T(8,128)(2,1)S(1)}, u32[]{:S(2)}, u32[]{:S(2)}) collective-permute-start(bf16[64,4096]{1,0:T(8,128)(2,1)S(1)} %slice.33), channel_id=1, source_target_pairs={{0,8},{8,16},{16,24},{24,0},{1,9},{9,17},{17,25},{25,1},{2,10},{10... | collective-permute-start | bytes 1572872 | tf_op jit(solution)/shard_map/ppermute | solution.py:12
  47.4 21.3 %collective-permute-start.10 = (bf16[64,4096]{1,0:T(8,128)(2,1)S(1)}, bf16[64,4096]{1,0:T(8,128)(2,1)S(1)}, u32[]{:S(2)}, u32[]{:S(2)}) collective-permute-start(bf16[64,4096]{1,0:T(8,128)(2,1)S(1)} %slice.34), channel_id=1, source_target_pairs={{0,38},{2,0},{4,2},{6,4},{32,6},{34,32},{36,34},{38,36},{1,39},{3,... | collective-permute-start | bytes 1572872 | tf_op jit(solution)/shard_map/ppermute | solution.py:12
  47.6 21.1 %collective-permute-start.11 = (bf16[64,4096]{1,0:T(8,128)(2,1)S(1)}, bf16[64,4096]{1,0:T(8,128)(2,1)S(1)}, u32[]{:S(2)}, u32[]{:S(2)}) collective-permute-start(bf16[64,4096]{1,0:T(8,128)(2,1)S(1)} %slice.35), channel_id=1, source_target_pairs={{0,2},{2,4},{4,6},{6,32},{32,34},{34,36},{36,38},{38,0},{1,3},{3,5... | collective-permute-start | bytes 1572872 | tf_op jit(solution)/shard_map/ppermute | solution.py:12
  49.6 9.4 %collective-permute-start.2 = (bf16[128,4096]{1,0:T(8,128)(2,1)}, bf16[128,4096]{1,0:T(8,128)(2,1)S(1)}, u32[]{:S(2)}, u32[]{:S(2)}) collective-permute-start(bf16[128,4096]{1,0:T(8,128)(2,1)} %collective-permute-done.1), channel_id=1, source_target_pairs={{0,1},{1,0},{2,3},{3,2},{4,5},{5,4},{6,7},{7,6},{8,9},{9,8},{10,11... | collective-permute-start | bytes 3145736 | tf_op jit(solution)/shard_map/ppermute | solution.py:12
  56.3 6.1 %collective-permute-start.4 = (bf16[128,4096]{1,0:T(8,128)(2,1)}, bf16[128,4096]{1,0:T(8,128)(2,1)S(1)}, u32[]{:S(2)}, u32[]{:S(2)}) collective-permute-start(bf16[128,4096]{1,0:T(8,128)(2,1)} %collective-permute-done.3), channel_id=1, source_target_pairs={{0,1},{1,0},{2,3},{3,2},{4,5},{5,4},{6,7},{7,6},{8,9},{9,8},{10,11... | collective-permute-start | bytes 3145736 | tf_op jit(solution)/shard_map/ppermute | solution.py:12
  58.8 6.0 %collective-permute-start.7 = (bf16[128,4096]{1,0:T(8,128)(2,1)S(1)}, bf16[128,4096]{1,0:T(8,128)(2,1)S(1)}, u32[]{:S(2)}, u32[]{:S(2)}) collective-permute-start(bf16[128,4096]{1,0:T(8,128)(2,1)S(1)} %constant_dynamic-update-slice_fusion.8), channel_id=1, source_target_pairs={{0,1},{1,0},{2,3},{3,2},{4,5},{5,4},{6,7},{7,6},{8,9},{9,8},{10,11... | collective-permute-start | bytes 3145736 | tf_op jit(solution)/shard_map/ppermute | solution.py:12
  60.1 5.7 %copy-start = (bf16[8,128,512]{2,1,0:T(8,128)(2,1)S(1)}, bf16[8,128,512]{2,1,0:T(8,128)(2,1)}, u32[]{:S(2)}) copy-start(bf16[8,128,512]{2,1,0:T(8,128)(2,1)} %copy.21) | copy-start | bytes 3145732
  68.8 21.9 %collective-permute-start.15 = (bf16[512,512]{1,0:T(8,128)(2,1)S(1)}, bf16[512,512]{1,0:T(8,128)(2,1)S(1)}, u32[]{:S(2)}, u32[]{:S(2)}) collective-permute-start(bf16[512,512]{1,0:T(8,128)(2,1)S(1)} %get-tuple-element.29), channel_id=1, source_target_pairs={{0,192},{64,0},{128,64},{192,128},{1,193},{65,1},{129,65},{193,129... | collective-permute-start | bytes 1572872 | tf_op jit(solution)/shard_map/ppermute | solution.py:12
  71.6 15.3 %collective-permute-start.16 = (bf16[512,512]{1,0:T(8,128)(2,1)S(1)}, bf16[512,512]{1,0:T(8,128)(2,1)S(1)}, u32[]{:S(2)}, u32[]{:S(2)}) collective-permute-start(bf16[512,512]{1,0:T(8,128)(2,1)S(1)} %get-tuple-element.28), channel_id=1, source_target_pairs={{0,64},{64,128},{128,192},{192,0},{1,65},{65,129},{129,193},{193,1... | collective-permute-start | bytes 1572872 | tf_op jit(solution)/shard_map/ppermute | solution.py:12
  90.7 30.7 %collective-permute-start.17 = (bf16[1024,512]{1,0:T(8,128)(2,1)}, bf16[1024,512]{1,0:T(8,128)(2,1)}, u32[]{:S(2)}, u32[]{:S(2)}) collective-permute-start(bf16[1024,512]{1,0:T(8,128)(2,1)} %add_convert_fusion.1), channel_id=1, source_target_pairs={{0,64},{64,128},{128,192},{192,0},{1,65},{65,129},{129,193},{193,1... | collective-permute-start | bytes 3145736 | tf_op jit(solution)/shard_map/ppermute | solution.py:12
  94.6 26.9 %collective-permute-start.18 = (bf16[1024,512]{1,0:T(8,128)(2,1)}, bf16[1024,512]{1,0:T(8,128)(2,1)}, u32[]{:S(2)}, u32[]{:S(2)}) collective-permute-start(bf16[1024,512]{1,0:T(8,128)(2,1)} %add_convert_fusion.2), channel_id=1, source_target_pairs={{0,192},{64,0},{128,64},{192,128},{1,193},{65,1},{129,65},{193,129... | collective-permute-start | bytes 3145736 | tf_op jit(solution)/shard_map/ppermute | solution.py:12
  98.0 20.6 %collective-permute-start.12 = (bf16[1024,128]{1,0:T(8,128)(2,1)S(1)}, bf16[1024,128]{1,0:T(8,128)(2,1)S(1)}, u32[]{:S(2)}, u32[]{:S(2)}) collective-permute-start(bf16[1024,128]{1,0:T(8,128)(2,1)S(1)} %get-tuple-element.32), channel_id=1, source_target_pairs={{0,2},{2,4},{4,6},{6,0},{1,3},{3,5},{5,7},{7,1},{8,10},{10,12},{12... | collective-permute-start | bytes 786440 | tf_op jit(solution)/shard_map/ppermute | solution.py:12
  100.0 18.6 %collective-permute-start.13 = (bf16[1024,128]{1,0:T(8,128)(2,1)S(1)}, bf16[1024,128]{1,0:T(8,128)(2,1)S(1)}, u32[]{:S(2)}, u32[]{:S(2)}) collective-permute-start(bf16[1024,128]{1,0:T(8,128)(2,1)S(1)} %get-tuple-element.31), channel_id=1, source_target_pairs={{0,4},{2,6},{4,0},{6,2},{1,5},{3,7},{5,1},{7,3},{8,12},{10,14},{12... | collective-permute-start | bytes 786440 | tf_op jit(solution)/shard_map/ppermute | solution.py:12
  100.0 21.5 %collective-permute-start.14 = (bf16[1024,128]{1,0:T(8,128)(2,1)S(1)}, bf16[1024,128]{1,0:T(8,128)(2,1)S(1)}, u32[]{:S(2)}, u32[]{:S(2)}) collective-permute-start(bf16[1024,128]{1,0:T(8,128)(2,1)S(1)} %get-tuple-element.30), channel_id=1, source_target_pairs={{0,6},{2,0},{4,2},{6,4},{1,7},{3,1},{5,3},{7,5},{8,14},{10,8},{12,... | collective-permute-start | bytes 786440 | tf_op jit(solution)/shard_map/ppermute | solution.py:12
  123.5 18.9 %collective-permute-start.19 = (bf16[1024,128]{1,0:T(8,128)(2,1)S(1)}, bf16[1024,128]{1,0:T(8,128)(2,1)S(1)}, u32[]{:S(2)}, u32[]{:S(2)}) collective-permute-start(bf16[1024,128]{1,0:T(8,128)(2,1)S(1)} %get-tuple-element.26), channel_id=1, source_target_pairs={{0,2},{2,4},{4,6},{6,32},{32,34},{34,36},{36,38},{38,0},{1,3},{3,5... | collective-permute-start | bytes 786440 | tf_op jit(solution)/shard_map/ppermute | solution.py:12
  125.6 16.8 %collective-permute-start.20 = (bf16[1024,128]{1,0:T(8,128)(2,1)S(1)}, bf16[1024,128]{1,0:T(8,128)(2,1)S(1)}, u32[]{:S(2)}, u32[]{:S(2)}) collective-permute-start(bf16[1024,128]{1,0:T(8,128)(2,1)S(1)} %get-tuple-element.27), channel_id=1, source_target_pairs={{0,38},{2,0},{4,2},{6,4},{32,6},{34,32},{36,34},{38,36},{1,39},{3,... | collective-permute-start | bytes 786440 | tf_op jit(solution)/shard_map/ppermute | solution.py:12
  126.2 16.2 %collective-permute-start.21 = (bf16[512,128]{1,0:T(8,128)(2,1)S(1)}, bf16[512,128]{1,0:T(8,128)(2,1)S(1)}, u32[]{:S(2)}, u32[]{:S(2)}) collective-permute-start(bf16[512,128]{1,0:T(8,128)(2,1)S(1)} %get-tuple-element.24), channel_id=1, source_target_pairs={{0,36},{2,38},{4,0},{6,2},{32,4},{34,6},{36,32},{38,34},{1,37},{3,... | collective-permute-start | bytes 393224 | tf_op jit(solution)/shard_map/ppermute | solution.py:12
  130.3 12.2 %collective-permute-start.22 = (bf16[512,128]{1,0:T(8,128)(2,1)S(1)}, bf16[512,128]{1,0:T(8,128)(2,1)S(1)}, u32[]{:S(2)}, u32[]{:S(2)}) collective-permute-start(bf16[512,128]{1,0:T(8,128)(2,1)S(1)} %get-tuple-element.25), channel_id=1, source_target_pairs={{0,4},{2,6},{4,32},{6,34},{32,36},{34,38},{36,0},{38,2},{1,5},{3,7... | collective-permute-start | bytes 393224 | tf_op jit(solution)/shard_map/ppermute | solution.py:12
  142.6 14.7 %collective-permute-start.23 = (bf16[1024,128]{1,0:T(8,128)(2,1)S(1)}, bf16[1024,128]{1,0:T(8,128)(2,1)S(1)}, u32[]{:S(2)}, u32[]{:S(2)}) collective-permute-start(bf16[1024,128]{1,0:T(8,128)(2,1)S(1)} %add_convert_fusion.4), channel_id=1, source_target_pairs={{0,32},{32,0},{1,33},{33,1},{2,34},{34,2},{3,35},{35,3},{4,36},{36... | collective-permute-start | bytes 786440 | tf_op jit(solution)/shard_map/ppermute | solution.py:12
  157.4 14.7 %collective-permute-start.24 = (bf16[128,1024]{0,1:T(8,128)(2,1)S(1)}, bf16[128,1024]{0,1:T(8,128)(2,1)}, u32[]{:S(2)}, u32[]{:S(2)}) collective-permute-start(bf16[128,1024]{0,1:T(8,128)(2,1)S(1)} %fusion.14), channel_id=1, source_target_pairs={{0,64},{64,128},{128,192},{192,0},{1,65},{65,129},{129,193},{193,1... | collective-permute-start | bytes 786440 | tf_op jit(solution)/shard_map/ppermute | solution.py:12
  157.5 15.7 %collective-permute-start.25 = (bf16[128,1024]{0,1:T(8,128)(2,1)S(1)}, bf16[128,1024]{0,1:T(8,128)(2,1)S(1)}, u32[]{:S(2)}, u32[]{:S(2)}) collective-permute-start(bf16[128,1024]{0,1:T(8,128)(2,1)S(1)} %fusion.14), channel_id=1, source_target_pairs={{0,128},{64,192},{128,0},{192,64},{1,129},{65,193},{129,1},{193,65... | collective-permute-start | bytes 786440 | tf_op jit(solution)/shard_map/ppermute | solution.py:12
  157.9 15.7 %copy-start.2 = (bf16[4,4,256,128]{3,2,1,0:T(8,128)(2,1)}, bf16[4,4,256,128]{3,2,1,0:T(8,128)(2,1)S(1)}, u32[]{:S(2)}) copy-start(bf16[4,4,256,128]{3,2,1,0:T(8,128)(2,1)S(1)} %constant_dynamic-update-slice_fusion.4) | copy-start | bytes 3145732
  158.0 15.3 %collective-permute-start.26 = (bf16[128,1024]{0,1:T(8,128)(2,1)S(1)}, bf16[128,1024]{0,1:T(8,128)(2,1)S(1)}, u32[]{:S(2)}, u32[]{:S(2)}) collective-permute-start(bf16[128,1024]{0,1:T(8,128)(2,1)S(1)} %fusion.14), channel_id=1, source_target_pairs={{0,192},{64,0},{128,64},{192,128},{1,193},{65,1},{129,65},{193,129... | collective-permute-start | bytes 786440 | tf_op jit(solution)/shard_map/ppermute | solution.py:12
  173.6 1.0 copy-start.1

commit v11 on v10

--- a/solution.py
+++ b/solution.py
@@ -66,8 +66,9 @@
     w = after(w_out, a)
     w_above, w_below = shift(w, RING8, -1), shift(w, RING8, 1)
     weights = jnp.zeros((4, heads, feats), BF16)
-    for piece, d in ((w_out, 0), (w_above, 1), (w_below, 3)):
-        weights = put(weights, piece, (l + d) & 3)
+    weights = put(weights, w_out, l)
+    for piece, d in ((w_above, 1), (w_below, 3)):
+        weights = put(weights, after(piece, far), (l + d) & 3)
     w_far_a = shift(after(w_above[:half], half_a, half_b), RING8, -1)
     w_far_b = shift(after(w_below[half:], half_a, half_b), RING8, 1)
     weights = put(weights, after(w_far_a, far), (l + 2) & 3, 0)

time: 175 us -> 175 us (level)
  transfers between devices with their start and end apart: 28 -> 28, of which waited for: 8 -> 9; matrix products, arithmetic and copies ran while one was open for 32% -> 32% of each run, Pallas kernels for 0% -> 0%
where the time goes in v11:
time: 175 us
  waiting for transfers between devices  76.3 us (44%)
  starting transfers between devices  37.6 us (21%)
  local copies, waits for them, and re-layouts  35 us (20%)
  matrix products  22.7 us (13%)
  other arithmetic  2.19 us (1%)
    ppermute x27, waiting for transfers between devices, shift(): return lax.ppermute(v, axis, [(i, (i + by) % n) for i in range(n)])  57.8 us
    ppermute x27, starting transfers between devices, shift(): return lax.ppermute(v, axis, [(i, (i + by) % n) for i in range(n)])  33.1 us
    all_to_all x1, waiting for transfers between devices, exchange(): return lax.all_to_all(v, axis, split_axis=0, concat_axis=0, tiled=True)  18.5 us
    dynamic_update_slice x13, local copies, waits for them, and re-layouts, put(): lax.dynamic_update_slice(buffer, piece.reshape((1,) * (buffer.ndim - piec...  18.5 us
    dot_general x4, matrix products, partial(): lax.dot_general(columns, acts, (((0,), (0,)), ((), ())), preferred_elemen...  13.6 us
    dot_general x1, matrix products, local(): lax.dot_general(after(tokens, far), weights, (((1,), (1,)), ((), ())), pr...  9.09 us
    all_to_all x1, starting transfers between devices, exchange(): return lax.all_to_all(v, axis, split_axis=0, concat_axis=0, tiled=True)  4.51 us
    broadcast_in_dim x1, local copies, waits for them, and re-layouts, local(): tokens = jnp.zeros((4, 2, toks, feats), BF16)  4.32 us
  transfers between devices with their start and end apart: 28, of which 9 were waited for; matrix products, arithmetic and copies ran while one was open for 32% of the time, Pallas kernels for 0%

profile of v11, /device:TPU:64, one launch (start us, length us, event | category | flops | bytes accessed | tf_op | source)
XLA Modules:
  0.0 174.6 jit_solution(8147631148887757689)
XLA Ops:
  0.7 3.1 %collective-permute-start.1 = (bf16[128,4096]{1,0:T(8,128)(2,1)}, bf16[128,4096]{1,0:T(8,128)(2,1)}, u32[]{:S(2)}, u32[]{:S(2)}) collective-permute-start(bf16[128,4096]{1,0:T(8,128)(2,1)} %bitcast.61), channel_id=1, source_target_pairs={{0,24},{8,0},{16,8},{24,16},{1,25},{9,1},{17,9},{25,17},{2,26},{10... | collective-permute-start | bytes 3145736 | tf_op jit(solution)/shard_map/ppermute | solution.py:12
  6.5 4.5 %all-to-all-start = ((bf16[8,128,512]{1,2,0:T(8,128)(2,1)}), bf16[8,128,512]{1,2,0:T(8,128)(2,1)S(1)}, u32[]{:S(2)}, u32[]{:S(2)}) async-start(bf16[8,128,512]{1,2,0:T(8,128)(2,1)} %bitcast.9), calls=%async_computation | async-start | bytes 2097152 | tf_op jit(solution)/shard_map/all_to_all | solution.py:16
  11.1 1.9 %collective-permute-start.9 = (bf16[128,4096]{1,0:T(8,128)(2,1)}, bf16[128,4096]{1,0:T(8,128)(2,1)S(1)}, u32[]{:S(2)}, u32[]{:S(2)}) collective-permute-start(bf16[128,4096]{1,0:T(8,128)(2,1)} %param.5), channel_id=1, source_target_pairs={{0,2},{2,4},{4,6},{6,32},{32,34},{34,36},{36,38},{38,0},{1,3},{3,5... | collective-permute-start | bytes 3145736 | tf_op jit(solution)/shard_map/ppermute | solution.py:12
  13.0 2.5 %broadcast_in_dim.14 = bf16[4,128,4096]{2,1,0:T(8,128)(2,1)} broadcast(bf16[]{:T(256)} %constant.17.clone.1), dimensions={} | broadcast | bytes 4194306 | tf_op jit(solution)/shard_map/broadcast_in_dim | solution.py:68
  15.5 2.3 %bitcast_dynamic-update-slice_fusion.2 = bf16[4,128,4096]{2,1,0:T(8,128)(2,1)} fusion(bf16[4,128,4096]{2,1,0:T(8,128)(2,1)} %broadcast_in_dim.14, s32[]{:T(128)S(6)} %select_n.100, bf16[128,4096]{1,0:T(8,128)(2,1)} %param.5), kind=kLoop, calls=%fused_computation.16 | loop fusion | bytes 2097156 | tf_op jit(solution)/shard_map/dynamic_update_slice | solution.py:29
  17.8 4.3 %broadcast_in_dim.13 = bf16[4,2,128,4096]{3,2,1,0:T(8,128)(2,1)} broadcast(bf16[]{:T(256)} %constant.17.clone.1), dimensions={} | broadcast | bytes 8388610 | tf_op jit(solution)/shard_map/broadcast_in_dim | solution.py:50
  23.2 18.5 %all-to-all-done = bf16[8,128,512]{1,2,0:T(8,128)(2,1)S(1)} async-done(((bf16[8,128,512]{1,2,0:T(8,128)(2,1)}), bf16[8,128,512]{1,2,0:T(8,128)(2,1)S(1)}, u32[]{:S(2)}, u32[]{:S(2)}) %all-to-all-start) | async-done | bytes 1048608 | tf_op jit(solution)/shard_map/all_to_all | solution.py:16
  47.6 2.0 %collective-permute-start.11 = (bf16[64,4096]{1,0:T(8,128)(2,1)S(1)}, bf16[64,4096]{1,0:T(8,128)(2,1)S(1)}, u32[]{:S(2)}, u32[]{:S(2)}) collective-permute-start(bf16[64,4096]{1,0:T(8,128)(2,1)S(1)} %slice.35), channel_id=1, source_target_pairs={{0,2},{2,4},{4,6},{6,32},{32,34},{34,36},{36,38},{38,0},{1,3},{3,5... | collective-permute-start | bytes 1572872 | tf_op jit(solution)/shard_map/ppermute | solution.py:12
  49.6 2.3 %bitcast_dynamic-update-slice_fusion.9 = bf16[4,2,128,4096]{3,2,1,0:T(8,128)(2,1)} fusion(bf16[4,2,128,4096]{3,2,1,0:T(8,128)(2,1)} %bitcast_dynamic-update-slice_fusion.10, s32[]{:T(128)S(6)} %select_n.93, s32[]{:T(128)S(6)} %select_n.95, bf16[128,4096]{1,0:T(8,128)(2,1)} %collective-permute-done), kind=kLoop, calls=%fused_computation.23 | loop fusion | bytes 2097160 | tf_op jit(solution)/shard_map/dynamic_update_slice | solution.py:29
  51.9 2.3 %bitcast_dynamic-update-slice_fusion.8 = bf16[4,2,128,4096]{3,2,1,0:T(8,128)(2,1)} fusion(bf16[4,2,128,4096]{3,2,1,0:T(8,128)(2,1)} %bitcast_dynamic-update-slice_fusion.9, s32[]{:T(128)S(6)} %select_n.96, s32[]{:T(128)S(6)} %select_n.94, bf16[128,4096]{1,0:T(8,128)(2,1)} %collective-permute-done.1), kind=kLoop, calls=%fused_computation.22 | loop fusion | bytes 2097160 | tf_op jit(solution)/shard_map/dynamic_update_slice | solution.py:29
  54.2 2.1 %collective-permute-done.5 = bf16[64,4096]{1,0:T(8,128)(2,1)S(1)} collective-permute-done((bf16[64,4096]{1,0:T(8,128)(2,1)S(1)}, bf16[64,4096]{1,0:T(8,128)(2,1)S(1)}, u32[]{:S(2)}, u32[]{:S(2)}) %collective-permute-start.5) | collective-permute-done | bytes 524320 | tf_op jit(solution)/shard_map/ppermute | solution.py:12
  56.4 2.4 %collective-permute-done.6 = bf16[64,4096]{1,0:T(8,128)(2,1)S(1)} collective-permute-done((bf16[64,4096]{1,0:T(8,128)(2,1)S(1)}, bf16[64,4096]{1,0:T(8,128)(2,1)S(1)}, u32[]{:S(2)}, u32[]{:S(2)}) %collective-permute-start.6) | collective-permute-done | bytes 524320 | tf_op jit(solution)/shard_map/ppermute | solution.py:12
  59.9 2.4 %bitcast_dynamic-update-slice_fusion.6 = bf16[4,2,128,4096]{3,2,1,0:T(8,128)(2,1)} fusion(bf16[4,2,128,4096]{3,2,1,0:T(8,128)(2,1)} %bitcast_dynamic-update-slice_fusion.7, s32[]{:T(128)S(6)} %select_n.97, s32[]{:T(128)S(6)} %select_n.94, bf16[128,4096]{1,0:T(8,128)(2,1)} %collective-permute-done.3), kind=kLoop, calls=%fused_computation.20 | loop fusion | bytes 2097160 | tf_op jit(solution)/shard_map/dynamic_update_slice | solution.py:29
  65.6 2.9 %fusion.8 = bf16[1024,512]{1,0:T(8,128)(2,1)S(1)} fusion(bf16[1024,512]{1,0:T(8,128)(2,1)S(1)} %bitcast.55, bf16[1024,4096]{1,0:T(8,128)(2,1)} %bitcast.13, s32[]{:T(128)S(6)} %select_n.99), kind=kOutput, calls=%fused_computation.12 | convolution fusion | flops 1074266112 | bytes 4194308 | tf_op jit(solution)/shard_map/dot_general | solution.py:58
  68.6 3.0 %collective-permute-start.15 = (bf16[512,512]{1,0:T(8,128)(2,1)S(1)}, bf16[512,512]{1,0:T(8,128)(2,1)S(1)}, u32[]{:S(2)}, u32[]{:S(2)}) collective-permute-start(bf16[512,512]{1,0:T(8,128)(2,1)S(1)} %get-tuple-element.33), channel_id=1, source_target_pairs={{0,192},{64,0},{128,64},{192,128},{1,193},{65,1},{129,65},{193,129... | collective-permute-start | bytes 1572872 | tf_op jit(solution)/shard_map/ppermute | solution.py:12
  75.4 9.1 %convolution_convert_fusion = bf16[1024,512]{1,0:T(8,128)(2,1)S(1)} fusion(bf16[1024,4096]{1,0:T(8,128)(2,1)} %bitcast.13, bf16[512,4096]{1,0:T(8,128)(2,1)} %bitcast.19), kind=kOutput, calls=%fused_computation.11 | convolution fusion | flops 4295491584 | bytes 13631488 | tf_op jit(solution)/shard_map/dot_general | solution.py:78
  84.5 2.3 %collective-permute-done.16 = bf16[512,512]{1,0:T(8,128)(2,1)S(1)} collective-permute-done((bf16[512,512]{1,0:T(8,128)(2,1)S(1)}, bf16[512,512]{1,0:T(8,128)(2,1)S(1)}, u32[]{:S(2)}, u32[]{:S(2)}) %collective-permute-start.16) | collective-permute-done | bytes 524320 | tf_op jit(solution)/shard_map/ppermute | solution.py:12
  86.9 3.9 %add_convert_fusion.1 = bf16[1024,512]{1,0:T(8,128)(2,1)} fusion(bf16[512,512]{1,0:T(8,128)(2,1)S(1)} %collective-permute-done.16, bf16[1024,512]{1,0:T(8,128)(2,1)S(1)} %bitcast.56, bf16[1024,4096]{1,0:T(8,128)(2,1)} %bitcast.13, s32[]{:T(128)S(6)} %select_n.114), kind=kOutput, calls=%fused_computation.1 | convolution fusion | flops 1075314688 | bytes 4718596 | tf_op jit(solution)/shard_map/dot_general | solution.py:58
  90.8 4.0 %add_convert_fusion.2 = bf16[1024,512]{1,0:T(8,128)(2,1)} fusion(bf16[512,512]{1,0:T(8,128)(2,1)S(1)} %collective-permute-done.15, bf16[1024,512]{1,0:T(8,128)(2,1)S(1)} %bitcast.57, bf16[1024,4096]{1,0:T(8,128)(2,1)} %bitcast.13, s32[]{:T(128)S(6)} %select_n.112), kind=kOutput, calls=%fused_computation.6 | convolution fusion | flops 1075314688 | bytes 4718596 | tf_op jit(solution)/shard_map/dot_general | solution.py:58
  94.7 3.1 %collective-permute-start.18 = (bf16[1024,512]{1,0:T(8,128)(2,1)}, bf16[1024,512]{1,0:T(8,128)(2,1)}, u32[]{:S(2)}, u32[]{:S(2)}) collective-permute-start(bf16[1024,512]{1,0:T(8,128)(2,1)} %add_convert_fusion.2), channel_id=1, source_target_pairs={{0,192},{64,0},{128,64},{192,128},{1,193},{65,1},{129,65},{193,129... | collective-permute-start | bytes 3145736 | tf_op jit(solution)/shard_map/ppermute | solution.py:12
  98.0 2.0 %collective-permute-start.12 = (bf16[1024,128]{1,0:T(8,128)(2,1)S(1)}, bf16[1024,128]{1,0:T(8,128)(2,1)S(1)}, u32[]{:S(2)}, u32[]{:S(2)}) collective-permute-start(bf16[1024,128]{1,0:T(8,128)(2,1)S(1)} %get-tuple-element.36), channel_id=1, source_target_pairs={{0,2},{2,4},{4,6},{6,0},{1,3},{3,5},{5,7},{7,1},{8,10},{10,12},{12... | collective-permute-start | bytes 786440 | tf_op jit(solution)/shard_map/ppermute | solution.py:12
  101.6 2.9 %fusion.11 = bf16[1024,512]{1,0:T(8,128)(2,1)S(1)} fusion(bf16[1024,512]{1,0:T(8,128)(2,1)S(1)} %bitcast.58, bf16[1024,4096]{1,0:T(8,128)(2,1)} %bitcast.13, s32[]{:T(128)S(6)} %select_n.113), kind=kOutput, calls=%fused_computation.13 | convolution fusion | flops 1074266112 | bytes 4194308 | tf_op jit(solution)/shard_map/dot_general | solution.py:58
  104.5 14.1 %collective-permute-done.12 = bf16[1024,128]{1,0:T(8,128)(2,1)S(1)} collective-permute-done((bf16[1024,128]{1,0:T(8,128)(2,1)S(1)}, bf16[1024,128]{1,0:T(8,128)(2,1)S(1)}, u32[]{:S(2)}, u32[]{:S(2)}) %collective-permute-start.12) | collective-permute-done | bytes 262176 | tf_op jit(solution)/shard_map/ppermute | solution.py:12
  118.6 2.6 %collective-permute-done.14 = bf16[1024,128]{1,0:T(8,128)(2,1)S(1)} collective-permute-done((bf16[1024,128]{1,0:T(8,128)(2,1)S(1)}, bf16[1024,128]{1,0:T(8,128)(2,1)S(1)}, u32[]{:S(2)}, u32[]{:S(2)}) %collective-permute-start.14) | collective-permute-done | bytes 262176 | tf_op jit(solution)/shard_map/ppermute | solution.py:12
  121.2 2.0 %add_convert_fusion = bf16[1024,512]{1,0:T(8,128)(2,1)S(1)} fusion(bf16[1024,512]{1,0:T(8,128)(2,1)} %collective-permute-done.18, bf16[1024,512]{1,0:T(8,128)(2,1)} %collective-permute-done.17, bf16[1024,512]{1,0:T(8,128)(2,1)S(1)} %fusion.11), kind=kLoop, calls=%fused_computation | loop fusion | flops 3145728 | bytes 4194304 | tf_op jit(solution)/shard_map/convert_element_type | solution.py:92
  123.3 2.3 %collective-permute-start.19 = (bf16[1024,128]{1,0:T(8,128)(2,1)S(1)}, bf16[1024,128]{1,0:T(8,128)(2,1)S(1)}, u32[]{:S(2)}, u32[]{:S(2)}) collective-permute-start(bf16[1024,128]{1,0:T(8,128)(2,1)S(1)} %get-tuple-element.30), channel_id=1, source_target_pairs={{0,2},{2,4},{4,6},{6,32},{32,34},{34,36},{36,38},{38,0},{1,3},{3,5... | collective-permute-start | bytes 786440 | tf_op jit(solution)/shard_map/ppermute | solution.py:12
  126.0 4.4 %collective-permute-start.21 = (bf16[512,128]{1,0:T(8,128)(2,1)S(1)}, bf16[512,128]{1,0:T(8,128)(2,1)S(1)}, u32[]{:S(2)}, u32[]{:S(2)}) collective-permute-start(bf16[512,128]{1,0:T(8,128)(2,1)S(1)} %get-tuple-element.28), channel_id=1, source_target_pairs={{0,36},{2,38},{4,0},{6,2},{32,4},{34,6},{36,32},{38,34},{1,37},{3,... | collective-permute-start | bytes 393224 | tf_op jit(solution)/shard_map/ppermute | solution.py:12
  131.1 11.4 %collective-permute-done.21 = bf16[512,128]{1,0:T(8,128)(2,1)S(1)} collective-permute-done((bf16[512,128]{1,0:T(8,128)(2,1)S(1)}, bf16[512,128]{1,0:T(8,128)(2,1)S(1)}, u32[]{:S(2)}, u32[]{:S(2)}) %collective-permute-start.21) | collective-permute-done | bytes 131104 | tf_op jit(solution)/shard_map/ppermute | solution.py:12
  142.6 2.5 %collective-permute-start.23 = (bf16[1024,128]{1,0:T(8,128)(2,1)S(1)}, bf16[1024,128]{1,0:T(8,128)(2,1)S(1)}, u32[]{:S(2)}, u32[]{:S(2)}) collective-permute-start(bf16[1024,128]{1,0:T(8,128)(2,1)S(1)} %add_convert_fusion.4), channel_id=1, source_target_pairs={{0,32},{32,0},{1,33},{33,1},{2,34},{34,2},{3,35},{35,3},{4,36},{36... | collective-permute-start | bytes 786440 | tf_op jit(solution)/shard_map/ppermute | solution.py:12
  145.5 11.9 %collective-permute-done.23 = bf16[1024,128]{1,0:T(8,128)(2,1)S(1)} collective-permute-done((bf16[1024,128]{1,0:T(8,128)(2,1)S(1)}, bf16[1024,128]{1,0:T(8,128)(2,1)S(1)}, u32[]{:S(2)}, u32[]{:S(2)}) %collective-permute-start.23) | collective-permute-done | bytes 262176 | tf_op jit(solution)/shard_map/ppermute | solution.py:12
  157.9 3.2 %collective-permute-start.26 = (bf16[128,1024]{0,1:T(8,128)(2,1)S(1)}, bf16[128,1024]{0,1:T(8,128)(2,1)S(1)}, u32[]{:S(2)}, u32[]{:S(2)}) collective-permute-start(bf16[128,1024]{0,1:T(8,128)(2,1)S(1)} %fusion.14), channel_id=1, source_target_pairs={{0,192},{64,0},{128,64},{192,128},{1,193},{65,1},{129,65},{193,129... | collective-permute-start | bytes 786440 | tf_op jit(solution)/shard_map/ppermute | solution.py:12
  161.2 10.9 %collective-permute-done.24 = bf16[128,1024]{0,1:T(8,128)(2,1)} collective-permute-done((bf16[128,1024]{0,1:T(8,128)(2,1)S(1)}, bf16[128,1024]{0,1:T(8,128)(2,1)}, u32[]{:S(2)}, u32[]{:S(2)}) %collective-permute-start.24) | collective-permute-done | bytes 262176 | tf_op jit(solution)/shard_map/ppermute | solution.py:12
  (84 shorter events, 24.7 us)
Async XLA Ops:
  0.6 49.0 %collective-permute-start = (bf16[128,4096]{1,0:T(8,128)(2,1)}, bf16[128,4096]{1,0:T(8,128)(2,1)}, u32[]{:S(2)}, u32[]{:S(2)}) collective-permute-start(bf16[128,4096]{1,0:T(8,128)(2,1)} %bitcast.60), channel_id=1, source_target_pairs={{0,1},{1,0},{2,3},{3,2},{4,5},{5,4},{6,7},{7,6},{8,9},{9,8},{10,11... | collective-permute-start | bytes 3145736 | tf_op jit(solution)/shard_map/ppermute | solution.py:12
  0.7 42.3 %collective-permute-start.1 = (bf16[128,4096]{1,0:T(8,128)(2,1)}, bf16[128,4096]{1,0:T(8,128)(2,1)}, u32[]{:S(2)}, u32[]{:S(2)}) collective-permute-start(bf16[128,4096]{1,0:T(8,128)(2,1)} %bitcast.61), channel_id=1, source_target_pairs={{0,24},{8,0},{16,8},{24,16},{1,25},{9,1},{17,9},{25,17},{2,26},{10... | collective-permute-start | bytes 3145736 | tf_op jit(solution)/shard_map/ppermute | solution.py:12
  3.8 40.6 %collective-permute-start.3 = (bf16[128,4096]{1,0:T(8,128)(2,1)}, bf16[128,4096]{1,0:T(8,128)(2,1)}, u32[]{:S(2)}, u32[]{:S(2)}) collective-permute-start(bf16[128,4096]{1,0:T(8,128)(2,1)} %bitcast.62), channel_id=1, source_target_pairs={{0,8},{8,16},{16,24},{24,0},{1,9},{9,17},{17,25},{25,1},{2,10},{10... | collective-permute-start | bytes 3145736 | tf_op jit(solution)/shard_map/ppermute | solution.py:12
  6.5 35.2 %all-to-all-start = ((bf16[8,128,512]{1,2,0:T(8,128)(2,1)}), bf16[8,128,512]{1,2,0:T(8,128)(2,1)S(1)}, u32[]{:S(2)}, u32[]{:S(2)}) async-start(bf16[8,128,512]{1,2,0:T(8,128)(2,1)} %bitcast.9), calls=%async_computation | async-start | bytes 2097152 | tf_op jit(solution)/shard_map/all_to_all | solution.py:16
  11.0 36.4 %collective-permute-start.8 = (bf16[128,4096]{1,0:T(8,128)(2,1)}, bf16[128,4096]{1,0:T(8,128)(2,1)S(1)}, u32[]{:S(2)}, u32[]{:S(2)}) collective-permute-start(bf16[128,4096]{1,0:T(8,128)(2,1)} %param.5), channel_id=1, source_target_pairs={{0,38},{2,0},{4,2},{6,4},{32,6},{34,32},{36,34},{38,36},{1,39},{3,... | collective-permute-start | bytes 3145736 | tf_op jit(solution)/shard_map/ppermute | solution.py:12
  11.1 36.5 %collective-permute-start.9 = (bf16[128,4096]{1,0:T(8,128)(2,1)}, bf16[128,4096]{1,0:T(8,128)(2,1)S(1)}, u32[]{:S(2)}, u32[]{:S(2)}) collective-permute-start(bf16[128,4096]{1,0:T(8,128)(2,1)} %param.5), channel_id=1, source_target_pairs={{0,2},{2,4},{4,6},{6,32},{32,34},{34,36},{36,38},{38,0},{1,3},{3,5... | collective-permute-start | bytes 3145736 | tf_op jit(solution)/shard_map/ppermute | solution.py:12
  17.8 4.3 %copy-start.4 = (bf16[1,128,4096]{2,1,0:T(8,128)(2,1)S(1)}, bf16[1,128,4096]{2,1,0:T(8,128)(2,1)}, u32[]{:S(2)}) copy-start(bf16[1,128,4096]{2,1,0:T(8,128)(2,1)} %param.3) | copy-start | bytes 3145732
  44.1 12.2 %collective-permute-start.5 = (bf16[64,4096]{1,0:T(8,128)(2,1)S(1)}, bf16[64,4096]{1,0:T(8,128)(2,1)S(1)}, u32[]{:S(2)}, u32[]{:S(2)}) collective-permute-start(bf16[64,4096]{1,0:T(8,128)(2,1)S(1)} %slice.32), channel_id=1, source_target_pairs={{0,24},{8,0},{16,8},{24,16},{1,25},{9,1},{17,9},{25,17},{2,26},{10... | collective-permute-start | bytes 1572872 | tf_op jit(solution)/shard_map/ppermute | solution.py:12
  45.5 13.2 %collective-permute-start.6 = (bf16[64,4096]{1,0:T(8,128)(2,1)S(1)}, bf16[64,4096]{1,0:T(8,128)(2,1)S(1)}, u32[]{:S(2)}, u32[]{:S(2)}) collective-permute-start(bf16[64,4096]{1,0:T(8,128)(2,1)S(1)} %slice.33), channel_id=1, source_target_pairs={{0,8},{8,16},{16,24},{24,0},{1,9},{9,17},{17,25},{25,1},{2,10},{10... | collective-permute-start | bytes 1572872 | tf_op jit(solution)/shard_map/ppermute | solution.py:12
  47.4 21.1 %collective-permute-start.10 = (bf16[64,4096]{1,0:T(8,128)(2,1)S(1)}, bf16[64,4096]{1,0:T(8,128)(2,1)S(1)}, u32[]{:S(2)}, u32[]{:S(2)}) collective-permute-start(bf16[64,4096]{1,0:T(8,128)(2,1)S(1)} %slice.34), channel_id=1, source_target_pairs={{0,38},{2,0},{4,2},{6,4},{32,6},{34,32},{36,34},{38,36},{1,39},{3,... | collective-permute-start | bytes 1572872 | tf_op jit(solution)/shard_map/ppermute | solution.py:12
  47.6 21.0 %collective-permute-start.11 = (bf16[64,4096]{1,0:T(8,128)(2,1)S(1)}, bf16[64,4096]{1,0:T(8,128)(2,1)S(1)}, u32[]{:S(2)}, u32[]{:S(2)}) collective-permute-start(bf16[64,4096]{1,0:T(8,128)(2,1)S(1)} %slice.35), channel_id=1, source_target_pairs={{0,2},{2,4},{4,6},{6,32},{32,34},{34,36},{36,38},{38,0},{1,3},{3,5... | collective-permute-start | bytes 1572872 | tf_op jit(solution)/shard_map/ppermute | solution.py:12
  49.6 9.2 %collective-permute-start.2 = (bf16[128,4096]{1,0:T(8,128)(2,1)}, bf16[128,4096]{1,0:T(8,128)(2,1)S(1)}, u32[]{:S(2)}, u32[]{:S(2)}) collective-permute-start(bf16[128,4096]{1,0:T(8,128)(2,1)} %collective-permute-done.1), channel_id=1, source_target_pairs={{0,1},{1,0},{2,3},{3,2},{4,5},{5,4},{6,7},{7,6},{8,9},{9,8},{10,11... | collective-permute-start | bytes 3145736 | tf_op jit(solution)/shard_map/ppermute | solution.py:12
  56.3 6.0 %collective-permute-start.4 = (bf16[128,4096]{1,0:T(8,128)(2,1)}, bf16[128,4096]{1,0:T(8,128)(2,1)S(1)}, u32[]{:S(2)}, u32[]{:S(2)}) collective-permute-start(bf16[128,4096]{1,0:T(8,128)(2,1)} %collective-permute-done.3), channel_id=1, source_target_pairs={{0,1},{1,0},{2,3},{3,2},{4,5},{5,4},{6,7},{7,6},{8,9},{9,8},{10,11... | collective-permute-start | bytes 3145736 | tf_op jit(solution)/shard_map/ppermute | solution.py:12
  58.8 5.8 %collective-permute-start.7 = (bf16[128,4096]{1,0:T(8,128)(2,1)S(1)}, bf16[128,4096]{1,0:T(8,128)(2,1)S(1)}, u32[]{:S(2)}, u32[]{:S(2)}) collective-permute-start(bf16[128,4096]{1,0:T(8,128)(2,1)S(1)} %constant_dynamic-update-slice_fusion.8), channel_id=1, source_target_pairs={{0,1},{1,0},{2,3},{3,2},{4,5},{5,4},{6,7},{7,6},{8,9},{9,8},{10,11... | collective-permute-start | bytes 3145736 | tf_op jit(solution)/shard_map/ppermute | solution.py:12
  59.9 5.7 %copy-start = (bf16[8,128,512]{2,1,0:T(8,128)(2,1)S(1)}, bf16[8,128,512]{2,1,0:T(8,128)(2,1)}, u32[]{:S(2)}) copy-start(bf16[8,128,512]{2,1,0:T(8,128)(2,1)} %copy.21) | copy-start | bytes 3145732
  68.6 22.2 %collective-permute-start.15 = (bf16[512,512]{1,0:T(8,128)(2,1)S(1)}, bf16[512,512]{1,0:T(8,128)(2,1)S(1)}, u32[]{:S(2)}, u32[]{:S(2)}) collective-permute-start(bf16[512,512]{1,0:T(8,128)(2,1)S(1)} %get-tuple-element.33), channel_id=1, source_target_pairs={{0,192},{64,0},{128,64},{192,128},{1,193},{65,1},{129,65},{193,129... | collective-permute-start | bytes 1572872 | tf_op jit(solution)/shard_map/ppermute | solution.py:12
  71.6 15.3 %collective-permute-start.16 = (bf16[512,512]{1,0:T(8,128)(2,1)S(1)}, bf16[512,512]{1,0:T(8,128)(2,1)S(1)}, u32[]{:S(2)}, u32[]{:S(2)}) collective-permute-start(bf16[512,512]{1,0:T(8,128)(2,1)S(1)} %get-tuple-element.32), channel_id=1, source_target_pairs={{0,64},{64,128},{128,192},{192,0},{1,65},{65,129},{129,193},{193,1... | collective-permute-start | bytes 1572872 | tf_op jit(solution)/shard_map/ppermute | solution.py:12
  90.8 10.9 %copy-start.1 = (bf16[8,128,512]{2,1,0:T(8,128)(2,1)S(1)}, bf16[8,128,512]{2,1,0:T(8,128)(2,1)}, u32[]{:S(2)}) copy-start(bf16[8,128,512]{2,1,0:T(8,128)(2,1)} %copy.21) | copy-start | bytes 3145732
  90.8 30.5 %collective-permute-start.17 = (bf16[1024,512]{1,0:T(8,128)(2,1)}, bf16[1024,512]{1,0:T(8,128)(2,1)}, u32[]{:S(2)}, u32[]{:S(2)}) collective-permute-start(bf16[1024,512]{1,0:T(8,128)(2,1)} %add_convert_fusion.1), channel_id=1, source_target_pairs={{0,64},{64,128},{128,192},{192,0},{1,65},{65,129},{129,193},{193,1... | collective-permute-start | bytes 3145736 | tf_op jit(solution)/shard_map/ppermute | solution.py:12
  94.7 26.5 %collective-permute-start.18 = (bf16[1024,512]{1,0:T(8,128)(2,1)}, bf16[1024,512]{1,0:T(8,128)(2,1)}, u32[]{:S(2)}, u32[]{:S(2)}) collective-permute-start(bf16[1024,512]{1,0:T(8,128)(2,1)} %add_convert_fusion.2), channel_id=1, source_target_pairs={{0,192},{64,0},{128,64},{192,128},{1,193},{65,1},{129,65},{193,129... | collective-permute-start | bytes 3145736 | tf_op jit(solution)/shard_map/ppermute | solution.py:12
  98.0 20.6 %collective-permute-start.12 = (bf16[1024,128]{1,0:T(8,128)(2,1)S(1)}, bf16[1024,128]{1,0:T(8,128)(2,1)S(1)}, u32[]{:S(2)}, u32[]{:S(2)}) collective-permute-start(bf16[1024,128]{1,0:T(8,128)(2,1)S(1)} %get-tuple-element.36), channel_id=1, source_target_pairs={{0,2},{2,4},{4,6},{6,0},{1,3},{3,5},{5,7},{7,1},{8,10},{10,12},{12... | collective-permute-start | bytes 786440 | tf_op jit(solution)/shard_map/ppermute | solution.py:12
  100.0 18.6 %collective-permute-start.13 = (bf16[1024,128]{1,0:T(8,128)(2,1)S(1)}, bf16[1024,128]{1,0:T(8,128)(2,1)S(1)}, u32[]{:S(2)}, u32[]{:S(2)}) collective-permute-start(bf16[1024,128]{1,0:T(8,128)(2,1)S(1)} %get-tuple-element.35), channel_id=1, source_target_pairs={{0,4},{2,6},{4,0},{6,2},{1,5},{3,7},{5,1},{7,3},{8,12},{10,14},{12... | collective-permute-start | bytes 786440 | tf_op jit(solution)/shard_map/ppermute | solution.py:12
  100.0 21.2 %collective-permute-start.14 = (bf16[1024,128]{1,0:T(8,128)(2,1)S(1)}, bf16[1024,128]{1,0:T(8,128)(2,1)S(1)}, u32[]{:S(2)}, u32[]{:S(2)}) collective-permute-start(bf16[1024,128]{1,0:T(8,128)(2,1)S(1)} %get-tuple-element.34), channel_id=1, source_target_pairs={{0,6},{2,0},{4,2},{6,4},{1,7},{3,1},{5,3},{7,5},{8,14},{10,8},{12,... | collective-permute-start | bytes 786440 | tf_op jit(solution)/shard_map/ppermute | solution.py:12
  123.3 19.2 %collective-permute-start.19 = (bf16[1024,128]{1,0:T(8,128)(2,1)S(1)}, bf16[1024,128]{1,0:T(8,128)(2,1)S(1)}, u32[]{:S(2)}, u32[]{:S(2)}) collective-permute-start(bf16[1024,128]{1,0:T(8,128)(2,1)S(1)} %get-tuple-element.30), channel_id=1, source_target_pairs={{0,2},{2,4},{4,6},{6,32},{32,34},{34,36},{36,38},{38,0},{1,3},{3,5... | collective-permute-start | bytes 786440 | tf_op jit(solution)/shard_map/ppermute | solution.py:12
  125.6 16.8 %collective-permute-start.20 = (bf16[1024,128]{1,0:T(8,128)(2,1)S(1)}, bf16[1024,128]{1,0:T(8,128)(2,1)S(1)}, u32[]{:S(2)}, u32[]{:S(2)}) collective-permute-start(bf16[1024,128]{1,0:T(8,128)(2,1)S(1)} %get-tuple-element.31), channel_id=1, source_target_pairs={{0,38},{2,0},{4,2},{6,4},{32,6},{34,32},{36,34},{38,36},{1,39},{3,... | collective-permute-start | bytes 786440 | tf_op jit(solution)/shard_map/ppermute | solution.py:12
  126.0 16.5 %collective-permute-start.21 = (bf16[512,128]{1,0:T(8,128)(2,1)S(1)}, bf16[512,128]{1,0:T(8,128)(2,1)S(1)}, u32[]{:S(2)}, u32[]{:S(2)}) collective-permute-start(bf16[512,128]{1,0:T(8,128)(2,1)S(1)} %get-tuple-element.28), channel_id=1, source_target_pairs={{0,36},{2,38},{4,0},{6,2},{32,4},{34,6},{36,32},{38,34},{1,37},{3,... | collective-permute-start | bytes 393224 | tf_op jit(solution)/shard_map/ppermute | solution.py:12
  130.3 12.1 %collective-permute-start.22 = (bf16[512,128]{1,0:T(8,128)(2,1)S(1)}, bf16[512,128]{1,0:T(8,128)(2,1)S(1)}, u32[]{:S(2)}, u32[]{:S(2)}) collective-permute-start(bf16[512,128]{1,0:T(8,128)(2,1)S(1)} %get-tuple-element.29), channel_id=1, source_target_pairs={{0,4},{2,6},{4,32},{6,34},{32,36},{34,38},{36,0},{38,2},{1,5},{3,7... | collective-permute-start | bytes 393224 | tf_op jit(solution)/shard_map/ppermute | solution.py:12
  142.6 14.7 %collective-permute-start.23 = (bf16[1024,128]{1,0:T(8,128)(2,1)S(1)}, bf16[1024,128]{1,0:T(8,128)(2,1)S(1)}, u32[]{:S(2)}, u32[]{:S(2)}) collective-permute-start(bf16[1024,128]{1,0:T(8,128)(2,1)S(1)} %add_convert_fusion.4), channel_id=1, source_target_pairs={{0,32},{32,0},{1,33},{33,1},{2,34},{34,2},{3,35},{35,3},{4,36},{36... | collective-permute-start | bytes 786440 | tf_op jit(solution)/shard_map/ppermute | solution.py:12
  157.5 14.7 %collective-permute-start.24 = (bf16[128,1024]{0,1:T(8,128)(2,1)S(1)}, bf16[128,1024]{0,1:T(8,128)(2,1)}, u32[]{:S(2)}, u32[]{:S(2)}) collective-permute-start(bf16[128,1024]{0,1:T(8,128)(2,1)S(1)} %fusion.14), channel_id=1, source_target_pairs={{0,64},{64,128},{128,192},{192,0},{1,65},{65,129},{129,193},{193,1... | collective-permute-start | bytes 786440 | tf_op jit(solution)/shard_map/ppermute | solution.py:12
  157.5 15.7 %collective-permute-start.25 = (bf16[128,1024]{0,1:T(8,128)(2,1)S(1)}, bf16[128,1024]{0,1:T(8,128)(2,1)S(1)}, u32[]{:S(2)}, u32[]{:S(2)}) collective-permute-start(bf16[128,1024]{0,1:T(8,128)(2,1)S(1)} %fusion.14), channel_id=1, source_target_pairs={{0,128},{64,192},{128,0},{192,64},{1,129},{65,193},{129,1},{193,65... | collective-permute-start | bytes 786440 | tf_op jit(solution)/shard_map/ppermute | solution.py:12
  157.7 15.9 %copy-start.3 = (bf16[4,4,256,128]{3,2,1,0:T(8,128)(2,1)}, bf16[4,4,256,128]{3,2,1,0:T(8,128)(2,1)S(1)}, u32[]{:S(2)}) copy-start(bf16[4,4,256,128]{3,2,1,0:T(8,128)(2,1)S(1)} %constant_dynamic-update-slice_fusion.4) | copy-start | bytes 3145732
  157.9 15.6 %collective-permute-start.26 = (bf16[128,1024]{0,1:T(8,128)(2,1)S(1)}, bf16[128,1024]{0,1:T(8,128)(2,1)S(1)}, u32[]{:S(2)}, u32[]{:S(2)}) collective-permute-start(bf16[128,1024]{0,1:T(8,128)(2,1)S(1)} %fusion.14), channel_id=1, source_target_pairs={{0,192},{64,0},{128,64},{192,128},{1,193},{65,1},{129,65},{193,129... | collective-permute-start | bytes 786440 | tf_op jit(solution)/shard_map/ppermute | solution.py:12
  (1 other events, 1.0 us)

commit v12 on v10

--- a/solution.py
+++ b/solution.py
@@ -87,7 +87,7 @@
     bottom = lax.pad(bottom, none, ((cols // 2, 0, 0), (0, 0, 0))).astype(F32)
     near_a, near_b = partial(1, after(tokens, res), top), partial(3, after(tokens, res), bottom)
     own = partial(0, after(tokens, near_b))
-    tot = [after(own, *back[1:]), shift(near_a, "x", 1), shift(near_b, "x", -1)]
+    tot = [own, shift(near_a, "x", 1), shift(near_b, "x", -1)]
     tot = sum(t.astype(F32) for t in tot).astype(BF16)
     far = block(tot, l + 2)
     acc = block(tot, l).astype(F32)

time: 175 us -> 185 us (1.057)
  the two profiles are of different devices: /device:TPU:64 before, /device:TPU:38 now
where the time goes in v12:
time: 185 us
  waiting for transfers between devices  82.7 us (45%)
  local copies, waits for them, and re-layouts  38.3 us (21%)
  starting transfers between devices  36.9 us (20%)
  matrix products  22.5 us (12%)
  other arithmetic  3.13 us (2%)
    ppermute x27, waiting for transfers between devices, shift(): return lax.ppermute(v, axis, [(i, (i + by) % n) for i in range(n)])  64.3 us
    ppermute x27, starting transfers between devices, shift(): return lax.ppermute(v, axis, [(i, (i + by) % n) for i in range(n)])  32.4 us
    dynamic_update_slice x13, local copies, waits for them, and re-layouts, put(): lax.dynamic_update_slice(buffer, piece.reshape((1,) * (buffer.ndim - piec...  18.5 us
    all_to_all x1, waiting for transfers between devices, exchange(): return lax.all_to_all(v, axis, split_axis=0, concat_axis=0, tiled=True)  18.5 us
    dot_general x4, matrix products, partial(): lax.dot_general(columns, acts, (((0,), (0,)), ((), ())), preferred_elemen...  13.4 us
    dot_general x1, matrix products, local(): lax.dot_general(after(tokens, far), weights, (((1,), (1,)), ((), ())), pr...  9.09 us
    all_to_all x1, starting transfers between devices, exchange(): return lax.all_to_all(v, axis, split_axis=0, concat_axis=0, tiled=True)  4.51 us
    broadcast_in_dim x1, local copies, waits for them, and re-layouts, local(): tokens = jnp.zeros((4, 2, toks, feats), BF16)  4.33 us
  transfers between devices with their start and end apart: 28, of which 10 were waited for; matrix products, arithmetic and copies ran while one was open for 33% of the time, Pallas kernels for 0%

profile of v12, /device:TPU:38, one launch (start us, length us, event | category | flops | bytes accessed | tf_op | source)
XLA Modules:
  0.0 184.5 jit_solution(17605553052582206139)
XLA Ops:
  0.7 3.1 %collective-permute-start.1 = (bf16[128,4096]{1,0:T(8,128)(2,1)}, bf16[128,4096]{1,0:T(8,128)(2,1)}, u32[]{:S(2)}, u32[]{:S(2)}) collective-permute-start(bf16[128,4096]{1,0:T(8,128)(2,1)} %bitcast.61), channel_id=1, source_target_pairs={{0,24},{8,0},{16,8},{24,16},{1,25},{9,1},{17,9},{25,17},{2,26},{10... | collective-permute-start | bytes 3145736 | tf_op jit(solution)/shard_map/ppermute | solution.py:12
  6.5 4.5 %all-to-all-start = ((bf16[8,128,512]{1,2,0:T(8,128)(2,1)}), bf16[8,128,512]{1,2,0:T(8,128)(2,1)S(1)}, u32[]{:S(2)}, u32[]{:S(2)}) async-start(bf16[8,128,512]{1,2,0:T(8,128)(2,1)} %bitcast.9), calls=%async_computation | async-start | bytes 2097152 | tf_op jit(solution)/shard_map/all_to_all | solution.py:16
  11.1 1.9 %collective-permute-start.9 = (bf16[128,4096]{1,0:T(8,128)(2,1)}, bf16[128,4096]{1,0:T(8,128)(2,1)S(1)}, u32[]{:S(2)}, u32[]{:S(2)}) collective-permute-start(bf16[128,4096]{1,0:T(8,128)(2,1)} %param.5), channel_id=1, source_target_pairs={{0,2},{2,4},{4,6},{6,32},{32,34},{34,36},{36,38},{38,0},{1,3},{3,5... | collective-permute-start | bytes 3145736 | tf_op jit(solution)/shard_map/ppermute | solution.py:12
  13.0 2.5 %broadcast_in_dim.14 = bf16[4,128,4096]{2,1,0:T(8,128)(2,1)} broadcast(bf16[]{:T(256)} %constant.17.clone.1), dimensions={} | broadcast | bytes 4194306 | tf_op jit(solution)/shard_map/broadcast_in_dim | solution.py:68
  15.5 2.3 %bitcast_dynamic-update-slice_fusion.2 = bf16[4,128,4096]{2,1,0:T(8,128)(2,1)} fusion(bf16[4,128,4096]{2,1,0:T(8,128)(2,1)} %broadcast_in_dim.14, s32[]{:T(128)S(6)} %select_n.98, bf16[128,4096]{1,0:T(8,128)(2,1)} %param.5), kind=kLoop, calls=%fused_computation.16 | loop fusion | bytes 2097156 | tf_op jit(solution)/shard_map/dynamic_update_slice | solution.py:29
  17.9 4.3 %broadcast_in_dim.13 = bf16[4,2,128,4096]{3,2,1,0:T(8,128)(2,1)} broadcast(bf16[]{:T(256)} %constant.17.clone.1), dimensions={} | broadcast | bytes 8388610 | tf_op jit(solution)/shard_map/broadcast_in_dim | solution.py:50
  23.2 18.5 %all-to-all-done = bf16[8,128,512]{1,2,0:T(8,128)(2,1)S(1)} async-done(((bf16[8,128,512]{1,2,0:T(8,128)(2,1)}), bf16[8,128,512]{1,2,0:T(8,128)(2,1)S(1)}, u32[]{:S(2)}, u32[]{:S(2)}) %all-to-all-start) | async-done | bytes 1048608 | tf_op jit(solution)/shard_map/all_to_all | solution.py:16
  45.5 1.8 collective-permute-start.6
  47.6 2.0 %collective-permute-start.11 = (bf16[64,4096]{1,0:T(8,128)(2,1)S(1)}, bf16[64,4096]{1,0:T(8,128)(2,1)S(1)}, u32[]{:S(2)}, u32[]{:S(2)}) collective-permute-start(bf16[64,4096]{1,0:T(8,128)(2,1)S(1)} %slice.35), channel_id=1, source_target_pairs={{0,2},{2,4},{4,6},{6,32},{32,34},{34,36},{36,38},{38,0},{1,3},{3,5... | collective-permute-start | bytes 1572872 | tf_op jit(solution)/shard_map/ppermute | solution.py:12
  49.6 2.3 %bitcast_dynamic-update-slice_fusion.9 = bf16[4,2,128,4096]{3,2,1,0:T(8,128)(2,1)} fusion(bf16[4,2,128,4096]{3,2,1,0:T(8,128)(2,1)} %bitcast_dynamic-update-slice_fusion.10, s32[]{:T(128)S(6)} %select_n.91, s32[]{:T(128)S(6)} %select_n.93, bf16[128,4096]{1,0:T(8,128)(2,1)} %collective-permute-done), kind=kLoop, calls=%fused_computation.23 | loop fusion | bytes 2097160 | tf_op jit(solution)/shard_map/dynamic_update_slice | solution.py:29
  51.9 2.3 %bitcast_dynamic-update-slice_fusion.8 = bf16[4,2,128,4096]{3,2,1,0:T(8,128)(2,1)} fusion(bf16[4,2,128,4096]{3,2,1,0:T(8,128)(2,1)} %bitcast_dynamic-update-slice_fusion.9, s32[]{:T(128)S(6)} %select_n.94, s32[]{:T(128)S(6)} %select_n.92, bf16[128,4096]{1,0:T(8,128)(2,1)} %collective-permute-done.1), kind=kLoop, calls=%fused_computation.22 | loop fusion | bytes 2097160 | tf_op jit(solution)/shard_map/dynamic_update_slice | solution.py:29
  56.9 1.8 collective-permute-done.6
  60.1 2.4 %bitcast_dynamic-update-slice_fusion.6 = bf16[4,2,128,4096]{3,2,1,0:T(8,128)(2,1)} fusion(bf16[4,2,128,4096]{3,2,1,0:T(8,128)(2,1)} %bitcast_dynamic-update-slice_fusion.7, s32[]{:T(128)S(6)} %select_n.95, s32[]{:T(128)S(6)} %select_n.92, bf16[128,4096]{1,0:T(8,128)(2,1)} %collective-permute-done.3), kind=kLoop, calls=%fused_computation.20 | loop fusion | bytes 2097160 | tf_op jit(solution)/shard_map/dynamic_update_slice | solution.py:29
  65.8 2.9 %fusion.8 = bf16[1024,512]{1,0:T(8,128)(2,1)S(1)} fusion(bf16[1024,512]{1,0:T(8,128)(2,1)S(1)} %bitcast.55, bf16[1024,4096]{1,0:T(8,128)(2,1)} %bitcast.13, s32[]{:T(128)S(6)} %select_n.97), kind=kOutput, calls=%fused_computation.12 | convolution fusion | flops 1074266112 | bytes 4194308 | tf_op jit(solution)/shard_map/dot_general | solution.py:58
  69.7 2.4 %collective-permute-start.16 = (bf16[512,512]{1,0:T(8,128)(2,1)S(1)}, bf16[512,512]{1,0:T(8,128)(2,1)S(1)}, u32[]{:S(2)}, u32[]{:S(2)}) collective-permute-start(bf16[512,512]{1,0:T(8,128)(2,1)S(1)} %get-tuple-element.26), channel_id=1, source_target_pairs={{0,64},{64,128},{128,192},{192,0},{1,65},{65,129},{129,193},{193,1... | collective-permute-start | bytes 1572872 | tf_op jit(solution)/shard_map/ppermute | solution.py:12
  73.8 9.1 %convolution_convert_fusion = bf16[1024,512]{1,0:T(8,128)(2,1)S(1)} fusion(bf16[1024,4096]{1,0:T(8,128)(2,1)} %bitcast.13, bf16[512,4096]{1,0:T(8,128)(2,1)} %bitcast.19), kind=kOutput, calls=%fused_computation.11 | convolution fusion | flops 4295491584 | bytes 13631488 | tf_op jit(solution)/shard_map/dot_general | solution.py:77
  83.7 3.8 %add_convert_fusion.1 = bf16[1024,512]{1,0:T(8,128)(2,1)} fusion(bf16[512,512]{1,0:T(8,128)(2,1)S(1)} %collective-permute-done.16, bf16[1024,512]{1,0:T(8,128)(2,1)S(1)} %bitcast.56, bf16[1024,4096]{1,0:T(8,128)(2,1)} %bitcast.13, s32[]{:T(128)S(6)} %select_n.111), kind=kOutput, calls=%fused_computation.1 | convolution fusion | flops 1075314688 | bytes 4718596 | tf_op jit(solution)/shard_map/dot_general | solution.py:58
  87.6 3.6 %collective-permute-start.17 = (bf16[1024,512]{1,0:T(8,128)(2,1)}, bf16[1024,512]{1,0:T(8,128)(2,1)}, u32[]{:S(2)}, u32[]{:S(2)}) collective-permute-start(bf16[1024,512]{1,0:T(8,128)(2,1)} %add_convert_fusion.1), channel_id=1, source_target_pairs={{0,64},{64,128},{128,192},{192,0},{1,65},{65,129},{129,193},{193,1... | collective-permute-start | bytes 3145736 | tf_op jit(solution)/shard_map/ppermute | solution.py:12
  91.2 3.8 %add_convert_fusion.2 = bf16[1024,512]{1,0:T(8,128)(2,1)} fusion(bf16[512,512]{1,0:T(8,128)(2,1)S(1)} %collective-permute-done.15, bf16[1024,512]{1,0:T(8,128)(2,1)S(1)} %bitcast.57, bf16[1024,4096]{1,0:T(8,128)(2,1)} %bitcast.13, s32[]{:T(128)S(6)} %select_n.109), kind=kOutput, calls=%fused_computation.6 | convolution fusion | flops 1075314688 | bytes 4718596 | tf_op jit(solution)/shard_map/dot_general | solution.py:58
  95.0 2.9 %fusion.11 = bf16[1024,512]{1,0:T(8,128)(2,1)S(1)} fusion(bf16[1024,512]{1,0:T(8,128)(2,1)S(1)} %bitcast.58, bf16[1024,4096]{1,0:T(8,128)(2,1)} %bitcast.13, s32[]{:T(128)S(6)} %select_n.110), kind=kOutput, calls=%fused_computation.13 | convolution fusion | flops 1074266112 | bytes 4194308 | tf_op jit(solution)/shard_map/dot_general | solution.py:58
  97.9 15.6 %collective-permute-done.17 = bf16[1024,512]{1,0:T(8,128)(2,1)} collective-permute-done((bf16[1024,512]{1,0:T(8,128)(2,1)}, bf16[1024,512]{1,0:T(8,128)(2,1)}, u32[]{:S(2)}, u32[]{:S(2)}) %collective-permute-start.17) | collective-permute-done | bytes 1048608 | tf_op jit(solution)/shard_map/ppermute | solution.py:12
  113.5 7.3 %collective-permute-done.18 = bf16[1024,512]{1,0:T(8,128)(2,1)} collective-permute-done((bf16[1024,512]{1,0:T(8,128)(2,1)}, bf16[1024,512]{1,0:T(8,128)(2,1)}, u32[]{:S(2)}, u32[]{:S(2)}) %collective-permute-start.18) | collective-permute-done | bytes 1048608 | tf_op jit(solution)/shard_map/ppermute | solution.py:12
  120.8 2.0 %add_convert_fusion = bf16[1024,512]{1,0:T(8,128)(2,1)S(1)} fusion(bf16[1024,512]{1,0:T(8,128)(2,1)} %collective-permute-done.18, bf16[1024,512]{1,0:T(8,128)(2,1)} %collective-permute-done.17, bf16[1024,512]{1,0:T(8,128)(2,1)S(1)} %fusion.11), kind=kLoop, calls=%fused_computation | loop fusion | flops 3145728 | bytes 4194304 | tf_op jit(solution)/shard_map/convert_element_type | solution.py:91
  123.5 1.9 %collective-permute-start.19 = (bf16[1024,128]{1,0:T(8,128)(2,1)}, bf16[1024,128]{1,0:T(8,128)(2,1)S(1)}, u32[]{:S(2)}, u32[]{:S(2)}) collective-permute-start(bf16[1024,128]{1,0:T(8,128)(2,1)} %get-tuple-element.24), channel_id=1, source_target_pairs={{0,2},{2,4},{4,6},{6,32},{32,34},{34,36},{36,38},{38,0},{1,3},{3,5... | collective-permute-start | bytes 786440 | tf_op jit(solution)/shard_map/ppermute | solution.py:12
  125.8 5.3 %collective-permute-start.21 = (bf16[512,128]{1,0:T(8,128)(2,1)S(1)}, bf16[512,128]{1,0:T(8,128)(2,1)S(1)}, u32[]{:S(2)}, u32[]{:S(2)}) collective-permute-start(bf16[512,128]{1,0:T(8,128)(2,1)S(1)} %get-tuple-element.22), channel_id=1, source_target_pairs={{0,36},{2,38},{4,0},{6,2},{32,4},{34,6},{36,32},{38,34},{1,37},{3,... | collective-permute-start | bytes 393224 | tf_op jit(solution)/shard_map/ppermute | solution.py:12
  131.9 2.3 %collective-permute-start.12 = (bf16[1024,128]{1,0:T(8,128)(2,1)}, bf16[1024,128]{1,0:T(8,128)(2,1)}, u32[]{:S(2)}, u32[]{:S(2)}) collective-permute-start(bf16[1024,128]{1,0:T(8,128)(2,1)} %get-tuple-element.30), channel_id=1, source_target_pairs={{0,2},{2,4},{4,6},{6,0},{1,3},{3,5},{5,7},{7,1},{8,10},{10,12},{12... | collective-permute-start | bytes 786440 | tf_op jit(solution)/shard_map/ppermute | solution.py:12
  134.2 8.5 %collective-permute-done.21 = bf16[512,128]{1,0:T(8,128)(2,1)S(1)} collective-permute-done((bf16[512,128]{1,0:T(8,128)(2,1)S(1)}, bf16[512,128]{1,0:T(8,128)(2,1)S(1)}, u32[]{:S(2)}, u32[]{:S(2)}) %collective-permute-start.21) | collective-permute-done | bytes 131104 | tf_op jit(solution)/shard_map/ppermute | solution.py:12
  143.9 3.2 %collective-permute-start.23 = (bf16[1024,128]{1,0:T(8,128)(2,1)S(1)}, bf16[1024,128]{1,0:T(8,128)(2,1)S(1)}, u32[]{:S(2)}, u32[]{:S(2)}) collective-permute-start(bf16[1024,128]{1,0:T(8,128)(2,1)S(1)} %add_convert_fusion.4), channel_id=1, source_target_pairs={{0,32},{32,0},{1,33},{33,1},{2,34},{34,2},{3,35},{35,3},{4,36},{36... | collective-permute-start | bytes 786440 | tf_op jit(solution)/shard_map/ppermute | solution.py:12
  149.0 10.8 %collective-permute-done.23 = bf16[1024,128]{1,0:T(8,128)(2,1)S(1)} collective-permute-done((bf16[1024,128]{1,0:T(8,128)(2,1)S(1)}, bf16[1024,128]{1,0:T(8,128)(2,1)S(1)}, u32[]{:S(2)}, u32[]{:S(2)}) %collective-permute-start.23) | collective-permute-done | bytes 262176 | tf_op jit(solution)/shard_map/ppermute | solution.py:12
  161.3 8.3 %collective-permute-done.13 = bf16[1024,128]{1,0:T(8,128)(2,1)S(1)} collective-permute-done((bf16[1024,128]{1,0:T(8,128)(2,1)S(1)}, bf16[1024,128]{1,0:T(8,128)(2,1)S(1)}, u32[]{:S(2)}, u32[]{:S(2)}) %collective-permute-start.13) | collective-permute-done | bytes 262176 | tf_op jit(solution)/shard_map/ppermute | solution.py:12
  169.6 4.1 %collective-permute-done.14 = bf16[1024,128]{1,0:T(8,128)(2,1)S(1)} collective-permute-done((bf16[1024,128]{1,0:T(8,128)(2,1)S(1)}, bf16[1024,128]{1,0:T(8,128)(2,1)S(1)}, u32[]{:S(2)}, u32[]{:S(2)}) %collective-permute-start.14) | collective-permute-done | bytes 262176 | tf_op jit(solution)/shard_map/ppermute | solution.py:12
  176.3 7.0 %collective-permute-done.26 = bf16[128,1024]{0,1:T(8,128)(2,1)S(1)} collective-permute-done((bf16[128,1024]{0,1:T(8,128)(2,1)S(1)}, bf16[128,1024]{0,1:T(8,128)(2,1)S(1)}, u32[]{:S(2)}, u32[]{:S(2)}) %collective-permute-start.26) | collective-permute-done | bytes 262176 | tf_op jit(solution)/shard_map/ppermute | solution.py:12
  (82 shorter events, 29.2 us)
Async XLA Ops:
  0.6 49.0 %collective-permute-start = (bf16[128,4096]{1,0:T(8,128)(2,1)}, bf16[128,4096]{1,0:T(8,128)(2,1)}, u32[]{:S(2)}, u32[]{:S(2)}) collective-permute-start(bf16[128,4096]{1,0:T(8,128)(2,1)} %bitcast.60), channel_id=1, source_target_pairs={{0,1},{1,0},{2,3},{3,2},{4,5},{5,4},{6,7},{7,6},{8,9},{9,8},{10,11... | collective-permute-start | bytes 3145736 | tf_op jit(solution)/shard_map/ppermute | solution.py:12
  0.7 42.3 %collective-permute-start.1 = (bf16[128,4096]{1,0:T(8,128)(2,1)}, bf16[128,4096]{1,0:T(8,128)(2,1)}, u32[]{:S(2)}, u32[]{:S(2)}) collective-permute-start(bf16[128,4096]{1,0:T(8,128)(2,1)} %bitcast.61), channel_id=1, source_target_pairs={{0,24},{8,0},{16,8},{24,16},{1,25},{9,1},{17,9},{25,17},{2,26},{10... | collective-permute-start | bytes 3145736 | tf_op jit(solution)/shard_map/ppermute | solution.py:12
  3.8 40.6 %collective-permute-start.3 = (bf16[128,4096]{1,0:T(8,128)(2,1)}, bf16[128,4096]{1,0:T(8,128)(2,1)}, u32[]{:S(2)}, u32[]{:S(2)}) collective-permute-start(bf16[128,4096]{1,0:T(8,128)(2,1)} %bitcast.62), channel_id=1, source_target_pairs={{0,8},{8,16},{16,24},{24,0},{1,9},{9,17},{17,25},{25,1},{2,10},{10... | collective-permute-start | bytes 3145736 | tf_op jit(solution)/shard_map/ppermute | solution.py:12
  6.5 35.2 %all-to-all-start = ((bf16[8,128,512]{1,2,0:T(8,128)(2,1)}), bf16[8,128,512]{1,2,0:T(8,128)(2,1)S(1)}, u32[]{:S(2)}, u32[]{:S(2)}) async-start(bf16[8,128,512]{1,2,0:T(8,128)(2,1)} %bitcast.9), calls=%async_computation | async-start | bytes 2097152 | tf_op jit(solution)/shard_map/all_to_all | solution.py:16
  11.0 36.4 %collective-permute-start.8 = (bf16[128,4096]{1,0:T(8,128)(2,1)}, bf16[128,4096]{1,0:T(8,128)(2,1)S(1)}, u32[]{:S(2)}, u32[]{:S(2)}) collective-permute-start(bf16[128,4096]{1,0:T(8,128)(2,1)} %param.5), channel_id=1, source_target_pairs={{0,38},{2,0},{4,2},{6,4},{32,6},{34,32},{36,34},{38,36},{1,39},{3,... | collective-permute-start | bytes 3145736 | tf_op jit(solution)/shard_map/ppermute | solution.py:12
  11.1 36.5 %collective-permute-start.9 = (bf16[128,4096]{1,0:T(8,128)(2,1)}, bf16[128,4096]{1,0:T(8,128)(2,1)S(1)}, u32[]{:S(2)}, u32[]{:S(2)}) collective-permute-start(bf16[128,4096]{1,0:T(8,128)(2,1)} %param.5), channel_id=1, source_target_pairs={{0,2},{2,4},{4,6},{6,32},{32,34},{34,36},{36,38},{38,0},{1,3},{3,5... | collective-permute-start | bytes 3145736 | tf_op jit(solution)/shard_map/ppermute | solution.py:12
  17.9 4.3 %copy-start.3 = (bf16[1,128,4096]{2,1,0:T(8,128)(2,1)S(1)}, bf16[1,128,4096]{2,1,0:T(8,128)(2,1)}, u32[]{:S(2)}) copy-start(bf16[1,128,4096]{2,1,0:T(8,128)(2,1)} %param.3) | copy-start | bytes 3145732
  44.1 12.2 %collective-permute-start.5 = (bf16[64,4096]{1,0:T(8,128)(2,1)S(1)}, bf16[64,4096]{1,0:T(8,128)(2,1)S(1)}, u32[]{:S(2)}, u32[]{:S(2)}) collective-permute-start(bf16[64,4096]{1,0:T(8,128)(2,1)S(1)} %slice.32), channel_id=1, source_target_pairs={{0,24},{8,0},{16,8},{24,16},{1,25},{9,1},{17,9},{25,17},{2,26},{10... | collective-permute-start | bytes 1572872 | tf_op jit(solution)/shard_map/ppermute | solution.py:12
  45.5 13.2 %collective-permute-start.6 = (bf16[64,4096]{1,0:T(8,128)(2,1)S(1)}, bf16[64,4096]{1,0:T(8,128)(2,1)S(1)}, u32[]{:S(2)}, u32[]{:S(2)}) collective-permute-start(bf16[64,4096]{1,0:T(8,128)(2,1)S(1)} %slice.33), channel_id=1, source_target_pairs={{0,8},{8,16},{16,24},{24,0},{1,9},{9,17},{17,25},{25,1},{2,10},{10... | collective-permute-start | bytes 1572872 | tf_op jit(solution)/shard_map/ppermute | solution.py:12
  47.4 21.3 %collective-permute-start.10 = (bf16[64,4096]{1,0:T(8,128)(2,1)S(1)}, bf16[64,4096]{1,0:T(8,128)(2,1)S(1)}, u32[]{:S(2)}, u32[]{:S(2)}) collective-permute-start(bf16[64,4096]{1,0:T(8,128)(2,1)S(1)} %slice.34), channel_id=1, source_target_pairs={{0,38},{2,0},{4,2},{6,4},{32,6},{34,32},{36,34},{38,36},{1,39},{3,... | collective-permute-start | bytes 1572872 | tf_op jit(solution)/shard_map/ppermute | solution.py:12
  47.6 21.2 %collective-permute-start.11 = (bf16[64,4096]{1,0:T(8,128)(2,1)S(1)}, bf16[64,4096]{1,0:T(8,128)(2,1)S(1)}, u32[]{:S(2)}, u32[]{:S(2)}) collective-permute-start(bf16[64,4096]{1,0:T(8,128)(2,1)S(1)} %slice.35), channel_id=1, source_target_pairs={{0,2},{2,4},{4,6},{6,32},{32,34},{34,36},{36,38},{38,0},{1,3},{3,5... | collective-permute-start | bytes 1572872 | tf_op jit(solution)/shard_map/ppermute | solution.py:12
  49.6 9.4 %collective-permute-start.2 = (bf16[128,4096]{1,0:T(8,128)(2,1)}, bf16[128,4096]{1,0:T(8,128)(2,1)S(1)}, u32[]{:S(2)}, u32[]{:S(2)}) collective-permute-start(bf16[128,4096]{1,0:T(8,128)(2,1)} %collective-permute-done.1), channel_id=1, source_target_pairs={{0,1},{1,0},{2,3},{3,2},{4,5},{5,4},{6,7},{7,6},{8,9},{9,8},{10,11... | collective-permute-start | bytes 3145736 | tf_op jit(solution)/shard_map/ppermute | solution.py:12
  56.3 6.1 %collective-permute-start.4 = (bf16[128,4096]{1,0:T(8,128)(2,1)}, bf16[128,4096]{1,0:T(8,128)(2,1)S(1)}, u32[]{:S(2)}, u32[]{:S(2)}) collective-permute-start(bf16[128,4096]{1,0:T(8,128)(2,1)} %collective-permute-done.3), channel_id=1, source_target_pairs={{0,1},{1,0},{2,3},{3,2},{4,5},{5,4},{6,7},{7,6},{8,9},{9,8},{10,11... | collective-permute-start | bytes 3145736 | tf_op jit(solution)/shard_map/ppermute | solution.py:12
  58.8 6.0 %collective-permute-start.7 = (bf16[128,4096]{1,0:T(8,128)(2,1)S(1)}, bf16[128,4096]{1,0:T(8,128)(2,1)S(1)}, u32[]{:S(2)}, u32[]{:S(2)}) collective-permute-start(bf16[128,4096]{1,0:T(8,128)(2,1)S(1)} %constant_dynamic-update-slice_fusion.8), channel_id=1, source_target_pairs={{0,1},{1,0},{2,3},{3,2},{4,5},{5,4},{6,7},{7,6},{8,9},{9,8},{10,11... | collective-permute-start | bytes 3145736 | tf_op jit(solution)/shard_map/ppermute | solution.py:12
  60.1 5.7 %copy-start = (bf16[8,128,512]{2,1,0:T(8,128)(2,1)S(1)}, bf16[8,128,512]{2,1,0:T(8,128)(2,1)}, u32[]{:S(2)}) copy-start(bf16[8,128,512]{2,1,0:T(8,128)(2,1)} %copy.21) | copy-start | bytes 3145732
  68.8 22.4 %collective-permute-start.15 = (bf16[512,512]{1,0:T(8,128)(2,1)S(1)}, bf16[512,512]{1,0:T(8,128)(2,1)S(1)}, u32[]{:S(2)}, u32[]{:S(2)}) collective-permute-start(bf16[512,512]{1,0:T(8,128)(2,1)S(1)} %get-tuple-element.27), channel_id=1, source_target_pairs={{0,192},{64,0},{128,64},{192,128},{1,193},{65,1},{129,65},{193,129... | collective-permute-start | bytes 1572872 | tf_op jit(solution)/shard_map/ppermute | solution.py:12
  69.7 14.0 %collective-permute-start.16 = (bf16[512,512]{1,0:T(8,128)(2,1)S(1)}, bf16[512,512]{1,0:T(8,128)(2,1)S(1)}, u32[]{:S(2)}, u32[]{:S(2)}) collective-permute-start(bf16[512,512]{1,0:T(8,128)(2,1)S(1)} %get-tuple-element.26), channel_id=1, source_target_pairs={{0,64},{64,128},{128,192},{192,0},{1,65},{65,129},{129,193},{193,1... | collective-permute-start | bytes 1572872 | tf_op jit(solution)/shard_map/ppermute | solution.py:12
  87.6 25.9 %collective-permute-start.17 = (bf16[1024,512]{1,0:T(8,128)(2,1)}, bf16[1024,512]{1,0:T(8,128)(2,1)}, u32[]{:S(2)}, u32[]{:S(2)}) collective-permute-start(bf16[1024,512]{1,0:T(8,128)(2,1)} %add_convert_fusion.1), channel_id=1, source_target_pairs={{0,64},{64,128},{128,192},{192,0},{1,65},{65,129},{129,193},{193,1... | collective-permute-start | bytes 3145736 | tf_op jit(solution)/shard_map/ppermute | solution.py:12
  95.0 25.7 %collective-permute-start.18 = (bf16[1024,512]{1,0:T(8,128)(2,1)}, bf16[1024,512]{1,0:T(8,128)(2,1)}, u32[]{:S(2)}, u32[]{:S(2)}) collective-permute-start(bf16[1024,512]{1,0:T(8,128)(2,1)} %add_convert_fusion.2), channel_id=1, source_target_pairs={{0,192},{64,0},{128,64},{192,128},{1,193},{65,1},{129,65},{193,129... | collective-permute-start | bytes 3145736 | tf_op jit(solution)/shard_map/ppermute | solution.py:12
  123.5 19.3 %collective-permute-start.19 = (bf16[1024,128]{1,0:T(8,128)(2,1)}, bf16[1024,128]{1,0:T(8,128)(2,1)S(1)}, u32[]{:S(2)}, u32[]{:S(2)}) collective-permute-start(bf16[1024,128]{1,0:T(8,128)(2,1)} %get-tuple-element.24), channel_id=1, source_target_pairs={{0,2},{2,4},{4,6},{6,32},{32,34},{34,36},{36,38},{38,0},{1,3},{3,5... | collective-permute-start | bytes 786440 | tf_op jit(solution)/shard_map/ppermute | solution.py:12
  125.4 17.3 %collective-permute-start.20 = (bf16[1024,128]{1,0:T(8,128)(2,1)S(1)}, bf16[1024,128]{1,0:T(8,128)(2,1)}, u32[]{:S(2)}, u32[]{:S(2)}) collective-permute-start(bf16[1024,128]{1,0:T(8,128)(2,1)S(1)} %get-tuple-element.25), channel_id=1, source_target_pairs={{0,38},{2,0},{4,2},{6,4},{32,6},{34,32},{36,34},{38,36},{1,39},{3,... | collective-permute-start | bytes 786440 | tf_op jit(solution)/shard_map/ppermute | solution.py:12
  125.8 17.0 %collective-permute-start.21 = (bf16[512,128]{1,0:T(8,128)(2,1)S(1)}, bf16[512,128]{1,0:T(8,128)(2,1)S(1)}, u32[]{:S(2)}, u32[]{:S(2)}) collective-permute-start(bf16[512,128]{1,0:T(8,128)(2,1)S(1)} %get-tuple-element.22), channel_id=1, source_target_pairs={{0,36},{2,38},{4,0},{6,2},{32,4},{34,6},{36,32},{38,34},{1,37},{3,... | collective-permute-start | bytes 393224 | tf_op jit(solution)/shard_map/ppermute | solution.py:12
  131.1 11.7 %collective-permute-start.22 = (bf16[512,128]{1,0:T(8,128)(2,1)S(1)}, bf16[512,128]{1,0:T(8,128)(2,1)S(1)}, u32[]{:S(2)}, u32[]{:S(2)}) collective-permute-start(bf16[512,128]{1,0:T(8,128)(2,1)S(1)} %get-tuple-element.23), channel_id=1, source_target_pairs={{0,4},{2,6},{4,32},{6,34},{32,36},{34,38},{36,0},{38,2},{1,5},{3,7... | collective-permute-start | bytes 393224 | tf_op jit(solution)/shard_map/ppermute | solution.py:12
  131.9 16.1 %collective-permute-start.12 = (bf16[1024,128]{1,0:T(8,128)(2,1)}, bf16[1024,128]{1,0:T(8,128)(2,1)}, u32[]{:S(2)}, u32[]{:S(2)}) collective-permute-start(bf16[1024,128]{1,0:T(8,128)(2,1)} %get-tuple-element.30), channel_id=1, source_target_pairs={{0,2},{2,4},{4,6},{6,0},{1,3},{3,5},{5,7},{7,1},{8,10},{10,12},{12... | collective-permute-start | bytes 786440 | tf_op jit(solution)/shard_map/ppermute | solution.py:12
  143.9 16.0 %collective-permute-start.23 = (bf16[1024,128]{1,0:T(8,128)(2,1)S(1)}, bf16[1024,128]{1,0:T(8,128)(2,1)S(1)}, u32[]{:S(2)}, u32[]{:S(2)}) collective-permute-start(bf16[1024,128]{1,0:T(8,128)(2,1)S(1)} %add_convert_fusion.4), channel_id=1, source_target_pairs={{0,32},{32,0},{1,33},{33,1},{2,34},{34,2},{3,35},{35,3},{4,36},{36... | collective-permute-start | bytes 786440 | tf_op jit(solution)/shard_map/ppermute | solution.py:12
  147.0 22.5 %collective-permute-start.13 = (bf16[1024,128]{1,0:T(8,128)(2,1)S(1)}, bf16[1024,128]{1,0:T(8,128)(2,1)S(1)}, u32[]{:S(2)}, u32[]{:S(2)}) collective-permute-start(bf16[1024,128]{1,0:T(8,128)(2,1)S(1)} %get-tuple-element.29), channel_id=1, source_target_pairs={{0,4},{2,6},{4,0},{6,2},{1,5},{3,7},{5,1},{7,3},{8,12},{10,14},{12... | collective-permute-start | bytes 786440 | tf_op jit(solution)/shard_map/ppermute | solution.py:12
  147.8 25.9 %collective-permute-start.14 = (bf16[1024,128]{1,0:T(8,128)(2,1)S(1)}, bf16[1024,128]{1,0:T(8,128)(2,1)S(1)}, u32[]{:S(2)}, u32[]{:S(2)}) collective-permute-start(bf16[1024,128]{1,0:T(8,128)(2,1)S(1)} %get-tuple-element.28), channel_id=1, source_target_pairs={{0,6},{2,0},{4,2},{6,4},{1,7},{3,1},{5,3},{7,5},{8,14},{10,8},{12,... | collective-permute-start | bytes 786440 | tf_op jit(solution)/shard_map/ppermute | solution.py:12
  159.9 14.1 %collective-permute-start.24 = (bf16[128,1024]{0,1:T(8,128)(2,1)S(1)}, bf16[128,1024]{0,1:T(8,128)(2,1)}, u32[]{:S(2)}, u32[]{:S(2)}) collective-permute-start(bf16[128,1024]{0,1:T(8,128)(2,1)S(1)} %fusion.14), channel_id=1, source_target_pairs={{0,64},{64,128},{128,192},{192,0},{1,65},{65,129},{129,193},{193,1... | collective-permute-start | bytes 786440 | tf_op jit(solution)/shard_map/ppermute | solution.py:12
  160.0 15.2 %collective-permute-start.25 = (bf16[128,1024]{0,1:T(8,128)(2,1)S(1)}, bf16[128,1024]{0,1:T(8,128)(2,1)}, u32[]{:S(2)}, u32[]{:S(2)}) collective-permute-start(bf16[128,1024]{0,1:T(8,128)(2,1)S(1)} %fusion.14), channel_id=1, source_target_pairs={{0,128},{64,192},{128,0},{192,64},{1,129},{65,193},{129,1},{193,65... | collective-permute-start | bytes 786440 | tf_op jit(solution)/shard_map/ppermute | solution.py:12
  173.7 9.9 %copy-start.2 = (bf16[4,4,256,128]{3,2,1,0:T(8,128)(2,1)}, bf16[4,4,256,128]{3,2,1,0:T(8,128)(2,1)S(1)}, u32[]{:S(2)}) copy-start(bf16[4,4,256,128]{3,2,1,0:T(8,128)(2,1)S(1)} %constant_dynamic-update-slice_fusion.4) | copy-start | bytes 3145732
  173.8 9.5 %collective-permute-start.26 = (bf16[128,1024]{0,1:T(8,128)(2,1)S(1)}, bf16[128,1024]{0,1:T(8,128)(2,1)S(1)}, u32[]{:S(2)}, u32[]{:S(2)}) collective-permute-start(bf16[128,1024]{0,1:T(8,128)(2,1)S(1)} %fusion.14), channel_id=1, source_target_pairs={{0,192},{64,0},{128,64},{192,128},{1,193},{65,1},{129,65},{193,129... | collective-permute-start | bytes 786440 | tf_op jit(solution)/shard_map/ppermute | solution.py:12
  183.5 1.0 copy-start.1
